TPU v7x, 32 devices: a whole 2x2x4 slice. The times are simulated.
32 devices in a mesh: row: 8 (over y, x, core), col: 4 (over z).
Axes of the slice: x: 2, y: 2, z: 4, core: 2. Of those that a mesh axis runs over, the one named last changes fastest.
Arguments:
- tokens_in: bfloat16 [32768, 1024], P('row', 'col'), may hold values from -36 to 36
- pad_offsets: int32 [8, 2], P('row'), may hold values from 0 to 6
- norm1_gain: float32 [1024], P('col'), may hold values from 0.5 to 1.5
- norm1_bias: float32 [1024], P('col'), may hold values from -1.25 to 1.25
- qkv_weight: bfloat16 [1024, 3, 1024], P('row', None, 'col'), may hold values from -0.1875 to 0.1875
- qv_bias: bfloat16 [2, 1024], P(None, 'col'), may hold values from -1.75 to 1.75
- table_height: float32 [27, 64], replicated, may hold values from -0.875 to 0.875
- table_width: float32 [27, 64], replicated, may hold values from -0.875 to 0.875
- proj_weight: bfloat16 [1024, 1024], P('col', 'row'), may hold values from -0.5 to 0.5
- proj_bias: bfloat16 [1024], P('col'), may hold values from -1.75 to 1.75
- norm2_gain: float32 [1024], P('col'), may hold values from 0.5 to 1.5
- norm2_bias: float32 [1024], P('col'), may hold values from -1.25 to 1.25
- fc1_weight: bfloat16 [1024, 4096], P('row', 'col'), may hold values from -0.1875 to 0.1875
- fc1_bias: bfloat16 [4096], P('col'), may hold values from -1.75 to 1.75
- fc2_weight: bfloat16 [4096, 1024], P('col', 'row'), may hold values from -0.09375 to 0.09375
- fc2_bias: bfloat16 [1024], P('col'), may hold values from -1.75 to 1.75
- out_grad: bfloat16 [32768, 1024], P('row', 'col'), may hold values from -8 to 8
Outputs:
- block_out: bfloat16 [32768, 1024], P('row', 'col')
- input_grad: float32 [32768, 1024], P('row', 'col')
- norm1_gain_grad: float32 [1024], P('col')
- norm1_bias_grad: float32 [1024], P('col')
- qkv_weight_grad: float32 [1024, 3, 1024], P('row', None, 'col')
- qv_bias_grad: float32 [2, 1024], P(None, 'col')
- table_height_grad: float32 [27, 64], replicated
- table_width_grad: float32 [27, 64], replicated
- proj_weight_grad: float32 [1024, 1024], P('col', 'row')
- proj_bias_grad: float32 [1024], P('col')
- norm2_gain_grad: float32 [1024], P('col')
- norm2_bias_grad: float32 [1024], P('col')
- fc1_weight_grad: float32 [1024, 4096], P('row', 'col')
- fc1_bias_grad: float32 [4096], P('col')
- fc2_weight_grad: float32 [4096, 1024], P('col', 'row')
- fc2_bias_grad: float32 [1024], P('col')
All inputs are finite; a program needn't handle non-finite values.
Results may differ from a plain program's by a relative error of at most 0.012.
The roundings to bfloat16 on the way count: a program that leaves them out, or rounds other values in their place, can miss the bound.
Values may be sent and summed in bfloat16 or wider, within the bound.
No kernel may reach another device: no remote copies, remote signals or barrier semaphores. Data moves between devices by JAX's collectives and lax.ppermute only.
A program may use at most 256 MiB of HBM per device.

v0:
```python
from functools import partial
import math

import jax
import jax.numpy as jnp
from jax import lax
from jax.sharding import PartitionSpec as P

D = 1024
HD = 64
WIN = 14
SIDE = 64
GRID = 5
SLOTS = 4900
PIX = 4096


EPSILON = 1e-06
HIGHEST = lax.Precision.HIGHEST


def slot_layout(offsets):
    top_row = offsets[0]
    left_col = offsets[1]
    slot_ids = jnp.arange(SLOTS, dtype=jnp.int32)
    window = slot_ids // (WIN * WIN)
    inside = slot_ids % (WIN * WIN)
    canvas_row = window // GRID * WIN + inside // WIN - top_row
    canvas_col = window % GRID * WIN + inside % WIN - left_col
    present = (canvas_row >= 0) & (canvas_row < SIDE) & (canvas_col >= 0) & (canvas_col < SIDE)
    source = jnp.clip(canvas_row, 0, SIDE - 1) * SIDE + jnp.clip(canvas_col, 0, SIDE - 1)
    pixels = jnp.arange(PIX, dtype=jnp.int32)
    pixel_row = pixels // SIDE + top_row
    pixel_col = pixels % SIDE + left_col
    target = (
        (pixel_row // WIN * GRID + pixel_col // WIN) * WIN + pixel_row % WIN
    ) * WIN + pixel_col % WIN
    return (source, present, target)


def pick_tables():
    places = jnp.arange(WIN * WIN, dtype=jnp.int32)
    others = jnp.arange(WIN, dtype=jnp.int32)
    rel_index = jnp.arange(2 * WIN - 1, dtype=jnp.int32)
    pick_h = (
        (places // WIN)[:, None, None] - others[None, :, None] + WIN - 1 == rel_index[None, None, :]
    ).astype(jnp.float32)
    pick_w = (
        (places % WIN)[:, None, None] - others[None, :, None] + WIN - 1 == rel_index[None, None, :]
    ).astype(jnp.float32)
    return (pick_h, pick_w)


def feature_moments(first, second):
    return lax.psum((first, second), "col")


def norm_forward(values, gain_vec, bias_vec):
    sum_one, square = feature_moments(jnp.sum(values, axis=1), jnp.sum(values * values, axis=1))
    row_mean = sum_one / D
    spread = square / D - row_mean * row_mean
    inv_std = lax.rsqrt(spread + EPSILON)
    x_hat = (values - row_mean[:, None]) * inv_std[:, None]
    return (x_hat * gain_vec + bias_vec, x_hat, inv_std)


def norm_backward(grad_in, x_hat, inv_std, gain_vec):
    scaled = grad_in * gain_vec
    sum_one, cross_sum = feature_moments(jnp.sum(scaled, axis=1), jnp.sum(scaled * x_hat, axis=1))
    back_val = (scaled - sum_one[:, None] / D - x_hat * (cross_sum[:, None] / D)) * inv_std[:, None]
    return (back_val, jnp.sum(grad_in * x_hat, axis=0), jnp.sum(grad_in, axis=0))


def block_weights(w_in, w_out):
    return (
        lax.all_gather(w_in, "row", axis=0, tiled=True),
        lax.all_gather(w_out, "row", axis=1, tiled=True),
    )


def widen(values):
    return lax.all_gather(values, "col", axis=1, tiled=True)


def widen_grad(values):
    return lax.all_gather(values, "col", axis=1, tiled=True)


def send_weight_grads(grad_first, grad_second):
    return (
        lax.psum_scatter(grad_first, "row", scatter_dimension=0, tiled=True),
        lax.psum_scatter(grad_second, "row", scatter_dimension=1, tiled=True),
    )


def row_blocks(row_count):
    block_rows = math.gcd(row_count, 1024)
    return (row_count // block_rows, block_rows)


def reduce_outputs(act_rows, w_out):
    num_blocks, block_rows = row_blocks(act_rows.shape[0])

    def reduce_block(block_in):
        partial_term = jnp.dot(block_in, w_out, preferred_element_type=jnp.float32)
        return lax.psum_scatter(partial_term, "col", scatter_dimension=1, tiled=True)

    shaped = act_rows.reshape(num_blocks, block_rows, act_rows.shape[1])
    return lax.map(reduce_block, shaped).reshape(act_rows.shape[0], -1)


def reduce_inputs(grad_rows, w_in):
    num_blocks, block_rows = row_blocks(grad_rows.shape[0])

    def reduce_block(block_in):
        partial_term = lax.dot_general(
            block_in, w_in, (((1,), (1,)), ((), ())), preferred_element_type=jnp.float32
        )
        return lax.psum_scatter(partial_term, "col", scatter_dimension=1, tiled=True)

    shaped = grad_rows.reshape(num_blocks, block_rows, grad_rows.shape[1])
    return lax.map(reduce_block, shaped).reshape(grad_rows.shape[0], -1)


def transpose_dot(left_op, right_op):
    return lax.dot_general(
        left_op, right_op, (((0,), (0,)), ((), ())), preferred_element_type=jnp.float32
    )


def contract_last(left_op, right_op):
    return lax.dot_general(
        left_op, right_op, (((1,), (1,)), ((), ())), preferred_element_type=jnp.float32
    )


def place_slots(values, sources, presents, filler):
    picked = jnp.take(values, sources.reshape(-1), axis=0)
    return jnp.where(presents.reshape(-1)[:, None], picked, filler[None, :])


def place_tokens(values, targets):
    return jnp.take(values, targets.reshape(-1), axis=0)


def window_scores(queries, keys_in, table_h, table_w, pick_pair):
    pick_h, pick_w = pick_pair
    groups = queries.shape[0]
    head_count = queries.shape[2]
    direct = jnp.einsum(
        "wqhc,wkhc->whqk", queries, keys_in, preferred_element_type=jnp.float32
    ) * HD ** (-0.5)
    along_h = jnp.einsum("wqhc,jc->wqhj", queries, table_h, preferred_element_type=jnp.float32)
    along_w = jnp.einsum("wqhc,jc->wqhj", queries, table_w, preferred_element_type=jnp.float32)
    rel_h = jnp.einsum("wqhj,qkj->whqk", along_h, pick_h, precision=HIGHEST)
    rel_w = jnp.einsum("wqhj,qkj->whqk", along_w, pick_w, precision=HIGHEST)
    scores = (
        direct.reshape(groups, head_count, WIN * WIN, WIN, WIN)
        + rel_h[..., :, None]
        + rel_w[..., None, :]
    )
    return scores.reshape(groups, head_count, WIN * WIN, WIN * WIN)


def attend_group(window_set, table_h, table_w, pick_pair):
    queries = window_set[:, :, 0]
    keys_in = window_set[:, :, 1]
    values_in = window_set[:, :, 2]
    scores = window_scores(queries, keys_in, table_h, table_w, pick_pair)
    row_peak = jnp.max(scores, axis=-1, keepdims=True)
    weights = jnp.exp(scores - row_peak)
    denom_sum = jnp.sum(weights, axis=-1, keepdims=True)
    log_total = row_peak + jnp.log(denom_sum)
    probs_low = (weights / denom_sum).astype(jnp.bfloat16)
    attended = jnp.einsum(
        "whqk,wkhc->wqhc", probs_low, values_in, preferred_element_type=jnp.float32
    )
    return (attended.astype(jnp.bfloat16), log_total[..., 0])


def attend_back(window_set, grad_piece, log_piece, table_h, table_w, pick_pair):
    pick_h, pick_w = pick_pair
    queries = window_set[:, :, 0]
    keys_in = window_set[:, :, 1]
    values_in = window_set[:, :, 2]
    groups = queries.shape[0]
    head_count = queries.shape[2]
    scores = window_scores(queries, keys_in, table_h, table_w, pick_pair)
    probs_f = jnp.exp(scores - log_piece[..., None])
    probs_low = probs_f.astype(jnp.bfloat16)
    probs_grad = jnp.einsum(
        "wqhc,wkhc->whqk", grad_piece, values_in, preferred_element_type=jnp.float32
    )
    values_grad = jnp.einsum(
        "whqk,wqhc->wkhc", probs_low, grad_piece, preferred_element_type=jnp.float32
    )
    row_dot = jnp.sum(probs_f * probs_grad, axis=-1, keepdims=True)
    scores_grad = (probs_f * (probs_grad - row_dot)).astype(jnp.bfloat16)
    queries_grad = jnp.einsum(
        "whqk,wkhc->wqhc", scores_grad, keys_in, preferred_element_type=jnp.float32
    ) * HD ** (-0.5)
    keys_grad = jnp.einsum(
        "whqk,wqhc->wkhc", scores_grad, queries, preferred_element_type=jnp.float32
    ) * HD ** (-0.5)
    shaped = scores_grad.astype(jnp.float32).reshape(groups, head_count, WIN * WIN, WIN, WIN)
    sum_h = jnp.sum(shaped, axis=-1)
    sum_w = jnp.sum(shaped, axis=-2)
    back_h = jnp.einsum("whqk,qkj->wqhj", sum_h, pick_h, precision=HIGHEST)
    back_w = jnp.einsum("whqk,qkj->wqhj", sum_w, pick_w, precision=HIGHEST)
    queries_grad = queries_grad + jnp.einsum(
        "wqhj,jc->wqhc", back_h, table_h.astype(jnp.float32), precision=HIGHEST
    )
    queries_grad = queries_grad + jnp.einsum(
        "wqhj,jc->wqhc", back_w, table_w.astype(jnp.float32), precision=HIGHEST
    )
    queries_f = queries.astype(jnp.float32)
    table_h_grad = jnp.einsum("wqhj,wqhc->jc", back_h, queries_f, precision=HIGHEST)
    table_w_grad = jnp.einsum("wqhj,wqhc->jc", back_w, queries_f, precision=HIGHEST)
    stacked = jnp.stack([queries_grad, keys_grad, values_grad], axis=2).astype(jnp.bfloat16)
    return (stacked, table_h_grad, table_w_grad)


def body(
    tokens_in,
    pad_offsets,
    norm1_gain,
    norm1_bias,
    qkv_weight,
    qv_bias,
    table_height,
    table_width,
    proj_weight,
    proj_bias,
    norm2_gain,
    norm2_bias,
    fc1_weight,
    fc1_bias,
    fc2_weight,
    fc2_bias,
    out_grad,
):
    images = pad_offsets.shape[0]
    local_width = tokens_in.shape[1]
    head_count = local_width // HD
    sources, presents, targets = jax.vmap(slot_layout)(pad_offsets)
    starts = jnp.arange(images, dtype=jnp.int32)
    sources = sources + (starts * PIX)[:, None]
    targets = targets + (starts * SLOTS)[:, None]
    pick_pair = pick_tables()
    table_h = table_height.astype(jnp.bfloat16)
    table_w = table_width.astype(jnp.bfloat16)
    inputs = tokens_in.astype(jnp.float32)
    norm_one, hat_one, inv_one = norm_forward(inputs, norm1_gain, norm1_bias)
    norm_one_low = norm_one.astype(jnp.bfloat16)
    qkv_local = qkv_weight.reshape(qkv_weight.shape[0], 3 * local_width)
    qkv_full, proj_full = block_weights(qkv_local, proj_weight)
    norm_one_wide = widen(norm_one_low)
    bias_row = jnp.concatenate([qv_bias[0], jnp.zeros_like(qv_bias[0]), qv_bias[1]])
    qkv_tok = jnp.dot(
        norm_one_wide, qkv_full, preferred_element_type=jnp.float32
    ) + bias_row.astype(jnp.float32)
    slot_vals = place_slots(qkv_tok.astype(jnp.bfloat16), sources, presents, bias_row)
    grouped = slot_vals.reshape(images * GRID, GRID, WIN * WIN, 3, head_count, HD)

    def forward_group(window_set):
        return attend_group(window_set, table_h, table_w, pick_pair)

    attended, log_totals = lax.map(forward_group, grouped)
    attended_tok = place_tokens(attended.reshape(images * SLOTS, local_width), targets)
    proj_out = reduce_outputs(attended_tok, proj_full) + proj_bias.astype(jnp.float32)
    residual = inputs + proj_out
    norm_two, hat_two, inv_two = norm_forward(residual, norm2_gain, norm2_bias)
    norm_two_low = norm_two.astype(jnp.bfloat16)
    fc1_full, fc2_full = block_weights(fc1_weight, fc2_weight)
    norm_two_wide = widen(norm_two_low)
    pre_act = jnp.dot(
        norm_two_wide, fc1_full, preferred_element_type=jnp.float32
    ) + fc1_bias.astype(jnp.float32)
    act_low = jax.nn.gelu(pre_act, approximate=False).astype(jnp.bfloat16)
    mlp_out = reduce_outputs(act_low, fc2_full) + fc2_bias.astype(jnp.float32)
    block_out = (residual + mlp_out).astype(jnp.bfloat16)
    cotangent = out_grad.astype(jnp.float32)
    fc2_bias_grad = jnp.sum(out_grad, axis=0, dtype=jnp.float32)
    gelu_value, gelu_pull = jax.vjp(partial(jax.nn.gelu, approximate=False), pre_act)
    grad_wide = widen_grad(out_grad)
    act_grad = contract_last(grad_wide, fc2_full)
    pre_grad = gelu_pull(act_grad)[0].astype(jnp.bfloat16)
    fc2_grad_wide = transpose_dot(act_low, grad_wide)
    fc1_grad_wide = transpose_dot(norm_two_wide, pre_grad)
    fc1_bias_grad = jnp.sum(pre_grad, axis=0, dtype=jnp.float32)
    norm_two_grad = reduce_inputs(pre_grad, fc1_full)
    fc1_weight_grad, fc2_weight_grad = send_weight_grads(fc1_grad_wide, fc2_grad_wide)
    resid_part, norm2_gain_grad, norm2_bias_grad = norm_backward(
        norm_two_grad, hat_two, inv_two, norm2_gain
    )
    resid_grad = cotangent + resid_part
    proj_grad = resid_grad.astype(jnp.bfloat16)
    proj_bias_grad = jnp.sum(proj_grad, axis=0, dtype=jnp.float32)
    proj_grad_wide = widen_grad(proj_grad)
    proj_weight_wide = transpose_dot(attended_tok, proj_grad_wide)
    attended_grad = contract_last(proj_grad_wide, proj_full).astype(jnp.bfloat16)
    zero_row = jnp.zeros((local_width,), jnp.bfloat16)
    attended_slots = place_slots(attended_grad, sources, presents, zero_row)
    grouped_grad = attended_slots.reshape(images * GRID, GRID, WIN * WIN, head_count, HD)

    def backward_group(running, inputs_at):
        window_set, grad_piece, log_piece = inputs_at
        stacked, grad_h, grad_w = attend_back(
            window_set, grad_piece, log_piece, table_h, table_w, pick_pair
        )
        return ((running[0] + grad_h, running[1] + grad_w), stacked)

    start_tables = (
        jnp.zeros(table_height.shape, jnp.float32),
        jnp.zeros(table_width.shape, jnp.float32),
    )
    table_sums, slot_grads = lax.scan(
        backward_group, start_tables, (grouped, grouped_grad, log_totals)
    )
    slot_grads = slot_grads.reshape(images * SLOTS, 3 * local_width)
    part_sums = jnp.sum(slot_grads, axis=0, dtype=jnp.float32).reshape(3, local_width)
    qv_bias_grad = jnp.stack([part_sums[0], part_sums[2]])
    qkv_grad = place_tokens(slot_grads, targets)
    qkv_weight_wide = transpose_dot(norm_one_wide, qkv_grad)
    norm_one_grad = reduce_inputs(qkv_grad, qkv_full)
    qkv_weight_grad, proj_weight_grad = send_weight_grads(qkv_weight_wide, proj_weight_wide)
    input_part, norm1_gain_grad, norm1_bias_grad = norm_backward(
        norm_one_grad, hat_one, inv_one, norm1_gain
    )
    input_grad = resid_grad + input_part
    small_sums = lax.psum(
        (
            norm1_gain_grad,
            norm1_bias_grad,
            qv_bias_grad,
            proj_bias_grad,
            norm2_gain_grad,
            norm2_bias_grad,
            fc1_bias_grad,
            fc2_bias_grad,
        ),
        "row",
    )
    table_grads = lax.psum((table_sums[0], table_sums[1]), ("row", "col"))
    return (
        block_out,
        input_grad,
        small_sums[0],
        small_sums[1],
        qkv_weight_grad.reshape(qkv_weight_grad.shape[0], 3, local_width),
        small_sums[2],
        table_grads[0],
        table_grads[1],
        proj_weight_grad,
        small_sums[3],
        small_sums[4],
        small_sums[5],
        fc1_weight_grad,
        small_sums[6],
        fc2_weight_grad,
        small_sums[7],
    )


def solution(mesh):
    placed = (
        P("row", "col"),
        P("row", None),
        P("col"),
        P("col"),
        P("row", None, "col"),
        P(None, "col"),
        P(),
        P(),
        P("col", "row"),
        P("col"),
        P("col"),
        P("col"),
        P("row", "col"),
        P("col"),
        P("col", "row"),
        P("col"),
        P("row", "col"),
    )
    return jax.shard_map(
        body,
        mesh=mesh,
        in_specs=placed,
        out_specs=(
            P("row", "col"),
            P("row", "col"),
            P("col"),
            P("col"),
            P("row", None, "col"),
            P(None, "col"),
            P(),
            P(),
            P("col", "row"),
            P("col"),
            P("col"),
            P("col"),
            P("row", "col"),
            P("col"),
            P("col", "row"),
            P("col"),
        ),
        check_vma=False,
    )
```

profile of v0, /device:TPU:0, one launch (start us, length us, event | category | flops | bytes accessed | tf_op | source)
XLA Modules:
  0.0 3361.7 jit_solution(16300424236201338936)
XLA Ops:
  12.0 20.9 all-reduce.5
  43.7 11.1 all_gather.26
  57.8 132.6 %all-gather.8.cloned.1.call-done = bf16[4096,1024]{1,0:T(8,128)(2,1)} async-done(((bf16[4096,256]{1,0:T(8,128)(2,1)}), bf16[4096,1024]{1,0:T(8,128)(2,1)}) %all-gather.8.cloned.1.call-update) | async-done | bytes 8388624 | tf_op jit(solution)/shard_map/all_gather | solution.py:82
  190.4 11.4 add_convert_fusion.1
  201.9 22.8 gather_fusion
  224.7 10.2 copy.112
  235.0 23.2 gather.25
  258.1 8.6 select_select_fusion
  272.0 210.6 %while.73 = (s32[]{:T(128)}, bf16[5,5,196,4,64]{2,4,3,1,0:T(8,128)(2,1)}, f32[5,5,4,196]{3,2,1,0:T(4,128)}, bf16[5,5,196,3,4,64]{2,5,4,1,3,0:T(8,128)(2,1)}, bf1...) while((s32[]{:T(128)}, ...), condition=%wide.region_7.8_spmd.clone, body=%wide.region_4.7_spmd.clone.sunk | while | flops 266805392 | bytes 52209772 | solution.py:268
  482.6 11.3 copy.139
  501.1 16.9 gather_fusion.1
  523.4 331.5 %while.69 = (s32[]{:T(128)}, f32[4,1024,256]{2,1,0:T(8,128)}, bf16[4,1024,256]{2,1,0:T(8,128)(2,1)}, bf16[256,1024]{1,0:T(8,128)(2,1)S(1)}, s32[]{:T(128)}) while((s32[]{:T(128)}, f32[4,1024,256]{2,1,0:T(8,128)}, bf16[4,1024,256]{2,1,0:T(8,128)(2,1)}, bf16[256,1024]{1,0:T(8,128)(2,1)S(1)}, s32[]{:T(128)}) %tuple.188), condition=%wide.region_10.11_spmd, body=%wide.region_8.10_spmd.sunk | while | flops 536870912 | bytes 23068788 | solution.py:109
  527.3 75.1 %reduce-scatter.17.cloned.1.call-done = f32[1024,256]{1,0:T(8,128)} async-done(((f32[1024,1024]{1,0:T(8,128)}), f32[1024,256]{1,0:T(8,128)}) %reduce-scatter.17.cloned.1.call-update) | async-done | bytes 1048592 | tf_op jit(solution)/shard_map/while/body/eval_jaxpr/reduce_scatter | solution.py:106
  608.4 77.4 %reduce-scatter.17.cloned.1.call-done = f32[1024,256]{1,0:T(8,128)} async-done(((f32[1024,1024]{1,0:T(8,128)}), f32[1024,256]{1,0:T(8,128)}) %reduce-scatter.17.cloned.1.call-update) | async-done | bytes 1048592 | tf_op jit(solution)/shard_map/while/body/eval_jaxpr/reduce_scatter | solution.py:106
  691.8 77.4 %reduce-scatter.17.cloned.1.call-done = f32[1024,256]{1,0:T(8,128)} async-done(((f32[1024,1024]{1,0:T(8,128)}), f32[1024,256]{1,0:T(8,128)}) %reduce-scatter.17.cloned.1.call-update) | async-done | bytes 1048592 | tf_op jit(solution)/shard_map/while/body/eval_jaxpr/reduce_scatter | solution.py:106
  775.3 77.4 %reduce-scatter.17.cloned.1.call-done = f32[1024,256]{1,0:T(8,128)} async-done(((f32[1024,1024]{1,0:T(8,128)}), f32[1024,256]{1,0:T(8,128)}) %reduce-scatter.17.cloned.1.call-update) | async-done | bytes 1048592 | tf_op jit(solution)/shard_map/while/body/eval_jaxpr/reduce_scatter | solution.py:106
  860.6 18.3 all-reduce.4
  886.1 151.3 %all-gather.12.cloned.1.call-done = bf16[4096,1024]{1,0:T(8,128)(2,1)} async-done(((bf16[4096,256]{1,0:T(8,128)(2,1)}), bf16[4096,1024]{1,0:T(8,128)(2,1)}) %all-gather.12.cloned.1.call-update) | async-done | bytes 8388624 | tf_op jit(solution)/shard_map/all_gather | solution.py:82
  1037.4 16.1 fusion.215
  1053.4 12.2 all-gather.16.cloned.1.call-done
  1065.7 150.6 %all-gather.18.cloned.1.call-done = bf16[4096,1024]{1,0:T(8,128)(2,1)} async-done(((bf16[4096,256]{1,0:T(8,128)(2,1)}), bf16[4096,1024]{1,0:T(8,128)(2,1)}) %all-gather.18.cloned.1.call-update) | async-done | bytes 8388624 | tf_op jit(solution)/shard_map/all_gather | solution.py:86
  1216.2 52.5 %convert_reduce_fusion.1 = (f32[1024]{0:T(1024)}, bf16[4096,1024]{1,0:T(8,128)(2,1)}, f32[4096,1024]{1,0:T(8,128)}) fusion(f32[4096,1024]{1,0:T(8,128)} %fusion.215, f32[1024]{0:T(1024)S(1)} %convert_element_type.114, bf16[4096,1024]{1,0:T(8,128)(2,1)} %all-gather.18.cloned.1.call-done, bf16[1024,1024]{1,0:T(8,128)(2,1)} %all-gather.16.cloned.1.call-done), kind=kOutput, calls=%fused_computation.129 | convolution fusion | flops 8904506368 | bytes 52436992 | tf_op jit(solution)/shard_map/dot_general | solution.py:132
  1271.1 341.2 %while.71 = (s32[]{:T(128)}, f32[4,1024,256]{2,1,0:T(8,128)}, bf16[4,1024,1024]{2,1,0:T(8,128)(2,1)}, bf16[1024,1024]{1,0:T(8,128)(2,1)S(1)}, s32[]{:T(128)}) while((s32[]{:T(128)}, f32[4,1024,256]{2,1,0:T(8,128)}, bf16[4,1024,1024]{2,1,0:T(8,128)(2,1)}, bf16[1024,1024]{1,0:T(8,128)(2,1)S(1)}, s32[]{:T(128)}) %tuple.194), condition=%wide.region_20.21_spmd, body=%wide.region_18.20_spmd.sunk | while | flops 2147483648 | bytes 26214516 | solution.py:122
  1277.5 75.1 %reduce-scatter.21.cloned.1.call-done = f32[1024,256]{1,0:T(8,128)} async-done(((f32[1024,1024]{1,0:T(8,128)}), f32[1024,256]{1,0:T(8,128)}) %reduce-scatter.21.cloned.1.call-update) | async-done | bytes 1048592 | tf_op jit(solution)/shard_map/while/body/eval_jaxpr/reduce_scatter | solution.py:119
  1361.0 77.4 %reduce-scatter.21.cloned.1.call-done = f32[1024,256]{1,0:T(8,128)} async-done(((f32[1024,1024]{1,0:T(8,128)}), f32[1024,256]{1,0:T(8,128)}) %reduce-scatter.21.cloned.1.call-update) | async-done | bytes 1048592 | tf_op jit(solution)/shard_map/while/body/eval_jaxpr/reduce_scatter | solution.py:119
  1446.8 77.4 %reduce-scatter.21.cloned.1.call-done = f32[1024,256]{1,0:T(8,128)} async-done(((f32[1024,1024]{1,0:T(8,128)}), f32[1024,256]{1,0:T(8,128)}) %reduce-scatter.21.cloned.1.call-update) | async-done | bytes 1048592 | tf_op jit(solution)/shard_map/while/body/eval_jaxpr/reduce_scatter | solution.py:119
  1532.6 77.4 %reduce-scatter.21.cloned.1.call-done = f32[1024,256]{1,0:T(8,128)} async-done(((f32[1024,1024]{1,0:T(8,128)}), f32[1024,256]{1,0:T(8,128)}) %reduce-scatter.21.cloned.1.call-update) | async-done | bytes 1048592 | tf_op jit(solution)/shard_map/while/body/eval_jaxpr/reduce_scatter | solution.py:119
  1619.9 15.1 multiply_convert_fusion.1
  1635.0 18.3 all-reduce.3
  1655.6 343.5 %while.70 = (s32[]{:T(128)}, f32[4,1024,256]{2,1,0:T(8,128)}, bf16[4,1024,1024]{2,1,0:T(8,128)(2,1)}, bf16[1024,1024]{1,0:T(8,128)(2,1)}, s32[]{:T(128)}) while((s32[]{:T(128)}, f32[4,1024,256]{2,1,0:T(8,128)}, bf16[4,1024,1024]{2,1,0:T(8,128)(2,1)}, bf16[1024,1024]{1,0:T(8,128)(2,1)}, s32[]{:T(128)}) %tuple.189), condition=%wide.region_17.18_spmd, body=%wide.region_15.17_spmd.sunk | while | flops 2147483648 | bytes 26214516 | solution.py:109
  1662.4 75.3 %reduce-scatter.19.cloned.1.call-done = f32[1024,256]{1,0:T(8,128)} async-done(((f32[1024,1024]{1,0:T(8,128)}), f32[1024,256]{1,0:T(8,128)}) %reduce-scatter.19.cloned.1.call-update) | async-done | bytes 1048592 | tf_op jit(solution)/shard_map/while/body/eval_jaxpr/reduce_scatter | solution.py:106
  1746.7 77.4 %reduce-scatter.19.cloned.1.call-done = f32[1024,256]{1,0:T(8,128)} async-done(((f32[1024,1024]{1,0:T(8,128)}), f32[1024,256]{1,0:T(8,128)}) %reduce-scatter.19.cloned.1.call-update) | async-done | bytes 1048592 | tf_op jit(solution)/shard_map/while/body/eval_jaxpr/reduce_scatter | solution.py:106
  1833.0 77.4 %reduce-scatter.19.cloned.1.call-done = f32[1024,256]{1,0:T(8,128)} async-done(((f32[1024,1024]{1,0:T(8,128)}), f32[1024,256]{1,0:T(8,128)}) %reduce-scatter.19.cloned.1.call-update) | async-done | bytes 1048592 | tf_op jit(solution)/shard_map/while/body/eval_jaxpr/reduce_scatter | solution.py:106
  1919.4 77.4 %reduce-scatter.19.cloned.1.call-done = f32[1024,256]{1,0:T(8,128)} async-done(((f32[1024,1024]{1,0:T(8,128)}), f32[1024,256]{1,0:T(8,128)}) %reduce-scatter.19.cloned.1.call-update) | async-done | bytes 1048592 | tf_op jit(solution)/shard_map/while/body/eval_jaxpr/reduce_scatter | solution.py:106
  1999.1 11.7 convert_reduce_fusion.4
  2015.5 145.1 %all-gather.20.cloned.1.call-done = bf16[4096,1024]{1,0:T(8,128)(2,1)} async-done(((bf16[4096,256]{1,0:T(8,128)(2,1)}), bf16[4096,1024]{1,0:T(8,128)(2,1)}) %all-gather.20.cloned.1.call-update) | async-done | bytes 8388624 | tf_op jit(solution)/shard_map/all_gather | solution.py:86
  2166.4 15.1 gather_fusion.2
  2197.4 518.5 %while.74 = (s32[]{:T(128)}, f32[27,64]{1,0:T(8,128)S(1)}, f32[27,64]{1,0:T(8,128)S(1)}, bf16[5,5,196,3,4,64]{2,5,4,1,3,0:T(8,128)(2,1)}, bf16[5,5,196,3,4,64]{2...) while((s32[]{:T(128)}, f32[27,64]{1,0:T(8,128)S(1)}, ...), condition=%wide.region_29.30_spmd.clone.clone, body=%wide.region_25.29_spmd.clone.clone.sunk | while | flops 931062592 | bytes 126190336 | solution.py:317
  2207.0 8.8 convolution_bitcast_fusion.14
  2225.0 8.8 convolution_bitcast_fusion.15
  2308.9 8.8 convolution_bitcast_fusion.14
  2327.2 8.8 convolution_bitcast_fusion.15
  2411.1 8.8 convolution_bitcast_fusion.14
  2429.1 8.8 convolution_bitcast_fusion.15
  2512.9 8.8 convolution_bitcast_fusion.14
  2531.0 8.8 convolution_bitcast_fusion.15
  2615.0 8.8 convolution_bitcast_fusion.14
  2633.3 8.8 convolution_bitcast_fusion.15
  2715.9 31.4 copy.140
  2747.3 21.8 reshape.793
  2769.1 23.2 gather_fusion.3
  2800.1 12.2 fusion.115
  2814.7 337.7 %while.72 = (s32[]{:T(128)}, f32[4,1024,256]{2,1,0:T(8,128)}, bf16[4,1024,768]{2,1,0:T(8,128)(2,1)}, bf16[1024,768]{1,0:T(8,128)(2,1)S(1)}, s32[]{:T(128)}) while((s32[]{:T(128)}, f32[4,1024,256]{2,1,0:T(8,128)}, bf16[4,1024,768]{2,1,0:T(8,128)(2,1)}, bf16[1024,768]{1,0:T(8,128)(2,1)S(1)}, s32[]{:T(128)}) %tuple.192), condition=%wide.region_32.33_spmd, body=%wide.region_30.32_spmd.sunk | while | flops 1610612736 | bytes 25165940 | solution.py:122
  2820.0 75.1 %reduce-scatter.23.cloned.1.call-done = f32[1024,256]{1,0:T(8,128)} async-done(((f32[1024,1024]{1,0:T(8,128)}), f32[1024,256]{1,0:T(8,128)}) %reduce-scatter.23.cloned.1.call-update) | async-done | bytes 1048592 | tf_op jit(solution)/shard_map/while/body/eval_jaxpr/reduce_scatter | solution.py:119
  2902.7 77.4 %reduce-scatter.23.cloned.1.call-done = f32[1024,256]{1,0:T(8,128)} async-done(((f32[1024,1024]{1,0:T(8,128)}), f32[1024,256]{1,0:T(8,128)}) %reduce-scatter.23.cloned.1.call-update) | async-done | bytes 1048592 | tf_op jit(solution)/shard_map/while/body/eval_jaxpr/reduce_scatter | solution.py:119
  2987.7 77.4 %reduce-scatter.23.cloned.1.call-done = f32[1024,256]{1,0:T(8,128)} async-done(((f32[1024,1024]{1,0:T(8,128)}), f32[1024,256]{1,0:T(8,128)}) %reduce-scatter.23.cloned.1.call-update) | async-done | bytes 1048592 | tf_op jit(solution)/shard_map/while/body/eval_jaxpr/reduce_scatter | solution.py:119
  3072.7 77.4 %reduce-scatter.23.cloned.1.call-done = f32[1024,256]{1,0:T(8,128)} async-done(((f32[1024,1024]{1,0:T(8,128)}), f32[1024,256]{1,0:T(8,128)}) %reduce-scatter.23.cloned.1.call-update) | async-done | bytes 1048592 | tf_op jit(solution)/shard_map/while/body/eval_jaxpr/reduce_scatter | solution.py:119
  3153.0 15.3 fusion.216
  3168.4 15.3 fusion.217
  3195.3 18.9 all-reduce.2
  3222.9 22.8 all-reduce.1
  3245.7 38.2 %all-reduce = (f32[27,64]{1,0:T(8,128)}, f32[27,64]{1,0:T(8,128)}) all-reduce(f32[27,64]{1,0:T(8,128)S(1)} %get-tuple-element.921, f32[27,64]{1,0:T(8,128)S(1)} %get-tuple-element.922), channel_id=1, replica_groups=mesh['row'=8,'col'=4] {'row','col'}, use_global_device_ids=true, to_apply=%region_44.45 | all-reduce | flops 3456 | bytes 27648 | tf_op jit(solution)/shard_map/psum | solution.py:344
  3293.8 20.7 reduce-scatter.15.cloned.1.call-done
  3314.5 40.0 %reduce-scatter.11.cloned.1.call-done = f32[256,128]{1,0:T(8,128)} async-done(((f32[256,1024]{1,0:T(8,128)}), f32[256,128]{1,0:T(8,128)}) %reduce-scatter.11.cloned.1.call-update) | async-done | bytes 131088 | tf_op jit(solution)/shard_map/reduce_scatter | solution.py:92
  (608 shorter events, 851.8 us)
Async XLA Ops:
  7.2 26.3 copy-start.11
  7.2 50.6 %all-gather.10.cloned.1.call-start = ((), (), s32[]{:S(2)}) async-start(), calls=%async_computation.9 | async-start | bytes 1769472 | tf_op jit(solution)/shard_map/all_gather | solution.py:76
  9.1 28.3 copy-start.59
  9.2 28.5 copy-start.49
  9.2 28.5 copy-start.50
  9.2 28.5 copy-start.62
  9.2 34.5 %copy-start.46 = (bf16[256,128]{1,0:T(8,128)(2,1)S(1)}, bf16[256,128]{1,0:T(8,128)(2,1)}, u32[]{:S(2)}) copy-start(bf16[256,128]{1,0:T(8,128)(2,1)} %param.37) | copy-start | bytes 196612
  9.2 181.2 %all-gather.8.cloned.1.call-start = ((), (), s32[]{:S(2)}) async-start(), calls=%async_computation.8 | async-start | bytes 10485760 | tf_op jit(solution)/shard_map/all_gather | solution.py:82
  43.7 214.5 %copy-start.42 = (pred[5,5,196]{2,1,0:T(8,128)(4,1)}, pred[5,5,196]{2,1,0:T(8,128)(4,1)S(1)}, u32[]{:S(2)}) copy-start(pred[5,5,196]{2,1,0:T(8,128)(4,1)S(1)} %get-tuple-element.532) | copy-start | bytes 14704
  43.7 214.5 %copy-start.44 = (pred[5,5,196]{2,1,0:T(8,128)(4,1)}, pred[5,5,196]{2,1,0:T(8,128)(4,1)S(1)}, u32[]{:S(2)}) copy-start(pred[5,5,196]{2,1,0:T(8,128)(4,1)S(1)} %get-tuple-element.533) | copy-start | bytes 14704
  43.7 158.2 %copy-start.38 = (s32[5120]{0:T(1024)}, s32[5120]{0:T(1024)S(1)}, u32[]{:S(2)}) copy-start(s32[5120]{0:T(1024)S(1)} %pad_clamp_fusion) | copy-start | bytes 61444
  482.6 18.5 copy-start.16
  482.6 18.5 copy-start.25
  482.6 18.5 copy-start.27
  501.1 16.9 copy-start.47
  523.4 332.3 %copy-start.66 = (bf16[256]{0:T(256)(128)(2,1)S(1)}, bf16[256]{0:T(256)(128)(2,1)}, u32[]{:S(2)}) copy-start(bf16[256]{0:T(256)(128)(2,1)} %param.38) | copy-start | bytes 1540
  523.4 332.4 %copy-start.12 = (bf16[4096,256]{1,0:T(8,128)(2,1)S(1)}, bf16[4096,256]{1,0:T(8,128)(2,1)}, u32[]{:S(2)}) copy-start(bf16[4096,256]{1,0:T(8,128)(2,1)} %param.29) | copy-start | bytes 6291460
  523.4 79.0 %reduce-scatter.17.cloned.1.call-start = ((), (), s32[]{:S(2)}) async-start(), calls=%async_computation.19 | async-start | bytes 5242880 | tf_op jit(solution)/shard_map/while/body/eval_jaxpr/reduce_scatter | solution.py:106
  604.7 81.2 %reduce-scatter.17.cloned.1.call-start = ((), (), s32[]{:S(2)}) async-start(), calls=%async_computation.19 | async-start | bytes 5242880 | tf_op jit(solution)/shard_map/while/body/eval_jaxpr/reduce_scatter | solution.py:106
  688.1 81.2 %reduce-scatter.17.cloned.1.call-start = ((), (), s32[]{:S(2)}) async-start(), calls=%async_computation.19 | async-start | bytes 5242880 | tf_op jit(solution)/shard_map/while/body/eval_jaxpr/reduce_scatter | solution.py:106
  771.5 81.1 %reduce-scatter.17.cloned.1.call-start = ((), (), s32[]{:S(2)}) async-start(), calls=%async_computation.19 | async-start | bytes 5242880 | tf_op jit(solution)/shard_map/while/body/eval_jaxpr/reduce_scatter | solution.py:106
  854.9 31.2 all-gather.14.cloned.1.call-start
  855.7 181.7 %all-gather.12.cloned.1.call-start = ((), (), s32[]{:S(2)}) async-start(), calls=%async_computation.10 | async-start | bytes 10485760 | tf_op jit(solution)/shard_map/all_gather | solution.py:82
  855.7 23.8 copy-start.51
  855.7 23.7 copy-start.63
  883.4 182.3 %all-gather.16.cloned.1.call-start = ((), (), s32[]{:S(2)}) async-start(), calls=%async_computation.12 | async-start | bytes 2359296 | tf_op jit(solution)/shard_map/all_gather | solution.py:77
  884.1 332.2 %all-gather.18.cloned.1.call-start = ((), (), s32[]{:S(2)}) async-start(), calls=%async_computation.13 | async-start | bytes 10485760 | tf_op jit(solution)/shard_map/all_gather | solution.py:86
  1271.1 341.2 %copy-start.52 = (f32[256]{0:T(256)S(1)}, f32[256]{0:T(256)}, u32[]{:S(2)}) copy-start(f32[256]{0:T(256)} %param.39) | copy-start | bytes 3076
  1271.1 344.7 %copy-start.33 = (f32[4096]{0:T(1024)S(1)}, f32[4096]{0:T(1024)}, u32[]{:S(2)}) copy-start(f32[4096]{0:T(1024)} %copy-done.32) | copy-start | bytes 49156
  1271.3 81.3 %reduce-scatter.21.cloned.1.call-start = ((), (), s32[]{:S(2)}) async-start(), calls=%async_computation.21 | async-start | bytes 5242880 | tf_op jit(solution)/shard_map/while/body/eval_jaxpr/reduce_scatter | solution.py:119
  1354.8 83.6 %reduce-scatter.21.cloned.1.call-start = ((), (), s32[]{:S(2)}) async-start(), calls=%async_computation.21 | async-start | bytes 5242880 | tf_op jit(solution)/shard_map/while/body/eval_jaxpr/reduce_scatter | solution.py:119
  1440.7 83.5 %reduce-scatter.21.cloned.1.call-start = ((), (), s32[]{:S(2)}) async-start(), calls=%async_computation.21 | async-start | bytes 5242880 | tf_op jit(solution)/shard_map/while/body/eval_jaxpr/reduce_scatter | solution.py:119
  1526.5 83.5 %reduce-scatter.21.cloned.1.call-start = ((), (), s32[]{:S(2)}) async-start(), calls=%async_computation.21 | async-start | bytes 5242880 | tf_op jit(solution)/shard_map/while/body/eval_jaxpr/reduce_scatter | solution.py:119
  1655.6 343.5 %copy-start.24 = (bf16[4096,256]{1,0:T(8,128)(2,1)S(1)}, bf16[4096,256]{1,0:T(8,128)(2,1)}, u32[]{:S(2)}) copy-start(bf16[4096,256]{1,0:T(8,128)(2,1)} %param.45) | copy-start | bytes 6291460
  1655.6 343.5 %copy-start.64 = (f32[256]{0:T(256)S(1)}, f32[256]{0:T(256)}, u32[]{:S(2)}) copy-start(f32[256]{0:T(256)} %convert_element_type.116) | copy-start | bytes 3076
  1655.6 82.1 %reduce-scatter.19.cloned.1.call-start = ((), (), s32[]{:S(2)}) async-start(), calls=%async_computation.20 | async-start | bytes 5242880 | tf_op jit(solution)/shard_map/while/body/eval_jaxpr/reduce_scatter | solution.py:106
  1740.0 84.2 %reduce-scatter.19.cloned.1.call-start = ((), (), s32[]{:S(2)}) async-start(), calls=%async_computation.20 | async-start | bytes 5242880 | tf_op jit(solution)/shard_map/while/body/eval_jaxpr/reduce_scatter | solution.py:106
  1826.4 84.1 %reduce-scatter.19.cloned.1.call-start = ((), (), s32[]{:S(2)}) async-start(), calls=%async_computation.20 | async-start | bytes 5242880 | tf_op jit(solution)/shard_map/while/body/eval_jaxpr/reduce_scatter | solution.py:106
  1912.7 84.1 %reduce-scatter.19.cloned.1.call-start = ((), (), s32[]{:S(2)}) async-start(), calls=%async_computation.20 | async-start | bytes 5242880 | tf_op jit(solution)/shard_map/while/body/eval_jaxpr/reduce_scatter | solution.py:106
  1999.1 161.6 %all-gather.20.cloned.1.call-start = ((), (), s32[]{:S(2)}) async-start(), calls=%async_computation.14 | async-start | bytes 10485760 | tf_op jit(solution)/shard_map/all_gather | solution.py:86
  2010.8 149.8 %copy-start.23 = (bf16[256,1024]{1,0:T(8,128)(2,1)S(1)}, bf16[256,1024]{1,0:T(8,128)(2,1)}, u32[]{:S(2)}) copy-start(bf16[256,1024]{1,0:T(8,128)(2,1)} %all_gather.26) | copy-start | bytes 1572868
  2015.5 150.9 %copy-start.39 = (s32[5120]{0:T(1024)S(1)}, s32[5120]{0:T(1024)}, u32[]{:S(2)}) copy-start(s32[5120]{0:T(1024)} %copy-done.38) | copy-start | bytes 61444
  2199.3 39.2 %copy-start.3 = (bf16[5,196,3,4,64]{1,4,3,0,2:T(8,128)(2,1)}, bf16[5,196,3,4,64]{1,4,3,0,2:T(8,128)(2,1)S(1)}, u32[]{:S(2)}) copy-start(bf16[5,196,3,4,64]{1,4,3,0,2:T(8,128)(2,1)S(1)} %dynamic-slice_bitcast_fusion.7) | copy-start | bytes 4515844 | tf_op jit(solution)/shard_map/while
  2283.9 11.5 copy-start.20
  2301.1 39.4 %copy-start.3 = (bf16[5,196,3,4,64]{1,4,3,0,2:T(8,128)(2,1)}, bf16[5,196,3,4,64]{1,4,3,0,2:T(8,128)(2,1)S(1)}, u32[]{:S(2)}) copy-start(bf16[5,196,3,4,64]{1,4,3,0,2:T(8,128)(2,1)S(1)} %dynamic-slice_bitcast_fusion.7) | copy-start | bytes 4515844 | tf_op jit(solution)/shard_map/while
  2385.9 11.6 copy-start.20
  2403.4 39.2 %copy-start.3 = (bf16[5,196,3,4,64]{1,4,3,0,2:T(8,128)(2,1)}, bf16[5,196,3,4,64]{1,4,3,0,2:T(8,128)(2,1)S(1)}, u32[]{:S(2)}) copy-start(bf16[5,196,3,4,64]{1,4,3,0,2:T(8,128)(2,1)S(1)} %dynamic-slice_bitcast_fusion.7) | copy-start | bytes 4515844 | tf_op jit(solution)/shard_map/while
  2488.0 11.5 copy-start.20
  2505.2 39.2 %copy-start.3 = (bf16[5,196,3,4,64]{1,4,3,0,2:T(8,128)(2,1)}, bf16[5,196,3,4,64]{1,4,3,0,2:T(8,128)(2,1)S(1)}, u32[]{:S(2)}) copy-start(bf16[5,196,3,4,64]{1,4,3,0,2:T(8,128)(2,1)S(1)} %dynamic-slice_bitcast_fusion.7) | copy-start | bytes 4515844 | tf_op jit(solution)/shard_map/while
  2589.9 11.6 copy-start.20
  2607.2 39.4 %copy-start.3 = (bf16[5,196,3,4,64]{1,4,3,0,2:T(8,128)(2,1)}, bf16[5,196,3,4,64]{1,4,3,0,2:T(8,128)(2,1)S(1)}, u32[]{:S(2)}) copy-start(bf16[5,196,3,4,64]{1,4,3,0,2:T(8,128)(2,1)S(1)} %dynamic-slice_bitcast_fusion.7) | copy-start | bytes 4515844 | tf_op jit(solution)/shard_map/while
  2691.9 11.6 copy-start.20
  2747.3 21.8 copy-start.41
  2769.1 23.2 copy-start.48
  2814.7 80.4 %reduce-scatter.23.cloned.1.call-start = ((), (), s32[]{:S(2)}) async-start(), calls=%async_computation.22 | async-start | bytes 5242880 | tf_op jit(solution)/shard_map/while/body/eval_jaxpr/reduce_scatter | solution.py:119
  2897.5 82.7 %reduce-scatter.23.cloned.1.call-start = ((), (), s32[]{:S(2)}) async-start(), calls=%async_computation.22 | async-start | bytes 5242880 | tf_op jit(solution)/shard_map/while/body/eval_jaxpr/reduce_scatter | solution.py:119
  2982.5 82.7 %reduce-scatter.23.cloned.1.call-start = ((), (), s32[]{:S(2)}) async-start(), calls=%async_computation.22 | async-start | bytes 5242880 | tf_op jit(solution)/shard_map/while/body/eval_jaxpr/reduce_scatter | solution.py:119
  3067.4 82.7 %reduce-scatter.23.cloned.1.call-start = ((), (), s32[]{:S(2)}) async-start(), calls=%async_computation.22 | async-start | bytes 5242880 | tf_op jit(solution)/shard_map/while/body/eval_jaxpr/reduce_scatter | solution.py:119
  3152.4 139.3 %reduce-scatter.9.cloned.1.call-start = ((), (), s32[]{:S(2)}) async-start(), calls=%async_computation.15 | async-start | bytes 3538944 | tf_op jit(solution)/shard_map/reduce_scatter | solution.py:91
  3153.0 140.8 %reduce-scatter.13.cloned.1.call-start = ((), (), s32[]{:S(2)}) async-start(), calls=%async_computation.17 | async-start | bytes 4718592 | tf_op jit(solution)/shard_map/reduce_scatter | solution.py:91
  3168.3 146.1 %reduce-scatter.15.cloned.1.call-start = ((), (), s32[]{:S(2)}) async-start(), calls=%async_computation.18 | async-start | bytes 4718592 | tf_op jit(solution)/shard_map/reduce_scatter | solution.py:92
  3183.8 170.7 %reduce-scatter.11.cloned.1.call-start = ((), (), s32[]{:S(2)}) async-start(), calls=%async_computation.16 | async-start | bytes 1179648 | tf_op jit(solution)/shard_map/reduce_scatter | solution.py:92
  3183.8 8.9 copy-start.13
  3214.2 8.7 copy-start.54
  (83 other events, 336.8 us)
Sparse Core Ops, SparseCore 0:
  10.5 28.5 all-gather.9
  41.2 149.1 all-gather.7
  527.4 74.9 reduce-scatter.16
  608.5 77.2 reduce-scatter.16
  691.9 77.2 reduce-scatter.16
  775.4 77.2 reduce-scatter.16
  857.6 28.3 all-gather.13
  888.2 149.1 all-gather.11
  1039.3 26.3 all-gather.15
  1067.1 149.1 all-gather.17
  1277.6 74.9 reduce-scatter.20
  1361.1 77.2 reduce-scatter.20
  1446.9 77.2 reduce-scatter.20
  1532.7 77.2 reduce-scatter.20
  1662.5 75.1 reduce-scatter.18
  1746.8 77.2 reduce-scatter.18
  1833.2 77.2 reduce-scatter.18
  1919.5 77.2 reduce-scatter.18
  2010.9 149.6 all-gather.19
  2820.1 74.9 reduce-scatter.22
  2902.9 77.2 reduce-scatter.22
  2987.8 77.2 reduce-scatter.22
  3072.8 77.2 reduce-scatter.22
  3156.3 46.7 reduce-scatter.8
  3207.4 51.8 reduce-scatter.12
  3263.1 51.3 reduce-scatter.14
  3318.4 35.9 reduce-scatter.10
where the time goes:
time: 3380 us; the launch traced here: 3360 us
  waiting for transfers between devices  1890 us (56%)
  matrix products  643 us (19%)
  local copies, waits for them, and re-layouts  496 us (15%)
  blocking collectives  148 us (4%)
  other arithmetic  131 us (4%)
  loops' own time  41.7 us (1%)
    reduce_scatter x16, waiting for transfers between devices, reduce_block(): lax.psum_scatter(partial_term, 'col', scatter_dimension=1, tiled=True)  1230 us
    all_gather x2, waiting for transfers between devices, widen_grad(): return lax.all_gather(values, 'col', axis=1, tiled=True)  296 us
    all_gather x2, waiting for transfers between devices, widen(): return lax.all_gather(values, 'col', axis=1, tiled=True)  284 us
    gather x6, local copies, waits for them, and re-layouts, place_slots(): picked = jnp.take(values, sources.reshape(-1), axis=0)  81.4 us
    dot_general x10, matrix products, window_scores(): rel_h = jnp.einsum('wqhj,qkj->whqk', along_h, pick_h, precision=HIGHEST)  78 us
    dot_general x10, matrix products, window_scores(): rel_w = jnp.einsum('wqhj,qkj->whqk', along_w, pick_w, precision=HIGHEST)  78 us
    psum x4, blocking collectives, feature_moments(): return lax.psum((first, second), 'col')  76.2 us
  transfers between devices with their start and end apart: 27, of which 24 were waited for; matrix products, arithmetic and copies ran while one was open for 3% of the time, Pallas kernels for 0%

commit v1 on v0

v1 whole, which is shorter than its diff:
```python
from functools import partial
import math

import jax
import jax.numpy as jnp
import numpy as np
from jax import lax
from jax.experimental import pallas as pl
from jax.experimental.pallas import tpu as pltpu
from jax.sharding import PartitionSpec as P

D = 1024
HD = 64
WIN = 14
SIDE = 64
GRID = 5
WINDOWS = 25
REAL = 196
SLOT = 200
KEYS = 256
PIX = 4096
EPSILON = 1e-06
MARGIN = 6
PADROWS = 84
BF = jnp.bfloat16
F32 = jnp.float32
VMEM_LIMIT = 60 * 1024 * 1024


def iota(shape, dim):
    return lax.broadcasted_iota(jnp.int32, shape, dim)


def params(n=1):
    return pltpu.CompilerParams(
        dimension_semantics=("arbitrary",) * n, vmem_limit_bytes=VMEM_LIMIT
    )


def nt_dot(a, b):
    return lax.dot_general(a, b, (((1,), (1,)), ((), ())), preferred_element_type=F32)


def tn_dot(a, b):
    return lax.dot_general(a, b, (((0,), (0,)), ((), ())), preferred_element_type=F32)


def nn_dot(a, b):
    return lax.dot_general(a, b, (((1,), (0,)), ((), ())), preferred_element_type=F32)


def spread_kernel(cols, per, info, x_ref, *refs):
    outs, padded = refs[:cols], refs[cols]
    step = pl.program_id(0)
    me = info[0]
    top = info[1]
    left = info[2]
    width = x_ref.shape[1]

    @pl.when(step == 0)
    def _():
        padded[: MARGIN * SIDE, :] = jnp.zeros((MARGIN * SIDE, width), BF)
        padded[(MARGIN + SIDE) * SIDE :, :] = jnp.zeros(
            ((PADROWS - MARGIN - SIDE) * SIDE, width), BF
        )
        padded[MARGIN * SIDE : (MARGIN + SIDE) * SIDE, :] = x_ref[...]

    slot = iota((56, 256), 0)
    token = iota((56, 256), 1)
    same_row = slot // WIN == token // SIDE
    for k in range(cols):
        window = (me ^ k) * per + step
        win_row = jnp.minimum(window // GRID, GRID - 1)
        win_col = window % GRID
        pick = same_row & (slot % WIN + (WIN * win_col - left) == token % SIDE)
        pick = pick & (window < WINDOWS)
        tail = pick & (slot < 28)
        pick = pick.astype(F32).astype(BF)
        tail = tail.astype(F32).astype(BF)
        parts = []
        for g in range(4):
            base = pl.multiple_of((WIN * win_row + 4 * g - top + MARGIN) * SIDE, SIDE)
            rows = padded[pl.ds(base, 256), :]
            parts.append(nn_dot(pick if g < 3 else tail[:32], rows))
        outs[k][0] = jnp.concatenate(parts, axis=0).astype(BF)


def spread(x, info, cols, per):
    width = x.shape[1]
    piece = jax.ShapeDtypeStruct((per, SLOT, width), BF)
    return pl.pallas_call(
        partial(spread_kernel, cols, per),
        out_shape=[piece] * cols,
        grid_spec=pltpu.PrefetchScalarGridSpec(
            num_scalar_prefetch=1,
            grid=(per,),
            in_specs=[pl.BlockSpec((PIX, width), lambda i, s: (0, 0))],
            out_specs=[pl.BlockSpec((1, SLOT, width), lambda i, s: (i, 0, 0))] * cols,
            scratch_shapes=[pltpu.VMEM((PADROWS * SIDE, width), BF)],
        ),
        compiler_params=params(),
        name="spread",
    )(info, x)


def collect_kernel(cols, per, info, *refs):
    pieces, out, held, picks, padded = refs[:cols], refs[cols], refs[cols + 1], refs[cols + 2], refs[cols + 3]
    step = pl.program_id(0)
    me = info[0]
    top = info[1]
    left = info[2]

    @pl.when(step == 0)
    def _():
        for k in range(cols):
            first = (me ^ k) * per
            for i in range(per):
                held[first + i] = pieces[k][i]
        token = iota((WIN * SIDE, SLOT), 0)
        slot = iota((WIN * SIDE, SLOT), 1)
        same_row = (slot // WIN == token // SIDE) & (slot < REAL)
        shift = token % SIDE - slot % WIN + left
        for j in range(GRID):
            picks[j] = (same_row & (shift == WIN * j)).astype(F32).astype(BF)

    total = nn_dot(picks[0], held[step * GRID])
    for j in range(1, GRID):
        total = total + nn_dot(picks[j], held[step * GRID + j])
    base = pl.multiple_of((WIN * step - top + MARGIN) * SIDE, SIDE)
    padded[pl.ds(base, WIN * SIDE), :] = total.astype(padded.dtype)

    @pl.when(step == GRID - 1)
    def _():
        out[...] = padded[MARGIN * SIDE : (MARGIN + SIDE) * SIDE, :].astype(out.dtype)


def collect(pieces, info, cols, per, dtype):
    width = pieces[0].shape[-1]
    return pl.pallas_call(
        partial(collect_kernel, cols, per),
        out_shape=jax.ShapeDtypeStruct((PIX, width), dtype),
        grid_spec=pltpu.PrefetchScalarGridSpec(
            num_scalar_prefetch=1,
            grid=(GRID,),
            in_specs=[pl.BlockSpec((per, SLOT, width), lambda i, s: (0, 0, 0))] * cols,
            out_specs=pl.BlockSpec((PIX, width), lambda i, s: (0, 0)),
            scratch_shapes=[
                pltpu.VMEM((cols * per, SLOT, width), BF),
                pltpu.VMEM((GRID, WIN * SIDE, SLOT), BF),
                pltpu.VMEM((PADROWS * SIDE, width), BF),
            ],
        ),
        compiler_params=params(),
        name="collect",
    )(info, *pieces)


def present_mask(window, top, left, shape):
    slot = iota(shape, 0)
    row = WIN * (window // GRID) - top + slot // WIN
    col = WIN * (window % GRID) - left + slot % WIN
    inside = (row >= 0) & (row < SIDE) & (col >= 0) & (col < SIDE)
    return inside & (slot < REAL) & (window < WINDOWS)


def gather_features(pieces, me, whole):
    width = pieces[0].shape[-1]
    for k, piece in enumerate(pieces):
        first = pl.multiple_of((me ^ k) * width, 128)
        whole[:, pl.ds(first, width)] = piece[0].astype(F32)
    return whole[...]


def norm1_kernel(cols, per, info, *refs):
    pieces = refs[:cols]
    gain, bias, x_out, n_out, whole = refs[cols:]
    me = info[0]
    values = gather_features(pieces, me, whole)
    x_out[...] = values.astype(BF)
    mean = jnp.mean(values, axis=1, keepdims=True)
    centred = values - mean
    spread_sq = jnp.mean(centred * centred, axis=1, keepdims=True)
    normed = centred * lax.rsqrt(spread_sq + EPSILON) * gain[...] + bias[...]
    keep = present_mask(me * per + pl.program_id(0), info[1], info[2], (SLOT, D))
    n_out[...] = jnp.where(keep, normed, 0.0).astype(BF)


def norm1(pieces, info, gain, bias, cols, per):
    width = pieces[0].shape[-1]
    rows = per * SLOT
    vec = pl.BlockSpec((1, D), lambda i, s: (0, 0))
    out = jax.ShapeDtypeStruct((rows, D), BF)
    return pl.pallas_call(
        partial(norm1_kernel, cols, per),
        out_shape=[out, out],
        grid_spec=pltpu.PrefetchScalarGridSpec(
            num_scalar_prefetch=1,
            grid=(per,),
            in_specs=[pl.BlockSpec((1, SLOT, width), lambda i, s: (i, 0, 0))] * cols + [vec, vec],
            out_specs=[pl.BlockSpec((SLOT, D), lambda i, s: (i, 0))] * 2,
            scratch_shapes=[pltpu.VMEM((SLOT, D), F32)],
        ),
        compiler_params=params(),
        name="norm1",
    )(info, *pieces, gain, bias)


def join_kernel(cols, info, *refs):
    pieces, out, whole = refs[:cols], refs[cols], refs[cols + 1]
    out[...] = gather_features(pieces, info[0], whole).astype(BF)


def join(pieces, info, cols, per):
    width = pieces[0].shape[-1]
    return pl.pallas_call(
        partial(join_kernel, cols),
        out_shape=jax.ShapeDtypeStruct((per * SLOT, D), BF),
        grid_spec=pltpu.PrefetchScalarGridSpec(
            num_scalar_prefetch=1,
            grid=(per,),
            in_specs=[pl.BlockSpec((1, SLOT, width), lambda i, s: (i, 0, 0))] * cols,
            out_specs=pl.BlockSpec((SLOT, D), lambda i, s: (i, 0)),
            scratch_shapes=[pltpu.VMEM((SLOT, D), F32)],
        ),
        compiler_params=params(),
        name="join",
    )(info, *pieces)


def rel_constants():
    place = np.arange(SLOT)
    lanes = np.arange(128)
    group = lanes // 32
    row_shift = np.clip(WIN - 1 - place // WIN, 0, WIN - 1)
    col_shift = WIN - 1 - place % WIN
    shifts = np.where(group[None, :] % 2 == 0, row_shift[:, None], col_shift[:, None])
    onehot = np.zeros((2, KEYS, 128), np.float32)
    for head in range(2):
        for key in range(KEYS):
            if key >= REAL:
                onehot[head, key, 64 * head + 28] = -1e9
                continue
            for extra in (0, WIN):
                onehot[head, key, 64 * head + key // WIN + extra] = 1.0
                onehot[head, key, 64 * head + 32 + key % WIN + extra] = 1.0
    return shifts.astype(np.int32), onehot


def table_matrix(table_h, table_w):
    flipped = jnp.stack([table_h, table_w])[:, ::-1, :].astype(BF)
    block = jnp.pad(jnp.transpose(flipped, (2, 0, 1)), ((0, 0), (0, 0), (0, 5)))
    block = block.reshape(HD, HD)
    zero = jnp.zeros_like(block)
    return jnp.concatenate(
        [jnp.concatenate([block, zero], axis=1), jnp.concatenate([zero, block], axis=1)], axis=0
    )


def shift_left(values, shifts):
    for bit in (1, 2, 4, 8):
        values = jnp.where((shifts & bit) != 0, pltpu.roll(values, 128 - bit, 1), values)
    return values


def shift_right(values, shifts):
    for bit in (1, 2, 4, 8):
        values = jnp.where((shifts & bit) != 0, pltpu.roll(values, bit, 1), values)
    return values


def attend_kernel(width, qkv, tables, shifts, onehot, att, exps, inv, keys, vals):
    first = (pl.program_id(0) == 0) & (pl.program_id(1) == 0)

    @pl.when(first)
    def _():
        for head in range(2):
            keys[head, :, :128] = jnp.zeros((KEYS, 128), BF)
            keys[head, :, 128:] = onehot[head]
        vals[:, :128] = jnp.zeros((KEYS, 128), BF)
        vals[:, 128:] = jnp.ones((KEYS, 128), BF)

    lane = iota((SLOT, 128), 1)
    low = lane < HD
    inner = lane % 32
    for pair in range(width // 128):
        at = pair * 128
        q2 = qkv[:, at : at + 128]
        k2 = qkv[:, width + at : width + at + 128]
        v2 = qkv[:, 2 * width + at : 2 * width + at + 128]
        rel = shift_left(nn_dot(q2, tables[...]), shifts[...])
        rel_hi = rel.astype(BF).astype(F32)
        rel_lo = pltpu.roll(rel - rel_hi, WIN, 1)
        rel = jnp.where(inner < WIN, rel_hi, jnp.where(inner < 2 * WIN, rel_lo, 1.0))
        queries = jnp.concatenate([q2 * BF(0.125), rel.astype(BF)], axis=1)
        vals[:SLOT, :128] = v2
        zero = jnp.zeros_like(k2)
        keys[0, :SLOT, :128] = jnp.where(low, k2, zero)
        keys[1, :SLOT, :128] = jnp.where(low, zero, k2)
        outs = []
        for head in range(2):
            scores = nt_dot(queries, keys[head])
            peak = jnp.max(scores, axis=1, keepdims=True)
            weights = jnp.exp(scores - peak).astype(BF)
            exps[pair * 2 + head] = weights
            outs.append(nn_dot(weights, vals[...]))
        total = jnp.where(low, outs[0][:, 128:], outs[1][:, 128:])
        scale = 1.0 / total
        inv[:, at : at + 128] = scale
        att[:, at : at + 128] = (
            jnp.where(low, outs[0][:, :128], outs[1][:, :128]) * scale
        ).astype(BF)


def attend(qkv, tables, shifts, onehot, cols, per):
    rows = per * SLOT
    width = D // cols
    pairs = width // 128
    return pl.pallas_call(
        partial(attend_kernel, width),
        out_shape=[
            jax.ShapeDtypeStruct((rows, D), BF),
            jax.ShapeDtypeStruct((D // HD, rows, KEYS), BF),
            jax.ShapeDtypeStruct((rows, D), F32),
        ],
        grid=(cols, per),
        in_specs=[
            pl.BlockSpec((SLOT, 3 * width), lambda c, w: (w, c)),
            pl.BlockSpec((128, 128), lambda c, w: (0, 0)),
            pl.BlockSpec((SLOT, 128), lambda c, w: (0, 0)),
            pl.BlockSpec((2, KEYS, 128), lambda c, w: (0, 0, 0)),
        ],
        out_specs=[
            pl.BlockSpec((SLOT, width), lambda c, w: (w, c)),
            pl.BlockSpec((2 * pairs, SLOT, KEYS), lambda c, w: (c, w, 0)),
            pl.BlockSpec((SLOT, width), lambda c, w: (w, c)),
        ],
        scratch_shapes=[pltpu.VMEM((2, KEYS, 256), BF), pltpu.VMEM((KEYS, 256), BF)],
        compiler_params=params(2),
        name="attend",
    )(qkv, tables, shifts, onehot)


def attend_back_kernel(
    width, qkv, exps, inv, att, att_grad, tables2, shifts, onehot, out, table_sum, bias_sum, keys, vals
):
    first = (pl.program_id(0) == 0) & (pl.program_id(1) == 0)

    @pl.when(first)
    def _():
        for head in range(2):
            keys[head, :, :128] = jnp.zeros((KEYS, 128), BF)
            keys[head, :, 128:] = onehot[head]
        vals[...] = jnp.zeros_like(vals)
        table_sum[...] = jnp.zeros_like(table_sum)

    @pl.when(pl.program_id(1) == 0)
    def _():
        bias_sum[...] = jnp.zeros_like(bias_sum)

    lane = iota((SLOT, 128), 1)
    low = lane < HD
    inner = lane % 32

    def eight(values):
        total = values[:8]
        for r in range(8, SLOT, 8):
            total = total + values[r : r + 8]
        return total

    for pair in range(width // 128):
        at = pair * 128
        q2 = qkv[:, at : at + 128]
        k2 = qkv[:, width + at : width + at + 128]
        v2 = qkv[:, 2 * width + at : 2 * width + at + 128]
        zero = jnp.zeros_like(k2)
        keys[0, :SLOT, :128] = jnp.where(low, k2, zero)
        keys[1, :SLOT, :128] = jnp.where(low, zero, k2)
        vals[0, :SLOT, :] = jnp.where(low, v2, zero)
        vals[1, :SLOT, :] = jnp.where(low, zero, v2)
        grad = (att_grad[:, at : at + 128].astype(F32) * inv[:, at : at + 128]).astype(BF)
        cross = grad.astype(F32) * att[:, at : at + 128].astype(F32)
        dots = (
            jnp.sum(jnp.where(low, cross, 0.0), axis=1, keepdims=True),
            jnp.sum(jnp.where(low, 0.0, cross), axis=1, keepdims=True),
        )
        q_scaled = q2 * BF(0.125)
        grad_heads = (jnp.where(low, grad, zero), jnp.where(low, zero, grad))
        q_heads = (jnp.where(low, q_scaled, zero), jnp.where(low, zero, q_scaled))
        q_sum = jnp.zeros((SLOT, 256), F32)
        k_sum = jnp.zeros((KEYS, 128), F32)
        v_sum = jnp.zeros((KEYS, 128), F32)
        for head in range(2):
            weights = exps[pair * 2 + head]
            probs_grad = nt_dot(grad, vals[head])
            scores_grad = (weights.astype(F32) * (probs_grad - dots[head])).astype(BF)
            q_sum = q_sum + nn_dot(scores_grad, keys[head])
            k_sum = k_sum + tn_dot(scores_grad, q_heads[head])
            v_sum = v_sum + tn_dot(weights, grad_heads[head])
        rel = shift_right(jnp.where(inner < WIN, q_sum[:, 128:], 0.0), shifts[...])
        rel_hi = rel.astype(BF)
        rel_lo = (rel - rel_hi.astype(F32)).astype(BF)
        rel2 = jnp.concatenate([rel_hi, rel_lo], axis=1)
        q_grad = q_sum[:, :128] * 0.125 + nt_dot(rel2, tables2[...])
        table_sum[...] += tn_dot(q2, rel2)
        k_grad = k_sum[:SLOT]
        v_grad = v_sum[:SLOT]
        out[:, at : at + 128] = q_grad.astype(BF)
        out[:, width + at : width + at + 128] = k_grad.astype(BF)
        out[:, 2 * width + at : 2 * width + at + 128] = v_grad.astype(BF)
        bias_sum[:, at : at + 128] += eight(q_grad)
        bias_sum[:, 2 * width + at : 2 * width + at + 128] += eight(v_grad)


def attend_back(qkv, exps, inv, att, att_grad, tables, shifts, onehot, cols, per):
    rows = per * SLOT
    width = D // cols
    pairs = width // 128
    tables2 = jnp.concatenate([tables, tables], axis=1)
    return pl.pallas_call(
        partial(attend_back_kernel, width),
        out_shape=[
            jax.ShapeDtypeStruct((rows, 3 * D), BF),
            jax.ShapeDtypeStruct((128, 256), F32),
            jax.ShapeDtypeStruct((8, 3 * D), F32),
        ],
        grid=(cols, per),
        in_specs=[
            pl.BlockSpec((SLOT, 3 * width), lambda c, w: (w, c)),
            pl.BlockSpec((2 * pairs, SLOT, KEYS), lambda c, w: (c, w, 0)),
            pl.BlockSpec((SLOT, width), lambda c, w: (w, c)),
            pl.BlockSpec((SLOT, width), lambda c, w: (w, c)),
            pl.BlockSpec((SLOT, width), lambda c, w: (w, c)),
            pl.BlockSpec((128, 256), lambda c, w: (0, 0)),
            pl.BlockSpec((SLOT, 128), lambda c, w: (0, 0)),
            pl.BlockSpec((2, KEYS, 128), lambda c, w: (0, 0, 0)),
        ],
        out_specs=[
            pl.BlockSpec((SLOT, 3 * width), lambda c, w: (w, c)),
            pl.BlockSpec((128, 256), lambda c, w: (0, 0)),
            pl.BlockSpec((8, 3 * width), lambda c, w: (0, c)),
        ],
        scratch_shapes=[pltpu.VMEM((2, KEYS, 256), BF), pltpu.VMEM((2, KEYS, 128), BF)],
        compiler_params=params(2),
        name="attend_back",
    )(qkv, exps, inv, att, att_grad, tables2, shifts, onehot)


def split_table(total):
    total = (total[:, :128] + total[:, 128:]).reshape(2, HD, 2, 2, 32)
    both = total[0, :, 0] + total[1, :, 1]
    both = jnp.transpose(both, (1, 2, 0))[:, :27][:, ::-1]
    return both[0], both[1]


def exchange(pieces, cols):
    return [pieces[0]] + [
        lax.ppermute(pieces[k], "col", [(i, i ^ k) for i in range(cols)]) for k in range(1, cols)
    ]


def pieces_of(full, me, cols, per):
    width = D // cols
    parts = full.reshape(per, SLOT, cols, width)
    return [
        lax.dynamic_index_in_dim(parts, me ^ k, 2, keepdims=False) for k in range(cols)
    ]


def norm_stats(values):
    mean = jnp.mean(values, axis=1, keepdims=True)
    centred = values - mean
    var = jnp.mean(centred * centred, axis=1, keepdims=True)
    inv = lax.rsqrt(var + EPSILON)
    return centred * inv, inv


def norm_back(grad, hat, inv, gain):
    scaled = grad * gain
    first = jnp.mean(scaled, axis=1, keepdims=True)
    second = jnp.mean(scaled * hat, axis=1, keepdims=True)
    return (scaled - first - hat * second) * inv


def body(
    cols,
    rows_n,
    tokens_in,
    pad_offsets,
    norm1_gain,
    norm1_bias,
    qkv_weight,
    qv_bias,
    table_height,
    table_width,
    proj_weight,
    proj_bias,
    norm2_gain,
    norm2_bias,
    fc1_weight,
    fc1_bias,
    fc2_weight,
    fc2_bias,
    out_grad,
):
    width = D // cols
    per = -(-WINDOWS // cols)
    rows = per * SLOT
    me = lax.axis_index("col")
    info = jnp.concatenate([me.astype(jnp.int32)[None], pad_offsets[0]])
    both = ("row", "col")

    x_pieces = exchange(spread(tokens_in, info, cols, per), cols)
    g_pieces = exchange(spread(out_grad, info, cols, per), cols)

    vec = jnp.concatenate(
        [
            norm1_gain,
            norm1_bias,
            norm2_gain,
            norm2_bias,
            proj_bias.astype(F32),
            fc2_bias.astype(F32),
            qv_bias[0].astype(F32),
            qv_bias[1].astype(F32),
            fc1_bias.astype(F32),
        ]
    )
    vecs = lax.all_gather(vec, "col", axis=0)
    picked = [vecs[:, i * width : (i + 1) * width].reshape(1, D) for i in range(8)]
    gain1, bias1, gain2, bias2, bias_p, bias_2, bias_q, bias_v = picked
    bias_h = vecs[:, 8 * width :].reshape(1, -1)
    bias_qkv = jnp.stack(
        [bias_q.reshape(cols, width), jnp.zeros((cols, width), F32), bias_v.reshape(cols, width)],
        axis=1,
    ).reshape(1, 3 * D)

    w_qkv = lax.all_gather(qkv_weight.reshape(-1, 3 * width), both, axis=0)
    w_qkv = w_qkv.reshape(rows_n, cols, -1, 3 * width).transpose(0, 2, 1, 3).reshape(D, 3 * D)
    w_proj = lax.all_gather(proj_weight, both, axis=0)
    w_proj = w_proj.reshape(rows_n, cols, width, -1).transpose(1, 2, 0, 3).reshape(D, D)
    fc_local = jnp.stack([fc1_weight, fc2_weight.T])
    fc_full = lax.all_gather(fc_local, both, axis=0)
    fc_full = fc_full.reshape(rows_n, cols, 2, fc_local.shape[1], fc_local.shape[2])
    fc_full = fc_full.transpose(2, 0, 3, 1, 4).reshape(2, D, -1)
    w_fc1, w_fc2 = fc_full[0], fc_full[1]

    x_full, n1 = norm1(x_pieces, info, gain1, bias1, cols, per)
    qkv = (nn_dot(n1, w_qkv) + bias_qkv).astype(BF)
    shifts_np, onehot_np = rel_constants()
    shifts = jnp.asarray(shifts_np)
    onehot = jnp.asarray(onehot_np, BF)
    tables = table_matrix(table_height, table_width)
    att, exps, inv = attend(qkv, tables, shifts, onehot, cols, per)

    resid = x_full.astype(F32) + nn_dot(att, w_proj) + bias_p
    hat2, inv2 = norm_stats(resid)
    n2 = (hat2 * gain2 + bias2).astype(BF)
    g_full = join(g_pieces, info, cols, per)

    pre = nn_dot(n2, w_fc1) + bias_h
    act_f, pull = jax.vjp(partial(jax.nn.gelu, approximate=False), pre)
    act = act_f.astype(BF)
    mlp = nt_dot(act, w_fc2) + bias_2
    block = (resid + mlp).astype(BF)
    block_pieces = exchange(pieces_of(block, me, cols, per), cols)
    block_out = collect(block_pieces, info, cols, per, BF)

    act_grad = nn_dot(g_full, w_fc2)
    pre_grad = pull(act_grad)[0].astype(BF)
    fc2_grad = tn_dot(g_full, act).astype(BF)
    fc1_grad = tn_dot(n2, pre_grad).astype(BF)
    n2_grad = nt_dot(pre_grad, w_fc1)

    def scatter(grad, r_dim):
        return lax.psum_scatter(grad, both, scatter_dimension=0, tiled=True)

    fc_grads = jnp.stack([fc1_grad, fc2_grad]).reshape(2, rows_n, D // rows_n, cols, -1)
    fc_grads = fc_grads.transpose(1, 3, 0, 2, 4).reshape(rows_n * cols, 2, D // rows_n, -1)
    fc_mine = scatter(fc_grads, 0)[0]

    g_f = g_full.astype(F32)
    resid_grad = g_f + norm_back(n2_grad, hat2, inv2, gain2)
    proj_grad = resid_grad.astype(BF)
    proj_w_grad = tn_dot(att, proj_grad).astype(BF)
    att_grad = nt_dot(proj_grad, w_proj).astype(BF)
    dqkv, table_sum, bias_sum = attend_back(
        qkv, exps, inv, att, att_grad, tables, shifts, onehot, cols, per
    )
    qkv_w_grad = tn_dot(n1, dqkv).astype(BF)
    n1_grad = nt_dot(dqkv, w_qkv)
    qkv_mine = scatter(
        qkv_w_grad.reshape(rows_n, D // rows_n, cols, 3 * width)
        .transpose(0, 2, 1, 3)
        .reshape(rows_n * cols, D // rows_n, 3 * width),
        0,
    )[0]
    proj_mine = scatter(
        proj_w_grad.reshape(cols, width, rows_n, D // rows_n)
        .transpose(2, 0, 1, 3)
        .reshape(rows_n * cols, width, D // rows_n),
        0,
    )[0]

    hat1, inv1 = norm_stats(x_full.astype(F32))
    input_part = (resid_grad + norm_back(n1_grad, hat1, inv1, gain1)).astype(BF)
    in_pieces = exchange(pieces_of(input_part, me, cols, per), cols)
    input_grad = collect(in_pieces, info, cols, per, F32)

    slot_windows = jnp.arange(per, dtype=jnp.int32)[:, None] + me * per
    place = jnp.arange(SLOT, dtype=jnp.int32)[None, :]
    row = WIN * (slot_windows // GRID) - info[1] + place // WIN
    col = WIN * (slot_windows % GRID) - info[2] + place % WIN
    keep = (row >= 0) & (row < SIDE) & (col >= 0) & (col < SIDE)
    keep = (keep & (place < REAL) & (slot_windows < WINDOWS)).reshape(rows, 1)
    n1_kept = jnp.where(keep, n1_grad, 0.0)
    bias_cols = jnp.sum(bias_sum, axis=0).reshape(cols, 3, width)

    def by_col(v):
        return v.reshape(cols, width)

    small = jnp.concatenate(
        [
            by_col(jnp.sum(n1_kept * hat1, axis=0)),
            by_col(jnp.sum(n1_kept, axis=0)),
            bias_cols[:, 0],
            bias_cols[:, 2],
            by_col(jnp.sum(proj_grad.astype(F32), axis=0)),
            by_col(jnp.sum(n2_grad * hat2, axis=0)),
            by_col(jnp.sum(n2_grad, axis=0)),
            by_col(jnp.sum(g_f, axis=0)),
            jnp.sum(pre_grad.astype(F32), axis=0).reshape(cols, -1),
        ],
        axis=1,
    )
    table_h_grad, table_w_grad = split_table(table_sum)
    small, table_h_grad, table_w_grad = lax.psum((small, table_h_grad, table_w_grad), both)
    mine = lax.dynamic_index_in_dim(small, me, 0, keepdims=False)

    def part(i):
        return mine[i * width : (i + 1) * width]

    return (
        block_out,
        input_grad,
        part(0),
        part(1),
        qkv_mine.astype(F32).reshape(-1, 3, width),
        jnp.stack([part(2), part(3)]),
        table_h_grad,
        table_w_grad,
        proj_mine.astype(F32),
        part(4),
        part(5),
        part(6),
        fc_mine[0].astype(F32),
        mine[8 * width :],
        fc_mine[1].astype(F32).T,
        part(7),
    )


def solution(mesh):
    placed = (
        P("row", "col"),
        P("row", None),
        P("col"),
        P("col"),
        P("row", None, "col"),
        P(None, "col"),
        P(),
        P(),
        P("col", "row"),
        P("col"),
        P("col"),
        P("col"),
        P("row", "col"),
        P("col"),
        P("col", "row"),
        P("col"),
        P("row", "col"),
    )
    return jax.shard_map(
        partial(body, mesh.shape["col"], mesh.shape["row"]),
        mesh=mesh,
        in_specs=placed,
        out_specs=(
            P("row", "col"),
            P("row", "col"),
            P("col"),
            P("col"),
            P("row", None, "col"),
            P(None, "col"),
            P(),
            P(),
            P("col", "row"),
            P("col"),
            P("col"),
            P("col"),
            P("row", "col"),
            P("col"),
            P("col", "row"),
            P("col"),
        ),
        check_vma=False,
    )
```

time: 3380 us -> 1220 us (0.36)
  waiting for transfers between devices: 1890 us -> 322 us
  matrix products: 643 us -> 247 us
  local copies, waits for them, and re-layouts: 496 us -> 157 us
  Pallas kernels: 0 us -> 150 us
  blocking collectives: 148 us -> 264 us
  other arithmetic: 131 us -> 36.5 us
  loops' own time: 41.7 us -> 0 us
    reduce_scatter x20 -> x3, waiting for transfers between devices: 1290 us -> 232 us  [scatter(): return lax.psum_scatter(grad, both, scatter_dimension=0, tiled=True)]
    all_gather x7 -> x3, waiting for transfers between devices: 593 us -> 60.3 us  [the longest x1 30.4 us: body(): fc_full = lax.all_gather(fc_local, both, axis=0)]
    dot_general x129 -> x12, matrix products: 643 us -> 247 us  [the longest x4 121 us: nn_dot(): lax.dot_general(a, b, (((1,), (0,)), ((), ())), preferred_element_type=F32)]
    pallas_call x0 -> x8, Pallas kernels: none -> 150 us  [the longest x1 54.1 us: attend(): pl.pallas_call(partial(attend_kernel, width), out_shape=[jax.ShapeDtypeSt...]
    gather x8 -> x0, local copies, waits for them, and re-layouts: 122 us -> none  [the longest x6 81.4 us: place_slots(): picked = jnp.take(values, sources.reshape(-1), axis=0)]
    all_gather x1, blocking collectives: 11.1 us -> 97.5 us  [body(): vecs = lax.all_gather(vec, 'col', axis=0)]
    dot_general x20 -> x0, local copies, waits for them, and re-layouts: 64.8 us -> none  [the longest x10 33.3 us: window_scores(): jnp.einsum('wqhc,jc->wqhj', queries, table_h, preferred_element_type=jnp....]
    reduce_sum x10 -> x0, local copies, waits for them, and re-layouts: 48 us -> none  [the longest x5 26 us: attend_back(): sum_w = jnp.sum(shaped, axis=-2)]
  transfers between devices with their start and end apart: 27 -> 18, of which waited for: 24 -> 5; matrix products, arithmetic and copies ran while one was open for 3% -> 22% of each run, Pallas kernels for 0% -> 12%
where the time goes in v1:
time: 1220 us; the launch traced here: 1210 us
  waiting for transfers between devices  322 us (26%)
  blocking collectives  264 us (22%)
  matrix products  247 us (20%)
  local copies, waits for them, and re-layouts  157 us (13%)
  Pallas kernels  150 us (12%)
  other arithmetic  36.5 us (3%)
  starting transfers between devices  18 us (1%)
  between operations  15.2 us (1%)
    reduce_scatter x3, waiting for transfers between devices, scatter(): return lax.psum_scatter(grad, both, scatter_dimension=0, tiled=True)  232 us
    psum x1, blocking collectives, body(): lax.psum((small, table_h_grad, table_w_grad), both)  166 us
    dot_general x4, matrix products, nn_dot(): lax.dot_general(a, b, (((1,), (0,)), ((), ())), preferred_element_type=F32)  121 us
    all_gather x1, blocking collectives, body(): vecs = lax.all_gather(vec, 'col', axis=0)  97.5 us
    dot_general x4, matrix products, nt_dot(): lax.dot_general(a, b, (((1,), (1,)), ((), ())), preferred_element_type=F32)  67.2 us
    dot_general x4, matrix products, tn_dot(): lax.dot_general(a, b, (((0,), (0,)), ((), ())), preferred_element_type=F32)  59.1 us
    pallas_call x1, Pallas kernels, attend(): pl.pallas_call(partial(attend_kernel, width), out_shape=[jax.ShapeDtypeSt...  54.1 us
    pallas_call x1, Pallas kernels, attend_back(): pl.pallas_call(partial(attend_back_kernel, width), out_shape=[jax.ShapeDt...  48.3 us
  transfers between devices with their start and end apart: 18, of which 5 were waited for; matrix products, arithmetic and copies ran while one was open for 22% of the time, Pallas kernels for 12%

profile of v1, /device:TPU:0, one launch (start us, length us, event | category | flops | bytes accessed | tf_op | source)
XLA Modules:
  0.0 1209.8 jit_solution(15953421850982274422)
XLA Ops:
  8.1 1.1 copy.68
  10.1 1.1 copy.75
  11.2 1.8 pad_maximum_fusion
  13.0 1.2 pad_add_fusion.info
  14.2 7.0 spread.2
  21.2 3.0 collective-permute-start
  24.3 2.6 collective-permute-start.1
  26.9 7.0 spread.3
  34.8 3.5 collective-permute-start.7
  38.4 97.5 %all-gather = f32[12288]{0:T(1024)S(1)} all-gather(f32[3072]{0:T(1024)S(1)} %constant_dynamic-update-slice_fusion.10), channel_id=2, replica_groups=mesh['row'=8,'col'=4] {'col'}, dimensions={0}, use_global_device_ids=true | all-gather | bytes 61440 | tf_op jit(solution)/shard_map/all_gather | solution.py:528
  137.8 1.4 collective-permute-start.8
  140.9 15.2 %collective-permute-done.8.refs_3_ = bf16[7,200,256]{2,1,0:T(8,128)(2,1)} collective-permute-done((bf16[7,200,256]{2,1,0:T(8,128)(2,1)}, bf16[7,200,256]{2,1,0:T(8,128)(2,1)}, u32[]{:S(2)}, u32[]{:S(2)}) %collective-permute-start.8) | collective-permute-done | bytes 716832 | tf_op jit(solution)/shard_map/ppermute | solution.py:457
  156.1 6.7 join.1
  164.2 8.5 norm1.1
  172.6 4.3 copy.74
  176.9 29.9 %all-gather.7.cloned.1.call-done = bf16[32,128,768]{2,1,0:T(8,128)(2,1)} async-done(((bf16[1,128,768]{2,1,0:T(8,128)(2,1)}), bf16[32,128,768]{2,1,0:T(8,128)(2,1)}) %all-gather.7.cloned.1.call-update) | async-done | bytes 6291472 | tf_op jit(solution)/shard_map/all_gather | solution.py:537
  206.8 9.2 copy.70
  216.0 14.4 %add_convert_fusion.1.qkv = bf16[1400,3072]{1,0:T(8,128)(2,1)} fusion(bf16[1400,1024]{1,0:T(8,128)(2,1)S(1)} %copy-done.34, f32[3072]{0:T(1024)S(1)} %add.211, bf16[384,8,8,128]{3,2,1,0:T(8,128)(2,1)} %bitcast.196), kind=kOutput, calls=%fused_computation.18 | convolution fusion | flops 8816640000 | bytes 17772544 | tf_op jit(solution)/shard_map/dot_general | solution.py:49
  230.4 54.1 %attend.1 = (bf16[1400,1024]{1,0:T(8,128)(2,1)}, bf16[16,1400,256]{2,1,0:T(8,128)(2,1)}, f32[1400,1024]{1,0:T(8,128)}) custom-call(bf16[1400,3072]{1,0:T(8,128)(2,1)} %add_convert_fusion.1.qkv, bf16[128,128]{1,0:T(8,128)(2,1)} %pad_maximum_fusion.2.tables, s32[200,128]{1,0:T(8,128)} %constant.163.clone.shifts, bf16[2,256,128]{2,1,0:T(8,128)(2,1)} %constant.164.clone.onehot), custom_call_target="tpu_custom_call" | custom-call | tf_op jit(solution)/shard_map/attend/pallas_call | solution.py:318
  284.5 6.0 fusion.62
  290.5 2.4 copy-done.3
  293.6 30.4 %all-gather.11.cloned.1.call-done = bf16[64,128,1024]{2,1,0:T(8,128)(2,1)} async-done(((bf16[2,128,1024]{2,1,0:T(8,128)(2,1)}), bf16[64,128,1024]{2,1,0:T(8,128)(2,1)}) %all-gather.11.cloned.1.call-update) | async-done | bytes 16777232 | tf_op jit(solution)/shard_map/all_gather | solution.py:542
  324.0 23.7 %copy.76 = bf16[8,4,2,128,1024]{3,0,4,1,2:T(8,128)(2,1)} copy(bf16[8,4,2,128,1024]{4,3,2,1,0:T(8,128)(2,1)} %bitcast.189) | data formatting | bytes 33554432 | tf_op jit(solution)/shard_map/reshape | solution.py:543
  347.7 11.3 fusion.56
  359.0 70.1 %multiply_convert_fusion = (bf16[1400,4096]{1,0:T(8,128)(2,1)}, f32[1400,4096]{1,0:T(8,128)}, f32[1400,4096]{1,0:T(8,128)}) fusion(f32[4096]{0:T(1024)S(1)} %bitcast.223, bf16[512,8,8,128]{3,2,1,0:T(8,128)(2,1)} %bitcast.194, f32[1400,1024]{1,0:T(8,128)} %copy-done.3, f32[1024]{0:T(1024)S(1)} %bitcast.225, f32[1024]{0:T(1024)S(1)} %bitcast.213, ...), kind=kOutput, calls=%fused_computation.4 | convolution fusion | flops 12129689600 | bytes 71502784 | tf_op jit(solution)/shard_map/dot_general | solution.py:49
  429.2 30.1 %convert_reduce_fusion = (f32[4096]{0:T(1024)}, bf16[1400,4096]{1,0:T(8,128)(2,1)}) fusion(f32[1400,4096]{1,0:T(8,128)} %get-tuple-element.94, bf16[1400,1024]{1,0:T(8,128)(2,1)S(1)} %copy-done.5, bf16[512,8,8,128]{3,2,1,0:T(8,128)(2,1)} %bitcast.192, f32[1400,4096]{1,0:T(8,128)} %get-tuple-element.137, f32[4096]{0:T(1024)S(1)} %bitcast.224), kind=kOutput, calls=%fused_computation.2 | convolution fusion | flops 11841531904 | bytes 68632576 | tf_op jit(solution)/shard_map/dot_general | solution.py:49
  459.3 21.7 %multiply_reduce_fusion = (f32[1024]{0:T(1024)}, f32[1400]{0:T(1024)S(1)}, f32[1400]{0:T(1024)S(1)}, f32[1024]{0:T(1024)}, f32[1400,1024]{1,0:T(8,128)S(1)}) fusion(f32[1400,1024]{1,0:T(8,128)} %copy-done.3, f32[1400]{0:T(1024)S(1)} %add_rsqrt_fusion.1, f32[1400]{0:T(1024)S(1)} %broadcast_multiply_fusion.5, f32[1024]{0:T(1024)S(1)} %bitcast.214, ...), kind=kOutput, calls=%fused_computation.54 | convolution fusion | flops 11756949504 | bytes 31360896 | tf_op jit(solution)/shard_map/dot_general | solution.py:41
  481.0 3.8 convert_reduce_fusion.3
  484.8 3.9 convert_bitcast_fusion
  489.5 1.8 copy.88
  492.1 8.1 convolution_convert_fusion.3.att_grad
  500.1 48.3 %attend_back.1 = (bf16[1400,3072]{1,0:T(8,128)(2,1)}, f32[128,256]{1,0:T(8,128)}, f32[8,3072]{1,0:T(8,128)}) custom-call(bf16[1400,3072]{1,0:T(8,128)(2,1)} %add_convert_fusion.1.qkv, bf16[16,1400,256]{2,1,0:T(8,128)(2,1)} %get-tuple-element.43.exps, f32[1400,1024]{1,0:T(8,128)} %get-tuple-element.44.inv, bf16[1400,1024]{1,0:T(8,128)(2,1)} %get-tuple-element.38.att, ...), custom_call_target="tpu_custom_call" | custom-call | tf_op jit(solution)/shard_map/attend_back/pallas_call | solution.py:419
  548.4 15.1 %convolution_convert_fusion.2 = bf16[1024,3072]{1,0:T(8,128)(2,1)} fusion(bf16[1400,1024]{1,0:T(8,128)(2,1)} %get-tuple-element.37, bf16[1400,3072]{1,0:T(8,128)(2,1)} %get-tuple-element.45), kind=kOutput, calls=%fused_computation.60 | convolution fusion | flops 8811184128 | bytes 17760256 | tf_op jit(solution)/shard_map/dot_general | solution.py:45
  563.6 12.3 %reshape.362 = bf16[8,128,4,768]{3,2,1,0:T(4,128)(2,1)} reshape(bf16[1024,3072]{1,0:T(8,128)(2,1)} %convolution_convert_fusion.2) | data formatting | bytes 12582912 | tf_op jit(solution)/shard_map/reshape | solution.py:592
  575.9 6.7 copy.85
  582.6 21.5 %convolution_convert_fusion.1 = bf16[1024,4096]{1,0:T(8,128)(2,1)} fusion(bf16[1400,4096]{1,0:T(8,128)(2,1)} %get-tuple-element.141, f32[1400,1024]{1,0:T(8,128)} %copy-done.3, f32[1024]{0:T(1024)S(1)} %bitcast.226, f32[1024]{0:T(1024)S(1)} %bitcast.216, f32[1400]{0:T(1024)S(1)} %add_rsqrt_fusion.1, f32[1400]{0:T(1024)S(1)} %broadcast_multiply_fusion.5), kind=kOutput, calls=%fused_computation.31 | convolution fusion | flops 11755413504 | bytes 25611200 | tf_op jit(solution)/shard_map/dot_general | solution.py:45
  604.2 14.5 %stack.43 = bf16[1,8,128,4,1024]{4,3,2,1,0:T(4,128)(2,1)} reshape(bf16[1024,4096]{1,0:T(8,128)(2,1)} %convolution_convert_fusion.1) | data formatting | bytes 16777216 | tf_op jit(solution)/shard_map/stack | solution.py:577
  618.7 18.5 %convolution_convert_fusion = bf16[1024,4096]{1,0:T(8,128)(2,1)} fusion(bf16[1400,1024]{1,0:T(8,128)(2,1)S(1)} %copy-done.5, bf16[1400,4096]{1,0:T(8,128)(2,1)} %get-tuple-element.93), kind=kOutput, calls=%fused_computation.30 | convolution fusion | flops 11748245504 | bytes 22724608 | tf_op jit(solution)/shard_map/dot_general | solution.py:45
  637.2 14.7 %stack.44 = bf16[1,8,128,4,1024]{4,3,2,1,0:T(4,128)(2,1)} reshape(bf16[1024,4096]{1,0:T(8,128)(2,1)} %convolution_convert_fusion) | data formatting | bytes 16777216 | tf_op jit(solution)/shard_map/stack | solution.py:577
  651.9 13.9 %maximum_bitcast_fusion = bf16[8,4,2,128,1024]{4,1,3,0,2:T(4,128)(2,1)S(1)} fusion(bf16[1,8,128,4,1024]{4,3,2,1,0:T(4,128)(2,1)} %stack.44, bf16[1,8,128,4,1024]{4,3,2,1,0:T(4,128)(2,1)} %stack.43), kind=kLoop, calls=%fused_computation.19 | loop fusion | flops 8388608 | bytes 33554432 | tf_op jit(solution)/shard_map/transpose | solution.py:578
  665.8 8.7 copy.89
  675.7 1.3 fusion.50
  678.6 18.6 %fusion.30 = (f32[1024]{0:T(1024)S(1)}, f32[1400]{0:T(1024)S(1)}, f32[1400]{0:T(1024)S(1)}, f32[1024]{0:T(1024)S(1)}, f32[1400,1024]{1,0:T(8,128)}) fusion(bf16[1400,1024]{1,0:T(8,128)(2,1)S(1)} %copy-done.1, f32[1400]{0:T(1024)S(1)} %add_rsqrt_fusion, f32[1400]{0:T(1024)S(1)} %broadcast_multiply_fusion.1, pred[1400]{0:T(1024)(128)(4,1)S(1)} %reshape.376, ...), kind=kOutput, calls=%fused_computation.51 | convolution fusion | flops 8823803904 | bytes 23530744 | tf_op jit(solution)/shard_map/dot_general | solution.py:41
  697.3 6.8 fusion.29
  704.1 5.2 reshape.353
  709.3 6.8 constant_dynamic-slice_fusion.1
  716.1 1.0 copy.172
  718.8 1.2 collective-permute-start.11
  720.0 1.1 copy.173
  721.1 1.6 collective-permute-start.9
  722.7 18.9 %add_convert_fusion.2 = bf16[1400,1024]{1,0:T(8,128)(2,1)} fusion(f32[1400,1024]{1,0:T(8,128)} %copy-done.3, bf16[1400,4096]{1,0:T(8,128)(2,1)} %get-tuple-element.93, bf16[512,8,8,128]{3,2,1,0:T(8,128)(2,1)} %bitcast.193, f32[1024]{0:T(1024)S(1)} %bitcast.228), kind=kOutput, calls=%fused_computation.57 | convolution fusion | flops 11748352000 | bytes 28463104 | tf_op jit(solution)/shard_map/dot_general | solution.py:41
  741.6 5.2 reshape.352
  746.8 7.0 constant_dynamic-slice_fusion.5
  756.2 1.2 collective-permute-start.4
  757.7 2.4 copy.175
  760.2 13.5 %collective-permute-done.10.refs_2_ = bf16[7,200,256]{2,1,0:T(8,128)(2,1)} collective-permute-done((bf16[7,200,256]{2,1,0:T(8,128)(2,1)}, bf16[7,200,256]{2,1,0:T(8,128)(2,1)}, u32[]{:S(2)}, u32[]{:S(2)}) %collective-permute-start.10) | collective-permute-done | bytes 716832 | tf_op jit(solution)/shard_map/ppermute | solution.py:457
  773.7 1.3 collective-permute-start.5
  777.1 166.4 %all-reduce.3 = (f32[4,3072]{1,0:T(4,128)S(1)}, f32[27,64]{1,0:T(8,128)}, f32[27,64]{1,0:T(8,128)}) all-reduce(f32[4,3072]{1,0:T(4,128)S(1)} %constant_dynamic-update-slice_fusion.1, f32[27,64]{1,0:T(8,128)S(1)} %bitcast.209, f32[27,64]{1,0:T(8,128)S(1)} %bitcast.210), channel_id=1, replica_groups=mesh['row'=8,'col'=4] {'row','col'}, use_global_device_ids=true, to_apply=%region_16.17 | all-reduce | flops 15744 | bytes 125952 | tf_op jit(solution)/shard_map/psum | solution.py:636
  945.3 9.6 collect.3
  954.9 8.8 collect.2
  963.7 1.5 bitcast_convert_fusion
  965.2 1.1 copy.86
  967.2 232.5 %reduce-scatter.8.cloned.1.call-done = bf16[1,2,128,1024]{3,2,1,0:T(8,128)(2,1)} async-done(((bf16[32,2,128,1024]{3,2,1,0:T(8,128)(2,1)}), bf16[1,2,128,1024]{3,2,1,0:T(8,128)(2,1)}) %reduce-scatter.8.cloned.1.call-update) | async-done | bytes 524304 | tf_op jit(solution)/shard_map/reduce_scatter | solution.py:575
  1199.7 1.9 convert_bitcast_fusion.1
  (191 shorter events, 23.0 us)
Async XLA Ops:
  7.2 31.1 %copy-start.30 = (f32[256]{0:T(256)S(1)}, f32[256]{0:T(256)}, u32[]{:S(2)}) copy-start(f32[256]{0:T(256)} %param.21) | copy-start | bytes 3076
  7.2 31.1 %copy-start.31 = (f32[256]{0:T(256)S(1)}, f32[256]{0:T(256)}, u32[]{:S(2)}) copy-start(f32[256]{0:T(256)} %param.22) | copy-start | bytes 3076
  7.2 31.1 %copy-start.32 = (f32[256]{0:T(256)S(1)}, f32[256]{0:T(256)}, u32[]{:S(2)}) copy-start(f32[256]{0:T(256)} %param.29) | copy-start | bytes 3076
  7.2 31.1 %copy-start.33 = (f32[256]{0:T(256)S(1)}, f32[256]{0:T(256)}, u32[]{:S(2)}) copy-start(f32[256]{0:T(256)} %param.30) | copy-start | bytes 3076
  7.2 31.1 %copy-start.35 = (bf16[256]{0:T(256)(128)(2,1)S(1)}, bf16[256]{0:T(256)(128)(2,1)}, u32[]{:S(2)}) copy-start(bf16[256]{0:T(256)(128)(2,1)} %param.28) | copy-start | bytes 1540
  7.2 31.1 %copy-start.27 = (bf16[2,256]{1,0:T(2,128)(2,1)S(1)}, bf16[2,256]{1,0:T(2,128)(2,1)}, u32[]{:S(2)}) copy-start(bf16[2,256]{1,0:T(2,128)(2,1)} %param.24) | copy-start | bytes 3076
  7.2 31.1 %copy-start.36 = (bf16[256]{0:T(256)(128)(2,1)S(1)}, bf16[256]{0:T(256)(128)(2,1)}, u32[]{:S(2)}) copy-start(bf16[256]{0:T(256)(128)(2,1)} %param.34) | copy-start | bytes 1540
  7.3 31.2 %copy-start.28 = (bf16[1024]{0:T(1024)(128)(2,1)S(1)}, bf16[1024]{0:T(1024)(128)(2,1)}, u32[]{:S(2)}) copy-start(bf16[1024]{0:T(1024)(128)(2,1)} %param.32) | copy-start | bytes 6148
  7.3 132.1 %copy-start.21 = (f32[27,64]{1,0:T(8,128)S(1)}, f32[27,64]{1,0:T(8,128)}, u32[]{:S(2)}) copy-start(f32[27,64]{1,0:T(8,128)} %param.25) | copy-start | bytes 20740
  7.3 132.1 %copy-start.20 = (f32[27,64]{1,0:T(8,128)S(1)}, f32[27,64]{1,0:T(8,128)}, u32[]{:S(2)}) copy-start(f32[27,64]{1,0:T(8,128)} %param.26) | copy-start | bytes 20740
  7.3 165.4 %all-gather.9.cloned.1.call-start = ((), (), s32[]{:S(2)}) async-start(), calls=%async_computation.7 | async-start | bytes 2162688 | tf_op jit(solution)/shard_map/all_gather | solution.py:539
  8.0 198.8 %all-gather.7.cloned.1.call-start = ((), (), s32[]{:S(2)}) async-start(), calls=%async_computation.3 | async-start | bytes 6488064 | tf_op jit(solution)/shard_map/all_gather | solution.py:537
  10.0 314.0 %all-gather.11.cloned.1.call-start = ((), (), s32[]{:S(2)}) async-start(), calls=%async_computation.8 | async-start | bytes 17301504 | tf_op jit(solution)/shard_map/all_gather | solution.py:542
  13.0 950.8 %reduce-scatter.6.cloned.1.call-start = ((), (), s32[]{:S(2)}) async-start(), calls=%async_computation.5 | async-start | bytes 2162688 | tf_op jit(solution)/shard_map/reduce_scatter | solution.py:575
  21.2 141.5 %collective-permute-start = (bf16[7,200,256]{2,1,0:T(8,128)(2,1)}, bf16[7,200,256]{2,1,0:T(8,128)(2,1)S(1)}, u32[]{:S(2)}, u32[]{:S(2)}) collective-permute-start(bf16[7,200,256]{2,1,0:T(8,128)(2,1)} %get-tuple-element.33), channel_id=1, source_target_pairs={{0,1},{1,0},{2,3},{3,2},{4,5},{5,4},{6,7},{7,6},{8,9},{9,8},{10,11... | collective-permute-start | bytes 2150408 | tf_op jit(solution)/shard_map/ppermute | solution.py:457
  24.3 138.5 %collective-permute-start.1 = (bf16[7,200,256]{2,1,0:T(8,128)(2,1)}, bf16[7,200,256]{2,1,0:T(8,128)(2,1)S(1)}, u32[]{:S(2)}, u32[]{:S(2)}) collective-permute-start(bf16[7,200,256]{2,1,0:T(8,128)(2,1)} %get-tuple-element.34), channel_id=1, source_target_pairs={{0,2},{1,3},{2,0},{3,1},{4,6},{5,7},{6,4},{7,5},{8,10},{9,11},{10,... | collective-permute-start | bytes 2150408 | tf_op jit(solution)/shard_map/ppermute | solution.py:457
  26.9 136.0 %collective-permute-start.2 = (bf16[7,200,256]{2,1,0:T(8,128)(2,1)}, bf16[7,200,256]{2,1,0:T(8,128)(2,1)S(1)}, u32[]{:S(2)}, u32[]{:S(2)}) collective-permute-start(bf16[7,200,256]{2,1,0:T(8,128)(2,1)} %get-tuple-element.35), channel_id=1, source_target_pairs={{0,3},{1,2},{2,1},{3,0},{4,7},{5,6},{6,5},{7,4},{8,11},{9,10},{10,... | collective-permute-start | bytes 2150408 | tf_op jit(solution)/shard_map/ppermute | solution.py:457
  33.9 104.0 %collective-permute-start.6 = (bf16[7,200,256]{2,1,0:T(8,128)(2,1)}, bf16[7,200,256]{2,1,0:T(8,128)(2,1)S(1)}, u32[]{:S(2)}, u32[]{:S(2)}) collective-permute-start(bf16[7,200,256]{2,1,0:T(8,128)(2,1)} %get-tuple-element.40), channel_id=1, source_target_pairs={{0,1},{1,0},{2,3},{3,2},{4,5},{5,4},{6,7},{7,6},{8,9},{9,8},{10,11... | collective-permute-start | bytes 2150408 | tf_op jit(solution)/shard_map/ppermute | solution.py:457
  34.8 106.1 %collective-permute-start.7 = (bf16[7,200,256]{2,1,0:T(8,128)(2,1)}, bf16[7,200,256]{2,1,0:T(8,128)(2,1)}, u32[]{:S(2)}, u32[]{:S(2)}) collective-permute-start(bf16[7,200,256]{2,1,0:T(8,128)(2,1)} %get-tuple-element.41), channel_id=1, source_target_pairs={{0,2},{1,3},{2,0},{3,1},{4,6},{5,7},{6,4},{7,5},{8,10},{9,11},{10,... | collective-permute-start | bytes 2150408 | tf_op jit(solution)/shard_map/ppermute | solution.py:457
  137.8 18.2 %copy-start.12 = (bf16[7,200,256]{2,1,0:T(8,128)(2,1)}, bf16[7,200,256]{2,1,0:T(8,128)(2,1)S(1)}, u32[]{:S(2)}) copy-start(bf16[7,200,256]{2,1,0:T(8,128)(2,1)S(1)} %collective-permute-done.6.refs_1_) | copy-start | bytes 2150404
  137.8 18.2 %collective-permute-start.8 = (bf16[7,200,256]{2,1,0:T(8,128)(2,1)}, bf16[7,200,256]{2,1,0:T(8,128)(2,1)}, u32[]{:S(2)}, u32[]{:S(2)}) collective-permute-start(bf16[7,200,256]{2,1,0:T(8,128)(2,1)} %get-tuple-element.42), channel_id=1, source_target_pairs={{0,3},{1,2},{2,1},{3,0},{4,7},{5,6},{6,5},{7,4},{8,11},{9,10},{10,... | collective-permute-start | bytes 2150408 | tf_op jit(solution)/shard_map/ppermute | solution.py:457
  139.7 0.6 copy-start.13
  139.7 1.2 copy-start.15
  162.8 0.9 copy-start.9
  162.8 1.1 copy-start.10
  162.8 1.4 copy-start.11
  206.8 9.2 copy-start.34
  230.4 54.1 %copy-start = (bf16[1400,1024]{1,0:T(8,128)(2,1)S(1)}, bf16[1400,1024]{1,0:T(8,128)(2,1)}, u32[]{:S(2)}) copy-start(bf16[1400,1024]{1,0:T(8,128)(2,1)} %get-tuple-element.36) | copy-start | bytes 8601604
  290.5 2.4 copy-start.3
  359.0 70.2 %copy-start.5 = (bf16[1400,1024]{1,0:T(8,128)(2,1)S(1)}, bf16[1400,1024]{1,0:T(8,128)(2,1)}, u32[]{:S(2)}) copy-start(bf16[1400,1024]{1,0:T(8,128)(2,1)} %join.1) | copy-start | bytes 8601604
  459.3 21.7 %copy-start.4 = (f32[1400,1024]{1,0:T(8,128)S(1)}, f32[1400,1024]{1,0:T(8,128)}, u32[]{:S(2)}) copy-start(f32[1400,1024]{1,0:T(8,128)} %copy-done.3) | copy-start | bytes 17203204
  481.0 3.8 copy-start.8
  484.8 4.0 copy-start.2
  489.4 2.1 copy-start.14
  489.4 2.1 copy-start.16
  491.4 473.8 %reduce-scatter.4.cloned.1.call-start = ((), (), s32[]{:S(2)}) async-start(), calls=%async_computation.4 | async-start | bytes 6488064 | tf_op jit(solution)/shard_map/reduce_scatter | solution.py:575
  582.6 617.1 %reduce-scatter.8.cloned.1.call-start = ((), (), s32[]{:S(2)}) async-start(), calls=%async_computation.6 | async-start | bytes 17301504 | tf_op jit(solution)/shard_map/reduce_scatter | solution.py:575
  674.4 0.7 copy-start.29
  674.4 2.7 copy-start.23
  674.4 2.8 copy-start.22
  674.4 2.8 copy-start.1
  678.6 18.6 %copy-start.18 = (f32[8,3072]{1,0:T(8,128)S(1)}, f32[8,3072]{1,0:T(8,128)}, u32[]{:S(2)}) copy-start(f32[8,3072]{1,0:T(8,128)} %get-tuple-element.46) | copy-start | bytes 294916
  717.2 56.5 %collective-permute-start.10 = (bf16[7,200,256]{2,1,0:T(8,128)(2,1)}, bf16[7,200,256]{2,1,0:T(8,128)(2,1)}, u32[]{:S(2)}, u32[]{:S(2)}) collective-permute-start(bf16[7,200,256]{2,1,0:T(8,128)(2,1)} %bitcast.177), channel_id=1, source_target_pairs={{0,2},{1,3},{2,0},{3,1},{4,6},{5,7},{6,4},{7,5},{8,10},{9,11},{10,... | collective-permute-start | bytes 2150408 | tf_op jit(solution)/shard_map/ppermute | solution.py:457
  718.8 226.5 %collective-permute-start.11 = (bf16[7,200,256]{2,1,0:T(8,128)(2,1)}, bf16[7,200,256]{2,1,0:T(8,128)(2,1)}, u32[]{:S(2)}, u32[]{:S(2)}) collective-permute-start(bf16[7,200,256]{2,1,0:T(8,128)(2,1)} %bitcast.176), channel_id=1, source_target_pairs={{0,3},{1,2},{2,1},{3,0},{4,7},{5,6},{6,5},{7,4},{8,11},{9,10},{10,... | collective-permute-start | bytes 2150408 | tf_op jit(solution)/shard_map/ppermute | solution.py:457
  721.1 224.3 %collective-permute-start.9 = (bf16[7,200,256]{2,1,0:T(8,128)(2,1)}, bf16[7,200,256]{2,1,0:T(8,128)(2,1)}, u32[]{:S(2)}, u32[]{:S(2)}) collective-permute-start(bf16[7,200,256]{2,1,0:T(8,128)(2,1)} %bitcast.178), channel_id=1, source_target_pairs={{0,1},{1,0},{2,3},{3,2},{4,5},{5,4},{6,7},{7,6},{8,9},{9,8},{10,11... | collective-permute-start | bytes 2150408 | tf_op jit(solution)/shard_map/ppermute | solution.py:457
  746.8 10.6 copy-start.17
  753.8 21.2 %copy-start.26 = (f32[1024]{0:T(1024)S(1)}, f32[1024]{0:T(1024)}, u32[]{:S(2)}) copy-start(f32[1024]{0:T(1024)} %get-tuple-element.80) | copy-start | bytes 12292
  753.8 21.2 %copy-start.25 = (f32[1024]{0:T(1024)S(1)}, f32[1024]{0:T(1024)}, u32[]{:S(2)}) copy-start(f32[1024]{0:T(1024)} %get-tuple-element.87) | copy-start | bytes 12292
  753.8 21.2 %copy-start.19 = (f32[1024]{0:T(1024)S(1)}, f32[1024]{0:T(1024)}, u32[]{:S(2)}) copy-start(f32[1024]{0:T(1024)} %get-tuple-element.97) | copy-start | bytes 12292
  753.8 21.2 %copy-start.24 = (f32[4096]{0:T(1024)S(1)}, f32[4096]{0:T(1024)}, u32[]{:S(2)}) copy-start(f32[4096]{0:T(1024)} %get-tuple-element.140) | copy-start | bytes 49156
  753.8 21.3 %copy-start.6 = (bf16[7,200,1,256]{3,2,1,0:T(2,128)(2,1)S(1)}, bf16[7,200,1,256]{3,2,1,0:T(2,128)(2,1)}, u32[]{:S(2)}) copy-start(bf16[7,200,1,256]{3,2,1,0:T(2,128)(2,1)} %get-tuple-element.101) | copy-start | bytes 2150404
  753.8 22.2 %copy-start.7 = (bf16[7,200,1,256]{3,2,1,0:T(2,128)(2,1)S(1)}, bf16[7,200,1,256]{3,2,1,0:T(2,128)(2,1)}, u32[]{:S(2)}) copy-start(bf16[7,200,1,256]{3,2,1,0:T(2,128)(2,1)} %get-tuple-element.105) | copy-start | bytes 2150404
  754.8 200.1 %collective-permute-start.3 = (bf16[7,200,256]{2,1,0:T(8,128)(2,1)}, bf16[7,200,256]{2,1,0:T(8,128)(2,1)}, u32[]{:S(2)}, u32[]{:S(2)}) collective-permute-start(bf16[7,200,256]{2,1,0:T(8,128)(2,1)} %bitcast.182), channel_id=1, source_target_pairs={{0,1},{1,0},{2,3},{3,2},{4,5},{5,4},{6,7},{7,6},{8,9},{9,8},{10,11... | collective-permute-start | bytes 2150408 | tf_op jit(solution)/shard_map/ppermute | solution.py:457
  756.2 198.7 %collective-permute-start.4 = (bf16[7,200,256]{2,1,0:T(8,128)(2,1)}, bf16[7,200,256]{2,1,0:T(8,128)(2,1)}, u32[]{:S(2)}, u32[]{:S(2)}) collective-permute-start(bf16[7,200,256]{2,1,0:T(8,128)(2,1)} %bitcast.181), channel_id=1, source_target_pairs={{0,2},{1,3},{2,0},{3,1},{4,6},{5,7},{6,4},{7,5},{8,10},{9,11},{10,... | collective-permute-start | bytes 2150408 | tf_op jit(solution)/shard_map/ppermute | solution.py:457
  773.7 181.3 %collective-permute-start.5 = (bf16[7,200,256]{2,1,0:T(8,128)(2,1)}, bf16[7,200,256]{2,1,0:T(8,128)(2,1)}, u32[]{:S(2)}, u32[]{:S(2)}) collective-permute-start(bf16[7,200,256]{2,1,0:T(8,128)(2,1)} %bitcast.180), channel_id=1, source_target_pairs={{0,3},{1,2},{2,1},{3,0},{4,7},{5,6},{6,5},{7,4},{8,11},{9,10},{10,... | collective-permute-start | bytes 2150408 | tf_op jit(solution)/shard_map/ppermute | solution.py:457
Sparse Core Ops, SparseCore 0:
  11.0 106.6 all-gather.8
  121.2 85.6 all-gather.6
  210.4 113.5 all-gather.10
  491.5 136.0 reduce-scatter.5
  634.1 148.9 reduce-scatter.3
  785.2 414.4 reduce-scatter.7

commit v2 on v1

v2 whole, which is shorter than its diff:
```python
from functools import partial

import jax
import jax.numpy as jnp
import numpy as np
from jax import lax
from jax.experimental import pallas as pl
from jax.experimental.pallas import tpu as pltpu
from jax.sharding import PartitionSpec as P

D = 1024
HD = 64
WIN = 14
SIDE = 64
GRID = 5
WINDOWS = 25
REAL = 196
SLOT = 200
KEYS = 256
PIX = 4096
EPSILON = 1e-06
MARGIN = 6
PADROWS = 84
BF = jnp.bfloat16
F32 = jnp.float32
VMEM_LIMIT = 60 * 1024 * 1024
SPLITS = 4
BLOCKS = 4
SLAB = 224
FIELDS = 7
HEAD = 5
TAIL = 16


def iota(shape, dim):
    return lax.broadcasted_iota(jnp.int32, shape, dim)


def params(n=1):
    return pltpu.CompilerParams(
        dimension_semantics=("arbitrary",) * n, vmem_limit_bytes=VMEM_LIMIT
    )


def cost(micros):
    return pl.CostEstimate(
        flops=int(micros * 1.1e9), bytes_accessed=int(micros * 1e6), transcendentals=0
    )


def nt_dot(a, b):
    return lax.dot_general(a, b, (((1,), (1,)), ((), ())), preferred_element_type=F32)


def tn_dot(a, b):
    return lax.dot_general(a, b, (((0,), (0,)), ((), ())), preferred_element_type=F32)


def nn_dot(a, b):
    return lax.dot_general(a, b, (((1,), (0,)), ((), ())), preferred_element_type=F32)


def window_sets(cols, per):
    units = [[0, 4, 20, 24]]
    units += [[j, 20 + j] for j in (1, 2, 3)] + [[5 * i, 5 * i + 4] for i in (1, 2, 3)]
    units += [[5 * i + j] for i in (1, 2, 3) for j in (1, 2, 3)]
    sizes = [484] + [308] * 6 + [196] * 9
    sets = [[] for _ in range(cols)]
    loads = [0] * cols
    for unit, size in zip(units, sizes):
        open_sets = [d for d in range(cols) if len(sets[d]) + len(unit) <= per]
        best = min(open_sets, key=lambda d: loads[d])
        sets[best] += unit
        loads[best] += size
    capacity = -(-(max(loads) + TAIL) // 64) * 64
    return [own + [WINDOWS] * (per - len(own)) for own in sets], capacity


def layout_info(sets, offsets, me, my_row):
    ids = np.array(sets, np.int32)
    win_row, win_col = ids // GRID, ids % GRID

    def extent(place, shift):
        low = jnp.maximum(0, shift - WIN * place)
        high = jnp.minimum(WIN, SIDE + shift - WIN * place)
        return low, jnp.maximum(high - low, 0)

    row_low, height = extent(win_row, offsets[0])
    col_low, width = extent(win_col, offsets[1])
    size = height * width
    earlier = np.tril(np.ones((ids.shape[1],) * 2, np.int32), -1)
    base = jnp.sum(size[:, None, :] * earlier[None], axis=2)
    kept_row = jnp.asarray(np.minimum(win_row, GRID - 1))
    fields = [base, row_low, height, col_low, width, kept_row, jnp.asarray(win_col)]
    own = jnp.arange(ids.shape[0], dtype=jnp.int32) == me
    count = jnp.sum(jnp.where(own[:, None], size, 0))
    head = jnp.concatenate([me[None], offsets, my_row[None], count[None]])
    return jnp.concatenate([head, jnp.stack(fields, axis=-1).reshape(-1)])


def window_at(info, index):
    at = HEAD + index * FIELDS
    return [info[at + f] for f in range(FIELDS)]


def target_of(field, left, row, token_col):
    base, row_low, height, col_low, width, _, win_col = field
    col = token_col + (left - WIN * win_col)
    inside = (row >= row_low) & (row < row_low + height) & (col >= col_low) & (col < col_low + width)
    return jnp.where(inside, base + (row - row_low) * width + (col - col_low), -(1 << 20))


def as_pick(mask):
    return mask.astype(F32).astype(BF)


def spread_kernel(per, info, x_ref, out, padded, total):
    top, left = info[1], info[2]
    cols, rows, width = out.shape
    padded[: MARGIN * SIDE, :] = jnp.zeros((MARGIN * SIDE, width), BF)
    padded[(MARGIN + SIDE) * SIDE :, :] = jnp.zeros(((PADROWS - MARGIN - SIDE) * SIDE, width), BF)
    padded[MARGIN * SIDE : (MARGIN + SIDE) * SIDE, :] = x_ref[...]
    token = iota((1, 256), 1)
    row, col = token // SIDE, token % SIDE
    line = iota((64, 256), 0)
    for d in range(cols):
        total[...] = jnp.zeros_like(total)

        def step(i, carry):
            field = window_at(info, d * per + i)
            base, row_low, height, _, across, win_row, _ = field
            for g in range(4):
                start = base + jnp.clip(4 * g - row_low, 0, height) * across
                start = pl.multiple_of(start // 8 * 8, 8)
                pick = as_pick(line == target_of(field, left, row + 4 * g, col) - start)
                first = pl.multiple_of((WIN * win_row + 4 * g - top + MARGIN) * SIDE, SIDE)
                total[pl.ds(start, 64), :] += nn_dot(pick, padded[pl.ds(first, 256), :])
            return carry

        lax.fori_loop(0, per, step, 0)
        out[d] = total[:rows].astype(BF)


def spread(x, info, cols, per, rows):
    width = x.shape[1]
    return pl.pallas_call(
        partial(spread_kernel, per),
        out_shape=jax.ShapeDtypeStruct((cols, rows, width), BF),
        grid_spec=pltpu.PrefetchScalarGridSpec(
            num_scalar_prefetch=1,
            grid=(1,),
            in_specs=[pl.BlockSpec((PIX, width), lambda i, s: (0, 0))],
            out_specs=pl.BlockSpec((cols, rows, width), lambda i, s: (0, 0, 0)),
            scratch_shapes=[
                pltpu.VMEM((PADROWS * SIDE, width), BF),
                pltpu.VMEM((rows + 64, width), F32),
            ],
        ),
        compiler_params=params(),
        cost_estimate=cost(7),
        name="spread",
    )(info, x)


def collect_kernel(per, info, pieces, out, padded):
    top, left = info[1], info[2]
    cols, rows, _ = pieces.shape
    padded[...] = jnp.zeros_like(padded)
    token = iota((1, 256), 1)
    row, col = token // SIDE, token % SIDE
    line = iota((80, 256), 0)
    for d in range(cols):

        def step(i, carry):
            field = window_at(info, d * per + i)
            base, row_low, height, _, across, win_row, _ = field
            for g in range(4):
                start = base + jnp.clip(4 * g - row_low, 0, height) * across
                start = pl.multiple_of(jnp.minimum(start // 16 * 16, rows - 80), 16)
                pick = as_pick(line == target_of(field, left, row + 4 * g, col) - start)
                first = pl.multiple_of((WIN * win_row + 4 * g - top + MARGIN) * SIDE, SIDE)
                padded[pl.ds(first, 256), :] += tn_dot(pick, pieces[d, pl.ds(start, 80), :])
            return carry

        lax.fori_loop(0, per, step, 0)
    out[...] = padded[MARGIN * SIDE : (MARGIN + SIDE) * SIDE, :].astype(out.dtype)


def collect(pieces, info, per, dtype):
    cols, rows, width = pieces.shape
    return pl.pallas_call(
        partial(collect_kernel, per),
        out_shape=jax.ShapeDtypeStruct((PIX, width), dtype),
        grid_spec=pltpu.PrefetchScalarGridSpec(
            num_scalar_prefetch=1,
            grid=(1,),
            in_specs=[pl.BlockSpec((cols, rows, width), lambda i, s: (0, 0, 0))],
            out_specs=pl.BlockSpec((PIX, width), lambda i, s: (0, 0)),
            scratch_shapes=[pltpu.VMEM((PADROWS * SIDE, width), F32)],
        ),
        compiler_params=params(),
        cost_estimate=cost(9),
        name="collect",
    )(info, pieces)


def chunk_place(col, part, width, info, parts):
    return (col * (width // 128) + part) ^ (info[3] // parts)


def swap_halves(values, info, parts):
    if parts == 1:
        return values
    return jnp.where(info[3] % 2 == 1, pltpu.roll(values.astype(F32), 64, 1), values.astype(F32))


def place_features(pieces, info, parts, whole):
    cols, _, width = pieces.shape
    for d in range(cols):
        for c in range(width // 128):
            at = pl.multiple_of(chunk_place(d, c, width, info, parts) * 128, 128)
            values = swap_halves(pieces[d, :, c * 128 : (c + 1) * 128], info, parts)
            whole[:, pl.ds(at, 128)] = values.astype(whole.dtype)


def take_features(whole, pieces, info, parts):
    cols, _, width = pieces.shape
    for d in range(cols):
        for c in range(width // 128):
            at = pl.multiple_of(chunk_place(d, c, width, info, parts) * 128, 128)
            values = swap_halves(whole[:, pl.ds(at, 128)], info, parts)
            pieces[d, :, c * 128 : (c + 1) * 128] = values.astype(BF)


def eight(values):
    total = values[:8]
    for r in range(8, values.shape[0], 8):
        total = total + values[r : r + 8]
    return total


def row_places(nr, flip):
    order = outer_bits(nr)
    order = order[::-1] if flip else order
    held = [0]
    for bit in order[:-1]:
        held = held + [place | bit for place in held]
    groups = [held, [place | order[-1] for place in held]]
    groups = groups + [[place | 1 for place in group] for group in groups]
    where = {place: (g, i) for g, group in enumerate(groups) for i, place in enumerate(group)}
    return [where[place] for place in range(nr)]


def outer_bits(nr):
    return [1 << b for b in range(1, nr.bit_length() - 1)]


def load_rows(bufs, flip, scratch, nr, first=0):
    stride = D // nr
    for p, (g, i) in enumerate(row_places(nr, flip)):
        cols, size, n = bufs[g].shape[1:]
        for k in range(cols):
            at = p * stride + first
            scratch[at : at + size, k * n : (k + 1) * n] = bufs[g][i, k]


def const_spec(shape):
    zeros = (0,) * len(shape)
    return pl.BlockSpec(shape, lambda *a: zeros, pipeline_mode=pl.Buffered(1))


def norm_qkv_kernel(cols, nr, info, *refs):
    pieces = refs[0]
    bufs_a, bufs_b = refs[1:5], refs[5:9]
    gain, bias, bias_qkv, x_out, n_out, qkv_out, whole, weight = refs[9:]
    parts = max(1, 128 * nr // D)
    bw = D // nr

    @pl.when(pl.program_id(0) == 0)
    def _():
        load_rows(bufs_a, False, weight, nr)
        load_rows(bufs_b, True, weight, nr, bw // 2)

    place_features(pieces, info, parts, whole)
    values = whole[...]
    x_out[...] = values.astype(BF)
    mean = jnp.mean(values, axis=1, keepdims=True)
    centred = values - mean
    spread_sq = jnp.mean(centred * centred, axis=1, keepdims=True)
    normed = centred * lax.rsqrt(spread_sq + EPSILON) * gain[...] + bias[...]
    size = values.shape[0]
    real = iota((size, 1), 0) < info[4] - pl.program_id(0) * size
    normed = jnp.where(real, normed, 0.0).astype(BF)
    n_out[...] = normed
    qkv_out[...] = (nn_dot(normed, weight[...]) + bias_qkv[...]).astype(BF)


def norm_qkv(pieces, bufs_a, bufs_b, info, gain, bias, bias_qkv, cols, rows, nr):
    width = D // cols
    return pl.pallas_call(
        partial(norm_qkv_kernel, cols, nr),
        out_shape=[
            jax.ShapeDtypeStruct((rows, D), BF),
            jax.ShapeDtypeStruct((rows, D), BF),
            jax.ShapeDtypeStruct((rows, 3 * D), BF),
        ],
        grid_spec=pltpu.PrefetchScalarGridSpec(
            num_scalar_prefetch=1,
            grid=(BLOCKS,),
            in_specs=[pl.BlockSpec((cols, rows // BLOCKS, width), lambda i, s: (0, i, 0))]
            + [const_spec(bufs_a[0].shape)] * 8
            + [const_spec((1, D)), const_spec((1, D)), const_spec((1, 3 * D))],
            out_specs=[
                pl.BlockSpec((rows // BLOCKS, D), lambda i, s: (i, 0)),
                pl.BlockSpec((rows // BLOCKS, D), lambda i, s: (i, 0)),
                pl.BlockSpec((rows // BLOCKS, 3 * D), lambda i, s: (i, 0)),
            ],
            scratch_shapes=[pltpu.VMEM((rows // BLOCKS, D), F32), pltpu.VMEM((D, 3 * D), BF)],
        ),
        compiler_params=params(),
        cost_estimate=cost(19),
        name="norm_qkv",
    )(info, pieces, *bufs_a, *bufs_b, gain, bias, bias_qkv)


def join_kernel(cols, nr, info, *refs):
    place_features(refs[0], info, max(1, 128 * nr // D), refs[1])


def join(pieces, info, cols, rows, nr):
    width = pieces.shape[-1]
    return pl.pallas_call(
        partial(join_kernel, cols, nr),
        out_shape=jax.ShapeDtypeStruct((rows, D), BF),
        grid_spec=pltpu.PrefetchScalarGridSpec(
            num_scalar_prefetch=1,
            grid=(BLOCKS,),
            in_specs=[pl.BlockSpec((cols, rows // BLOCKS, width), lambda i, s: (0, i, 0))],
            out_specs=pl.BlockSpec((rows // BLOCKS, D), lambda i, s: (i, 0)),
        ),
        compiler_params=params(),
        cost_estimate=cost(7),
        name="join",
    )(info, pieces)


def proj_norm_kernel(nr, *refs):
    att, x, bias_p, gain, bias, resid_out, n_out, weight = refs[4:]

    @pl.when(pl.program_id(0) == 0)
    def _():
        load_rows(refs[:4], False, weight, nr)

    values = x[...].astype(F32) + nt_dot(att[...], weight[...]) + bias_p[...]
    resid_out[...] = values
    mean = jnp.mean(values, axis=1, keepdims=True)
    centred = values - mean
    spread_sq = jnp.mean(centred * centred, axis=1, keepdims=True)
    n_out[...] = (centred * lax.rsqrt(spread_sq + EPSILON) * gain[...] + bias[...]).astype(BF)


def proj_spec(buf, cols, whole):
    n = D // cols
    shape = (buf.shape[0], cols if whole else 1, buf.shape[2], n)
    last = buf.shape[3] // n - 1
    if whole:
        return pl.BlockSpec(shape, lambda *a: (0, 0, 0, last), pipeline_mode=pl.Buffered(1))
    return pl.BlockSpec(shape, lambda k: (0, k, 0, last))


def proj_norm(bufs, att, x, bias_p, gain, bias, cols, rows, nr):
    row_spec = pl.BlockSpec((rows // BLOCKS, D), lambda i: (i, 0))
    return pl.pallas_call(
        partial(proj_norm_kernel, nr),
        out_shape=[jax.ShapeDtypeStruct((rows, D), F32), jax.ShapeDtypeStruct((rows, D), BF)],
        grid=(BLOCKS,),
        in_specs=[proj_spec(bufs[0], cols, True)] * 4
        + [row_spec, row_spec, const_spec((1, D)), const_spec((1, D)), const_spec((1, D))],
        out_specs=[row_spec, row_spec],
        scratch_shapes=[pltpu.VMEM((D, D), BF)],
        compiler_params=params(),
        cost_estimate=cost(11),
        name="proj_norm",
    )(*bufs, att, x, bias_p, gain, bias)


def gelu_and_slope(v):
    t = 1.0 / (1.0 + 0.23164189 * jnp.abs(v))
    poly = t * (
        0.127414796
        + t * (-0.142248368 + t * (0.7107068705 + t * (-0.7265760135 + t * 0.5307027145)))
    )
    bell = jnp.exp(-0.5 * v * v)
    half = poly * bell
    below = jnp.where(v >= 0, 1.0 - half, half)
    return v * below, below + v * bell * 0.3989422804014327


def store_halves(grad, keep, send, nr, lanes=slice(None)):
    bw = D // nr
    for q in range(nr // 2):
        at = 2 * q * bw
        keep[q, 0, :, lanes] = grad[at : at + bw].astype(BF)
        send[q, 0, :, lanes] = grad[at + bw : at + 2 * bw].astype(BF)


def mlp_grads_kernel(nr, *refs):
    n2, g, bias, act, pre_grad, keep, send, bias_sum, w1, w2 = refs[8:]
    n = w1.shape[1]
    load_rows(refs[:4], False, w1, nr)
    load_rows(refs[4:8], True, w2, nr)
    total = None
    size = n2.shape[0] // BLOCKS
    for r in range(0, n2.shape[0], size):
        pre = nn_dot(n2[r : r + size], w1[...]) + bias[0]
        act_grad = nn_dot(g[r : r + size], w2[...])
        value, slope = gelu_and_slope(pre)
        act[r : r + size] = value.astype(BF)
        grad = act_grad * slope
        pre_grad[r : r + size] = grad.astype(BF)
        part = eight(grad)
        total = part if total is None else total + part
    bias_sum[0] = total
    store_halves(tn_dot(n2[...], pre_grad[...]), keep, send, nr, slice(0, n))
    store_halves(tn_dot(g[...], act[...]), keep, send, nr, slice(n, 2 * n))


def mlp_grads(bufs1, bufs2, n2, g, bias, cols, rows, nr):
    bw = D // nr
    n = bufs2[0].shape[-1]
    w_spec = pl.BlockSpec((nr // 4, 1, bw, n), lambda k: (0, k, 0, 0))
    row_spec = pl.BlockSpec((rows, n), lambda k: (0, k))
    half_spec = pl.BlockSpec((nr // 2, 1, bw, 2 * n), lambda k: (0, k, 0, 0))
    half = jax.ShapeDtypeStruct((nr // 2, cols, bw, 2 * n), BF)
    act = jax.ShapeDtypeStruct((rows, cols * n), BF)
    return pl.pallas_call(
        partial(mlp_grads_kernel, nr),
        out_shape=[act, act, half, half, jax.ShapeDtypeStruct((cols, 8, n), F32)],
        grid=(cols,),
        in_specs=[w_spec] * 8
        + [const_spec((rows, D)), const_spec((rows, D)), pl.BlockSpec((1, 1, n), lambda k: (k, 0, 0))],
        out_specs=[row_spec, row_spec, half_spec, half_spec]
        + [pl.BlockSpec((1, 8, n), lambda k: (k, 0, 0))],
        scratch_shapes=[pltpu.VMEM((D, n), BF)] * 2,
        compiler_params=params(),
        cost_estimate=cost(38),
        name="mlp_grads",
    )(*bufs1, *bufs2, n2, g, bias)


def norm_back(grad, values, gain):
    mean = jnp.mean(values, axis=1, keepdims=True)
    centred = values - mean
    spread_sq = jnp.mean(centred * centred, axis=1, keepdims=True)
    inv = lax.rsqrt(spread_sq + EPSILON)
    hat = centred * inv
    scaled = grad * gain
    first = jnp.mean(scaled, axis=1, keepdims=True)
    second = jnp.mean(scaled * hat, axis=1, keepdims=True)
    return (scaled - first - hat * second) * inv, hat


def block_out_kernel(cols, nr, info, *refs):
    act0, act1, resid, bias_2 = refs[8:12]
    pieces, weight, whole = refs[12:]

    @pl.when(pl.program_id(0) == 0)
    def _():
        load_rows(refs[:4], True, weight.at[0], nr)
        load_rows(refs[4:8], True, weight.at[1], nr)

    out = nt_dot(act0[...], weight[0]) + nt_dot(act1[...], weight[1])
    whole[...] = resid[...] + out + bias_2[...]
    take_features(whole, pieces, info, max(1, 128 * nr // D))


def block_rows(groups, acts, resid, bias_2, info, cols, rows, nr):
    width = D // cols
    wide = acts[0].shape[1]
    row_spec = pl.BlockSpec((rows // BLOCKS, D), lambda i, s: (i, 0))
    wide_spec = pl.BlockSpec((rows // BLOCKS, wide), lambda i, s: (i, 0))
    flat = [b for group in groups for b in group]
    return pl.pallas_call(
        partial(block_out_kernel, cols, nr),
        out_shape=[jax.ShapeDtypeStruct((cols, rows, width), BF)],
        grid_spec=pltpu.PrefetchScalarGridSpec(
            num_scalar_prefetch=1,
            grid=(BLOCKS,),
            in_specs=[const_spec(flat[-1].shape)] * 8
            + [wide_spec] * 2
            + [row_spec, const_spec((1, D))],
            out_specs=[pl.BlockSpec((cols, rows // BLOCKS, width), lambda i, s: (0, i, 0))],
            scratch_shapes=[pltpu.VMEM((2, D, wide), BF), pltpu.VMEM((rows // BLOCKS, D), F32)],
        ),
        compiler_params=params(),
        cost_estimate=cost(26),
        name="block_rows",
    )(info, *flat, *acts, resid, bias_2)[0]


def mlp_back_kernel(nr, *refs):
    grad0, grad1, resid, g, gain, resid_grad, proj_grad, sums, weight = refs[8:]

    @pl.when(pl.program_id(0) == 0)
    def _():
        load_rows(refs[:4], False, weight.at[0], nr)
        load_rows(refs[4:8], False, weight.at[1], nr)
        sums[...] = jnp.zeros_like(sums)

    grad = nt_dot(grad0[...], weight[0]) + nt_dot(grad1[...], weight[1])
    g_f = g[...].astype(F32)
    back, hat = norm_back(grad, resid[...], gain[...])
    total = g_f + back
    resid_grad[...] = total
    low = total.astype(BF)
    proj_grad[...] = low
    sums[0] += eight(low.astype(F32))
    sums[1] += eight(grad * hat)
    sums[2] += eight(grad)
    sums[3] += eight(g_f)


def mlp_back(groups, grads, resid, g, gain, cols, rows, nr):
    wide = grads[0].shape[1]
    row_spec = pl.BlockSpec((rows // BLOCKS, D), lambda i: (i, 0))
    wide_spec = pl.BlockSpec((rows // BLOCKS, wide), lambda i: (i, 0))
    flat = [b for group in groups for b in group]
    shape = flat[-1].shape
    return pl.pallas_call(
        partial(mlp_back_kernel, nr),
        out_shape=[
            jax.ShapeDtypeStruct((rows, D), F32),
            jax.ShapeDtypeStruct((rows, D), BF),
            jax.ShapeDtypeStruct((4, 8, D), F32),
        ],
        grid=(BLOCKS,),
        in_specs=[const_spec(shape)] * 8
        + [wide_spec] * 2
        + [row_spec, row_spec, const_spec((1, D))],
        out_specs=[row_spec, row_spec, pl.BlockSpec((4, 8, D), lambda i: (0, 0, 0))],
        scratch_shapes=[pltpu.VMEM((2, D, wide), BF)],
        compiler_params=params(),
        cost_estimate=cost(28),
        name="mlp_back",
    )(*flat, *grads, resid, g, gain)


def proj_back_kernel(nr, *refs):
    proj_grad, att, att_grad, keep, send, weight = refs[4:]
    load_rows(refs[:4], False, weight, nr)
    store_halves(tn_dot(proj_grad[...], att[...]), keep, send, nr)
    att_grad[...] = nn_dot(proj_grad[...], weight[...]).astype(BF)


def proj_back(bufs, proj_grad, att, cols, rows, nr):
    bw = D // nr
    n = D // cols
    half = jax.ShapeDtypeStruct((nr // 2, cols, bw, n), BF)
    half_spec = pl.BlockSpec((nr // 2, 1, bw, n), lambda k: (0, k, 0, 0))
    col_spec = pl.BlockSpec((rows, n), lambda k: (0, k))
    return pl.pallas_call(
        partial(proj_back_kernel, nr),
        out_shape=[jax.ShapeDtypeStruct((rows, D), BF), half, half],
        grid=(cols,),
        in_specs=[proj_spec(bufs[0], cols, False)] * 4 + [const_spec((rows, D)), col_spec],
        out_specs=[col_spec, half_spec, half_spec],
        scratch_shapes=[pltpu.VMEM((D, n), BF)],
        compiler_params=params(),
        cost_estimate=cost(11),
        name="proj_back",
    )(*bufs, proj_grad, att)


def qkv_grad_kernel(nr, n1, dqkv, keep, send):
    store_halves(tn_dot(n1[...], dqkv[...]), keep, send, nr)


def qkv_grad(n1, dqkv, cols, rows, nr):
    n = 3 * D // cols
    bw = D // nr
    half = jax.ShapeDtypeStruct((nr // 2, cols, bw, n), BF)
    return pl.pallas_call(
        partial(qkv_grad_kernel, nr),
        out_shape=[half] * 2,
        grid=(cols,),
        in_specs=[const_spec((rows, D)), pl.BlockSpec((rows, n), lambda k: (0, k))],
        out_specs=[pl.BlockSpec((nr // 2, 1, bw, n), lambda k: (0, k, 0, 0))] * 2,
        compiler_params=params(),
        cost_estimate=cost(14),
        name="qkv_grad",
    )(n1, dqkv)


def input_back_kernel(cols, nr, info, *refs):
    bufs_a, bufs_b = refs[:4], refs[4:8]
    rest = refs[8:]
    dqkv, x, resid_grad, gain = rest[:4]
    pieces, sums, whole, weight = rest[4:]
    bw = D // nr

    @pl.when(pl.program_id(0) == 0)
    def _():
        load_rows(bufs_a, False, weight, nr)
        load_rows(bufs_b, True, weight, nr, bw // 2)
        sums[...] = jnp.zeros_like(sums)

    grad = nt_dot(dqkv[...], weight[...])
    back, hat = norm_back(grad, x[...].astype(F32), gain[...])
    whole[...] = resid_grad[...] + back
    take_features(whole, pieces, info, max(1, 128 * nr // D))
    sums[0] += eight(grad * hat)
    sums[1] += eight(grad)


def input_back(bufs_a, bufs_b, dqkv, x, resid_grad, gain, info, cols, rows, nr):
    width = D // cols
    row_spec = pl.BlockSpec((rows // BLOCKS, D), lambda i, s: (i, 0))
    piece = jax.ShapeDtypeStruct((cols, rows, width), BF)
    return pl.pallas_call(
        partial(input_back_kernel, cols, nr),
        out_shape=[piece, jax.ShapeDtypeStruct((2, 8, D), F32)],
        grid_spec=pltpu.PrefetchScalarGridSpec(
            num_scalar_prefetch=1,
            grid=(BLOCKS,),
            in_specs=[const_spec(bufs_a[0].shape)] * 8
            + [pl.BlockSpec((rows // BLOCKS, 3 * D), lambda i, s: (i, 0)), row_spec, row_spec]
            + [const_spec((1, D))],
            out_specs=[pl.BlockSpec((cols, rows // BLOCKS, width), lambda i, s: (0, i, 0))]
            + [pl.BlockSpec((2, 8, D), lambda i, s: (0, 0, 0))],
            scratch_shapes=[pltpu.VMEM((rows // BLOCKS, D), F32), pltpu.VMEM((D, 3 * D), BF)],
        ),
        compiler_params=params(),
        cost_estimate=cost(25),
        name="input_back",
    )(info, *bufs_a, *bufs_b, dqkv, x, resid_grad, gain)


def rel_constants():
    place = np.arange(SLOT)
    lanes = np.arange(128)
    group = lanes // 32
    row_shift = np.clip(WIN - 1 - place // WIN, 0, WIN - 1)
    col_shift = WIN - 1 - place % WIN
    shifts = np.where(group[None, :] % 2 == 0, row_shift[:, None], col_shift[:, None])
    onehot = np.zeros((2, KEYS, 128), np.float32)
    for head in range(2):
        for key in range(KEYS):
            if key >= REAL:
                onehot[head, key, 64 * head + 28] = -1e9
                continue
            for extra in (0, WIN):
                onehot[head, key, 64 * head + key // WIN + extra] = 1.0
                onehot[head, key, 64 * head + 32 + key % WIN + extra] = 1.0
    return shifts.astype(np.int32), onehot


def table_matrix(table_h, table_w):
    flipped = jnp.stack([table_h, table_w])[:, ::-1, :].astype(BF)
    block = jnp.pad(jnp.transpose(flipped, (2, 0, 1)), ((0, 0), (0, 0), (0, 5)))
    block = block.reshape(HD, HD)
    zero = jnp.zeros_like(block)
    return jnp.concatenate(
        [jnp.concatenate([block, zero], axis=1), jnp.concatenate([zero, block], axis=1)], axis=0
    )


def shift_left(values, shifts):
    for bit in (1, 2, 4, 8):
        values = jnp.where((shifts & bit) != 0, pltpu.roll(values, 128 - bit, 1), values)
    return values


def shift_right(values, shifts):
    for bit in (1, 2, 4, 8):
        values = jnp.where((shifts & bit) != 0, pltpu.roll(values, bit, 1), values)
    return values


def slot_target(field, start, rows, shape):
    base, row_low, height, col_low, width, _, _ = field
    slot = iota(shape, 0 if shape[0] > 1 else 1)
    row, col = slot // WIN, slot % WIN
    inside = (row >= row_low) & (row < row_low + height) & (col >= col_low) & (col < col_low + width)
    return jnp.where(inside, base - start + (row - row_low) * width + (col - col_low), rows)


def slots_from(field, start, source):
    rows = source.shape[0]
    line = iota((SLOT, SLAB + TAIL), 1)
    pick = as_pick(line == slot_target(field, start, SLAB + TAIL - 1, (SLOT, 1)))
    slab = jnp.concatenate([source[pl.ds(start, SLAB), :], source[rows - TAIL :, :]], axis=0)
    return pick, nn_dot(pick, slab)


def pack_of(field, start):
    line = iota((SLAB, SLOT), 0)
    return as_pick(line == slot_target(field, start, -1, (1, SLOT)))


def slab_start(field, rows):
    return pl.multiple_of(jnp.minimum(field[0] // 16 * 16, rows - SLAB), 16)


def attend_kernel(width, held, info, qkv, tables, shifts, onehot, *refs):
    att, exps, inv, keys, vals, slots, total = refs[held:]
    window = pl.program_id(1)
    first = (pl.program_id(0) == 0) & (window == 0)

    @pl.when(first)
    def _():
        for head in range(2):
            keys[head, :, :128] = jnp.zeros((KEYS, 128), BF)
            keys[head, :, 128:] = onehot[head]
        vals[:, :128] = jnp.zeros((KEYS, 128), BF)
        vals[:, 128:] = jnp.ones((KEYS, 128), BF)

    @pl.when(window == 0)
    def _():
        total[...] = jnp.zeros_like(total)

    field = window_at(info, info[0] * pl.num_programs(1) + window)
    start = slab_start(field, qkv.shape[0])
    slots[...] = slots_from(field, start, qkv)[1].astype(BF)

    lane = iota((SLOT, 128), 1)
    low = lane < HD
    inner = lane % 32
    parts = []
    for pair in range(width // 128):
        at = pair * 128
        q2 = slots[:, at : at + 128]
        k2 = slots[:, width + at : width + at + 128]
        v2 = slots[:, 2 * width + at : 2 * width + at + 128]
        rel = shift_left(nn_dot(q2, tables[...]), shifts[...])
        rel_hi = rel.astype(BF).astype(F32)
        rel_lo = pltpu.roll(rel - rel_hi, WIN, 1)
        rel = jnp.where(inner < WIN, rel_hi, jnp.where(inner < 2 * WIN, rel_lo, 1.0))
        queries = jnp.concatenate([q2 * BF(0.125), rel.astype(BF)], axis=1)
        vals[:SLOT, :128] = v2
        zero = jnp.zeros_like(k2)
        keys[0, :SLOT, :128] = jnp.where(low, k2, zero)
        keys[1, :SLOT, :128] = jnp.where(low, zero, k2)
        outs = []
        for head in range(2):
            scores = nt_dot(queries, keys[head])
            peak = jnp.max(scores, axis=1, keepdims=True)
            weights = jnp.exp(scores - peak).astype(BF)
            exps[pair * 2 + head] = weights
            outs.append(nn_dot(weights, vals[...]))
        scale = 1.0 / jnp.where(low, outs[0][:, 128:], outs[1][:, 128:])
        inv[:, at : at + 128] = scale
        parts.append((jnp.where(low, outs[0][:, :128], outs[1][:, :128]) * scale).astype(BF))
    pack = pack_of(field, start)
    total[pl.ds(start, SLAB), :] += nn_dot(pack, jnp.concatenate(parts, axis=1))

    @pl.when(window == pl.num_programs(1) - 1)
    def _():
        att[...] = total[...].astype(BF)


def attend(qkv, info, tables, shifts, onehot, base, count, held, cols, per):
    rows = qkv.shape[0]
    width = D // cols
    pairs = width // 128
    held = list(held)
    return pl.pallas_call(
        partial(attend_kernel, width, len(held)),
        out_shape=[
            jax.ShapeDtypeStruct((rows, D), BF),
            jax.ShapeDtypeStruct((D // HD, per * SLOT, KEYS), BF),
            jax.ShapeDtypeStruct((per * SLOT, D), F32),
        ],
        grid_spec=pltpu.PrefetchScalarGridSpec(
            num_scalar_prefetch=1,
            grid=(count, per),
            in_specs=[
                pl.BlockSpec((rows, 3 * width), lambda c, w, s: (0, c + base)),
                pl.BlockSpec((128, 128), lambda c, w, s: (0, 0)),
                pl.BlockSpec((SLOT, 128), lambda c, w, s: (0, 0)),
                pl.BlockSpec((2, KEYS, 128), lambda c, w, s: (0, 0, 0)),
            ]
            + [pl.BlockSpec(memory_space=pl.ANY)] * len(held),
            out_specs=[
                pl.BlockSpec((rows, width), lambda c, w, s: (0, c + base)),
                pl.BlockSpec((2 * pairs, SLOT, KEYS), lambda c, w, s: (c + base, w, 0)),
                pl.BlockSpec((SLOT, width), lambda c, w, s: (w, c + base)),
            ],
            scratch_shapes=[
                pltpu.VMEM((2, KEYS, 256), BF),
                pltpu.VMEM((KEYS, 256), BF),
                pltpu.VMEM((SLOT, 3 * width), BF),
                pltpu.VMEM((rows, width), F32),
            ],
        ),
        input_output_aliases={5 + i: i for i in range(len(held))},
        compiler_params=params(2),
        cost_estimate=cost(58 * count // cols),
        name="attend",
    )(info, qkv, tables, shifts, onehot, *held)


def attend_back_kernel(
    width, held, info, qkv, exps, inv, att, att_grad, tables2, shifts, onehot, *refs
):
    out, table_sum, bias_sum, keys, vals, slots, att_slots, grad_slots, fresh, total = refs[held:]
    window = pl.program_id(1)
    first = (pl.program_id(0) == 0) & (window == 0)

    @pl.when(first)
    def _():
        for head in range(2):
            keys[head, :, :128] = jnp.zeros((KEYS, 128), BF)
            keys[head, :, 128:] = onehot[head]
        vals[...] = jnp.zeros_like(vals)
        table_sum[...] = jnp.zeros_like(table_sum)

    @pl.when(window == 0)
    def _():
        bias_sum[...] = jnp.zeros_like(bias_sum)
        total[...] = jnp.zeros_like(total)

    field = window_at(info, info[0] * pl.num_programs(1) + window)
    start = slab_start(field, qkv.shape[0])
    pick, pulled = slots_from(field, start, qkv)
    slots[...] = pulled.astype(BF)
    att_slots[...] = nn_dot(pick[:, :SLAB], att[pl.ds(start, SLAB), :])
    grad_slots[...] = nn_dot(pick[:, :SLAB], att_grad[pl.ds(start, SLAB), :])

    lane = iota((SLOT, 128), 1)
    low = lane < HD
    inner = lane % 32
    for pair in range(width // 128):
        at = pair * 128
        q2 = slots[:, at : at + 128]
        k2 = slots[:, width + at : width + at + 128]
        v2 = slots[:, 2 * width + at : 2 * width + at + 128]
        zero = jnp.zeros_like(k2)
        keys[0, :SLOT, :128] = jnp.where(low, k2, zero)
        keys[1, :SLOT, :128] = jnp.where(low, zero, k2)
        vals[0, :SLOT, :] = jnp.where(low, v2, zero)
        vals[1, :SLOT, :] = jnp.where(low, zero, v2)
        grad = (grad_slots[:, at : at + 128] * inv[:, at : at + 128]).astype(BF)
        cross = grad.astype(F32) * att_slots[:, at : at + 128]
        dots = (
            jnp.sum(jnp.where(low, cross, 0.0), axis=1, keepdims=True),
            jnp.sum(jnp.where(low, 0.0, cross), axis=1, keepdims=True),
        )
        q_scaled = q2 * BF(0.125)
        grad_heads = (jnp.where(low, grad, zero), jnp.where(low, zero, grad))
        q_heads = (jnp.where(low, q_scaled, zero), jnp.where(low, zero, q_scaled))
        q_sum = jnp.zeros((SLOT, 256), F32)
        k_sum = jnp.zeros((KEYS, 128), F32)
        v_sum = jnp.zeros((KEYS, 128), F32)
        for head in range(2):
            weights = exps[pair * 2 + head]
            probs_grad = nt_dot(grad, vals[head])
            scores_grad = (weights.astype(F32) * (probs_grad - dots[head])).astype(BF)
            q_sum = q_sum + nn_dot(scores_grad, keys[head])
            k_sum = k_sum + tn_dot(scores_grad, q_heads[head])
            v_sum = v_sum + tn_dot(weights, grad_heads[head])
        rel = shift_right(jnp.where(inner < WIN, q_sum[:, 128:], 0.0), shifts[...])
        rel_hi = rel.astype(BF)
        rel_lo = (rel - rel_hi.astype(F32)).astype(BF)
        rel2 = jnp.concatenate([rel_hi, rel_lo], axis=1)
        q_grad = q_sum[:, :128] * 0.125 + nt_dot(rel2, tables2[...])
        table_sum[...] += tn_dot(q2, rel2)
        v_grad = v_sum[:SLOT]
        fresh[:, at : at + 128] = q_grad.astype(BF)
        fresh[:, width + at : width + at + 128] = k_sum[:SLOT].astype(BF)
        fresh[:, 2 * width + at : 2 * width + at + 128] = v_grad.astype(BF)
        bias_sum[:, at : at + 128] += eight(q_grad)
        bias_sum[:, 2 * width + at : 2 * width + at + 128] += eight(v_grad)
    pack = pack_of(field, start)
    total[pl.ds(start, SLAB), :] += nn_dot(pack, fresh[...])

    @pl.when(window == pl.num_programs(1) - 1)
    def _():
        out[...] = total[...].astype(BF)


def attend_back(
    qkv, info, exps, inv, att, att_grad, tables, shifts, onehot, base, count, held, cols, per
):
    rows = qkv.shape[0]
    width = D // cols
    pairs = width // 128
    tables2 = jnp.concatenate([tables, tables], axis=1)
    row_spec = pl.BlockSpec((rows, width), lambda c, w, s: (0, c + base))
    qkv_spec = pl.BlockSpec((rows, 3 * width), lambda c, w, s: (0, c + base))
    held = list(held)
    return pl.pallas_call(
        partial(attend_back_kernel, width, len(held)),
        out_shape=[
            jax.ShapeDtypeStruct((rows, 3 * D), BF),
            jax.ShapeDtypeStruct((128, 256), F32),
            jax.ShapeDtypeStruct((8, count * 3 * width), F32),
        ],
        grid_spec=pltpu.PrefetchScalarGridSpec(
            num_scalar_prefetch=1,
            grid=(count, per),
            in_specs=[
                qkv_spec,
                pl.BlockSpec((2 * pairs, SLOT, KEYS), lambda c, w, s: (c + base, w, 0)),
                pl.BlockSpec((SLOT, width), lambda c, w, s: (w, c + base)),
                row_spec,
                row_spec,
                pl.BlockSpec((128, 256), lambda c, w, s: (0, 0)),
                pl.BlockSpec((SLOT, 128), lambda c, w, s: (0, 0)),
                pl.BlockSpec((2, KEYS, 128), lambda c, w, s: (0, 0, 0)),
            ]
            + [pl.BlockSpec(memory_space=pl.ANY)] * len(held),
            out_specs=[
                qkv_spec,
                pl.BlockSpec((128, 256), lambda c, w, s: (0, 0)),
                pl.BlockSpec((8, 3 * width), lambda c, w, s: (0, c)),
            ],
            scratch_shapes=[
                pltpu.VMEM((2, KEYS, 256), BF),
                pltpu.VMEM((2, KEYS, 128), BF),
                pltpu.VMEM((SLOT, 3 * width), BF),
                pltpu.VMEM((SLOT, width), F32),
                pltpu.VMEM((SLOT, width), F32),
                pltpu.VMEM((SLOT, 3 * width), BF),
                pltpu.VMEM((rows, 3 * width), F32),
            ],
        ),
        input_output_aliases={9 + i: i for i in range(len(held))},
        compiler_params=params(2),
        cost_estimate=cost(54 * count // cols),
        name="attend_back",
    )(info, qkv, exps, inv, att, att_grad, tables2, shifts, onehot, *held)


def split_table(total):
    total = (total[:, :128] + total[:, 128:]).reshape(2, HD, 2, 2, 32)
    both = total[0, :, 0] + total[1, :, 1]
    both = jnp.transpose(both, (1, 2, 0))[:, :27][:, ::-1]
    return both[0], both[1]


def col_exchange(values):
    return lax.all_to_all(values, "col", 0, 0, tiled=True)


def row_swap(values, bit, nr):
    return lax.ppermute(values, "row", [(i, i ^ bit) for i in range(nr)])


def after(values, *others):
    return lax.optimization_barrier((values, *others))[0]


def gather_cols(shard, cols):
    return col_exchange(jnp.broadcast_to(shard[None], (cols,) + shard.shape))


def gather_rows(stack, nr, flip):
    order = outer_bits(nr)
    order = order[::-1] if flip else order
    held = stack[None]
    for bit in order[:-1]:
        held = jnp.concatenate([held, row_swap(held, bit, nr)], axis=0)
        yield [held]
    bufs = [held, row_swap(held, order[-1], nr)]
    yield bufs
    bufs = bufs + [row_swap(buf, 1, nr) for buf in bufs]
    yield bufs


def place_of(step, free, fixed, weights):
    total = sum(weights[b] for b in fixed)
    for i, bit in enumerate(free):
        total = total + ((step >> i) & 1) * weights[bit]
    return total


def add_kernel(counts, *refs):
    at = 0
    outs = refs[sum(counts) :]
    for count, out in zip(counts, outs):
        total = refs[at][...].astype(F32)
        for ref in refs[at + 1 : at + count]:
            total = total + ref[...].astype(F32)
        out[...] = total.astype(BF)
        at += count


def split_kernel(counts, axis, *refs):
    out = refs[sum(counts)]
    for k in range(out.shape[0]):
        at = 0
        for h, count in enumerate(counts):
            total = refs[at][0, k].astype(F32)
            for ref in refs[at + 1 : at + count]:
                total = total + ref[0, k].astype(F32)
            at += count
            size = total.shape[axis]
            where = slice(h * size, (h + 1) * size)
            if axis == -1:
                out[k, :, where] = total.astype(out.dtype)
            else:
                out[k, where, :] = total.astype(out.dtype)


def reduce_weight(keep, send, axis, cols, nr):
    arrived = row_swap(send, 1, nr)
    yield [arrived]
    bits = outer_bits(nr)
    _, _, bw, n = keep.shape
    shape = [bw, n]
    halves = 1
    if axis is not None:
        halves = 2
        shape[axis] //= 2
    block = (1, cols, shape[0], shape[1])
    terms = [[(keep, bits, True), (arrived, bits, True)] for _ in range(halves)]
    left = [list(bits) for _ in range(halves)]

    def spec(term, h, free, fixed):
        _, own, whole = term
        weights = {b: 1 << i for i, b in enumerate(own)}

        def place(step):
            spot = [place_of(step, free, fixed, weights), 0, 0, 0]
            if whole and axis is not None:
                spot[axis] = h
            return tuple(spot)

        return pl.BlockSpec(block, place)

    for step in range(len(bits)):
        sizes, specs, arrays, taken = [], [], [], []
        for h in range(halves):
            bit = bits[step] if h else bits[-1 - step]
            left[h].remove(bit)
            taken.append(bit)
            sizes.append(len(terms[h]))
            for term in terms[h]:
                specs.append(spec(term, h, left[h], [bit]))
                arrays.append(term[0])
        count = 1 << len(left[0])
        out_spec = pl.BlockSpec(block, lambda i: (i, 0, 0, 0))
        outs = pl.pallas_call(
            partial(add_kernel, sizes),
            out_shape=[jax.ShapeDtypeStruct((count,) + block[1:], BF)] * halves,
            grid=(count,),
            in_specs=specs,
            out_specs=[out_spec] * halves,
            compiler_params=params(),
            cost_estimate=cost(3),
            name="add_rows",
        )(*arrays)
        fresh = [row_swap(out, bit, nr) for out, bit in zip(outs, taken)]
        for h in range(halves):
            terms[h].append((fresh[h], list(left[h]), False))
        yield fresh

    sizes = [len(t) for t in terms]
    specs = [spec(term, h, [], []) for h in range(halves) for term in terms[h]]
    arrays = [term[0] for h in range(halves) for term in terms[h]]
    outs = pl.pallas_call(
        partial(split_kernel, sizes, -1 if axis is None else axis),
        out_shape=jax.ShapeDtypeStruct((cols, bw, n), BF),
        grid=(1,),
        in_specs=specs,
        out_specs=pl.BlockSpec((cols, bw, n), lambda i: (0, 0, 0)),
        compiler_params=params(),
        cost_estimate=cost(3),
        name="add_cols",
    )(*arrays)
    yield [outs]
    arrived = col_exchange(outs)
    yield [arrived]
    yield jnp.sum(arrived.astype(F32), axis=0)


def reduce_small(by_place, whole, cols, nr):
    size = by_place.shape[1]
    if whole is not None:
        whole = jnp.broadcast_to(whole, (cols,) + whole.shape)
        by_place = jnp.concatenate([by_place, whole], axis=1)
    arrived = col_exchange(by_place)
    yield arrived
    total = jnp.sum(arrived, axis=0)
    bit = 1
    while bit < nr:
        total = total + row_swap(total, bit, nr)
        bit *= 2
    yield total[:size], total[size:]


def pick_rows(values, order):
    rows = jnp.arange(values.shape[0], dtype=jnp.int32)
    chosen = (order[:, None] == rows[None, :]).reshape(order.shape + rows.shape + (1,) * (values.ndim - 1))
    return jnp.sum(jnp.where(chosen, values[None], 0.0), axis=1)


def body(
    cols,
    nr,
    tokens_in,
    pad_offsets,
    norm1_gain,
    norm1_bias,
    qkv_weight,
    qv_bias,
    table_height,
    table_width,
    proj_weight,
    proj_bias,
    norm2_gain,
    norm2_bias,
    fc1_weight,
    fc1_bias,
    fc2_weight,
    fc2_bias,
    out_grad,
):
    width = D // cols
    bw = D // nr
    per = -(-WINDOWS // cols)
    me = lax.axis_index("col").astype(jnp.int32)
    my_row = lax.axis_index("row").astype(jnp.int32)
    sets, rows = window_sets(cols, per)
    info = layout_info(sets, pad_offsets[0], me, my_row)
    row_order = my_row ^ jnp.arange(nr, dtype=jnp.int32)

    vec = jnp.concatenate(
        [
            norm1_gain,
            norm1_bias,
            norm2_gain,
            norm2_bias,
            proj_bias.astype(F32),
            fc2_bias.astype(F32),
            qv_bias[0].astype(F32),
            qv_bias[1].astype(F32),
            fc1_bias.astype(F32),
        ]
    )
    hidden = fc1_weight.shape[1]
    half = hidden // 2
    fc2_t = fc2_weight.T
    size = vec.shape[0]
    high = lax.reduce_precision(vec, 8, 7)
    mid = lax.reduce_precision(vec - high, 8, 7)
    low = vec - high - mid
    vec_rows = jnp.stack([high, mid, low]).astype(BF).reshape(-1, 3 * width)
    qkv_shard = jnp.concatenate([qkv_weight.reshape(bw, 3 * width), vec_rows], axis=0)
    x_sent = spread(tokens_in, info, cols, per, rows)
    qkv_stack = gather_cols(qkv_shard, cols)
    x_pieces = col_exchange(x_sent)
    vecs = jnp.sum(qkv_stack[:, bw:].astype(F32).reshape(cols, 3, size), axis=1)
    qkv_a = list(gather_rows(qkv_stack[:, : bw // 2], nr, False))[-1]
    qkv_b = list(gather_rows(qkv_stack[:, bw // 2 : bw], nr, True))[-1]
    wide0 = jnp.concatenate([fc1_weight[:, :half], proj_weight.T, fc2_t[:, :half]], axis=1)
    wide1 = jnp.concatenate([fc1_weight[:, half:], fc2_t[:, half:]], axis=1)
    stack0 = gather_cols(after(wide0, x_pieces, *qkv_a, *qkv_b), cols)
    first = half + width
    hops0 = [gather_rows(stack0[:, :, :first], nr, False), gather_rows(stack0[:, :, first:], nr, True)]

    features = vecs[:, : 6 * width].reshape(cols, 6, width // bw, bw)
    features = features.transpose(0, 2, 1, 3).reshape(nr, 6, bw)
    features = pick_rows(features, row_order).transpose(1, 0, 2).reshape(6, 1, D)
    gain1, bias1, gain2, bias2, bias_p, bias_2 = [features[i] for i in range(6)]
    q_bias = vecs[:, 6 * width : 7 * width]
    v_bias = vecs[:, 7 * width : 8 * width]
    bias_qkv = jnp.stack([q_bias, jnp.zeros_like(q_bias), v_bias], axis=1).reshape(1, 3 * D)
    bias_h = vecs[:, 8 * width :]

    x_full, n1, qkv = norm_qkv(
        x_pieces, qkv_a, qkv_b, info, gain1, bias1, bias_qkv, cols, rows, nr
    )
    shifts_np, onehot_np = rel_constants()
    shifts = jnp.asarray(shifts_np)
    onehot = jnp.asarray(onehot_np, BF)
    tables = table_matrix(table_height, table_width)
    g_pieces = col_exchange(spread(after(out_grad, n1), info, cols, per, rows))
    held = ()
    arrived = []
    for part, base in enumerate(range(0, cols, cols // SPLITS)):
        held = attend(
            after(qkv, *arrived),
            info,
            tables,
            shifts,
            onehot,
            base,
            cols // SPLITS,
            held,
            cols,
            per,
        )
        if part == 0:
            arrived = [stack0]
            stack1 = gather_cols(after(wide1, held[0]), cols)
            hops1 = [
                gather_rows(stack1[:, :, :half], nr, False),
                gather_rows(stack1[:, :, half:], nr, True),
            ]
        if part == 1:
            bufs0 = [next(hop) for hop in hops0]
            arrived = bufs0[0] + bufs0[1]
        if part == 2:
            bufs0 = [next(hop) for hop in hops0]
            arrived = bufs0[0] + bufs0[1] + [stack1]
    att, exps, inv = held
    bufs0 = [list(hop)[-1] for hop in hops0]
    bufs1 = [next(hop) for hop in hops1]
    resid, n2 = proj_norm(
        bufs0[0], after(att, *bufs1[0], *bufs1[1]), x_full, bias_p, gain2, bias2, cols, rows, nr
    )
    g_full = join(g_pieces, info, cols, rows, nr)
    bufs1 = [next(hop) for hop in hops1]
    n2 = after(n2, *bufs1[0], *bufs1[1])
    bufs1 = [list(hop)[-1] for hop in hops1]
    fc1_bufs = [bufs0[0], bufs1[0]]
    fc2_bufs = [bufs0[1], bufs1[1]]

    acts, grads, sends, hidden_sums = [], [], [], []
    for c in range(2):
        act, grad, keep, send, bias_sum = mlp_grads(
            fc1_bufs[c],
            fc2_bufs[c],
            n2,
            g_full,
            bias_h[:, None, c * half : (c + 1) * half],
            cols,
            rows,
            nr,
        )
        acts.append(act)
        grads.append(grad)
        hidden_sums.append(jnp.sum(bias_sum, axis=1))
        sends.append(reduce_weight(keep, send, -1, cols, nr))
    block_sent = block_rows(
        fc2_bufs, acts, after(resid, *next(sends[0])), bias_2, info, cols, rows, nr
    )
    block_pieces = col_exchange(block_sent)
    resid_grad, proj_grad, sums2 = mlp_back(
        fc1_bufs,
        grads,
        after(resid, block_sent, *next(sends[0]), *next(sends[1])),
        g_full,
        gain2,
        cols,
        rows,
        nr,
    )
    proj_grad = after(proj_grad, *next(sends[0]), *next(sends[1]))
    att_grad, keep, send = proj_back(fc1_bufs[0], proj_grad, att, cols, rows, nr)
    sends.append(reduce_weight(keep, send, None, cols, nr))
    held, table_sums, bias_sums = (), [], []
    for part, base in enumerate(range(0, cols, cols // SPLITS)):
        arrived = []
        if part == 1:
            arrived = [block_pieces, *next(sends[1]), *next(sends[2])]
        if part == 2:
            arrived = [*next(sends[0]), *next(sends[2])]
        if part == 3:
            arrived = [*next(sends[0]), *next(sends[1]), *next(sends[2])]
        dqkv, table_sum, bias_sum = attend_back(
            after(qkv, *arrived),
            info,
            exps,
            inv,
            att,
            att_grad,
            tables,
            shifts,
            onehot,
            base,
            cols // SPLITS,
            held,
            cols,
            per,
        )
        held = (dqkv,)
        table_sums.append(table_sum)
        bias_sums.append(bias_sum)
    table_sum = sum(table_sums[1:], table_sums[0])
    bias_sum = jnp.concatenate(bias_sums, axis=1)
    n1_back = after(n1, *next(sends[1]), *next(sends[2]), *next(sends[2]))
    keep, send = qkv_grad(n1_back, dqkv, cols, rows, nr)
    sends.append(reduce_weight(keep, send, -2, cols, nr))
    fc_grads = [list(sends[c])[-1] for c in range(2)]
    proj_w_grad = list(sends[2])[-1]
    qkv_w_grad = list(sends[3])[-1]
    ratio = width // bw
    places = jnp.arange(cols * ratio, dtype=jnp.int32) ^ my_row

    def by_col(sums):
        count = sums.shape[0]
        blocks = jnp.sum(sums, axis=1).reshape(count, nr, bw).transpose(1, 0, 2)
        picked = pick_rows(blocks, places).reshape(cols, ratio, count, bw)
        return picked.transpose(0, 2, 1, 3).reshape(cols, count * width)

    bias_cols = jnp.sum(bias_sum, axis=0).reshape(cols, 3, width)
    small = jnp.concatenate([by_col(sums2), bias_cols[:, 0], bias_cols[:, 2]] + hidden_sums, axis=1)
    table_h_grad, table_w_grad = split_table(table_sum)
    table_flat = jnp.concatenate([table_h_grad.reshape(-1), table_w_grad.reshape(-1)])
    early = reduce_small(small, table_flat, cols, nr)
    early_arrived = next(early)

    in_sent, in_sums = input_back(
        qkv_a,
        qkv_b,
        after(dqkv, keep, early_arrived),
        x_full,
        resid_grad,
        gain1,
        info,
        cols,
        rows,
        nr,
    )
    late = reduce_small(by_col(in_sums), None, cols, nr)
    late_arrived = next(late)
    in_pieces = col_exchange(after(in_sent, late_arrived))
    block_out = collect(after(block_pieces, in_sent), info, per, BF)
    input_grad = collect(in_pieces, info, per, F32)
    small, table_flat = list(early)[-1]
    late, _ = list(late)[-1]
    table_flat = table_flat.reshape(2, 27, HD)

    def part(i):
        return small[i * width : (i + 1) * width]

    return (
        block_out,
        input_grad,
        late[:width],
        late[width:],
        qkv_w_grad.reshape(bw, 3, width),
        jnp.stack([part(4), part(5)]),
        table_flat[0],
        table_flat[1],
        proj_w_grad.T,
        part(0),
        part(1),
        part(2),
        jnp.concatenate([grad[:, :half] for grad in fc_grads], axis=1),
        small[6 * width :],
        jnp.concatenate([grad[:, half:] for grad in fc_grads], axis=1).T,
        part(3),
    )


def solution(mesh):
    placed = (
        P("row", "col"),
        P("row", None),
        P("col"),
        P("col"),
        P("row", None, "col"),
        P(None, "col"),
        P(),
        P(),
        P("col", "row"),
        P("col"),
        P("col"),
        P("col"),
        P("row", "col"),
        P("col"),
        P("col", "row"),
        P("col"),
        P("row", "col"),
    )
    return jax.shard_map(
        partial(body, mesh.shape["col"], mesh.shape["row"]),
        mesh=mesh,
        in_specs=placed,
        out_specs=(
            P("row", "col"),
            P("row", "col"),
            P("col"),
            P("col"),
            P("row", None, "col"),
            P(None, "col"),
            P(),
            P(),
            P("col", "row"),
            P("col"),
            P("col"),
            P("col"),
            P("row", "col"),
            P("col"),
            P("col", "row"),
            P("col"),
        ),
        check_vma=False,
    )
```

time: 1220 us -> 733 us (0.60)
  Pallas kernels: 150 us -> 414 us
  blocking collectives: 264 us -> 0 us
  matrix products: 247 us -> 0 us
  waiting for transfers between devices: 322 us -> 132 us
  local copies, waits for them, and re-layouts: 157 us -> 38.9 us
  starting transfers between devices: 18 us -> 98 us
    pallas_call x8 -> x34, Pallas kernels: 150 us -> 414 us  [the longest x4 82.5 us: attend_back(): pl.pallas_call(partial(attend_back_kernel, width, len(held)), out_shape=[...]
    dot_general x12 -> x0, matrix products: 247 us -> none  [the longest x4 121 us: nn_dot(): lax.dot_general(a, b, (((1,), (0,)), ((), ())), preferred_element_type=F32)]
    reduce_scatter x3 -> x0, waiting for transfers between devices: 232 us -> none  [scatter(): return lax.psum_scatter(grad, both, scatter_dimension=0, tiled=True)]
    psum x1 -> x0, blocking collectives: 166 us -> none  [body(): lax.psum((small, table_h_grad, table_w_grad), both)]
    all_gather x1 -> x0, blocking collectives: 97.5 us -> none  [body(): vecs = lax.all_gather(vec, 'col', axis=0)]
    all_to_all x0 -> x13, waiting for transfers between devices: none -> 71.1 us  [col_exchange(): return lax.all_to_all(values, 'col', 0, 0, tiled=True)]
    reshape x14 -> x6, local copies, waits for them, and re-layouts: 66.5 us -> 1.79 us  [the longest x1 1.01 us: body(): vecs = jnp.sum(qkv_stack[:, bw:].astype(F32).reshape(cols, 3, size), axis=1)]
    all_to_all x0 -> x13, starting transfers between devices: none -> 60.4 us  [col_exchange(): return lax.all_to_all(values, 'col', 0, 0, tiled=True)]
  transfers between devices with their start and end apart: 18 -> 61, of which waited for: 5 -> 15; matrix products, arithmetic and copies ran while one was open for 22% -> 7% of each run, Pallas kernels for 12% -> 52%
where the time goes in v2:
time: 733 us; the launch traced here: 723 us
  Pallas kernels  414 us (56%)
  waiting for transfers between devices  132 us (18%)
  starting transfers between devices  98 us (13%)
  local copies, waits for them, and re-layouts  38.9 us (5%)
  other arithmetic  36.7 us (5%)
    pallas_call x4, Pallas kernels, attend_back(): pl.pallas_call(partial(attend_back_kernel, width, len(held)), out_shape=[...  82.5 us
    pallas_call x4, Pallas kernels, attend(): pl.pallas_call(partial(attend_kernel, width, len(held)), out_shape=[jax.S...  81.3 us
    all_to_all x13, waiting for transfers between devices, col_exchange(): return lax.all_to_all(values, 'col', 0, 0, tiled=True)  71.1 us
    pallas_call x2, Pallas kernels, mlp_grads(): pl.pallas_call(partial(mlp_grads_kernel, nr), out_shape=[act, act, half,...  62 us
    ppermute x48, waiting for transfers between devices, row_swap(): return lax.ppermute(values, 'row', [(i, i ^ bit) for i in range(nr)])  60.5 us
    all_to_all x13, starting transfers between devices, col_exchange(): return lax.all_to_all(values, 'col', 0, 0, tiled=True)  60.4 us
    ppermute x48, starting transfers between devices, row_swap(): return lax.ppermute(values, 'row', [(i, i ^ bit) for i in range(nr)])  37.6 us
    pallas_call x2, Pallas kernels, collect(): pl.pallas_call(partial(collect_kernel, per), out_shape=jax.ShapeDtypeStru...  29.9 us
  transfers between devices with their start and end apart: 61, of which 15 were waited for; matrix products, arithmetic and copies ran while one was open for 7% of the time, Pallas kernels for 52%

profile of v2, /device:TPU:0, one launch (start us, length us, event | category | flops | bytes accessed | tf_op | source)
XLA Modules:
  0.0 722.8 jit_solution(1537355677580556885)
XLA Ops:
  9.5 6.3 all-to-all-start.1
  17.7 2.0 select_reduce_fusion.3
  24.2 10.5 %spread.2 = bf16[4,1088,256]{2,1,0:T(8,128)(2,1)} custom-call(s32[201]{0:T(256)} %concatenate.107.info, bf16[4096,256]{1,0:T(8,128)(2,1)} %x_ref.1), custom_call_target="tpu_custom_call" | custom-call | flops 7699999744 | bytes 7000000 | tf_op jit(solution)/shard_map/spread/pallas_call | solution.py:146
  34.7 3.2 all-to-all-done.1
  38.0 3.6 all-to-all-start
  50.5 3.1 collective-permute-done
  53.6 2.1 pad_maximum_fusion.4.refs_1_.refs_0_
  64.4 9.1 %collective-permute-done.1.refs_2_.refs_1_ = bf16[2,4,64,768]{3,2,1,0:T(8,128)(2,1)} collective-permute-done((bf16[2,4,64,768]{3,2,1,0:T(8,128)(2,1)}, bf16[2,4,64,768]{3,2,1,0:T(8,128)(2,1)}, u32[]{:S(2)}, u32[]{:S(2)}) %collective-permute-start.1) | collective-permute-done | bytes 786464 | tf_op jit(solution)/shard_map/ppermute | solution.py:946
  73.6 3.2 collective-permute-done.5.refs_6_.refs_5_
  79.6 12.5 %all-to-all-done.refs_0_ = bf16[4,1088,256]{2,1,0:T(8,128)(2,1)S(1)} async-done(((bf16[4,1088,256]{2,1,0:T(8,128)(2,1)}), bf16[4,1088,256]{2,1,0:T(8,128)(2,1)S(1)}, u32[]{:S(2)}, u32[]{:S(2)}) %all-to-all-start) | async-done | bytes 2228256 | tf_op jit(solution)/shard_map/all_to_all | solution.py:942
  93.5 14.9 %norm_qkv.1 = (bf16[1088,1024]{1,0:T(8,128)(2,1)}, bf16[1088,1024]{1,0:T(8,128)(2,1)}, bf16[1088,3072]{1,0:T(8,128)(2,1)}) custom-call(s32[201]{0:T(256)} %concatenate.107.info, bf16[4,1088,256]{2,1,0:T(8,128)(2,1)} %copy-done.8, bf16[2,4,64,768]{3,2,1,0:T(8,128)(2,1)} %pad_maximum_fusion.4.refs_1_.refs_0_, ...), custom_call_target="tpu_custom_call" | custom-call | flops 20899999744 | bytes 19000000 | tf_op jit(solution)/shard_map/norm_qkv/pallas_call | solution.py:300
  108.3 20.4 %attend.4 = (bf16[1088,1024]{1,0:T(8,128)(2,1)}, bf16[16,1400,256]{2,1,0:T(8,128)(2,1)}, f32[1400,1024]{1,0:T(8,128)}) custom-call(s32[201]{0:T(256)} %concatenate.107.info, bf16[1088,3072]{1,0:T(8,128)(2,1)} %get-tuple-element.144.qkv, bf16[128,128]{1,0:T(8,128)(2,1)} %pad_maximum_fusion.11.tables, s32[200,128]{1,0:T(8,128)} %constant.41.clone.shifts, ...), custom_call_target="tpu_custom_call" | custom-call | flops 15399999488 | bytes 14000000 | tf_op jit(solution)/shard_map/attend/pallas_call | solution.py:766
  130.0 3.5 all-to-all-start.3
  133.9 24.8 %all-to-all-done.3 = bf16[4,128,1024]{2,1,0:T(8,128)(2,1)S(1)} async-done(((bf16[4,128,1024]{2,1,0:T(8,128)(2,1)}), bf16[4,128,1024]{2,1,0:T(8,128)(2,1)S(1)}, u32[]{:S(2)}, u32[]{:S(2)}) %all-to-all-start.3) | async-done | bytes 1048608 | tf_op jit(solution)/shard_map/all_to_all | solution.py:942
  159.8 3.5 all-to-all-start.2
  164.6 10.5 %spread.3 = bf16[4,1088,256]{2,1,0:T(8,128)(2,1)} custom-call(s32[201]{0:T(256)} %concatenate.107.info, bf16[4096,256]{1,0:T(8,128)(2,1)} %x_ref.2), custom_call_target="tpu_custom_call" | custom-call | flops 7699999744 | bytes 7000000 | tf_op jit(solution)/shard_map/spread/pallas_call | solution.py:146
  178.3 15.9 %all-to-all-done.2 = bf16[4,128,1280]{2,1,0:T(8,128)(2,1)S(1)} async-done(((bf16[4,128,1280]{2,1,0:T(8,128)(2,1)}), bf16[4,128,1280]{2,1,0:T(8,128)(2,1)S(1)}, u32[]{:S(2)}, u32[]{:S(2)}) %all-to-all-start.2) | async-done | bytes 1310752 | tf_op jit(solution)/shard_map/all_to_all | solution.py:942
  194.2 4.7 all-to-all-start.4
  202.1 20.3 %attend.5 = (bf16[1088,1024]{1,0:T(8,128)(2,1)}, bf16[16,1400,256]{2,1,0:T(8,128)(2,1)}, f32[1400,1024]{1,0:T(8,128)}) custom-call(s32[201]{0:T(256)} %concatenate.107.info, bf16[1088,3072]{1,0:T(8,128)(2,1)} %get-tuple-element.144.qkv, bf16[128,128]{1,0:T(8,128)(2,1)} %pad_maximum_fusion.11.tables, ...), custom_call_target="tpu_custom_call", output_to_operand_aliasing={{0}: (5, {}), {1}: (6, {}), {2}: (7, {})} | custom-call | flops 15399999488 | bytes 14000000 | tf_op jit(solution)/shard_map/attend/pallas_call | solution.py:766
  222.4 2.1 pad_maximum_fusion.2.refs_4_
  226.2 2.8 pad_maximum_fusion.refs_0_
  232.3 20.3 %attend.6 = (bf16[1088,1024]{1,0:T(8,128)(2,1)}, bf16[16,1400,256]{2,1,0:T(8,128)(2,1)}, f32[1400,1024]{1,0:T(8,128)}) custom-call(s32[201]{0:T(256)} %concatenate.107.info, bf16[1088,3072]{1,0:T(8,128)(2,1)} %get-tuple-element.144.qkv, bf16[128,128]{1,0:T(8,128)(2,1)} %pad_maximum_fusion.11.tables, ...), custom_call_target="tpu_custom_call", output_to_operand_aliasing={{0}: (5, {}), {1}: (6, {}), {2}: (7, {})} | custom-call | flops 15399999488 | bytes 14000000 | tf_op jit(solution)/shard_map/attend/pallas_call | solution.py:766
  252.6 13.6 %collective-permute-done.17.refs_1_ = bf16[2,4,128,768]{3,2,1,0:T(8,128)(2,1)} collective-permute-done((bf16[2,4,128,768]{3,2,1,0:T(8,128)(2,1)}, bf16[2,4,128,768]{3,2,1,0:T(8,128)(2,1)}, u32[]{:S(2)}, u32[]{:S(2)}) %collective-permute-start.17) | collective-permute-done | bytes 1572896 | tf_op jit(solution)/shard_map/ppermute | solution.py:946
  266.2 4.8 join.1.refs_9_.refs_11_
  271.4 20.3 %attend.7 = (bf16[1088,1024]{1,0:T(8,128)(2,1)}, bf16[16,1400,256]{2,1,0:T(8,128)(2,1)}, f32[1400,1024]{1,0:T(8,128)}) custom-call(s32[201]{0:T(256)} %concatenate.107.info, bf16[1088,3072]{1,0:T(8,128)(2,1)} %get-tuple-element.144.qkv, bf16[128,128]{1,0:T(8,128)(2,1)} %pad_maximum_fusion.11.tables, ...), custom_call_target="tpu_custom_call", output_to_operand_aliasing={{0}: (5, {}), {1}: (6, {}), {2}: (7, {})} | custom-call | flops 15399999488 | bytes 14000000 | tf_op jit(solution)/shard_map/attend/pallas_call | solution.py:766
  292.4 7.9 %proj_norm.1 = (f32[1088,1024]{1,0:T(8,128)}, bf16[1088,1024]{1,0:T(8,128)(2,1)}) custom-call(bf16[2,4,128,768]{3,2,1,0:T(8,128)(2,1)} %pad_maximum_fusion.refs_0_, bf16[2,4,128,768]{3,2,1,0:T(8,128)(2,1)} %collective-permute-done.17.refs_1_, bf16[2,4,128,768]{3,2,1,0:T(8,128)(2,1)} %collective-permute-done.18.refs_2_, ...), custom_call_target="tpu_custom_call" | custom-call | flops 12099999744 | bytes 11000000 | tf_op jit(solution)/shard_map/proj_norm/pallas_call | solution.py:373
  301.0 31.2 %mlp_grads.2 = (bf16[1088,2048]{1,0:T(8,128)(2,1)}, bf16[1088,2048]{1,0:T(8,128)(2,1)}, bf16[4,4,128,1024]{3,2,1,0:T(8,128)(2,1)}, bf16[4,4,128,1024]{3,2,1,0:T(8,128)(2,1)}, f32[4,8,512]{2,1,0:T(8,128)}) custom-call(bf16[2,4,128,768]{3,2,1,0:T(8,128)(2,1)} %pad_maximum_fusion.refs_0_, bf16[2,4,128,768]{3,2,1,0:T(8,128)(2,1)} %collective-permute-done.17.refs_1_, ...), custom_call_target="tpu_custom_call" | custom-call | flops 41799999488 | bytes 38000000 | tf_op jit(solution)/shard_map/mlp_grads/pallas_call | solution.py:436
  332.7 30.8 %mlp_grads.3 = (bf16[1088,2048]{1,0:T(8,128)(2,1)}, bf16[1088,2048]{1,0:T(8,128)(2,1)}, bf16[4,4,128,1024]{3,2,1,0:T(8,128)(2,1)}, bf16[4,4,128,1024]{3,2,1,0:T(8,128)(2,1)}, f32[4,8,512]{2,1,0:T(8,128)}) custom-call(bf16[2,4,128,512]{3,2,1,0:T(8,128)(2,1)} %copy-done.9, bf16[2,4,128,512]{3,2,1,0:T(8,128)(2,1)} %copy-done.44, ...), custom_call_target="tpu_custom_call" | custom-call | flops 41799999488 | bytes 38000000 | tf_op jit(solution)/shard_map/mlp_grads/pallas_call | solution.py:436
  366.4 3.3 add_rows.8
  372.8 3.3 add_rows.10
  377.3 17.7 %block_rows.1 = bf16[4,1088,256]{2,1,0:T(8,128)(2,1)} custom-call(s32[201]{0:T(256)} %concatenate.107.info, bf16[2,4,128,512]{3,2,1,0:T(8,128)(2,1)} %copy-done.10, bf16[2,4,128,512]{3,2,1,0:T(8,128)(2,1)} %collective-permute-done.9.refs_5_.refs_1_, bf16[2,4,128,512]{3,2,1,0:T(8,128)(2,1)} %collective-permute-done.10.refs_6_.refs_2_, ...), custom_call_target="tpu_custom_call" | custom-call | flops 28600000512 | bytes 26000000 | tf_op jit(solution)/shard_map/block_rows/pallas_call | solution.py:483
  395.0 5.1 all-to-all-start.5
  402.1 3.0 add_rows.9
  407.9 10.5 %collective-permute-done.30.refs_2_ = bf16[2,4,128,512]{3,2,1,0:T(8,128)(2,1)S(1)} collective-permute-done((bf16[2,4,128,512]{3,2,1,0:T(8,128)(2,1)}, bf16[2,4,128,512]{3,2,1,0:T(8,128)(2,1)S(1)}, u32[]{:S(2)}, u32[]{:S(2)}) %collective-permute-start.30) | collective-permute-done | bytes 1048608 | tf_op jit(solution)/shard_map/ppermute | solution.py:946
  420.1 3.0 add_rows.11
  425.5 19.4 %mlp_back.1 = (f32[1088,1024]{1,0:T(8,128)}, bf16[1088,1024]{1,0:T(8,128)(2,1)}, f32[4,8,1024]{2,1,0:T(8,128)}) custom-call(bf16[2,4,128,768]{3,2,1,0:T(8,128)(2,1)} %pad_maximum_fusion.refs_0_, bf16[2,4,128,768]{3,2,1,0:T(8,128)(2,1)} %collective-permute-done.17.refs_1_, bf16[2,4,128,768]{3,2,1,0:T(8,128)(2,1)} %collective-permute-done.18.refs_2_, ...), custom_call_target="tpu_custom_call" | custom-call | flops 30799998976 | bytes 28000000 | tf_op jit(solution)/shard_map/mlp_back/pallas_call | solution.py:529
  446.1 9.6 %proj_back.1 = (bf16[1088,1024]{1,0:T(8,128)(2,1)}, bf16[4,4,128,256]{3,2,1,0:T(8,128)(2,1)}, bf16[4,4,128,256]{3,2,1,0:T(8,128)(2,1)}) custom-call(bf16[2,4,128,768]{3,2,1,0:T(8,128)(2,1)} %pad_maximum_fusion.refs_0_, bf16[2,4,128,768]{3,2,1,0:T(8,128)(2,1)} %collective-permute-done.17.refs_1_, bf16[2,4,128,768]{3,2,1,0:T(8,128)(2,1)} %collective-permute-done.18.refs_2_, ...), custom_call_target="tpu_custom_call" | custom-call | flops 12099999744 | bytes 11000000 | tf_op jit(solution)/shard_map/proj_back/pallas_call | solution.py:561
  455.8 20.5 %attend_back.4 = (bf16[1088,3072]{1,0:T(8,128)(2,1)}, f32[128,256]{1,0:T(8,128)}, f32[8,768]{1,0:T(8,128)}) custom-call(s32[201]{0:T(256)} %concatenate.107.info, bf16[1088,3072]{1,0:T(8,128)(2,1)} %get-tuple-element.144.qkv, bf16[16,1400,256]{2,1,0:T(8,128)(2,1)} %get-tuple-element.140.exps, f32[1400,1024]{1,0:T(8,128)} %get-tuple-element.141.inv, ...), custom_call_target="tpu_custom_call" | custom-call | flops 14300000256 | bytes 13000000 | tf_op jit(solution)/shard_map/attend_back/pallas_call | solution.py:891
  477.3 2.0 add_rows.12
  480.5 3.7 add_cols.4
  485.7 3.6 add_cols.5
  489.4 4.5 collective-permute-done.35.refs_2_
  497.1 5.3 all-to-all-start.6
  502.4 20.6 %attend_back.5 = (bf16[1088,3072]{1,0:T(8,128)(2,1)}, f32[128,256]{1,0:T(8,128)}, f32[8,768]{1,0:T(8,128)}) custom-call(s32[201]{0:T(256)} %concatenate.107.info, bf16[1088,3072]{1,0:T(8,128)(2,1)} %get-tuple-element.144.qkv, bf16[16,1400,256]{2,1,0:T(8,128)(2,1)} %get-tuple-element.140.exps, ...), custom_call_target="tpu_custom_call", output_to_operand_aliasing={{0}: (9, {})} | custom-call | flops 14300000256 | bytes 13000000 | tf_op jit(solution)/shard_map/attend_back/pallas_call | solution.py:891
  523.0 20.6 %attend_back.6 = (bf16[1088,3072]{1,0:T(8,128)(2,1)}, f32[128,256]{1,0:T(8,128)}, f32[8,768]{1,0:T(8,128)}) custom-call(s32[201]{0:T(256)} %concatenate.107.info, bf16[1088,3072]{1,0:T(8,128)(2,1)} %get-tuple-element.144.qkv, bf16[16,1400,256]{2,1,0:T(8,128)(2,1)} %get-tuple-element.140.exps, ...), custom_call_target="tpu_custom_call", output_to_operand_aliasing={{0}: (9, {})} | custom-call | flops 14300000256 | bytes 13000000 | tf_op jit(solution)/shard_map/attend_back/pallas_call | solution.py:891
  543.6 5.1 all-to-all-start.7
  548.8 20.7 %attend_back.7 = (bf16[1088,3072]{1,0:T(8,128)(2,1)}, f32[128,256]{1,0:T(8,128)}, f32[8,768]{1,0:T(8,128)}) custom-call(s32[201]{0:T(256)} %concatenate.107.info, bf16[1088,3072]{1,0:T(8,128)(2,1)} %get-tuple-element.144.qkv, bf16[16,1400,256]{2,1,0:T(8,128)(2,1)} %get-tuple-element.140.exps, ...), custom_call_target="tpu_custom_call", output_to_operand_aliasing={{0}: (9, {})} | custom-call | flops 14300000256 | bytes 13000000 | tf_op jit(solution)/shard_map/attend_back/pallas_call | solution.py:891
  572.0 2.0 add_cols.6
  574.0 5.1 all-to-all-start.8
  579.8 6.1 all-to-all-done.8
  585.9 3.6 all-to-all-start.12
  589.5 12.5 %qkv_grad.1 = (bf16[4,4,128,768]{3,2,1,0:T(8,128)(2,1)}, bf16[4,4,128,768]{3,2,1,0:T(8,128)(2,1)}) custom-call(bf16[1088,1024]{1,0:T(8,128)(2,1)} %get-tuple-element.149.n1, bf16[1088,3072]{1,0:T(8,128)(2,1)} %get-tuple-element.151.dqkv.refs_8_), custom_call_target="tpu_custom_call" | custom-call | flops 15399999488 | bytes 14000000 | tf_op jit(solution)/shard_map/qkv_grad/pallas_call | solution.py:582
  602.1 16.2 %input_back.1 = (bf16[4,1088,256]{2,1,0:T(8,128)(2,1)}, f32[2,8,1024]{2,1,0:T(8,128)}) custom-call(s32[201]{0:T(256)} %concatenate.107.info, bf16[2,4,64,768]{3,2,1,0:T(8,128)(2,1)} %pad_maximum_fusion.4.refs_1_.refs_0_, bf16[2,4,64,768]{3,2,1,0:T(8,128)(2,1)} %collective-permute-done.1.refs_2_.refs_1_, bf16[2,4,64,768]{3,2,1,0:T(8,128)(2,1)} %copy-done.46, ...), custom_call_target="tpu_custom_call" | custom-call | flops 27499999232 | bytes 25000000 | tf_op jit(solution)/shard_map/input_back/pallas_call | solution.py:619
  620.0 5.1 all-to-all-start.10
  625.0 5.6 all-to-all-done.10
  630.6 4.5 all-to-all-start.9
  642.3 2.8 add_rows.14
  650.7 14.8 %collective-permute-done.47 = f32[6016]{0:T(1024)S(1)} collective-permute-done((f32[6016]{0:T(1024)S(1)}, f32[6016]{0:T(1024)S(1)}, u32[]{:S(2)}, u32[]{:S(2)}) %collective-permute-start.47) | collective-permute-done | bytes 24096 | tf_op jit(solution)/shard_map/ppermute | solution.py:946
  671.2 2.6 add_rows.15
  676.5 14.6 %collect.2 = bf16[4096,256]{1,0:T(8,128)(2,1)} custom-call(s32[201]{0:T(256)} %concatenate.107.info, bf16[4,1088,256]{2,1,0:T(8,128)(2,1)} %all-to-all-done.5.pieces), custom_call_target="tpu_custom_call" | custom-call | flops 9900000256 | bytes 9000000 | tf_op jit(solution)/shard_map/collect/pallas_call | solution.py:191
  693.4 3.1 add_cols.7
  696.5 5.0 all-to-all-start.11
  702.9 15.3 %collect.3 = f32[4096,256]{1,0:T(8,128)} custom-call(s32[201]{0:T(256)} %concatenate.107.info, bf16[4,1088,256]{2,1,0:T(8,128)(2,1)} %all-to-all-done.9.pieces), custom_call_target="tpu_custom_call" | custom-call | flops 9900000256 | bytes 9000000 | tf_op jit(solution)/shard_map/collect/pallas_call | solution.py:191
  718.3 2.9 all-to-all-done.11
  (331 shorter events, 107.9 us)
Async XLA Ops:
  9.5 28.5 %all-to-all-start.1 = ((bf16[4,140,768]{2,1,0:T(8,128)(2,1)}), bf16[4,140,768]{2,1,0:T(8,128)(2,1)S(1)}, u32[]{:S(2)}, u32[]{:S(2)}) async-start(bf16[4,140,768]{2,1,0:T(8,128)(2,1)} %broadcast_in_dim.141), calls=%async_computation.1 | async-start | bytes 1769472 | tf_op jit(solution)/shard_map/all_to_all | solution.py:942
  38.0 54.1 %all-to-all-start = ((bf16[4,1088,256]{2,1,0:T(8,128)(2,1)}), bf16[4,1088,256]{2,1,0:T(8,128)(2,1)S(1)}, u32[]{:S(2)}, u32[]{:S(2)}) async-start(bf16[4,1088,256]{2,1,0:T(8,128)(2,1)} %spread.2), calls=%async_computation | async-start | bytes 4456448 | tf_op jit(solution)/shard_map/all_to_all | solution.py:942
  43.2 10.4 %collective-permute-start = (bf16[1,4,64,768]{3,2,1,0:T(8,128)(2,1)}, bf16[1,4,64,768]{3,2,1,0:T(8,128)(2,1)}, u32[]{:S(2)}, u32[]{:S(2)}) collective-permute-start(bf16[1,4,64,768]{3,2,1,0:T(8,128)(2,1)} %get-tuple-element.257), channel_id=1, source_target_pairs={{0,8},{4,12},{8,0},{12,4},{16,24},{20,28},{24,16},{28,20},{1,9},{5... | collective-permute-start | bytes 1179656 | tf_op jit(solution)/shard_map/ppermute | solution.py:946
  44.7 12.5 %collective-permute-start.4 = (bf16[1,4,64,768]{3,2,1,0:T(8,128)(2,1)S(1)}, bf16[1,4,64,768]{3,2,1,0:T(8,128)(2,1)}, u32[]{:S(2)}, u32[]{:S(2)}) collective-permute-start(bf16[1,4,64,768]{3,2,1,0:T(8,128)(2,1)S(1)} %get-tuple-element.256), channel_id=1, source_target_pairs={{0,16},{4,20},{8,24},{12,28},{16,0},{20,4},{24,8},{28,12},{1,17},{... | collective-permute-start | bytes 1179656 | tf_op jit(solution)/shard_map/ppermute | solution.py:946
  55.7 17.9 %collective-permute-start.1 = (bf16[2,4,64,768]{3,2,1,0:T(8,128)(2,1)}, bf16[2,4,64,768]{3,2,1,0:T(8,128)(2,1)}, u32[]{:S(2)}, u32[]{:S(2)}) collective-permute-start(bf16[2,4,64,768]{3,2,1,0:T(8,128)(2,1)} %pad_maximum_fusion.4.refs_1_.refs_0_), channel_id=1, source_target_pairs={{0,16},{4,20},{8,24},{12,28},{16,0},{20,4},{24,8},{28,12},{1,17},{... | collective-permute-start | bytes 2359304 | tf_op jit(solution)/shard_map/ppermute | solution.py:946
  59.1 17.6 %collective-permute-start.5 = (bf16[2,4,64,768]{3,2,1,0:T(8,128)(2,1)}, bf16[2,4,64,768]{3,2,1,0:T(8,128)(2,1)}, u32[]{:S(2)}, u32[]{:S(2)}) collective-permute-start(bf16[2,4,64,768]{3,2,1,0:T(8,128)(2,1)} %pad_maximum_fusion.5.refs_5_.refs_4_), channel_id=1, source_target_pairs={{0,8},{4,12},{8,0},{12,4},{16,24},{20,28},{24,16},{28,20},{1,9},{5... | collective-permute-start | bytes 2359304 | tf_op jit(solution)/shard_map/ppermute | solution.py:946
  63.9 15.7 %collective-permute-start.2 = (bf16[2,4,64,768]{3,2,1,0:T(8,128)(2,1)}, bf16[2,4,64,768]{3,2,1,0:T(8,128)(2,1)S(1)}, u32[]{:S(2)}, u32[]{:S(2)}) collective-permute-start(bf16[2,4,64,768]{3,2,1,0:T(8,128)(2,1)} %pad_maximum_fusion.4.refs_1_.refs_0_), channel_id=1, source_target_pairs={{0,4},{4,0},{8,12},{12,8},{16,20},{20,16},{24,28},{28,24},{1,5},{5... | collective-permute-start | bytes 2359304 | tf_op jit(solution)/shard_map/ppermute | solution.py:946
  63.9 15.6 %collective-permute-start.6 = (bf16[2,4,64,768]{3,2,1,0:T(8,128)(2,1)}, bf16[2,4,64,768]{3,2,1,0:T(8,128)(2,1)}, u32[]{:S(2)}, u32[]{:S(2)}) collective-permute-start(bf16[2,4,64,768]{3,2,1,0:T(8,128)(2,1)} %pad_maximum_fusion.5.refs_5_.refs_4_), channel_id=1, source_target_pairs={{0,4},{4,0},{8,12},{12,8},{16,20},{20,16},{24,28},{28,24},{1,5},{5... | collective-permute-start | bytes 2359304 | tf_op jit(solution)/shard_map/ppermute | solution.py:946
  73.6 6.0 collective-permute-start.3
  76.7 2.8 collective-permute-start.7
  130.0 28.7 %all-to-all-start.3 = ((bf16[4,128,1024]{2,1,0:T(8,128)(2,1)}), bf16[4,128,1024]{2,1,0:T(8,128)(2,1)S(1)}, u32[]{:S(2)}, u32[]{:S(2)}) async-start(bf16[4,128,1024]{2,1,0:T(8,128)(2,1)} %broadcast_in_dim.150), calls=%async_computation.3 | async-start | bytes 2097152 | tf_op jit(solution)/shard_map/all_to_all | solution.py:942
  159.8 34.3 %all-to-all-start.2 = ((bf16[4,128,1280]{2,1,0:T(8,128)(2,1)}), bf16[4,128,1280]{2,1,0:T(8,128)(2,1)S(1)}, u32[]{:S(2)}, u32[]{:S(2)}) async-start(bf16[4,128,1280]{2,1,0:T(8,128)(2,1)} %broadcast_in_dim.144), calls=%async_computation.2 | async-start | bytes 2621440 | tf_op jit(solution)/shard_map/all_to_all | solution.py:942
  175.2 47.2 %collective-permute-start.12 = (bf16[1,4,128,512]{3,2,1,0:T(8,128)(2,1)S(1)}, bf16[1,4,128,512]{3,2,1,0:T(8,128)(2,1)}, u32[]{:S(2)}, u32[]{:S(2)}) collective-permute-start(bf16[1,4,128,512]{3,2,1,0:T(8,128)(2,1)S(1)} %get-tuple-element.255), channel_id=1, source_target_pairs={{0,16},{4,20},{8,24},{12,28},{16,0},{20,4},{24,8},{28,12},{1,17},{... | collective-permute-start | bytes 1572872 | tf_op jit(solution)/shard_map/ppermute | solution.py:946
  176.8 48.3 %collective-permute-start.20 = (bf16[1,4,128,512]{3,2,1,0:T(8,128)(2,1)S(1)}, bf16[1,4,128,512]{3,2,1,0:T(8,128)(2,1)}, u32[]{:S(2)}, u32[]{:S(2)}) collective-permute-start(bf16[1,4,128,512]{3,2,1,0:T(8,128)(2,1)S(1)} %get-tuple-element.254), channel_id=1, source_target_pairs={{0,8},{4,12},{8,0},{12,4},{16,24},{20,28},{24,16},{28,20},{1,9},{5... | collective-permute-start | bytes 1572872 | tf_op jit(solution)/shard_map/ppermute | solution.py:946
  194.2 72.0 %all-to-all-start.4 = ((bf16[4,1088,256]{2,1,0:T(8,128)(2,1)}), bf16[4,1088,256]{2,1,0:T(8,128)(2,1)}, u32[]{:S(2)}, u32[]{:S(2)}) async-start(bf16[4,1088,256]{2,1,0:T(8,128)(2,1)} %spread.3), calls=%async_computation.4 | async-start | bytes 4456448 | tf_op jit(solution)/shard_map/all_to_all | solution.py:942
  198.9 30.7 %collective-permute-start.8 = (bf16[1,4,128,512]{3,2,1,0:T(8,128)(2,1)S(1)}, bf16[1,4,128,512]{3,2,1,0:T(8,128)(2,1)}, u32[]{:S(2)}, u32[]{:S(2)}) collective-permute-start(bf16[1,4,128,512]{3,2,1,0:T(8,128)(2,1)S(1)} %slice_bitcast_fusion.3), channel_id=1, source_target_pairs={{0,16},{4,20},{8,24},{12,28},{16,0},{20,4},{24,8},{28,12},{1,17},{... | collective-permute-start | bytes 1572872 | tf_op jit(solution)/shard_map/ppermute | solution.py:946
  200.5 25.7 %collective-permute-start.16 = (bf16[1,4,128,768]{3,2,1,0:T(8,128)(2,1)S(1)}, bf16[1,4,128,768]{3,2,1,0:T(8,128)(2,1)}, u32[]{:S(2)}, u32[]{:S(2)}) collective-permute-start(bf16[1,4,128,768]{3,2,1,0:T(8,128)(2,1)S(1)} %slice_bitcast_fusion), channel_id=1, source_target_pairs={{0,8},{4,12},{8,0},{12,4},{16,24},{20,28},{24,16},{28,20},{1,9},{5... | collective-permute-start | bytes 2359304 | tf_op jit(solution)/shard_map/ppermute | solution.py:946
  224.5 75.7 %collective-permute-start.13 = (bf16[2,4,128,512]{3,2,1,0:T(8,128)(2,1)}, bf16[2,4,128,512]{3,2,1,0:T(8,128)(2,1)}, u32[]{:S(2)}, u32[]{:S(2)}) collective-permute-start(bf16[2,4,128,512]{3,2,1,0:T(8,128)(2,1)} %pad_maximum_fusion.2.refs_4_), channel_id=1, source_target_pairs={{0,8},{4,12},{8,0},{12,4},{16,24},{20,28},{24,16},{28,20},{1,9},{5... | collective-permute-start | bytes 3145736 | tf_op jit(solution)/shard_map/ppermute | solution.py:946
  225.1 107.6 %collective-permute-start.14 = (bf16[2,4,128,512]{3,2,1,0:T(8,128)(2,1)}, bf16[2,4,128,512]{3,2,1,0:T(8,128)(2,1)}, u32[]{:S(2)}, u32[]{:S(2)}) collective-permute-start(bf16[2,4,128,512]{3,2,1,0:T(8,128)(2,1)} %pad_maximum_fusion.2.refs_4_), channel_id=1, source_target_pairs={{0,4},{4,0},{8,12},{12,8},{16,20},{20,16},{24,28},{28,24},{1,5},{5... | collective-permute-start | bytes 3145736 | tf_op jit(solution)/shard_map/ppermute | solution.py:946
  226.2 74.0 %copy-start.9 = (bf16[2,4,128,512]{3,2,1,0:T(8,128)(2,1)}, bf16[2,4,128,512]{3,2,1,0:T(8,128)(2,1)S(1)}, u32[]{:S(2)}) copy-start(bf16[2,4,128,512]{3,2,1,0:T(8,128)(2,1)S(1)} %pad_maximum_fusion.3.refs_0_.refs_4_) | copy-start | bytes 3145732
  229.0 37.1 %collective-permute-start.17 = (bf16[2,4,128,768]{3,2,1,0:T(8,128)(2,1)}, bf16[2,4,128,768]{3,2,1,0:T(8,128)(2,1)}, u32[]{:S(2)}, u32[]{:S(2)}) collective-permute-start(bf16[2,4,128,768]{3,2,1,0:T(8,128)(2,1)} %pad_maximum_fusion.refs_0_), channel_id=1, source_target_pairs={{0,16},{4,20},{8,24},{12,28},{16,0},{20,4},{24,8},{28,12},{1,17},{... | collective-permute-start | bytes 4718600 | tf_op jit(solution)/shard_map/ppermute | solution.py:946
  230.7 61.1 %copy-start.10 = (bf16[2,4,128,512]{3,2,1,0:T(8,128)(2,1)}, bf16[2,4,128,512]{3,2,1,0:T(8,128)(2,1)S(1)}, u32[]{:S(2)}) copy-start(bf16[2,4,128,512]{3,2,1,0:T(8,128)(2,1)S(1)} %pad_maximum_fusion.1.refs_4_.refs_0_) | copy-start | bytes 3145732
  230.7 40.2 %collective-permute-start.9 = (bf16[2,4,128,512]{3,2,1,0:T(8,128)(2,1)S(1)}, bf16[2,4,128,512]{3,2,1,0:T(8,128)(2,1)}, u32[]{:S(2)}, u32[]{:S(2)}) collective-permute-start(bf16[2,4,128,512]{3,2,1,0:T(8,128)(2,1)S(1)} %pad_maximum_fusion.1.refs_4_.refs_0_), channel_id=1, source_target_pairs={{0,8},{4,12},{8,0},{12,4},{16,24},{20,28},{24,16},{28,20},{1,9},{5... | collective-permute-start | bytes 3145736 | tf_op jit(solution)/shard_map/ppermute | solution.py:946
  232.3 59.5 %collective-permute-start.18 = (bf16[2,4,128,768]{3,2,1,0:T(8,128)(2,1)}, bf16[2,4,128,768]{3,2,1,0:T(8,128)(2,1)}, u32[]{:S(2)}, u32[]{:S(2)}) collective-permute-start(bf16[2,4,128,768]{3,2,1,0:T(8,128)(2,1)} %pad_maximum_fusion.refs_0_), channel_id=1, source_target_pairs={{0,4},{4,0},{8,12},{12,8},{16,20},{20,16},{24,28},{28,24},{1,5},{5... | collective-permute-start | bytes 4718600 | tf_op jit(solution)/shard_map/ppermute | solution.py:946
  266.2 25.9 %collective-permute-start.19 = (bf16[2,4,128,768]{3,2,1,0:T(8,128)(2,1)}, bf16[2,4,128,768]{3,2,1,0:T(8,128)(2,1)}, u32[]{:S(2)}, u32[]{:S(2)}) collective-permute-start(bf16[2,4,128,768]{3,2,1,0:T(8,128)(2,1)} %collective-permute-done.17.refs_1_), channel_id=1, source_target_pairs={{0,4},{4,0},{8,12},{12,8},{16,20},{20,16},{24,28},{28,24},{1,5},{5... | collective-permute-start | bytes 4718600 | tf_op jit(solution)/shard_map/ppermute | solution.py:946
  270.9 29.6 %collective-permute-start.21 = (bf16[2,4,128,512]{3,2,1,0:T(8,128)(2,1)S(1)}, bf16[2,4,128,512]{3,2,1,0:T(8,128)(2,1)S(1)}, u32[]{:S(2)}, u32[]{:S(2)}) collective-permute-start(bf16[2,4,128,512]{3,2,1,0:T(8,128)(2,1)S(1)} %pad_maximum_fusion.3.refs_0_.refs_4_), channel_id=1, source_target_pairs={{0,16},{4,20},{8,24},{12,28},{16,0},{20,4},{24,8},{28,12},{1,17},{... | collective-permute-start | bytes 3145736 | tf_op jit(solution)/shard_map/ppermute | solution.py:946
  291.8 9.0 %collective-permute-start.10 = (bf16[2,4,128,512]{3,2,1,0:T(8,128)(2,1)S(1)}, bf16[2,4,128,512]{3,2,1,0:T(8,128)(2,1)}, u32[]{:S(2)}, u32[]{:S(2)}) collective-permute-start(bf16[2,4,128,512]{3,2,1,0:T(8,128)(2,1)S(1)} %pad_maximum_fusion.1.refs_4_.refs_0_), channel_id=1, source_target_pairs={{0,4},{4,0},{8,12},{12,8},{16,20},{20,16},{24,28},{28,24},{1,5},{5... | collective-permute-start | bytes 3145736 | tf_op jit(solution)/shard_map/ppermute | solution.py:946
  292.0 9.0 %collective-permute-start.11 = (bf16[2,4,128,512]{3,2,1,0:T(8,128)(2,1)}, bf16[2,4,128,512]{3,2,1,0:T(8,128)(2,1)}, u32[]{:S(2)}, u32[]{:S(2)}) collective-permute-start(bf16[2,4,128,512]{3,2,1,0:T(8,128)(2,1)} %collective-permute-done.9.refs_5_.refs_1_), channel_id=1, source_target_pairs={{0,4},{4,0},{8,12},{12,8},{16,20},{20,16},{24,28},{28,24},{1,5},{5... | collective-permute-start | bytes 3145736 | tf_op jit(solution)/shard_map/ppermute | solution.py:946
  300.2 32.4 %collective-permute-start.22 = (bf16[2,4,128,512]{3,2,1,0:T(8,128)(2,1)S(1)}, bf16[2,4,128,512]{3,2,1,0:T(8,128)(2,1)}, u32[]{:S(2)}, u32[]{:S(2)}) collective-permute-start(bf16[2,4,128,512]{3,2,1,0:T(8,128)(2,1)S(1)} %pad_maximum_fusion.3.refs_0_.refs_4_), channel_id=1, source_target_pairs={{0,4},{4,0},{8,12},{12,8},{16,20},{20,16},{24,28},{28,24},{1,5},{5... | collective-permute-start | bytes 3145736 | tf_op jit(solution)/shard_map/ppermute | solution.py:946
  300.5 32.2 %collective-permute-start.15 = (bf16[2,4,128,512]{3,2,1,0:T(8,128)(2,1)}, bf16[2,4,128,512]{3,2,1,0:T(8,128)(2,1)}, u32[]{:S(2)}, u32[]{:S(2)}) collective-permute-start(bf16[2,4,128,512]{3,2,1,0:T(8,128)(2,1)} %collective-permute-done.13.refs_5_), channel_id=1, source_target_pairs={{0,4},{4,0},{8,12},{12,8},{16,20},{20,16},{24,28},{28,24},{1,5},{5... | collective-permute-start | bytes 3145736 | tf_op jit(solution)/shard_map/ppermute | solution.py:946
  300.8 31.8 %collective-permute-start.23 = (bf16[2,4,128,512]{3,2,1,0:T(8,128)(2,1)S(1)}, bf16[2,4,128,512]{3,2,1,0:T(8,128)(2,1)}, u32[]{:S(2)}, u32[]{:S(2)}) collective-permute-start(bf16[2,4,128,512]{3,2,1,0:T(8,128)(2,1)S(1)} %collective-permute-done.21.refs_1_.refs_5_), channel_id=1, source_target_pairs={{0,4},{4,0},{8,12},{12,8},{16,20},{20,16},{24,28},{28,24},{1,5},{5... | collective-permute-start | bytes 3145736 | tf_op jit(solution)/shard_map/ppermute | solution.py:946
  332.2 32.1 %copy-start.29 = (f32[4,8,512]{2,1,0:T(8,128)S(1)}, f32[4,8,512]{2,1,0:T(8,128)}, u32[]{:S(2)}) copy-start(f32[4,8,512]{2,1,0:T(8,128)} %get-tuple-element.166) | copy-start | bytes 196612
  332.3 34.2 %collective-permute-start.24 = (bf16[4,4,128,1024]{3,2,1,0:T(8,128)(2,1)}, bf16[4,4,128,1024]{3,2,1,0:T(8,128)(2,1)}, u32[]{:S(2)}, u32[]{:S(2)}) collective-permute-start(bf16[4,4,128,1024]{3,2,1,0:T(8,128)(2,1)} %get-tuple-element.119), channel_id=1, source_target_pairs={{0,4},{4,0},{8,12},{12,8},{16,20},{20,16},{24,28},{28,24},{1,5},{5... | collective-permute-start | bytes 12582920 | tf_op jit(solution)/shard_map/ppermute | solution.py:946
  363.5 9.3 %collective-permute-start.29 = (bf16[4,4,128,1024]{3,2,1,0:T(8,128)(2,1)}, bf16[4,4,128,1024]{3,2,1,0:T(8,128)(2,1)}, u32[]{:S(2)}, u32[]{:S(2)}) collective-permute-start(bf16[4,4,128,1024]{3,2,1,0:T(8,128)(2,1)} %get-tuple-element.127), channel_id=1, source_target_pairs={{0,4},{4,0},{8,12},{12,8},{16,20},{20,16},{24,28},{28,24},{1,5},{5... | collective-permute-start | bytes 12582920 | tf_op jit(solution)/shard_map/ppermute | solution.py:946
  369.8 30.3 %collective-permute-start.25 = (bf16[2,4,128,512]{3,2,1,0:T(8,128)(2,1)}, bf16[2,4,128,512]{3,2,1,0:T(8,128)(2,1)S(1)}, u32[]{:S(2)}, u32[]{:S(2)}) collective-permute-start(bf16[2,4,128,512]{3,2,1,0:T(8,128)(2,1)} %get-tuple-element.122), channel_id=1, source_target_pairs={{0,16},{4,20},{8,24},{12,28},{16,0},{20,4},{24,8},{28,12},{1,17},{... | collective-permute-start | bytes 3145736 | tf_op jit(solution)/shard_map/ppermute | solution.py:946
  371.3 28.8 %collective-permute-start.26 = (bf16[2,4,128,512]{3,2,1,0:T(8,128)(2,1)}, bf16[2,4,128,512]{3,2,1,0:T(8,128)(2,1)S(1)}, u32[]{:S(2)}, u32[]{:S(2)}) collective-permute-start(bf16[2,4,128,512]{3,2,1,0:T(8,128)(2,1)} %get-tuple-element.123), channel_id=1, source_target_pairs={{0,8},{4,12},{8,0},{12,4},{16,24},{20,28},{24,16},{28,20},{1,9},{5... | collective-permute-start | bytes 3145736 | tf_op jit(solution)/shard_map/ppermute | solution.py:946
  376.1 42.3 %collective-permute-start.30 = (bf16[2,4,128,512]{3,2,1,0:T(8,128)(2,1)}, bf16[2,4,128,512]{3,2,1,0:T(8,128)(2,1)S(1)}, u32[]{:S(2)}, u32[]{:S(2)}) collective-permute-start(bf16[2,4,128,512]{3,2,1,0:T(8,128)(2,1)} %get-tuple-element.128), channel_id=1, source_target_pairs={{0,16},{4,20},{8,24},{12,28},{16,0},{20,4},{24,8},{28,12},{1,17},{... | collective-permute-start | bytes 3145736 | tf_op jit(solution)/shard_map/ppermute | solution.py:946
  376.6 43.5 %collective-permute-start.31 = (bf16[2,4,128,512]{3,2,1,0:T(8,128)(2,1)}, bf16[2,4,128,512]{3,2,1,0:T(8,128)(2,1)}, u32[]{:S(2)}, u32[]{:S(2)}) collective-permute-start(bf16[2,4,128,512]{3,2,1,0:T(8,128)(2,1)} %get-tuple-element.129), channel_id=1, source_target_pairs={{0,8},{4,12},{8,0},{12,4},{16,24},{20,28},{24,16},{28,20},{1,9},{5... | collective-permute-start | bytes 3145736 | tf_op jit(solution)/shard_map/ppermute | solution.py:946
  395.0 102.1 %all-to-all-start.5 = ((bf16[4,1088,256]{2,1,0:T(8,128)(2,1)}), bf16[4,1088,256]{2,1,0:T(8,128)(2,1)}, u32[]{:S(2)}, u32[]{:S(2)}) async-start(bf16[4,1088,256]{2,1,0:T(8,128)(2,1)} %block_rows.1), calls=%async_computation.5 | async-start | bytes 4456448 | tf_op jit(solution)/shard_map/all_to_all | solution.py:942
  405.1 41.0 %collective-permute-start.27 = (bf16[1,4,128,512]{3,2,1,0:T(8,128)(2,1)}, bf16[1,4,128,512]{3,2,1,0:T(8,128)(2,1)S(1)}, u32[]{:S(2)}, u32[]{:S(2)}) collective-permute-start(bf16[1,4,128,512]{3,2,1,0:T(8,128)(2,1)} %get-tuple-element.124), channel_id=1, source_target_pairs={{0,8},{4,12},{8,0},{12,4},{16,24},{20,28},{24,16},{28,20},{1,9},{5... | collective-permute-start | bytes 1572872 | tf_op jit(solution)/shard_map/ppermute | solution.py:946
  406.4 39.7 %collective-permute-start.28 = (bf16[1,4,128,512]{3,2,1,0:T(8,128)(2,1)}, bf16[1,4,128,512]{3,2,1,0:T(8,128)(2,1)S(1)}, u32[]{:S(2)}, u32[]{:S(2)}) collective-permute-start(bf16[1,4,128,512]{3,2,1,0:T(8,128)(2,1)} %get-tuple-element.125), channel_id=1, source_target_pairs={{0,16},{4,20},{8,24},{12,28},{16,0},{20,4},{24,8},{28,12},{1,17},{... | collective-permute-start | bytes 1572872 | tf_op jit(solution)/shard_map/ppermute | solution.py:946
  423.1 61.0 %collective-permute-start.32 = (bf16[1,4,128,512]{3,2,1,0:T(8,128)(2,1)}, bf16[1,4,128,512]{3,2,1,0:T(8,128)(2,1)S(1)}, u32[]{:S(2)}, u32[]{:S(2)}) collective-permute-start(bf16[1,4,128,512]{3,2,1,0:T(8,128)(2,1)} %get-tuple-element.130), channel_id=1, source_target_pairs={{0,8},{4,12},{8,0},{12,4},{16,24},{20,28},{24,16},{28,20},{1,9},{5... | collective-permute-start | bytes 1572872 | tf_op jit(solution)/shard_map/ppermute | solution.py:946
  424.6 59.6 %collective-permute-start.33 = (bf16[1,4,128,512]{3,2,1,0:T(8,128)(2,1)}, bf16[1,4,128,512]{3,2,1,0:T(8,128)(2,1)S(1)}, u32[]{:S(2)}, u32[]{:S(2)}) collective-permute-start(bf16[1,4,128,512]{3,2,1,0:T(8,128)(2,1)} %get-tuple-element.131), channel_id=1, source_target_pairs={{0,16},{4,20},{8,24},{12,28},{16,0},{20,4},{24,8},{28,12},{1,17},{... | collective-permute-start | bytes 1572872 | tf_op jit(solution)/shard_map/ppermute | solution.py:946
  455.7 20.6 %collective-permute-start.34 = (bf16[4,4,128,256]{3,2,1,0:T(8,128)(2,1)}, bf16[4,4,128,256]{3,2,1,0:T(8,128)(2,1)S(1)}, u32[]{:S(2)}, u32[]{:S(2)}) collective-permute-start(bf16[4,4,128,256]{3,2,1,0:T(8,128)(2,1)} %get-tuple-element.138), channel_id=1, source_target_pairs={{0,4},{4,0},{8,12},{12,8},{16,20},{20,16},{24,28},{28,24},{1,5},{5... | collective-permute-start | bytes 3145736 | tf_op jit(solution)/shard_map/ppermute | solution.py:946
  479.3 14.5 %collective-permute-start.35 = (bf16[2,4,128,256]{3,2,1,0:T(8,128)(2,1)}, bf16[2,4,128,256]{3,2,1,0:T(8,128)(2,1)S(1)}, u32[]{:S(2)}, u32[]{:S(2)}) collective-permute-start(bf16[2,4,128,256]{3,2,1,0:T(8,128)(2,1)} %add_rows.12), channel_id=1, source_target_pairs={{0,16},{4,20},{8,24},{12,28},{16,0},{20,4},{24,8},{28,12},{1,17},{... | collective-permute-start | bytes 1572872 | tf_op jit(solution)/shard_map/ppermute | solution.py:946
  496.5 52.2 %collective-permute-start.36 = (bf16[1,4,128,256]{3,2,1,0:T(8,128)(2,1)}, bf16[1,4,128,256]{3,2,1,0:T(8,128)(2,1)S(1)}, u32[]{:S(2)}, u32[]{:S(2)}) collective-permute-start(bf16[1,4,128,256]{3,2,1,0:T(8,128)(2,1)} %add_rows.13), channel_id=1, source_target_pairs={{0,8},{4,12},{8,0},{12,4},{16,24},{20,28},{24,16},{28,20},{1,9},{5... | collective-permute-start | bytes 786440 | tf_op jit(solution)/shard_map/ppermute | solution.py:946
  497.1 46.5 %all-to-all-start.6 = ((bf16[4,128,1024]{2,1,0:T(8,128)(2,1)}), bf16[4,128,1024]{2,1,0:T(8,128)(2,1)S(1)}, u32[]{:S(2)}, u32[]{:S(2)}) async-start(bf16[4,128,1024]{2,1,0:T(8,128)(2,1)} %add_cols.4), calls=%async_computation.6 | async-start | bytes 2097152 | tf_op jit(solution)/shard_map/all_to_all | solution.py:942
  543.6 30.4 %all-to-all-start.7 = ((bf16[4,128,1024]{2,1,0:T(8,128)(2,1)}), bf16[4,128,1024]{2,1,0:T(8,128)(2,1)S(1)}, u32[]{:S(2)}, u32[]{:S(2)}) async-start(bf16[4,128,1024]{2,1,0:T(8,128)(2,1)} %add_cols.5), calls=%async_computation.7 | async-start | bytes 2097152 | tf_op jit(solution)/shard_map/all_to_all | solution.py:942
  574.0 11.9 %all-to-all-start.8 = ((bf16[4,128,256]{2,1,0:T(8,128)(2,1)}), bf16[4,128,256]{2,1,0:T(8,128)(2,1)S(1)}, u32[]{:S(2)}, u32[]{:S(2)}) async-start(bf16[4,128,256]{2,1,0:T(8,128)(2,1)} %add_cols.6), calls=%async_computation.8 | async-start | bytes 524288 | tf_op jit(solution)/shard_map/all_to_all | solution.py:942
  585.9 34.0 %all-to-all-start.12 = ((f32[4,1,6016]{2,1,0:T(1,128)}), f32[4,1,6016]{2,1,0:T(1,128)S(1)}, u32[]{:S(2)}, u32[]{:S(2)}) async-start(f32[4,1,6016]{2,1,0:T(1,128)} %all_to_all.58), calls=%async_computation.12 | async-start | bytes 192512 | tf_op jit(solution)/shard_map/all_to_all | solution.py:942
  602.1 38.5 %collective-permute-start.40 = (bf16[4,4,128,768]{3,2,1,0:T(8,128)(2,1)}, bf16[4,4,128,768]{3,2,1,0:T(8,128)(2,1)S(1)}, u32[]{:S(2)}, u32[]{:S(2)}) collective-permute-start(bf16[4,4,128,768]{3,2,1,0:T(8,128)(2,1)} %get-tuple-element.156), channel_id=1, source_target_pairs={{0,4},{4,0},{8,12},{12,8},{16,20},{20,16},{24,28},{28,24},{1,5},{5... | collective-permute-start | bytes 9437192 | tf_op jit(solution)/shard_map/ppermute | solution.py:946
  620.0 10.7 %all-to-all-start.10 = ((f32[4,1,512]{2,1,0:T(1,128)}), f32[4,1,512]{2,1,0:T(1,128)S(1)}, u32[]{:S(2)}, u32[]{:S(2)}) async-start(f32[4,1,512]{2,1,0:T(1,128)} %copy.134), calls=%async_computation.10 | async-start | bytes 16384 | tf_op jit(solution)/shard_map/all_to_all | solution.py:942
  630.6 65.9 %all-to-all-start.9 = ((bf16[4,1088,256]{2,1,0:T(8,128)(2,1)}), bf16[4,1088,256]{2,1,0:T(8,128)(2,1)}, u32[]{:S(2)}, u32[]{:S(2)}) async-start(bf16[4,1088,256]{2,1,0:T(8,128)(2,1)} %get-tuple-element.153), calls=%async_computation.9 | async-start | bytes 4456448 | tf_op jit(solution)/shard_map/all_to_all | solution.py:942
  637.5 1.5 collective-permute-start.45
  639.1 7.8 %collective-permute-start.46 = (f32[6016]{0:T(1024)S(1)}, f32[6016]{0:T(1024)S(1)}, u32[]{:S(2)}, u32[]{:S(2)}) collective-permute-start(f32[6016]{0:T(1024)S(1)} %add.59), channel_id=1, source_target_pairs={{0,8},{4,12},{8,0},{12,4},{16,24},{20,28},{24,16},{28,20},{1,9},{5... | collective-permute-start | bytes 72200 | tf_op jit(solution)/shard_map/ppermute | solution.py:946
  645.1 24.3 %collective-permute-start.41 = (bf16[2,4,64,768]{3,2,1,0:T(8,128)(2,1)}, bf16[2,4,64,768]{3,2,1,0:T(8,128)(2,1)S(1)}, u32[]{:S(2)}, u32[]{:S(2)}) collective-permute-start(bf16[2,4,64,768]{3,2,1,0:T(8,128)(2,1)} %get-tuple-element.157), channel_id=1, source_target_pairs={{0,16},{4,20},{8,24},{12,28},{16,0},{20,4},{24,8},{28,12},{1,17},{... | collective-permute-start | bytes 2359304 | tf_op jit(solution)/shard_map/ppermute | solution.py:946
  646.3 23.1 %collective-permute-start.42 = (bf16[2,4,64,768]{3,2,1,0:T(8,128)(2,1)}, bf16[2,4,64,768]{3,2,1,0:T(8,128)(2,1)S(1)}, u32[]{:S(2)}, u32[]{:S(2)}) collective-permute-start(bf16[2,4,64,768]{3,2,1,0:T(8,128)(2,1)} %get-tuple-element.158), channel_id=1, source_target_pairs={{0,8},{4,12},{8,0},{12,4},{16,24},{20,28},{24,16},{28,20},{1,9},{5... | collective-permute-start | bytes 2359304 | tf_op jit(solution)/shard_map/ppermute | solution.py:946
  646.9 18.6 %collective-permute-start.47 = (f32[6016]{0:T(1024)S(1)}, f32[6016]{0:T(1024)S(1)}, u32[]{:S(2)}, u32[]{:S(2)}) collective-permute-start(f32[6016]{0:T(1024)S(1)} %add.60), channel_id=1, source_target_pairs={{0,16},{4,20},{8,24},{12,28},{16,0},{20,4},{24,8},{28,12},{1,17},{... | collective-permute-start | bytes 72200 | tf_op jit(solution)/shard_map/ppermute | solution.py:946
  666.2 2.6 collective-permute-start.37
  668.8 22.2 %collective-permute-start.38 = (f32[512]{0:T(512)S(1)}, f32[512]{0:T(512)S(1)}, u32[]{:S(2)}, u32[]{:S(2)}) collective-permute-start(f32[512]{0:T(512)S(1)} %add.50), channel_id=1, source_target_pairs={{0,8},{4,12},{8,0},{12,4},{16,24},{20,28},{24,16},{28,20},{1,9},{5... | collective-permute-start | bytes 6152 | tf_op jit(solution)/shard_map/ppermute | solution.py:946
  673.8 18.1 %collective-permute-start.43 = (bf16[1,4,64,768]{3,2,1,0:T(8,128)(2,1)}, bf16[1,4,64,768]{3,2,1,0:T(8,128)(2,1)S(1)}, u32[]{:S(2)}, u32[]{:S(2)}) collective-permute-start(bf16[1,4,64,768]{3,2,1,0:T(8,128)(2,1)} %get-tuple-element.159), channel_id=1, source_target_pairs={{0,8},{4,12},{8,0},{12,4},{16,24},{20,28},{24,16},{28,20},{1,9},{5... | collective-permute-start | bytes 1179656 | tf_op jit(solution)/shard_map/ppermute | solution.py:946
  675.3 16.6 %collective-permute-start.44 = (bf16[1,4,64,768]{3,2,1,0:T(8,128)(2,1)}, bf16[1,4,64,768]{3,2,1,0:T(8,128)(2,1)S(1)}, u32[]{:S(2)}, u32[]{:S(2)}) collective-permute-start(bf16[1,4,64,768]{3,2,1,0:T(8,128)(2,1)} %get-tuple-element.160), channel_id=1, source_target_pairs={{0,16},{4,20},{8,24},{12,28},{16,0},{20,4},{24,8},{28,12},{1,17},{... | collective-permute-start | bytes 1179656 | tf_op jit(solution)/shard_map/ppermute | solution.py:946
  691.0 11.3 %collective-permute-start.39 = (f32[512]{0:T(512)S(1)}, f32[512]{0:T(512)S(1)}, u32[]{:S(2)}, u32[]{:S(2)}) collective-permute-start(f32[512]{0:T(512)S(1)} %add.51), channel_id=1, source_target_pairs={{0,16},{4,20},{8,24},{12,28},{16,0},{20,4},{24,8},{28,12},{1,17},{... | collective-permute-start | bytes 6152 | tf_op jit(solution)/shard_map/ppermute | solution.py:946
  696.5 24.7 %all-to-all-start.11 = ((bf16[4,128,768]{2,1,0:T(8,128)(2,1)}), bf16[4,128,768]{2,1,0:T(8,128)(2,1)S(1)}, u32[]{:S(2)}, u32[]{:S(2)}) async-start(bf16[4,128,768]{2,1,0:T(8,128)(2,1)} %add_cols.7), calls=%async_computation.11 | async-start | bytes 1572864 | tf_op jit(solution)/shard_map/all_to_all | solution.py:942
  (46 other events, 539.2 us)

commit v3 on v2

--- a/solution.py
+++ b/solution.py
@@ -76,26 +76,88 @@
     return [own + [WINDOWS] * (per - len(own)) for own in sets], capacity
 
 
-def layout_info(sets, offsets, me, my_row):
-    ids = np.array(sets, np.int32)
-    win_row, win_col = ids // GRID, ids % GRID
-
-    def extent(place, shift):
-        low = jnp.maximum(0, shift - WIN * place)
-        high = jnp.minimum(WIN, SIDE + shift - WIN * place)
-        return low, jnp.maximum(high - low, 0)
-
-    row_low, height = extent(win_row, offsets[0])
-    col_low, width = extent(win_col, offsets[1])
-    size = height * width
-    earlier = np.tril(np.ones((ids.shape[1],) * 2, np.int32), -1)
-    base = jnp.sum(size[:, None, :] * earlier[None], axis=2)
-    kept_row = jnp.asarray(np.minimum(win_row, GRID - 1))
-    fields = [base, row_low, height, col_low, width, kept_row, jnp.asarray(win_col)]
-    own = jnp.arange(ids.shape[0], dtype=jnp.int32) == me
-    count = jnp.sum(jnp.where(own[:, None], size, 0))
-    head = jnp.concatenate([me[None], offsets, my_row[None], count[None]])
-    return jnp.concatenate([head, jnp.stack(fields, axis=-1).reshape(-1)])
+def plan_kernel(cols, per, ids, offsets, info):
+    top, left = offsets[0, 0], offsets[0, 1]
+    me = lax.axis_index("col").astype(jnp.int32)
+    info[0] = me
+    info[1] = top
+    info[2] = left
+    info[3] = lax.axis_index("row").astype(jnp.int32)
+
+    def each_set(d, carry):
+        def each_window(i, base):
+            at = d * per + i
+            win_row, win_col = ids[at] // GRID, ids[at] % GRID
+            row_low = jnp.maximum(0, top - WIN * win_row)
+            height = jnp.maximum(jnp.minimum(WIN, SIDE + top - WIN * win_row) - row_low, 0)
+            col_low = jnp.maximum(0, left - WIN * win_col)
+            width = jnp.maximum(jnp.minimum(WIN, SIDE + left - WIN * win_col) - col_low, 0)
+            first = HEAD + at * FIELDS
+            info[first] = base
+            info[first + 1] = row_low
+            info[first + 2] = height
+            info[first + 3] = col_low
+            info[first + 4] = width
+            info[first + 5] = jnp.minimum(win_row, GRID - 1)
+            info[first + 6] = win_col
+            return base + height * width
+
+        count = lax.fori_loop(0, per, each_window, jnp.int32(0))
+
+        @pl.when(d == me)
+        def _():
+            info[4] = count
+
+        return carry
+
+    lax.fori_loop(0, cols, each_set, jnp.int32(0))
+
+
+def plan(sets, offsets):
+    cols, per = len(sets), len(sets[0])
+    smem = pl.BlockSpec(memory_space=pltpu.SMEM)
+    return pl.pallas_call(
+        partial(plan_kernel, cols, per),
+        out_shape=jax.ShapeDtypeStruct((HEAD + cols * per * FIELDS,), jnp.int32),
+        in_specs=[smem, smem],
+        out_specs=smem,
+        cost_estimate=cost(2),
+        name="plan",
+    )(jnp.asarray(np.array(sets, np.int32).reshape(-1)), offsets)
+
+
+def pack_kernel(width, weight, *refs):
+    vectors, out = refs[:-1], refs[-1]
+    cols, _, n = out.shape
+    bw = weight.shape[0]
+    rows = []
+    held = jnp.concatenate([v[...].astype(F32) for v in vectors], axis=1)
+    count = held.shape[1] // n
+    lines = [held[:, r * n : (r + 1) * n] for r in range(count)]
+    for part in range(3):
+        for r in range(count):
+            low = lines[r].astype(BF)
+            rows.append(low.astype(F32))
+            lines[r] = lines[r] - low.astype(F32)
+    pad = -(3 * count) % 16
+    rows = rows + [jnp.zeros((pad, n), F32)] * (pad > 0)
+    extra = jnp.concatenate(rows, axis=0).astype(BF)
+    for d in range(cols):
+        out[d, :bw] = weight[...]
+        out[d, bw:] = extra
+
+
+def pack_first(weight, vectors, cols):
+    bw, n = weight.shape
+    total = sum(v.shape[0] for v in vectors)
+    lines = -(-(3 * total // n) // 16) * 16
+    return pl.pallas_call(
+        partial(pack_kernel, n),
+        out_shape=jax.ShapeDtypeStruct((cols, bw + lines, n), BF),
+        compiler_params=pltpu.CompilerParams(vmem_limit_bytes=VMEM_LIMIT),
+        cost_estimate=cost(2),
+        name="pack",
+    )(weight, *[v.reshape(1, -1) for v in vectors])
 
 
 def window_at(info, index):
@@ -162,44 +224,49 @@
     )(info, x)
 
 
-def collect_kernel(per, info, pieces, out, padded):
+def collect_kernel(places, per, info, pieces, out, padded):
     top, left = info[1], info[2]
-    cols, rows, _ = pieces.shape
-    padded[...] = jnp.zeros_like(padded)
+    _, rows, _ = pieces.shape
     token = iota((1, 256), 1)
     row, col = token // SIDE, token % SIDE
     line = iota((80, 256), 0)
-    for d in range(cols):
-
-        def step(i, carry):
-            field = window_at(info, d * per + i)
-            base, row_low, height, _, across, win_row, _ = field
-            for g in range(4):
+    for win_row in range(GRID):
+
+        def step(g, carry):
+            picks, slabs = [], []
+            for win_col in range(GRID):
+                d, i = places[win_row * GRID + win_col]
+                field = window_at(info, d * per + i)
+                base, row_low, height, _, across, _, _ = field
                 start = base + jnp.clip(4 * g - row_low, 0, height) * across
                 start = pl.multiple_of(jnp.minimum(start // 16 * 16, rows - 80), 16)
-                pick = as_pick(line == target_of(field, left, row + 4 * g, col) - start)
-                first = pl.multiple_of((WIN * win_row + 4 * g - top + MARGIN) * SIDE, SIDE)
-                padded[pl.ds(first, 256), :] += tn_dot(pick, pieces[d, pl.ds(start, 80), :])
+                picks.append(as_pick(line == target_of(field, left, row + 4 * g, col) - start))
+                slabs.append(pieces[d, pl.ds(start, 80), :])
+            found = tn_dot(jnp.concatenate(picks, axis=0), jnp.concatenate(slabs, axis=0))
+            first = pl.multiple_of((WIN * win_row + 4 * g - top + MARGIN) * SIDE, SIDE)
+            padded[pl.ds(first, 256), :] = found.astype(BF)
             return carry
 
-        lax.fori_loop(0, per, step, 0)
+        lax.fori_loop(0, 4, step, 0)
     out[...] = padded[MARGIN * SIDE : (MARGIN + SIDE) * SIDE, :].astype(out.dtype)
 
 
-def collect(pieces, info, per, dtype):
+def collect(pieces, sets, info, dtype):
     cols, rows, width = pieces.shape
+    per = len(sets[0])
+    places = {w: (d, i) for d, own in enumerate(sets) for i, w in enumerate(own)}
     return pl.pallas_call(
-        partial(collect_kernel, per),
+        partial(collect_kernel, places, per),
         out_shape=jax.ShapeDtypeStruct((PIX, width), dtype),
         grid_spec=pltpu.PrefetchScalarGridSpec(
             num_scalar_prefetch=1,
             grid=(1,),
             in_specs=[pl.BlockSpec((cols, rows, width), lambda i, s: (0, 0, 0))],
             out_specs=pl.BlockSpec((PIX, width), lambda i, s: (0, 0)),
-            scratch_shapes=[pltpu.VMEM((PADROWS * SIDE, width), F32)],
+            scratch_shapes=[pltpu.VMEM((PADROWS * SIDE, width), BF)],
         ),
         compiler_params=params(),
-        cost_estimate=cost(9),
+        cost_estimate=cost(8),
         name="collect",
     )(info, pieces)
 
@@ -385,14 +452,8 @@
 
 
 def gelu_and_slope(v):
-    t = 1.0 / (1.0 + 0.23164189 * jnp.abs(v))
-    poly = t * (
-        0.127414796
-        + t * (-0.142248368 + t * (0.7107068705 + t * (-0.7265760135 + t * 0.5307027145)))
-    )
-    bell = jnp.exp(-0.5 * v * v)
-    half = poly * bell
-    below = jnp.where(v >= 0, 1.0 - half, half)
+    below = 0.5 + 0.5 * lax.erf(v * 0.7071067811865476)
+    bell = jnp.exp(v * v * -0.5)
     return v * below, below + v * bell * 0.3989422804014327
 
 
@@ -708,11 +769,12 @@
 
     @pl.when(first)
     def _():
-        for head in range(2):
+        for head in range(2 * (width // 128)):
             keys[head, :, :128] = jnp.zeros((KEYS, 128), BF)
-            keys[head, :, 128:] = onehot[head]
-        vals[:, :128] = jnp.zeros((KEYS, 128), BF)
-        vals[:, 128:] = jnp.ones((KEYS, 128), BF)
+            keys[head, :, 128:] = onehot[head % 2]
+        for pair in range(width // 128):
+            vals[pair, :, :128] = jnp.zeros((KEYS, 128), BF)
+            vals[pair, :, 128:] = jnp.ones((KEYS, 128), BF)
 
     @pl.when(window == 0)
     def _():
@@ -725,31 +787,35 @@
     lane = iota((SLOT, 128), 1)
     low = lane < HD
     inner = lane % 32
-    parts = []
-    for pair in range(width // 128):
+    pairs = width // 128
+    queries = []
+    for pair in range(pairs):
         at = pair * 128
         q2 = slots[:, at : at + 128]
         k2 = slots[:, width + at : width + at + 128]
-        v2 = slots[:, 2 * width + at : 2 * width + at + 128]
+        vals[pair, :SLOT, :128] = slots[:, 2 * width + at : 2 * width + at + 128]
+        zero = jnp.zeros_like(k2)
+        keys[2 * pair, :SLOT, :128] = jnp.where(low, k2, zero)
+        keys[2 * pair + 1, :SLOT, :128] = jnp.where(low, zero, k2)
         rel = shift_left(nn_dot(q2, tables[...]), shifts[...])
         rel_hi = rel.astype(BF).astype(F32)
         rel_lo = pltpu.roll(rel - rel_hi, WIN, 1)
         rel = jnp.where(inner < WIN, rel_hi, jnp.where(inner < 2 * WIN, rel_lo, 1.0))
-        queries = jnp.concatenate([q2 * BF(0.125), rel.astype(BF)], axis=1)
-        vals[:SLOT, :128] = v2
-        zero = jnp.zeros_like(k2)
-        keys[0, :SLOT, :128] = jnp.where(low, k2, zero)
-        keys[1, :SLOT, :128] = jnp.where(low, zero, k2)
-        outs = []
-        for head in range(2):
-            scores = nt_dot(queries, keys[head])
-            peak = jnp.max(scores, axis=1, keepdims=True)
-            weights = jnp.exp(scores - peak).astype(BF)
-            exps[pair * 2 + head] = weights
-            outs.append(nn_dot(weights, vals[...]))
-        scale = 1.0 / jnp.where(low, outs[0][:, 128:], outs[1][:, 128:])
+        queries.append(jnp.concatenate([q2 * BF(0.125), rel.astype(BF)], axis=1))
+    scores = [nt_dot(queries[head // 2], keys[head]) for head in range(2 * pairs)]
+    weights = []
+    for head in range(2 * pairs):
+        peak = jnp.max(scores[head], axis=1, keepdims=True)
+        weights.append(jnp.exp(scores[head] - peak).astype(BF))
+        exps[head] = weights[head]
+    outs = [nn_dot(weights[head], vals[head // 2]) for head in range(2 * pairs)]
+    parts = []
+    for pair in range(pairs):
+        at = pair * 128
+        first, second = outs[2 * pair], outs[2 * pair + 1]
+        scale = 1.0 / jnp.where(low, first[:, 128:], second[:, 128:])
         inv[:, at : at + 128] = scale
-        parts.append((jnp.where(low, outs[0][:, :128], outs[1][:, :128]) * scale).astype(BF))
+        parts.append((jnp.where(low, first[:, :128], second[:, :128]) * scale).astype(BF))
     pack = pack_of(field, start)
     total[pl.ds(start, SLAB), :] += nn_dot(pack, jnp.concatenate(parts, axis=1))
 
@@ -786,8 +852,8 @@
                 pl.BlockSpec((SLOT, width), lambda c, w, s: (w, c + base)),
             ],
             scratch_shapes=[
-                pltpu.VMEM((2, KEYS, 256), BF),
-                pltpu.VMEM((KEYS, 256), BF),
+                pltpu.VMEM((2 * pairs, KEYS, 256), BF),
+                pltpu.VMEM((pairs, KEYS, 256), BF),
                 pltpu.VMEM((SLOT, 3 * width), BF),
                 pltpu.VMEM((rows, width), F32),
             ],
@@ -808,9 +874,9 @@
 
     @pl.when(first)
     def _():
-        for head in range(2):
+        for head in range(2 * (width // 128)):
             keys[head, :, :128] = jnp.zeros((KEYS, 128), BF)
-            keys[head, :, 128:] = onehot[head]
+            keys[head, :, 128:] = onehot[head % 2]
         vals[...] = jnp.zeros_like(vals)
         table_sum[...] = jnp.zeros_like(table_sum)
 
@@ -829,35 +895,45 @@
     lane = iota((SLOT, 128), 1)
     low = lane < HD
     inner = lane % 32
-    for pair in range(width // 128):
+    pairs = width // 128
+    q_all, grads, dots = [], [], []
+    for pair in range(pairs):
         at = pair * 128
         q2 = slots[:, at : at + 128]
         k2 = slots[:, width + at : width + at + 128]
         v2 = slots[:, 2 * width + at : 2 * width + at + 128]
         zero = jnp.zeros_like(k2)
-        keys[0, :SLOT, :128] = jnp.where(low, k2, zero)
-        keys[1, :SLOT, :128] = jnp.where(low, zero, k2)
-        vals[0, :SLOT, :] = jnp.where(low, v2, zero)
-        vals[1, :SLOT, :] = jnp.where(low, zero, v2)
+        keys[2 * pair, :SLOT, :128] = jnp.where(low, k2, zero)
+        keys[2 * pair + 1, :SLOT, :128] = jnp.where(low, zero, k2)
+        vals[2 * pair, :SLOT, :] = jnp.where(low, v2, zero)
+        vals[2 * pair + 1, :SLOT, :] = jnp.where(low, zero, v2)
         grad = (grad_slots[:, at : at + 128] * inv[:, at : at + 128]).astype(BF)
         cross = grad.astype(F32) * att_slots[:, at : at + 128]
-        dots = (
-            jnp.sum(jnp.where(low, cross, 0.0), axis=1, keepdims=True),
-            jnp.sum(jnp.where(low, 0.0, cross), axis=1, keepdims=True),
-        )
+        dots.append(jnp.sum(jnp.where(low, cross, 0.0), axis=1, keepdims=True))
+        dots.append(jnp.sum(jnp.where(low, 0.0, cross), axis=1, keepdims=True))
+        q_all.append(q2)
+        grads.append(grad)
+    probs_grads = [nt_dot(grads[head // 2], vals[head]) for head in range(2 * pairs)]
+    scores_grads = []
+    for head in range(2 * pairs):
+        weights = exps[head].astype(F32)
+        scores_grads.append((weights * (probs_grads[head] - dots[head])).astype(BF))
+    for pair in range(pairs):
+        at = pair * 128
+        q2, grad = q_all[pair], grads[pair]
+        zero = jnp.zeros_like(grad)
         q_scaled = q2 * BF(0.125)
         grad_heads = (jnp.where(low, grad, zero), jnp.where(low, zero, grad))
         q_heads = (jnp.where(low, q_scaled, zero), jnp.where(low, zero, q_scaled))
-        q_sum = jnp.zeros((SLOT, 256), F32)
-        k_sum = jnp.zeros((KEYS, 128), F32)
-        v_sum = jnp.zeros((KEYS, 128), F32)
+        q_sum, k_sum, v_sum = None, None, None
         for head in range(2):
-            weights = exps[pair * 2 + head]
-            probs_grad = nt_dot(grad, vals[head])
-            scores_grad = (weights.astype(F32) * (probs_grad - dots[head])).astype(BF)
-            q_sum = q_sum + nn_dot(scores_grad, keys[head])
-            k_sum = k_sum + tn_dot(scores_grad, q_heads[head])
-            v_sum = v_sum + tn_dot(weights, grad_heads[head])
+            which = 2 * pair + head
+            q_part = nn_dot(scores_grads[which], keys[which])
+            k_part = tn_dot(scores_grads[which], q_heads[head])
+            v_part = tn_dot(exps[which], grad_heads[head])
+            q_sum = q_part if q_sum is None else q_sum + q_part
+            k_sum = k_part if k_sum is None else k_sum + k_part
+            v_sum = v_part if v_sum is None else v_sum + v_part
         rel = shift_right(jnp.where(inner < WIN, q_sum[:, 128:], 0.0), shifts[...])
         rel_hi = rel.astype(BF)
         rel_lo = (rel - rel_hi.astype(F32)).astype(BF)
@@ -915,8 +991,8 @@
                 pl.BlockSpec((8, 3 * width), lambda c, w, s: (0, c)),
             ],
             scratch_shapes=[
-                pltpu.VMEM((2, KEYS, 256), BF),
-                pltpu.VMEM((2, KEYS, 128), BF),
+                pltpu.VMEM((2 * pairs, KEYS, 256), BF),
+                pltpu.VMEM((2 * pairs, KEYS, 128), BF),
                 pltpu.VMEM((SLOT, 3 * width), BF),
                 pltpu.VMEM((SLOT, width), F32),
                 pltpu.VMEM((SLOT, width), F32),
@@ -959,12 +1035,27 @@
     order = order[::-1] if flip else order
     held = stack[None]
     for bit in order[:-1]:
-        held = jnp.concatenate([held, row_swap(held, bit, nr)], axis=0)
-        yield [held]
-    bufs = [held, row_swap(held, order[-1], nr)]
-    yield bufs
+        fresh = row_swap(held, bit, nr)
+        gate = yield [fresh]
+        held = jnp.concatenate([held, after(fresh, *(gate or ()))], axis=0)
+    fresh = row_swap(held, order[-1], nr)
+    gate = yield [held, fresh]
+    bufs = [held, after(fresh, *(gate or ()))]
     bufs = bufs + [row_swap(buf, 1, nr) for buf in bufs]
     yield bufs
+
+
+class Hops(list):
+    def __init__(self, arrived, sent):
+        super().__init__(arrived)
+        self.sent = sent
+
+
+def last_terms(stages):
+    found = stages.send(None)
+    while isinstance(found, Hops):
+        found = stages.send(None)
+    return found
 
 
 def place_of(step, free, fixed, weights):
@@ -985,7 +1076,7 @@
         at += count
 
 
-def split_kernel(counts, axis, *refs):
+def split_kernel(counts, axis, lane, *refs):
     out = refs[sum(counts)]
     for k in range(out.shape[0]):
         at = 0
@@ -994,17 +1085,15 @@
             for ref in refs[at + 1 : at + count]:
                 total = total + ref[0, k].astype(F32)
             at += count
-            size = total.shape[axis]
-            where = slice(h * size, (h + 1) * size)
-            if axis == -1:
-                out[k, :, where] = total.astype(out.dtype)
-            else:
-                out[k, where, :] = total.astype(out.dtype)
+            high, wide = total.shape
+            row = h * high if axis == -2 else 0
+            col = lane + (h * wide if axis == -1 else 0)
+            out[k, row : row + high, col : col + wide] = total.astype(out.dtype)
 
 
 def reduce_weight(keep, send, axis, cols, nr):
     arrived = row_swap(send, 1, nr)
-    yield [arrived]
+    gate = yield [arrived]
     bits = outer_bits(nr)
     _, _, bw, n = keep.shape
     shape = [bw, n]
@@ -1039,6 +1128,7 @@
                 specs.append(spec(term, h, left[h], [bit]))
                 arrays.append(term[0])
         count = 1 << len(left[0])
+        arrays[0] = after(arrays[0], *(gate or ()))
         out_spec = pl.BlockSpec(block, lambda i: (i, 0, 0, 0))
         outs = pl.pallas_call(
             partial(add_kernel, sizes),
@@ -1053,40 +1143,76 @@
         fresh = [row_swap(out, bit, nr) for out, bit in zip(outs, taken)]
         for h in range(halves):
             terms[h].append((fresh[h], list(left[h]), False))
-        yield fresh
+        gate = yield Hops(fresh, outs)
 
     sizes = [len(t) for t in terms]
     specs = [spec(term, h, [], []) for h in range(halves) for term in terms[h]]
     arrays = [term[0] for h in range(halves) for term in terms[h]]
+    yield sizes, axis, specs, arrays, (cols, bw, n)
+
+
+def add_cols_kernel(groups, *refs):
+    outs = refs[-1]
+    at, lane = 0, 0
+    for sizes, axis, n in groups:
+        count = sum(sizes)
+        split_kernel(sizes, axis, lane, *refs[at : at + count], outs)
+        at += count
+        lane += n
+
+
+def finish_weights(parts, *gate):
+    cols, bw, _ = parts[0][4]
+    groups = [(sizes, axis, shape[2]) for sizes, axis, _, _, shape in parts]
+    wide = sum(n for _, _, n in groups)
+    arrays = [array for part in parts for array in part[3]]
+    arrays[0] = after(arrays[0], *gate)
     outs = pl.pallas_call(
-        partial(split_kernel, sizes, -1 if axis is None else axis),
-        out_shape=jax.ShapeDtypeStruct((cols, bw, n), BF),
+        partial(add_cols_kernel, groups),
+        out_shape=jax.ShapeDtypeStruct((cols, bw, wide), BF),
         grid=(1,),
-        in_specs=specs,
-        out_specs=pl.BlockSpec((cols, bw, n), lambda i: (0, 0, 0)),
+        in_specs=[sp for part in parts for sp in part[2]],
+        out_specs=pl.BlockSpec((cols, bw, wide), lambda i: (0, 0, 0)),
         compiler_params=params(),
         cost_estimate=cost(3),
         name="add_cols",
     )(*arrays)
-    yield [outs]
-    arrived = col_exchange(outs)
-    yield [arrived]
-    yield jnp.sum(arrived.astype(F32), axis=0)
-
-
-def reduce_small(by_place, whole, cols, nr):
+    return outs, col_exchange(outs)
+
+
+def last_sum(arrived, sizes, *gate):
+    total = jnp.sum(after(arrived, *gate).astype(F32), axis=0)
+    found, lane = [], 0
+    for n in sizes:
+        found.append(total[:, lane : lane + n])
+        lane += n
+    return found
+
+
+def sum_cols(by_place, whole, me, cols):
     size = by_place.shape[1]
     if whole is not None:
         whole = jnp.broadcast_to(whole, (cols,) + whole.shape)
         by_place = jnp.concatenate([by_place, whole], axis=1)
-    arrived = col_exchange(by_place)
-    yield arrived
-    total = jnp.sum(arrived, axis=0)
+    arrived = [lax.dynamic_index_in_dim(by_place, me, 0, keepdims=False)]
+    for k in range(1, cols):
+        sent = lax.dynamic_index_in_dim(by_place, me ^ k, 0, keepdims=False)
+        arrived.append(lax.ppermute(sent, "col", [(i, i ^ k) for i in range(cols)]))
+    gate = yield arrived[1:]
+    arrived = list(lax.optimization_barrier((*arrived, *(gate or ())))[:cols])
+    if whole is None:
+        yield sum(arrived[1:], arrived[0])
+    order = me ^ jnp.arange(cols, dtype=jnp.int32)
+    total = jnp.sum(pick_rows(jnp.stack(arrived), order), axis=0)
+    yield total[:size], total[size:]
+
+
+def sum_rows(total, nr):
     bit = 1
     while bit < nr:
         total = total + row_swap(total, bit, nr)
         bit *= 2
-    yield total[:size], total[size:]
+    return total
 
 
 def pick_rows(values, order):
@@ -1122,42 +1248,37 @@
     me = lax.axis_index("col").astype(jnp.int32)
     my_row = lax.axis_index("row").astype(jnp.int32)
     sets, rows = window_sets(cols, per)
-    info = layout_info(sets, pad_offsets[0], me, my_row)
+    info = plan(sets, pad_offsets)
     row_order = my_row ^ jnp.arange(nr, dtype=jnp.int32)
 
-    vec = jnp.concatenate(
-        [
-            norm1_gain,
-            norm1_bias,
-            norm2_gain,
-            norm2_bias,
-            proj_bias.astype(F32),
-            fc2_bias.astype(F32),
-            qv_bias[0].astype(F32),
-            qv_bias[1].astype(F32),
-            fc1_bias.astype(F32),
-        ]
-    )
+    vectors = [
+        norm1_gain,
+        norm1_bias,
+        norm2_gain,
+        norm2_bias,
+        proj_bias,
+        fc2_bias,
+        qv_bias[0],
+        qv_bias[1],
+        fc1_bias,
+    ]
     hidden = fc1_weight.shape[1]
     half = hidden // 2
     fc2_t = fc2_weight.T
-    size = vec.shape[0]
-    high = lax.reduce_precision(vec, 8, 7)
-    mid = lax.reduce_precision(vec - high, 8, 7)
-    low = vec - high - mid
-    vec_rows = jnp.stack([high, mid, low]).astype(BF).reshape(-1, 3 * width)
-    qkv_shard = jnp.concatenate([qkv_weight.reshape(bw, 3 * width), vec_rows], axis=0)
+    size = 8 * width + hidden
+    qkv_stack = col_exchange(pack_first(qkv_weight.reshape(bw, 3 * width), vectors, cols))
     x_sent = spread(tokens_in, info, cols, per, rows)
-    qkv_stack = gather_cols(qkv_shard, cols)
     x_pieces = col_exchange(x_sent)
-    vecs = jnp.sum(qkv_stack[:, bw:].astype(F32).reshape(cols, 3, size), axis=1)
+    lines = 3 * size // (3 * width)
+    vecs = qkv_stack[:, bw : bw + lines].astype(F32)
+    vecs = jnp.sum(vecs.reshape(cols, 3, size), axis=1)
     qkv_a = list(gather_rows(qkv_stack[:, : bw // 2], nr, False))[-1]
     qkv_b = list(gather_rows(qkv_stack[:, bw // 2 : bw], nr, True))[-1]
     wide0 = jnp.concatenate([fc1_weight[:, :half], proj_weight.T, fc2_t[:, :half]], axis=1)
     wide1 = jnp.concatenate([fc1_weight[:, half:], fc2_t[:, half:]], axis=1)
     stack0 = gather_cols(after(wide0, x_pieces, *qkv_a, *qkv_b), cols)
     first = half + width
-    hops0 = [gather_rows(stack0[:, :, :first], nr, False), gather_rows(stack0[:, :, first:], nr, True)]
+    g_sent = spread(after(out_grad, x_sent), info, cols, per, rows)
 
     features = vecs[:, : 6 * width].reshape(cols, 6, width // bw, bw)
     features = features.transpose(0, 2, 1, 3).reshape(nr, 6, bw)
@@ -1169,15 +1290,19 @@
     bias_h = vecs[:, 8 * width :]
 
     x_full, n1, qkv = norm_qkv(
-        x_pieces, qkv_a, qkv_b, info, gain1, bias1, bias_qkv, cols, rows, nr
+        after(x_pieces, g_sent), qkv_a, qkv_b, info, gain1, bias1, bias_qkv, cols, rows, nr
     )
     shifts_np, onehot_np = rel_constants()
     shifts = jnp.asarray(shifts_np)
     onehot = jnp.asarray(onehot_np, BF)
     tables = table_matrix(table_height, table_width)
-    g_pieces = col_exchange(spread(after(out_grad, n1), info, cols, per, rows))
+    stack0 = after(stack0, n1)
+    hops0 = [gather_rows(stack0[:, :, :first], nr, False), gather_rows(stack0[:, :, first:], nr, True)]
+    stack1 = gather_cols(after(wide1, stack0), cols)
+    bufs0 = [next(hop) for hop in hops0]
     held = ()
-    arrived = []
+    arrived = [stack0]
+    bits = outer_bits(nr)
     for part, base in enumerate(range(0, cols, cols // SPLITS)):
         held = attend(
             after(qkv, *arrived),
@@ -1191,34 +1316,38 @@
             cols,
             per,
         )
+        att = held[0]
+        arrived = []
         if part == 0:
-            arrived = [stack0]
-            stack1 = gather_cols(after(wide1, held[0]), cols)
+            stack1 = after(stack1, att)
+            g_pieces = col_exchange(after(g_sent, stack1))
+            bufs0 = [hop.send((att, *bufs0[0], *bufs0[1])) for hop in hops0]
+            arrived = [stack1]
+        if part == 2:
+            for _ in range(len(bits) - 2):
+                bufs0 = [hop.send(None) for hop in hops0]
+            bufs0 = [hop.send((att, *bufs0[0], *bufs0[1])) for hop in hops0]
+            stack1 = after(stack1, att)
             hops1 = [
                 gather_rows(stack1[:, :, :half], nr, False),
                 gather_rows(stack1[:, :, half:], nr, True),
             ]
-        if part == 1:
-            bufs0 = [next(hop) for hop in hops0]
-            arrived = bufs0[0] + bufs0[1]
-        if part == 2:
-            bufs0 = [next(hop) for hop in hops0]
-            arrived = bufs0[0] + bufs0[1] + [stack1]
+            bufs1 = [next(hop) for hop in hops1]
+        if part == 3:
+            bufs1 = [hop.send((att, *bufs1[0], *bufs1[1])) for hop in hops1]
     att, exps, inv = held
-    bufs0 = [list(hop)[-1] for hop in hops0]
-    bufs1 = [next(hop) for hop in hops1]
-    resid, n2 = proj_norm(
-        bufs0[0], after(att, *bufs1[0], *bufs1[1]), x_full, bias_p, gain2, bias2, cols, rows, nr
-    )
+    resid, n2 = proj_norm(bufs0[0], att, x_full, bias_p, gain2, bias2, cols, rows, nr)
     g_full = join(g_pieces, info, cols, rows, nr)
-    bufs1 = [next(hop) for hop in hops1]
-    n2 = after(n2, *bufs1[0], *bufs1[1])
-    bufs1 = [list(hop)[-1] for hop in hops1]
-    fc1_bufs = [bufs0[0], bufs1[0]]
-    fc2_bufs = [bufs0[1], bufs1[1]]
+    fc1_bufs, fc2_bufs = [bufs0[0]], [bufs0[1]]
 
     acts, grads, sends, hidden_sums = [], [], [], []
     for c in range(2):
+        if c == 1:
+            for _ in range(len(bits) - 2):
+                bufs1 = [hop.send(None) for hop in hops1]
+            bufs1 = [hop.send((acts[0], *bufs1[0], *bufs1[1])) for hop in hops1]
+            fc1_bufs.append(bufs1[0])
+            fc2_bufs.append(bufs1[1])
         act, grad, keep, send, bias_sum = mlp_grads(
             fc1_bufs[c],
             fc2_bufs[c],
@@ -1233,32 +1362,54 @@
         grads.append(grad)
         hidden_sums.append(jnp.sum(bias_sum, axis=1))
         sends.append(reduce_weight(keep, send, -1, cols, nr))
+    core0, core1 = [next(send) for send in sends]
+    rows0 = sends[0].send((*core0, acts[1]))
     block_sent = block_rows(
-        fc2_bufs, acts, after(resid, *next(sends[0])), bias_2, info, cols, rows, nr
+        fc2_bufs, acts, after(resid, *core1), bias_2, info, cols, rows, nr
     )
     block_pieces = col_exchange(block_sent)
+    rows0 = sends[0].send((*rows0, block_sent))
+    rows1 = sends[1].send((block_sent,))
     resid_grad, proj_grad, sums2 = mlp_back(
         fc1_bufs,
         grads,
-        after(resid, block_sent, *next(sends[0]), *next(sends[1])),
+        after(resid, block_sent),
         g_full,
         gain2,
         cols,
         rows,
         nr,
     )
-    proj_grad = after(proj_grad, *next(sends[0]), *next(sends[1]))
-    att_grad, keep, send = proj_back(fc1_bufs[0], proj_grad, att, cols, rows, nr)
+    rows1 = sends[1].send((*rows1, proj_grad))
+    att_grad, keep, send = proj_back(
+        fc1_bufs[0], after(proj_grad, *rows0), att, cols, rows, nr
+    )
     sends.append(reduce_weight(keep, send, None, cols, nr))
+    core2 = next(sends[2])
+    ratio = width // bw
+    places = jnp.arange(cols * ratio, dtype=jnp.int32) ^ my_row
+
+    def by_col(sums):
+        count = sums.shape[0]
+        blocks = jnp.sum(sums, axis=1).reshape(count, nr, bw).transpose(1, 0, 2)
+        picked = pick_rows(blocks, places).reshape(cols, ratio, count, bw)
+        return picked.transpose(0, 2, 1, 3).reshape(cols, count * width)
+
     held, table_sums, bias_sums = (), [], []
     for part, base in enumerate(range(0, cols, cols // SPLITS)):
         arrived = []
         if part == 1:
-            arrived = [block_pieces, *next(sends[1]), *next(sends[2])]
+            done0, arrived0 = finish_weights([last_terms(sends[0])], dqkv, block_pieces)
+            rows2 = sends[2].send((*core2, dqkv))
+            arrived = [block_pieces, *rows1, done0]
         if part == 2:
-            arrived = [*next(sends[0]), *next(sends[2])]
+            rows2 = sends[2].send((*rows2, dqkv))
         if part == 3:
-            arrived = [*next(sends[0]), *next(sends[1]), *next(sends[2])]
+            arrived = [arrived0]
+            done1, arrived1 = finish_weights(
+                [last_terms(sends[1]), last_terms(sends[2])], dqkv, arrived0, *rows2
+            )
+            arrived = [arrived0, done1]
         dqkv, table_sum, bias_sum = attend_back(
             after(qkv, *arrived),
             info,
@@ -1280,32 +1431,24 @@
         bias_sums.append(bias_sum)
     table_sum = sum(table_sums[1:], table_sums[0])
     bias_sum = jnp.concatenate(bias_sums, axis=1)
-    n1_back = after(n1, *next(sends[1]), *next(sends[2]), *next(sends[2]))
-    keep, send = qkv_grad(n1_back, dqkv, cols, rows, nr)
-    sends.append(reduce_weight(keep, send, -2, cols, nr))
-    fc_grads = [list(sends[c])[-1] for c in range(2)]
-    proj_w_grad = list(sends[2])[-1]
-    qkv_w_grad = list(sends[3])[-1]
-    ratio = width // bw
-    places = jnp.arange(cols * ratio, dtype=jnp.int32) ^ my_row
-
-    def by_col(sums):
-        count = sums.shape[0]
-        blocks = jnp.sum(sums, axis=1).reshape(count, nr, bw).transpose(1, 0, 2)
-        picked = pick_rows(blocks, places).reshape(cols, ratio, count, bw)
-        return picked.transpose(0, 2, 1, 3).reshape(cols, count * width)
-
     bias_cols = jnp.sum(bias_sum, axis=0).reshape(cols, 3, width)
-    small = jnp.concatenate([by_col(sums2), bias_cols[:, 0], bias_cols[:, 2]] + hidden_sums, axis=1)
     table_h_grad, table_w_grad = split_table(table_sum)
     table_flat = jnp.concatenate([table_h_grad.reshape(-1), table_w_grad.reshape(-1)])
-    early = reduce_small(small, table_flat, cols, nr)
-    early_arrived = next(early)
-
+    small = jnp.concatenate(
+        [by_col(sums2), bias_cols[:, 0], bias_cols[:, 2]] + hidden_sums, axis=1
+    )
+    early = sum_cols(small, table_flat, me, cols)
+    next(early)
+    keep, send = qkv_grad(after(n1, dqkv), dqkv, cols, rows, nr)
+    sends.append(reduce_weight(keep, send, -2, cols, nr))
+    core3 = next(sends[3])
+    block_out = collect(after(block_pieces, keep), sets, info, BF)
+    rows3 = sends[3].send((*core3, block_out))
+    small, table_flat = early.send((block_out,))
     in_sent, in_sums = input_back(
         qkv_a,
         qkv_b,
-        after(dqkv, keep, early_arrived),
+        after(dqkv, block_out, arrived1, small, *rows3.sent),
         x_full,
         resid_grad,
         gain1,
@@ -1314,14 +1457,24 @@
         rows,
         nr,
     )
-    late = reduce_small(by_col(in_sums), None, cols, nr)
+    late = sum_cols(by_col(in_sums), None, me, cols)
     late_arrived = next(late)
-    in_pieces = col_exchange(after(in_sent, late_arrived))
-    block_out = collect(after(block_pieces, in_sent), info, per, BF)
-    input_grad = collect(in_pieces, info, per, F32)
-    small, table_flat = list(early)[-1]
-    late, _ = list(late)[-1]
-    table_flat = table_flat.reshape(2, 27, HD)
+    in_pieces = col_exchange(after(in_sent, *late_arrived))
+    rows3 = sends[3].send((in_sent,))
+    for _ in range(len(outer_bits(nr)) - 2):
+        rows3 = sends[3].send(None)
+    sizes = [2 * width, small.shape[0], table_flat.shape[0]]
+    total = sum_rows(
+        jnp.concatenate([late.send(None), small, after(table_flat, *rows3.sent)]), nr
+    )
+    done3, arrived3 = finish_weights([sends[3].send(None)], in_pieces, total)
+    late, small = total[: sizes[0]], total[sizes[0] : sizes[0] + sizes[1]]
+    table_flat = total[sizes[0] + sizes[1] :].reshape(2, 27, HD)
+    input_grad = collect(after(in_pieces, done3), sets, info, F32)
+    (qkv_w_grad,) = last_sum(arrived3, [3 * width])
+    fc_grads = last_sum(arrived0, [2 * half], done3)
+    fc_grad, proj_w_grad = last_sum(arrived1, [2 * half, width], done3)
+    fc_grads.append(fc_grad)
 
     def part(i):
         return small[i * width : (i + 1) * width]

time: 733 us -> 635 us (0.87)
  Pallas kernels: 414 us -> 367 us
  waiting for transfers between devices: 132 us -> 102 us
  starting transfers between devices: 98 us -> 85.8 us
  other arithmetic: 36.7 us -> 25.6 us
    pallas_call x4, Pallas kernels: 81.3 us -> 56.1 us  [attend(): pl.pallas_call(partial(attend_kernel, width, len(held)), out_shape=[jax.S...]
    ppermute x48 -> x45, waiting for transfers between devices: 60.5 us -> 40.1 us  [row_swap(): return lax.ppermute(values, 'row', [(i, i ^ bit) for i in range(nr)])]
    all_to_all x13 -> x10, starting transfers between devices: 60.4 us -> 43.4 us  [col_exchange(): return lax.all_to_all(values, 'col', 0, 0, tiled=True)]
    all_to_all x13 -> x10, waiting for transfers between devices: 71.1 us -> 56.9 us  [col_exchange(): return lax.all_to_all(values, 'col', 0, 0, tiled=True)]
    ppermute x0 -> x6, starting transfers between devices: none -> 8.97 us  [sum_cols(): arrived.append(lax.ppermute(sent, 'col', [(i, i ^ k) for i in range(cols)]))]
    pallas_call x4, Pallas kernels: 82.5 us -> 73.9 us  [attend_back(): pl.pallas_call(partial(attend_back_kernel, width, len(held)), out_shape=[...]
    pallas_call x2, Pallas kernels: 62 us -> 54.3 us  [mlp_grads(): pl.pallas_call(partial(mlp_grads_kernel, nr), out_shape=[act, act, half,...]
    pallas_call x6 -> x7, Pallas kernels: 42.3 us -> 35.8 us  [the longest x2 20.8 us: collect(): pl.pallas_call(partial(collect_kernel, places, per), out_shape=jax.ShapeD...]
  transfers between devices with their start and end apart: 61 -> 61, of which waited for: 15 -> 19; matrix products, arithmetic and copies ran while one was open for 7% -> 7% of each run, Pallas kernels for 52% -> 55%
where the time goes in v3:
time: 635 us; the launch traced here: 625 us
  Pallas kernels  367 us (58%)
  waiting for transfers between devices  102 us (16%)
  starting transfers between devices  85.8 us (14%)
  local copies, waits for them, and re-layouts  42.6 us (7%)
  other arithmetic  25.6 us (4%)
    pallas_call x4, Pallas kernels, attend_back(): pl.pallas_call(partial(attend_back_kernel, width, len(held)), out_shape=[...  73.9 us
    all_to_all x10, waiting for transfers between devices, col_exchange(): return lax.all_to_all(values, 'col', 0, 0, tiled=True)  56.9 us
    pallas_call x4, Pallas kernels, attend(): pl.pallas_call(partial(attend_kernel, width, len(held)), out_shape=[jax.S...  56.1 us
    pallas_call x2, Pallas kernels, mlp_grads(): pl.pallas_call(partial(mlp_grads_kernel, nr), out_shape=[act, act, half,...  54.3 us
    all_to_all x10, starting transfers between devices, col_exchange(): return lax.all_to_all(values, 'col', 0, 0, tiled=True)  43.4 us
    ppermute x45, waiting for transfers between devices, row_swap(): return lax.ppermute(values, 'row', [(i, i ^ bit) for i in range(nr)])  40.1 us
    ppermute x45, starting transfers between devices, row_swap(): return lax.ppermute(values, 'row', [(i, i ^ bit) for i in range(nr)])  33.4 us
    pallas_call x8, Pallas kernels, reduce_weight(): pl.pallas_call(partial(add_kernel, sizes), out_shape=[jax.ShapeDtypeStruc...  22.1 us
  transfers between devices with their start and end apart: 61, of which 19 were waited for; matrix products, arithmetic and copies ran while one was open for 7% of the time, Pallas kernels for 55%

profile of v3, /device:TPU:0, one launch (start us, length us, event | category | flops | bytes accessed | tf_op | source)
XLA Modules:
  0.0 624.9 jit_solution(7375874021835811744)
XLA Ops:
  7.6 2.0 pack.1
  9.6 6.3 %all-to-all-start.1 = ((bf16[4,144,768]{2,1,0:T(8,128)(2,1)}), bf16[4,144,768]{2,1,0:T(8,128)(2,1)S(1)}, u32[]{:S(2)}, u32[]{:S(2)}) async-start(bf16[4,144,768]{2,1,0:T(8,128)(2,1)} %pack.1), calls=%async_computation.1 | async-start | bytes 1769472 | tf_op jit(solution)/shard_map/all_to_all | solution.py:1018
  16.0 2.1 plan.1.info
  18.8 10.5 %spread.2 = bf16[4,1088,256]{2,1,0:T(8,128)(2,1)} custom-call(s32[201]{0:T(256)} %plan.1.info, bf16[4096,256]{1,0:T(8,128)(2,1)} %x_ref.1), custom_call_target="tpu_custom_call" | custom-call | flops 7699999744 | bytes 7000000 | tf_op jit(solution)/shard_map/spread/pallas_call | solution.py:208
  29.3 8.9 %all-to-all-done.1 = bf16[4,144,768]{2,1,0:T(8,128)(2,1)S(1)} async-done(((bf16[4,144,768]{2,1,0:T(8,128)(2,1)}), bf16[4,144,768]{2,1,0:T(8,128)(2,1)S(1)}, u32[]{:S(2)}, u32[]{:S(2)}) %all-to-all-start.1) | async-done | bytes 884768 | tf_op jit(solution)/shard_map/all_to_all | solution.py:1018
  38.2 3.6 all-to-all-start
  53.6 2.6 collective-permute-done
  56.3 2.1 pad_maximum_fusion.4.refs_1_.refs_0_
  59.9 2.0 pad_maximum_fusion.5.refs_5_.refs_4_
  63.4 10.6 %spread.3 = bf16[4,1088,256]{2,1,0:T(8,128)(2,1)} custom-call(s32[201]{0:T(256)} %plan.1.info, bf16[4096,256]{1,0:T(8,128)(2,1)} %x_ref.2), custom_call_target="tpu_custom_call" | custom-call | flops 7699999744 | bytes 7000000 | tf_op jit(solution)/shard_map/spread/pallas_call | solution.py:208
  76.5 3.0 collective-permute-done.5.refs_6_.refs_5_
  82.9 9.4 %all-to-all-done.refs_0_ = bf16[4,1088,256]{2,1,0:T(8,128)(2,1)S(1)} async-done(((bf16[4,1088,256]{2,1,0:T(8,128)(2,1)}), bf16[4,1088,256]{2,1,0:T(8,128)(2,1)S(1)}, u32[]{:S(2)}, u32[]{:S(2)}) %all-to-all-start) | async-done | bytes 2228256 | tf_op jit(solution)/shard_map/all_to_all | solution.py:1018
  94.1 3.5 all-to-all-start.2
  99.6 14.9 %norm_qkv.1 = (bf16[1088,1024]{1,0:T(8,128)(2,1)}, bf16[1088,1024]{1,0:T(8,128)(2,1)}, bf16[1088,3072]{1,0:T(8,128)(2,1)}) custom-call(s32[201]{0:T(256)} %plan.1.info, bf16[4,1088,256]{2,1,0:T(8,128)(2,1)} %copy-done.8, bf16[2,4,64,768]{3,2,1,0:T(8,128)(2,1)} %pad_maximum_fusion.4.refs_1_.refs_0_, ...), custom_call_target="tpu_custom_call" | custom-call | flops 20899999744 | bytes 19000000 | tf_op jit(solution)/shard_map/norm_qkv/pallas_call | solution.py:367
  114.4 14.0 %all-to-all-done.2 = bf16[4,128,1280]{2,1,0:T(8,128)(2,1)S(1)} async-done(((bf16[4,128,1280]{2,1,0:T(8,128)(2,1)}), bf16[4,128,1280]{2,1,0:T(8,128)(2,1)S(1)}, u32[]{:S(2)}, u32[]{:S(2)}) %all-to-all-start.2) | async-done | bytes 1310752 | tf_op jit(solution)/shard_map/all_to_all | solution.py:1018
  132.8 3.5 all-to-all-start.3
  136.4 14.0 %attend.4 = (bf16[1088,1024]{1,0:T(8,128)(2,1)}, bf16[16,1400,256]{2,1,0:T(8,128)(2,1)}, f32[1400,1024]{1,0:T(8,128)}) custom-call(s32[201]{0:T(256)} %plan.1.info, bf16[1088,3072]{1,0:T(8,128)(2,1)} %get-tuple-element.197.qkv, bf16[128,128]{1,0:T(8,128)(2,1)} %pad_maximum_fusion.11.tables, s32[200,128]{1,0:T(8,128)} %constant.51.clone.shifts, ...), custom_call_target="tpu_custom_call" | custom-call | flops 15399999488 | bytes 14000000 | tf_op jit(solution)/shard_map/attend/pallas_call | solution.py:832
  152.0 2.4 pad_maximum_fusion.refs_0_
  155.2 5.8 all-to-all-done.3
  161.0 3.8 all-to-all-start.4
  164.8 14.0 %attend.5 = (bf16[1088,1024]{1,0:T(8,128)(2,1)}, bf16[16,1400,256]{2,1,0:T(8,128)(2,1)}, f32[1400,1024]{1,0:T(8,128)}) custom-call(s32[201]{0:T(256)} %plan.1.info, bf16[1088,3072]{1,0:T(8,128)(2,1)} %get-tuple-element.197.qkv, bf16[128,128]{1,0:T(8,128)(2,1)} %pad_maximum_fusion.11.tables, ...), custom_call_target="tpu_custom_call", output_to_operand_aliasing={{0}: (5, {}), {1}: (6, {}), {2}: (7, {})} | custom-call | flops 15399999488 | bytes 14000000 | tf_op jit(solution)/shard_map/attend/pallas_call | solution.py:832
  178.8 14.0 %attend.6 = (bf16[1088,1024]{1,0:T(8,128)(2,1)}, bf16[16,1400,256]{2,1,0:T(8,128)(2,1)}, f32[1400,1024]{1,0:T(8,128)}) custom-call(s32[201]{0:T(256)} %plan.1.info, bf16[1088,3072]{1,0:T(8,128)(2,1)} %get-tuple-element.197.qkv, bf16[128,128]{1,0:T(8,128)(2,1)} %pad_maximum_fusion.11.tables, ...), custom_call_target="tpu_custom_call", output_to_operand_aliasing={{0}: (5, {}), {1}: (6, {}), {2}: (7, {})} | custom-call | flops 15399999488 | bytes 14000000 | tf_op jit(solution)/shard_map/attend/pallas_call | solution.py:832
  194.8 14.0 %attend.7 = (bf16[1088,1024]{1,0:T(8,128)(2,1)}, bf16[16,1400,256]{2,1,0:T(8,128)(2,1)}, f32[1400,1024]{1,0:T(8,128)}) custom-call(s32[201]{0:T(256)} %plan.1.info, bf16[1088,3072]{1,0:T(8,128)(2,1)} %get-tuple-element.197.qkv, bf16[128,128]{1,0:T(8,128)(2,1)} %pad_maximum_fusion.11.tables, ...), custom_call_target="tpu_custom_call", output_to_operand_aliasing={{0}: (5, {}), {1}: (6, {}), {2}: (7, {})} | custom-call | flops 15399999488 | bytes 14000000 | tf_op jit(solution)/shard_map/attend/pallas_call | solution.py:832
  208.8 2.3 pad_maximum_fusion.2.refs_4_
  215.9 7.9 %proj_norm.1 = (f32[1088,1024]{1,0:T(8,128)}, bf16[1088,1024]{1,0:T(8,128)(2,1)}) custom-call(bf16[2,4,128,768]{3,2,1,0:T(8,128)(2,1)} %pad_maximum_fusion.refs_0_, bf16[2,4,128,768]{3,2,1,0:T(8,128)(2,1)} %collective-permute-done.11.refs_1_, bf16[2,4,128,768]{3,2,1,0:T(8,128)(2,1)} %collective-permute-done.17.refs_2_, ...), custom_call_target="tpu_custom_call" | custom-call | flops 12099999744 | bytes 11000000 | tf_op jit(solution)/shard_map/proj_norm/pallas_call | solution.py:440
  225.1 4.8 join.1.refs_9_.refs_11_
  230.0 27.0 %mlp_grads.2 = (bf16[1088,2048]{1,0:T(8,128)(2,1)}, bf16[1088,2048]{1,0:T(8,128)(2,1)}, bf16[4,4,128,1024]{3,2,1,0:T(8,128)(2,1)}, bf16[4,4,128,1024]{3,2,1,0:T(8,128)(2,1)}, f32[4,8,512]{2,1,0:T(8,128)}) custom-call(bf16[2,4,128,768]{3,2,1,0:T(8,128)(2,1)} %pad_maximum_fusion.refs_0_, bf16[2,4,128,768]{3,2,1,0:T(8,128)(2,1)} %collective-permute-done.11.refs_1_, ...), custom_call_target="tpu_custom_call" | custom-call | flops 41799999488 | bytes 38000000 | tf_op jit(solution)/shard_map/mlp_grads/pallas_call | solution.py:497
  258.6 2.2 collective-permute-done.21.refs_7_
  260.8 2.1 collective-permute-done.23.refs_3_.refs_7_
  263.9 27.3 %mlp_grads.3 = (bf16[1088,2048]{1,0:T(8,128)(2,1)}, bf16[1088,2048]{1,0:T(8,128)(2,1)}, bf16[4,4,128,1024]{3,2,1,0:T(8,128)(2,1)}, bf16[4,4,128,1024]{3,2,1,0:T(8,128)(2,1)}, f32[4,8,512]{2,1,0:T(8,128)}) custom-call(bf16[2,4,128,512]{3,2,1,0:T(8,128)(2,1)} %copy-done.13, bf16[2,4,128,512]{3,2,1,0:T(8,128)(2,1)} %collective-permute-done.19.refs_1_.refs_5_, ...), custom_call_target="tpu_custom_call" | custom-call | flops 41799999488 | bytes 38000000 | tf_op jit(solution)/shard_map/mlp_grads/pallas_call | solution.py:497
  294.8 3.4 add_rows.8
  299.2 17.5 %block_rows.1 = bf16[4,1088,256]{2,1,0:T(8,128)(2,1)} custom-call(s32[201]{0:T(256)} %plan.1.info, bf16[2,4,128,512]{3,2,1,0:T(8,128)(2,1)} %pad_maximum_fusion.1.refs_4_.refs_0_, bf16[2,4,128,512]{3,2,1,0:T(8,128)(2,1)} %collective-permute-done.10.refs_5_.refs_1_, bf16[2,4,128,512]{3,2,1,0:T(8,128)(2,1)} %collective-permute-done.12.refs_6_.refs_2_, ...), custom_call_target="tpu_custom_call" | custom-call | flops 28600000512 | bytes 26000000 | tf_op jit(solution)/shard_map/block_rows/pallas_call | solution.py:544
  316.8 5.2 all-to-all-start.5
  322.0 3.4 add_rows.10
  329.4 3.0 add_rows.9
  333.4 19.4 %mlp_back.1 = (f32[1088,1024]{1,0:T(8,128)}, bf16[1088,1024]{1,0:T(8,128)(2,1)}, f32[4,8,1024]{2,1,0:T(8,128)}) custom-call(bf16[2,4,128,768]{3,2,1,0:T(8,128)(2,1)} %pad_maximum_fusion.refs_0_, bf16[2,4,128,768]{3,2,1,0:T(8,128)(2,1)} %collective-permute-done.11.refs_1_, bf16[2,4,128,768]{3,2,1,0:T(8,128)(2,1)} %collective-permute-done.17.refs_2_, ...), custom_call_target="tpu_custom_call" | custom-call | flops 30799998976 | bytes 28000000 | tf_op jit(solution)/shard_map/mlp_back/pallas_call | solution.py:590
  354.0 8.7 %collective-permute-done.28.refs_3_ = bf16[1,4,128,512]{3,2,1,0:T(8,128)(2,1)S(1)} collective-permute-done((bf16[1,4,128,512]{3,2,1,0:T(8,128)(2,1)}, bf16[1,4,128,512]{3,2,1,0:T(8,128)(2,1)S(1)}, u32[]{:S(2)}, u32[]{:S(2)}) %collective-permute-start.28) | collective-permute-done | bytes 524320 | tf_op jit(solution)/shard_map/ppermute | solution.py:1022
  362.7 9.7 %proj_back.1 = (bf16[1088,1024]{1,0:T(8,128)(2,1)}, bf16[4,4,128,256]{3,2,1,0:T(8,128)(2,1)}, bf16[4,4,128,256]{3,2,1,0:T(8,128)(2,1)}) custom-call(bf16[2,4,128,768]{3,2,1,0:T(8,128)(2,1)} %pad_maximum_fusion.refs_0_, bf16[2,4,128,768]{3,2,1,0:T(8,128)(2,1)} %collective-permute-done.11.refs_1_, bf16[2,4,128,768]{3,2,1,0:T(8,128)(2,1)} %collective-permute-done.17.refs_2_, ...), custom_call_target="tpu_custom_call" | custom-call | flops 12099999744 | bytes 11000000 | tf_op jit(solution)/shard_map/proj_back/pallas_call | solution.py:622
  372.5 18.4 %attend_back.4 = (bf16[1088,3072]{1,0:T(8,128)(2,1)}, f32[128,256]{1,0:T(8,128)}, f32[8,768]{1,0:T(8,128)}) custom-call(s32[201]{0:T(256)} %plan.1.info, bf16[1088,3072]{1,0:T(8,128)(2,1)} %get-tuple-element.197.qkv, bf16[16,1400,256]{2,1,0:T(8,128)(2,1)} %get-tuple-element.165.exps, f32[1400,1024]{1,0:T(8,128)} %get-tuple-element.166.inv, ...), custom_call_target="tpu_custom_call" | custom-call | flops 14300000256 | bytes 13000000 | tf_op jit(solution)/shard_map/attend_back/pallas_call | solution.py:967
  392.9 3.0 add_rows.11
  402.3 3.6 add_cols.3
  406.0 4.8 all-to-all-start.6
  412.3 18.5 %attend_back.5 = (bf16[1088,3072]{1,0:T(8,128)(2,1)}, f32[128,256]{1,0:T(8,128)}, f32[8,768]{1,0:T(8,128)}) custom-call(s32[201]{0:T(256)} %plan.1.info, bf16[1088,3072]{1,0:T(8,128)(2,1)} %get-tuple-element.197.qkv, bf16[16,1400,256]{2,1,0:T(8,128)(2,1)} %get-tuple-element.165.exps, ...), custom_call_target="tpu_custom_call", output_to_operand_aliasing={{0}: (9, {})} | custom-call | flops 14300000256 | bytes 13000000 | tf_op jit(solution)/shard_map/attend_back/pallas_call | solution.py:967
  434.1 18.4 %attend_back.6 = (bf16[1088,3072]{1,0:T(8,128)(2,1)}, f32[128,256]{1,0:T(8,128)}, f32[8,768]{1,0:T(8,128)}) custom-call(s32[201]{0:T(256)} %plan.1.info, bf16[1088,3072]{1,0:T(8,128)(2,1)} %get-tuple-element.197.qkv, bf16[16,1400,256]{2,1,0:T(8,128)(2,1)} %get-tuple-element.165.exps, ...), custom_call_target="tpu_custom_call", output_to_operand_aliasing={{0}: (9, {})} | custom-call | flops 14300000256 | bytes 13000000 | tf_op jit(solution)/shard_map/attend_back/pallas_call | solution.py:967
  453.2 4.1 add_cols.4
  457.4 5.0 all-to-all-start.7
  462.4 18.6 %attend_back.7 = (bf16[1088,3072]{1,0:T(8,128)(2,1)}, f32[128,256]{1,0:T(8,128)}, f32[8,768]{1,0:T(8,128)}) custom-call(s32[201]{0:T(256)} %plan.1.info, bf16[1088,3072]{1,0:T(8,128)(2,1)} %get-tuple-element.197.qkv, bf16[16,1400,256]{2,1,0:T(8,128)(2,1)} %get-tuple-element.165.exps, ...), custom_call_target="tpu_custom_call", output_to_operand_aliasing={{0}: (9, {})} | custom-call | flops 14300000256 | bytes 13000000 | tf_op jit(solution)/shard_map/attend_back/pallas_call | solution.py:967
  481.1 12.7 %qkv_grad.1 = (bf16[4,4,128,768]{3,2,1,0:T(8,128)(2,1)}, bf16[4,4,128,768]{3,2,1,0:T(8,128)(2,1)}) custom-call(bf16[1088,1024]{1,0:T(8,128)(2,1)} %get-tuple-element.199.n1, bf16[1088,3072]{1,0:T(8,128)(2,1)} %get-tuple-element.221.dqkv.refs_8_), custom_call_target="tpu_custom_call" | custom-call | flops 15399999488 | bytes 14000000 | tf_op jit(solution)/shard_map/qkv_grad/pallas_call | solution.py:643
  495.0 2.1 collective-permute-start.37
  497.1 2.4 collective-permute-start.38
  499.5 10.0 %collect.2 = bf16[4096,256]{1,0:T(8,128)(2,1)} custom-call(s32[201]{0:T(256)} %plan.1.info, bf16[4,1088,256]{2,1,0:T(8,128)(2,1)} %all-to-all-done.5.pieces), custom_call_target="tpu_custom_call" | custom-call | flops 8800000000 | bytes 8000000 | tf_op jit(solution)/shard_map/collect/pallas_call | solution.py:258
  511.6 2.9 add_rows.14
  514.5 16.2 %input_back.1 = (bf16[4,1088,256]{2,1,0:T(8,128)(2,1)}, f32[2,8,1024]{2,1,0:T(8,128)}) custom-call(s32[201]{0:T(256)} %plan.1.info, bf16[2,4,64,768]{3,2,1,0:T(8,128)(2,1)} %pad_maximum_fusion.4.refs_1_.refs_0_, bf16[2,4,64,768]{3,2,1,0:T(8,128)(2,1)} %collective-permute-done.1.refs_2_.refs_1_, bf16[2,4,64,768]{3,2,1,0:T(8,128)(2,1)} %copy-done.49, ...), custom_call_target="tpu_custom_call" | custom-call | flops 27499999232 | bytes 25000000 | tf_op jit(solution)/shard_map/input_back/pallas_call | solution.py:680
  532.9 3.3 collective-permute-start.42
  537.7 3.8 collective-permute-done.43
  541.5 3.6 all-to-all-start.8
  547.2 15.6 %collective-permute-done.44.refs_2_ = bf16[2,4,64,768]{3,2,1,0:T(8,128)(2,1)S(1)} collective-permute-done((bf16[2,4,64,768]{3,2,1,0:T(8,128)(2,1)}, bf16[2,4,64,768]{3,2,1,0:T(8,128)(2,1)S(1)}, u32[]{:S(2)}, u32[]{:S(2)}) %collective-permute-start.44) | collective-permute-done | bytes 786464 | tf_op jit(solution)/shard_map/ppermute | solution.py:1022
  564.6 2.6 add_rows.15
  570.1 2.4 collective-permute-done.47
  579.8 14.7 %all-to-all-done.8.pieces = bf16[4,1088,256]{2,1,0:T(8,128)(2,1)S(1)} async-done(((bf16[4,1088,256]{2,1,0:T(8,128)(2,1)}), bf16[4,1088,256]{2,1,0:T(8,128)(2,1)S(1)}, u32[]{:S(2)}, u32[]{:S(2)}) %all-to-all-start.8) | async-done | bytes 2228256 | tf_op jit(solution)/shard_map/all_to_all | solution.py:1018
  596.7 3.1 add_cols.5
  599.8 3.9 all-to-all-start.9
  608.3 10.8 %collect.3 = f32[4096,256]{1,0:T(8,128)} custom-call(s32[201]{0:T(256)} %plan.1.info, bf16[4,1088,256]{2,1,0:T(8,128)(2,1)} %copy-done.9), custom_call_target="tpu_custom_call" | custom-call | flops 8800000000 | bytes 8000000 | tf_op jit(solution)/shard_map/collect/pallas_call | solution.py:258
  619.1 4.2 all-to-all-done.9
  (315 shorter events, 103.1 us)
Async XLA Ops:
  9.6 28.5 %all-to-all-start.1 = ((bf16[4,144,768]{2,1,0:T(8,128)(2,1)}), bf16[4,144,768]{2,1,0:T(8,128)(2,1)S(1)}, u32[]{:S(2)}, u32[]{:S(2)}) async-start(bf16[4,144,768]{2,1,0:T(8,128)(2,1)} %pack.1), calls=%async_computation.1 | async-start | bytes 1769472 | tf_op jit(solution)/shard_map/all_to_all | solution.py:1018
  38.2 54.1 %all-to-all-start = ((bf16[4,1088,256]{2,1,0:T(8,128)(2,1)}), bf16[4,1088,256]{2,1,0:T(8,128)(2,1)S(1)}, u32[]{:S(2)}, u32[]{:S(2)}) async-start(bf16[4,1088,256]{2,1,0:T(8,128)(2,1)} %spread.2), calls=%async_computation | async-start | bytes 4456448 | tf_op jit(solution)/shard_map/all_to_all | solution.py:1018
  45.9 10.4 %collective-permute-start = (bf16[1,4,64,768]{3,2,1,0:T(8,128)(2,1)}, bf16[1,4,64,768]{3,2,1,0:T(8,128)(2,1)}, u32[]{:S(2)}, u32[]{:S(2)}) collective-permute-start(bf16[1,4,64,768]{3,2,1,0:T(8,128)(2,1)} %get-tuple-element.325), channel_id=1, source_target_pairs={{0,8},{4,12},{8,0},{12,4},{16,24},{20,28},{24,16},{28,20},{1,9},{5... | collective-permute-start | bytes 1179656 | tf_op jit(solution)/shard_map/ppermute | solution.py:1022
  47.5 12.4 %collective-permute-start.4 = (bf16[1,4,64,768]{3,2,1,0:T(8,128)(2,1)S(1)}, bf16[1,4,64,768]{3,2,1,0:T(8,128)(2,1)}, u32[]{:S(2)}, u32[]{:S(2)}) collective-permute-start(bf16[1,4,64,768]{3,2,1,0:T(8,128)(2,1)S(1)} %get-tuple-element.324), channel_id=1, source_target_pairs={{0,16},{4,20},{8,24},{12,28},{16,0},{20,4},{24,8},{28,12},{1,17},{... | collective-permute-start | bytes 1179656 | tf_op jit(solution)/shard_map/ppermute | solution.py:1022
  58.4 18.1 %collective-permute-start.1 = (bf16[2,4,64,768]{3,2,1,0:T(8,128)(2,1)}, bf16[2,4,64,768]{3,2,1,0:T(8,128)(2,1)}, u32[]{:S(2)}, u32[]{:S(2)}) collective-permute-start(bf16[2,4,64,768]{3,2,1,0:T(8,128)(2,1)} %pad_maximum_fusion.4.refs_1_.refs_0_), channel_id=1, source_target_pairs={{0,16},{4,20},{8,24},{12,28},{16,0},{20,4},{24,8},{28,12},{1,17},{... | collective-permute-start | bytes 2359304 | tf_op jit(solution)/shard_map/ppermute | solution.py:1022
  61.9 17.6 %collective-permute-start.5 = (bf16[2,4,64,768]{3,2,1,0:T(8,128)(2,1)}, bf16[2,4,64,768]{3,2,1,0:T(8,128)(2,1)}, u32[]{:S(2)}, u32[]{:S(2)}) collective-permute-start(bf16[2,4,64,768]{3,2,1,0:T(8,128)(2,1)} %pad_maximum_fusion.5.refs_5_.refs_4_), channel_id=1, source_target_pairs={{0,8},{4,12},{8,0},{12,4},{16,24},{20,28},{24,16},{28,20},{1,9},{5... | collective-permute-start | bytes 2359304 | tf_op jit(solution)/shard_map/ppermute | solution.py:1022
  75.9 5.0 collective-permute-start.2
  75.9 4.9 collective-permute-start.6
  76.4 4.4 collective-permute-start.3
  79.5 3.4 collective-permute-start.7
  94.1 34.3 %all-to-all-start.2 = ((bf16[4,128,1280]{2,1,0:T(8,128)(2,1)}), bf16[4,128,1280]{2,1,0:T(8,128)(2,1)S(1)}, u32[]{:S(2)}, u32[]{:S(2)}) async-start(bf16[4,128,1280]{2,1,0:T(8,128)(2,1)} %broadcast_in_dim.135), calls=%async_computation.2 | async-start | bytes 2621440 | tf_op jit(solution)/shard_map/all_to_all | solution.py:1018
  128.5 21.9 %collective-permute-start.8 = (bf16[1,4,128,512]{3,2,1,0:T(8,128)(2,1)S(1)}, bf16[1,4,128,512]{3,2,1,0:T(8,128)(2,1)S(1)}, u32[]{:S(2)}, u32[]{:S(2)}) collective-permute-start(bf16[1,4,128,512]{3,2,1,0:T(8,128)(2,1)S(1)} %slice_bitcast_fusion.3), channel_id=1, source_target_pairs={{0,16},{4,20},{8,24},{12,28},{16,0},{20,4},{24,8},{28,12},{1,17},{... | collective-permute-start | bytes 1572872 | tf_op jit(solution)/shard_map/ppermute | solution.py:1022
  130.1 20.3 %collective-permute-start.9 = (bf16[1,4,128,768]{3,2,1,0:T(8,128)(2,1)S(1)}, bf16[1,4,128,768]{3,2,1,0:T(8,128)(2,1)}, u32[]{:S(2)}, u32[]{:S(2)}) collective-permute-start(bf16[1,4,128,768]{3,2,1,0:T(8,128)(2,1)S(1)} %slice_bitcast_fusion), channel_id=1, source_target_pairs={{0,8},{4,12},{8,0},{12,4},{16,24},{20,28},{24,16},{28,20},{1,9},{5... | collective-permute-start | bytes 2359304 | tf_op jit(solution)/shard_map/ppermute | solution.py:1022
  132.8 28.1 %all-to-all-start.3 = ((bf16[4,128,1024]{2,1,0:T(8,128)(2,1)}), bf16[4,128,1024]{2,1,0:T(8,128)(2,1)S(1)}, u32[]{:S(2)}, u32[]{:S(2)}) async-start(bf16[4,128,1024]{2,1,0:T(8,128)(2,1)} %broadcast_in_dim.142), calls=%async_computation.3 | async-start | bytes 2097152 | tf_op jit(solution)/shard_map/all_to_all | solution.py:1018
  151.5 42.8 %collective-permute-start.10 = (bf16[2,4,128,512]{3,2,1,0:T(8,128)(2,1)}, bf16[2,4,128,512]{3,2,1,0:T(8,128)(2,1)}, u32[]{:S(2)}, u32[]{:S(2)}) collective-permute-start(bf16[2,4,128,512]{3,2,1,0:T(8,128)(2,1)} %pad_maximum_fusion.1.refs_4_.refs_0_), channel_id=1, source_target_pairs={{0,8},{4,12},{8,0},{12,4},{16,24},{20,28},{24,16},{28,20},{1,9},{5... | collective-permute-start | bytes 3145736 | tf_op jit(solution)/shard_map/ppermute | solution.py:1022
  152.0 77.9 %collective-permute-start.12 = (bf16[2,4,128,512]{3,2,1,0:T(8,128)(2,1)}, bf16[2,4,128,512]{3,2,1,0:T(8,128)(2,1)}, u32[]{:S(2)}, u32[]{:S(2)}) collective-permute-start(bf16[2,4,128,512]{3,2,1,0:T(8,128)(2,1)} %pad_maximum_fusion.1.refs_4_.refs_0_), channel_id=1, source_target_pairs={{0,4},{4,0},{8,12},{12,8},{16,20},{20,16},{24,28},{28,24},{1,5},{5... | collective-permute-start | bytes 3145736 | tf_op jit(solution)/shard_map/ppermute | solution.py:1022
  154.4 40.4 %collective-permute-start.11 = (bf16[2,4,128,768]{3,2,1,0:T(8,128)(2,1)}, bf16[2,4,128,768]{3,2,1,0:T(8,128)(2,1)}, u32[]{:S(2)}, u32[]{:S(2)}) collective-permute-start(bf16[2,4,128,768]{3,2,1,0:T(8,128)(2,1)} %pad_maximum_fusion.refs_0_), channel_id=1, source_target_pairs={{0,16},{4,20},{8,24},{12,28},{16,0},{20,4},{24,8},{28,12},{1,17},{... | collective-permute-start | bytes 4718600 | tf_op jit(solution)/shard_map/ppermute | solution.py:1022
  154.9 59.1 %collective-permute-start.17 = (bf16[2,4,128,768]{3,2,1,0:T(8,128)(2,1)}, bf16[2,4,128,768]{3,2,1,0:T(8,128)(2,1)}, u32[]{:S(2)}, u32[]{:S(2)}) collective-permute-start(bf16[2,4,128,768]{3,2,1,0:T(8,128)(2,1)} %pad_maximum_fusion.refs_0_), channel_id=1, source_target_pairs={{0,4},{4,0},{8,12},{12,8},{16,20},{20,16},{24,28},{28,24},{1,5},{5... | collective-permute-start | bytes 4718600 | tf_op jit(solution)/shard_map/ppermute | solution.py:1022
  161.0 62.8 %all-to-all-start.4 = ((bf16[4,1088,256]{2,1,0:T(8,128)(2,1)}), bf16[4,1088,256]{2,1,0:T(8,128)(2,1)S(1)}, u32[]{:S(2)}, u32[]{:S(2)}) async-start(bf16[4,1088,256]{2,1,0:T(8,128)(2,1)} %spread.3), calls=%async_computation.4 | async-start | bytes 4456448 | tf_op jit(solution)/shard_map/all_to_all | solution.py:1018
  193.8 15.1 %collective-permute-start.14 = (bf16[1,4,128,512]{3,2,1,0:T(8,128)(2,1)}, bf16[1,4,128,512]{3,2,1,0:T(8,128)(2,1)S(1)}, u32[]{:S(2)}, u32[]{:S(2)}) collective-permute-start(bf16[1,4,128,512]{3,2,1,0:T(8,128)(2,1)} %get-tuple-element.323), channel_id=1, source_target_pairs={{0,16},{4,20},{8,24},{12,28},{16,0},{20,4},{24,8},{28,12},{1,17},{... | collective-permute-start | bytes 1572872 | tf_op jit(solution)/shard_map/ppermute | solution.py:1022
  194.3 14.6 %collective-permute-start.15 = (bf16[1,4,128,512]{3,2,1,0:T(8,128)(2,1)S(1)}, bf16[1,4,128,512]{3,2,1,0:T(8,128)(2,1)S(1)}, u32[]{:S(2)}, u32[]{:S(2)}) collective-permute-start(bf16[1,4,128,512]{3,2,1,0:T(8,128)(2,1)S(1)} %get-tuple-element.322), channel_id=1, source_target_pairs={{0,8},{4,12},{8,0},{12,4},{16,24},{20,28},{24,16},{28,20},{1,9},{5... | collective-permute-start | bytes 1572872 | tf_op jit(solution)/shard_map/ppermute | solution.py:1022
  194.8 19.6 %collective-permute-start.18 = (bf16[2,4,128,768]{3,2,1,0:T(8,128)(2,1)}, bf16[2,4,128,768]{3,2,1,0:T(8,128)(2,1)}, u32[]{:S(2)}, u32[]{:S(2)}) collective-permute-start(bf16[2,4,128,768]{3,2,1,0:T(8,128)(2,1)} %collective-permute-done.11.refs_1_), channel_id=1, source_target_pairs={{0,4},{4,0},{8,12},{12,8},{16,20},{20,16},{24,28},{28,24},{1,5},{5... | collective-permute-start | bytes 4718600 | tf_op jit(solution)/shard_map/ppermute | solution.py:1022
  211.1 45.8 %collective-permute-start.16 = (bf16[2,4,128,512]{3,2,1,0:T(8,128)(2,1)}, bf16[2,4,128,512]{3,2,1,0:T(8,128)(2,1)}, u32[]{:S(2)}, u32[]{:S(2)}) collective-permute-start(bf16[2,4,128,512]{3,2,1,0:T(8,128)(2,1)} %pad_maximum_fusion.2.refs_4_), channel_id=1, source_target_pairs={{0,8},{4,12},{8,0},{12,4},{16,24},{20,28},{24,16},{28,20},{1,9},{5... | collective-permute-start | bytes 3145736 | tf_op jit(solution)/shard_map/ppermute | solution.py:1022
  212.6 46.0 %collective-permute-start.20 = (bf16[2,4,128,512]{3,2,1,0:T(8,128)(2,1)}, bf16[2,4,128,512]{3,2,1,0:T(8,128)(2,1)}, u32[]{:S(2)}, u32[]{:S(2)}) collective-permute-start(bf16[2,4,128,512]{3,2,1,0:T(8,128)(2,1)} %pad_maximum_fusion.2.refs_4_), channel_id=1, source_target_pairs={{0,4},{4,0},{8,12},{12,8},{16,20},{20,16},{24,28},{28,24},{1,5},{5... | collective-permute-start | bytes 3145736 | tf_op jit(solution)/shard_map/ppermute | solution.py:1022
  214.0 15.9 %collective-permute-start.13 = (bf16[2,4,128,512]{3,2,1,0:T(8,128)(2,1)}, bf16[2,4,128,512]{3,2,1,0:T(8,128)(2,1)}, u32[]{:S(2)}, u32[]{:S(2)}) collective-permute-start(bf16[2,4,128,512]{3,2,1,0:T(8,128)(2,1)} %collective-permute-done.10.refs_5_.refs_1_), channel_id=1, source_target_pairs={{0,4},{4,0},{8,12},{12,8},{16,20},{20,16},{24,28},{28,24},{1,5},{5... | collective-permute-start | bytes 3145736 | tf_op jit(solution)/shard_map/ppermute | solution.py:1022
  214.4 42.6 %collective-permute-start.19 = (bf16[2,4,128,512]{3,2,1,0:T(8,128)(2,1)S(1)}, bf16[2,4,128,512]{3,2,1,0:T(8,128)(2,1)}, u32[]{:S(2)}, u32[]{:S(2)}) collective-permute-start(bf16[2,4,128,512]{3,2,1,0:T(8,128)(2,1)S(1)} %pad_maximum_fusion.3.refs_0_.refs_4_), channel_id=1, source_target_pairs={{0,16},{4,20},{8,24},{12,28},{16,0},{20,4},{24,8},{28,12},{1,17},{... | collective-permute-start | bytes 3145736 | tf_op jit(solution)/shard_map/ppermute | solution.py:1022
  229.9 28.7 %collective-permute-start.22 = (bf16[2,4,128,512]{3,2,1,0:T(8,128)(2,1)S(1)}, bf16[2,4,128,512]{3,2,1,0:T(8,128)(2,1)S(1)}, u32[]{:S(2)}, u32[]{:S(2)}) collective-permute-start(bf16[2,4,128,512]{3,2,1,0:T(8,128)(2,1)S(1)} %pad_maximum_fusion.3.refs_0_.refs_4_), channel_id=1, source_target_pairs={{0,4},{4,0},{8,12},{12,8},{16,20},{20,16},{24,28},{28,24},{1,5},{5... | collective-permute-start | bytes 3145736 | tf_op jit(solution)/shard_map/ppermute | solution.py:1022
  257.0 3.9 collective-permute-start.21
  257.5 5.4 collective-permute-start.23
  258.2 33.3 %copy-start.26 = (bf16[64,128]{1,0:T(8,128)(2,1)S(1)}, bf16[64,128]{1,0:T(8,128)(2,1)}, u32[]{:S(2)}) copy-start(bf16[64,128]{1,0:T(8,128)(2,1)} %copy-done.25) | copy-start | bytes 49156
  258.2 33.3 %copy-start.28 = (bf16[64,128]{1,0:T(8,128)(2,1)S(1)}, bf16[64,128]{1,0:T(8,128)(2,1)}, u32[]{:S(2)}) copy-start(bf16[64,128]{1,0:T(8,128)(2,1)} %copy-done.27) | copy-start | bytes 49156
  258.2 34.5 %copy-start.33 = (f32[4,8,512]{2,1,0:T(8,128)S(1)}, f32[4,8,512]{2,1,0:T(8,128)}, u32[]{:S(2)}) copy-start(f32[4,8,512]{2,1,0:T(8,128)} %get-tuple-element.207) | copy-start | bytes 196612
  258.2 36.6 %collective-permute-start.25 = (bf16[4,4,128,1024]{3,2,1,0:T(8,128)(2,1)}, bf16[4,4,128,1024]{3,2,1,0:T(8,128)(2,1)}, u32[]{:S(2)}, u32[]{:S(2)}) collective-permute-start(bf16[4,4,128,1024]{3,2,1,0:T(8,128)(2,1)} %get-tuple-element.171), channel_id=1, source_target_pairs={{0,4},{4,0},{8,12},{12,8},{16,20},{20,16},{24,28},{28,24},{1,5},{5... | collective-permute-start | bytes 12582920 | tf_op jit(solution)/shard_map/ppermute | solution.py:1022
  291.3 8.0 %collective-permute-start.24 = (bf16[4,4,128,1024]{3,2,1,0:T(8,128)(2,1)}, bf16[4,4,128,1024]{3,2,1,0:T(8,128)(2,1)}, u32[]{:S(2)}, u32[]{:S(2)}) collective-permute-start(bf16[4,4,128,1024]{3,2,1,0:T(8,128)(2,1)} %get-tuple-element.162), channel_id=1, source_target_pairs={{0,4},{4,0},{8,12},{12,8},{16,20},{20,16},{24,28},{28,24},{1,5},{5... | collective-permute-start | bytes 12582920 | tf_op jit(solution)/shard_map/ppermute | solution.py:1022
  298.2 30.2 %collective-permute-start.26 = (bf16[2,4,128,512]{3,2,1,0:T(8,128)(2,1)}, bf16[2,4,128,512]{3,2,1,0:T(8,128)(2,1)S(1)}, u32[]{:S(2)}, u32[]{:S(2)}) collective-permute-start(bf16[2,4,128,512]{3,2,1,0:T(8,128)(2,1)} %get-tuple-element.173), channel_id=1, source_target_pairs={{0,16},{4,20},{8,24},{12,28},{16,0},{20,4},{24,8},{28,12},{1,17},{... | collective-permute-start | bytes 3145736 | tf_op jit(solution)/shard_map/ppermute | solution.py:1022
  298.7 29.7 %collective-permute-start.27 = (bf16[2,4,128,512]{3,2,1,0:T(8,128)(2,1)}, bf16[2,4,128,512]{3,2,1,0:T(8,128)(2,1)}, u32[]{:S(2)}, u32[]{:S(2)}) collective-permute-start(bf16[2,4,128,512]{3,2,1,0:T(8,128)(2,1)} %get-tuple-element.174), channel_id=1, source_target_pairs={{0,8},{4,12},{8,0},{12,4},{16,24},{20,28},{24,16},{28,20},{1,9},{5... | collective-permute-start | bytes 3145736 | tf_op jit(solution)/shard_map/ppermute | solution.py:1022
  316.8 85.6 %all-to-all-start.5 = ((bf16[4,1088,256]{2,1,0:T(8,128)(2,1)}), bf16[4,1088,256]{2,1,0:T(8,128)(2,1)}, u32[]{:S(2)}, u32[]{:S(2)}) async-start(bf16[4,1088,256]{2,1,0:T(8,128)(2,1)} %block_rows.1), calls=%async_computation.5 | async-start | bytes 4456448 | tf_op jit(solution)/shard_map/all_to_all | solution.py:1018
  325.4 65.5 %collective-permute-start.30 = (bf16[2,4,128,512]{3,2,1,0:T(8,128)(2,1)}, bf16[2,4,128,512]{3,2,1,0:T(8,128)(2,1)S(1)}, u32[]{:S(2)}, u32[]{:S(2)}) collective-permute-start(bf16[2,4,128,512]{3,2,1,0:T(8,128)(2,1)} %get-tuple-element.184), channel_id=1, source_target_pairs={{0,16},{4,20},{8,24},{12,28},{16,0},{20,4},{24,8},{28,12},{1,17},{... | collective-permute-start | bytes 3145736 | tf_op jit(solution)/shard_map/ppermute | solution.py:1022
  326.9 64.0 %collective-permute-start.31 = (bf16[2,4,128,512]{3,2,1,0:T(8,128)(2,1)}, bf16[2,4,128,512]{3,2,1,0:T(8,128)(2,1)S(1)}, u32[]{:S(2)}, u32[]{:S(2)}) collective-permute-start(bf16[2,4,128,512]{3,2,1,0:T(8,128)(2,1)} %get-tuple-element.185), channel_id=1, source_target_pairs={{0,8},{4,12},{8,0},{12,4},{16,24},{20,28},{24,16},{28,20},{1,9},{5... | collective-permute-start | bytes 3145736 | tf_op jit(solution)/shard_map/ppermute | solution.py:1022
  332.4 30.3 %collective-permute-start.28 = (bf16[1,4,128,512]{3,2,1,0:T(8,128)(2,1)}, bf16[1,4,128,512]{3,2,1,0:T(8,128)(2,1)S(1)}, u32[]{:S(2)}, u32[]{:S(2)}) collective-permute-start(bf16[1,4,128,512]{3,2,1,0:T(8,128)(2,1)} %get-tuple-element.176), channel_id=1, source_target_pairs={{0,8},{4,12},{8,0},{12,4},{16,24},{20,28},{24,16},{28,20},{1,9},{5... | collective-permute-start | bytes 1572872 | tf_op jit(solution)/shard_map/ppermute | solution.py:1022
  332.9 29.8 %collective-permute-start.29 = (bf16[1,4,128,512]{3,2,1,0:T(8,128)(2,1)}, bf16[1,4,128,512]{3,2,1,0:T(8,128)(2,1)S(1)}, u32[]{:S(2)}, u32[]{:S(2)}) collective-permute-start(bf16[1,4,128,512]{3,2,1,0:T(8,128)(2,1)} %get-tuple-element.177), channel_id=1, source_target_pairs={{0,16},{4,20},{8,24},{12,28},{16,0},{20,4},{24,8},{28,12},{1,17},{... | collective-permute-start | bytes 1572872 | tf_op jit(solution)/shard_map/ppermute | solution.py:1022
  372.4 25.5 %collective-permute-start.34 = (bf16[4,4,128,256]{3,2,1,0:T(8,128)(2,1)}, bf16[4,4,128,256]{3,2,1,0:T(8,128)(2,1)S(1)}, u32[]{:S(2)}, u32[]{:S(2)}) collective-permute-start(bf16[4,4,128,256]{3,2,1,0:T(8,128)(2,1)} %get-tuple-element.193), channel_id=1, source_target_pairs={{0,4},{4,0},{8,12},{12,8},{16,20},{20,16},{24,28},{28,24},{1,5},{5... | collective-permute-start | bytes 3145736 | tf_op jit(solution)/shard_map/ppermute | solution.py:1022
  395.9 14.9 %collective-permute-start.32 = (bf16[1,4,128,512]{3,2,1,0:T(8,128)(2,1)}, bf16[1,4,128,512]{3,2,1,0:T(8,128)(2,1)S(1)}, u32[]{:S(2)}, u32[]{:S(2)}) collective-permute-start(bf16[1,4,128,512]{3,2,1,0:T(8,128)(2,1)} %get-tuple-element.187), channel_id=1, source_target_pairs={{0,8},{4,12},{8,0},{12,4},{16,24},{20,28},{24,16},{28,20},{1,9},{5... | collective-permute-start | bytes 1572872 | tf_op jit(solution)/shard_map/ppermute | solution.py:1022
  397.4 15.0 %collective-permute-start.33 = (bf16[1,4,128,512]{3,2,1,0:T(8,128)(2,1)}, bf16[1,4,128,512]{3,2,1,0:T(8,128)(2,1)S(1)}, u32[]{:S(2)}, u32[]{:S(2)}) collective-permute-start(bf16[1,4,128,512]{3,2,1,0:T(8,128)(2,1)} %get-tuple-element.188), channel_id=1, source_target_pairs={{0,16},{4,20},{8,24},{12,28},{16,0},{20,4},{24,8},{28,12},{1,17},{... | collective-permute-start | bytes 1572872 | tf_op jit(solution)/shard_map/ppermute | solution.py:1022
  400.8 30.0 %collective-permute-start.35 = (bf16[2,4,128,256]{3,2,1,0:T(8,128)(2,1)}, bf16[2,4,128,256]{3,2,1,0:T(8,128)(2,1)S(1)}, u32[]{:S(2)}, u32[]{:S(2)}) collective-permute-start(bf16[2,4,128,256]{3,2,1,0:T(8,128)(2,1)} %add_rows.12), channel_id=1, source_target_pairs={{0,16},{4,20},{8,24},{12,28},{16,0},{20,4},{24,8},{28,12},{1,17},{... | collective-permute-start | bytes 1572872 | tf_op jit(solution)/shard_map/ppermute | solution.py:1022
  406.0 46.6 %all-to-all-start.6 = ((bf16[4,128,1024]{2,1,0:T(8,128)(2,1)}), bf16[4,128,1024]{2,1,0:T(8,128)(2,1)S(1)}, u32[]{:S(2)}, u32[]{:S(2)}) async-start(bf16[4,128,1024]{2,1,0:T(8,128)(2,1)} %add_cols.3), calls=%async_computation.6 | async-start | bytes 2097152 | tf_op jit(solution)/shard_map/all_to_all | solution.py:1018
  433.5 19.0 %collective-permute-start.36 = (bf16[1,4,128,256]{3,2,1,0:T(8,128)(2,1)}, bf16[1,4,128,256]{3,2,1,0:T(8,128)(2,1)S(1)}, u32[]{:S(2)}, u32[]{:S(2)}) collective-permute-start(bf16[1,4,128,256]{3,2,1,0:T(8,128)(2,1)} %add_rows.13), channel_id=1, source_target_pairs={{0,8},{4,12},{8,0},{12,4},{16,24},{20,28},{24,16},{28,20},{1,9},{5... | collective-permute-start | bytes 786440 | tf_op jit(solution)/shard_map/ppermute | solution.py:1022
  457.4 57.1 %all-to-all-start.7 = ((bf16[4,128,1280]{2,1,0:T(8,128)(2,1)}), bf16[4,128,1280]{2,1,0:T(8,128)(2,1)}, u32[]{:S(2)}, u32[]{:S(2)}) async-start(bf16[4,128,1280]{2,1,0:T(8,128)(2,1)} %add_cols.4), calls=%async_computation.7 | async-start | bytes 2621440 | tf_op jit(solution)/shard_map/all_to_all | solution.py:1018
  494.3 15.6 %collective-permute-start.40 = (bf16[4,4,128,768]{3,2,1,0:T(8,128)(2,1)}, bf16[4,4,128,768]{3,2,1,0:T(8,128)(2,1)S(1)}, u32[]{:S(2)}, u32[]{:S(2)}) collective-permute-start(bf16[4,4,128,768]{3,2,1,0:T(8,128)(2,1)} %get-tuple-element.217), channel_id=1, source_target_pairs={{0,4},{4,0},{8,12},{12,8},{16,20},{20,16},{24,28},{28,24},{1,5},{5... | collective-permute-start | bytes 9437192 | tf_op jit(solution)/shard_map/ppermute | solution.py:1022
  495.0 14.5 %collective-permute-start.37 = (f32[6016]{0:T(1024)S(1)}, f32[6016]{0:T(1024)S(1)}, u32[]{:S(2)}, u32[]{:S(2)}) collective-permute-start(f32[6016]{0:T(1024)S(1)} %get-tuple-element.320), channel_id=1, source_target_pairs={{0,1},{1,0},{2,3},{3,2},{4,5},{5,4},{6,7},{7,6},{8,9},{9,8},{10,11... | collective-permute-start | bytes 72200 | tf_op jit(solution)/shard_map/ppermute | solution.py:1200
  497.1 12.5 %collective-permute-start.38 = (f32[6016]{0:T(1024)S(1)}, f32[6016]{0:T(1024)S(1)}, u32[]{:S(2)}, u32[]{:S(2)}) collective-permute-start(f32[6016]{0:T(1024)S(1)} %get-tuple-element.319), channel_id=1, source_target_pairs={{0,2},{1,3},{2,0},{3,1},{4,6},{5,7},{6,4},{7,5},{8,10},{9,11},{10,... | collective-permute-start | bytes 72200 | tf_op jit(solution)/shard_map/ppermute | solution.py:1200
  499.4 10.1 %collective-permute-start.39 = (f32[6016]{0:T(1024)S(1)}, f32[6016]{0:T(1024)S(1)}, u32[]{:S(2)}, u32[]{:S(2)}) collective-permute-start(f32[6016]{0:T(1024)S(1)} %get-tuple-element.318), channel_id=1, source_target_pairs={{0,3},{1,2},{2,1},{3,0},{4,7},{5,6},{6,5},{7,4},{8,11},{9,10},{10,... | collective-permute-start | bytes 72200 | tf_op jit(solution)/shard_map/ppermute | solution.py:1200
  531.8 4.5 collective-permute-start.41
  532.9 4.8 collective-permute-start.42
  536.1 5.4 collective-permute-start.43
  541.5 53.0 %all-to-all-start.8 = ((bf16[4,1088,256]{2,1,0:T(8,128)(2,1)}), bf16[4,1088,256]{2,1,0:T(8,128)(2,1)S(1)}, u32[]{:S(2)}, u32[]{:S(2)}) async-start(bf16[4,1088,256]{2,1,0:T(8,128)(2,1)} %get-tuple-element.225), calls=%async_computation.8 | async-start | bytes 4456448 | tf_op jit(solution)/shard_map/all_to_all | solution.py:1018
  545.2 17.7 %collective-permute-start.44 = (bf16[2,4,64,768]{3,2,1,0:T(8,128)(2,1)}, bf16[2,4,64,768]{3,2,1,0:T(8,128)(2,1)S(1)}, u32[]{:S(2)}, u32[]{:S(2)}) collective-permute-start(bf16[2,4,64,768]{3,2,1,0:T(8,128)(2,1)} %get-tuple-element.219), channel_id=1, source_target_pairs={{0,16},{4,20},{8,24},{12,28},{16,0},{20,4},{24,8},{28,12},{1,17},{... | collective-permute-start | bytes 2359304 | tf_op jit(solution)/shard_map/ppermute | solution.py:1022
  545.7 17.3 %collective-permute-start.45 = (bf16[2,4,64,768]{3,2,1,0:T(8,128)(2,1)}, bf16[2,4,64,768]{3,2,1,0:T(8,128)(2,1)S(1)}, u32[]{:S(2)}, u32[]{:S(2)}) collective-permute-start(bf16[2,4,64,768]{3,2,1,0:T(8,128)(2,1)} %get-tuple-element.220), channel_id=1, source_target_pairs={{0,8},{4,12},{8,0},{12,4},{16,24},{20,28},{24,16},{28,20},{1,9},{5... | collective-permute-start | bytes 2359304 | tf_op jit(solution)/shard_map/ppermute | solution.py:1022
  567.3 1.3 collective-permute-start.46
  568.5 3.9 collective-permute-start.47
  572.5 4.2 collective-permute-start.48
  573.3 21.2 %collective-permute-start.49 = (bf16[1,4,64,768]{3,2,1,0:T(8,128)(2,1)}, bf16[1,4,64,768]{3,2,1,0:T(8,128)(2,1)S(1)}, u32[]{:S(2)}, u32[]{:S(2)}) collective-permute-start(bf16[1,4,64,768]{3,2,1,0:T(8,128)(2,1)} %get-tuple-element.231), channel_id=1, source_target_pairs={{0,8},{4,12},{8,0},{12,4},{16,24},{20,28},{24,16},{28,20},{1,9},{5... | collective-permute-start | bytes 1179656 | tf_op jit(solution)/shard_map/ppermute | solution.py:1022
  574.8 19.7 %collective-permute-start.50 = (bf16[1,4,64,768]{3,2,1,0:T(8,128)(2,1)}, bf16[1,4,64,768]{3,2,1,0:T(8,128)(2,1)S(1)}, u32[]{:S(2)}, u32[]{:S(2)}) collective-permute-start(bf16[1,4,64,768]{3,2,1,0:T(8,128)(2,1)} %get-tuple-element.232), channel_id=1, source_target_pairs={{0,16},{4,20},{8,24},{12,28},{16,0},{20,4},{24,8},{28,12},{1,17},{... | collective-permute-start | bytes 1179656 | tf_op jit(solution)/shard_map/ppermute | solution.py:1022
  599.8 23.4 %all-to-all-start.9 = ((bf16[4,128,768]{2,1,0:T(8,128)(2,1)}), bf16[4,128,768]{2,1,0:T(8,128)(2,1)S(1)}, u32[]{:S(2)}, u32[]{:S(2)}) async-start(bf16[4,128,768]{2,1,0:T(8,128)(2,1)} %add_cols.5), calls=%async_computation.9 | async-start | bytes 1572864 | tf_op jit(solution)/shard_map/all_to_all | solution.py:1018
  (49 other events, 454.6 us)

commit v4 on v3

--- a/solution.py
+++ b/solution.py
@@ -23,7 +23,6 @@
 PADROWS = 84
 BF = jnp.bfloat16
 F32 = jnp.float32
-VMEM_LIMIT = 60 * 1024 * 1024
 SPLITS = 4
 BLOCKS = 4
 SLAB = 224
@@ -36,9 +35,9 @@
     return lax.broadcasted_iota(jnp.int32, shape, dim)
 
 
-def params(n=1):
+def params(n=1, mib=60):
     return pltpu.CompilerParams(
-        dimension_semantics=("arbitrary",) * n, vmem_limit_bytes=VMEM_LIMIT
+        dimension_semantics=("arbitrary",) * n, vmem_limit_bytes=mib * 1024 * 1024
     )
 
 
@@ -126,40 +125,6 @@
     )(jnp.asarray(np.array(sets, np.int32).reshape(-1)), offsets)
 
 
-def pack_kernel(width, weight, *refs):
-    vectors, out = refs[:-1], refs[-1]
-    cols, _, n = out.shape
-    bw = weight.shape[0]
-    rows = []
-    held = jnp.concatenate([v[...].astype(F32) for v in vectors], axis=1)
-    count = held.shape[1] // n
-    lines = [held[:, r * n : (r + 1) * n] for r in range(count)]
-    for part in range(3):
-        for r in range(count):
-            low = lines[r].astype(BF)
-            rows.append(low.astype(F32))
-            lines[r] = lines[r] - low.astype(F32)
-    pad = -(3 * count) % 16
-    rows = rows + [jnp.zeros((pad, n), F32)] * (pad > 0)
-    extra = jnp.concatenate(rows, axis=0).astype(BF)
-    for d in range(cols):
-        out[d, :bw] = weight[...]
-        out[d, bw:] = extra
-
-
-def pack_first(weight, vectors, cols):
-    bw, n = weight.shape
-    total = sum(v.shape[0] for v in vectors)
-    lines = -(-(3 * total // n) // 16) * 16
-    return pl.pallas_call(
-        partial(pack_kernel, n),
-        out_shape=jax.ShapeDtypeStruct((cols, bw + lines, n), BF),
-        compiler_params=pltpu.CompilerParams(vmem_limit_bytes=VMEM_LIMIT),
-        cost_estimate=cost(2),
-        name="pack",
-    )(weight, *[v.reshape(1, -1) for v in vectors])
-
-
 def window_at(info, index):
     at = HEAD + index * FIELDS
     return [info[at + f] for f in range(FIELDS)]
@@ -196,7 +161,9 @@
                 start = pl.multiple_of(start // 8 * 8, 8)
                 pick = as_pick(line == target_of(field, left, row + 4 * g, col) - start)
                 first = pl.multiple_of((WIN * win_row + 4 * g - top + MARGIN) * SIDE, SIDE)
-                total[pl.ds(start, 64), :] += nn_dot(pick, padded[pl.ds(first, 256), :])
+                found = nn_dot(pick, padded[pl.ds(first, 256), :])
+                total[pl.ds(start, 8), :] += found[:8]
+                total[pl.ds(pl.multiple_of(start + 8, 8), 56), :] = found[8:]
             return carry
 
         lax.fori_loop(0, per, step, 0)
@@ -325,10 +292,15 @@
 def load_rows(bufs, flip, scratch, nr, first=0):
     stride = D // nr
     for p, (g, i) in enumerate(row_places(nr, flip)):
-        cols, size, n = bufs[g].shape[1:]
+        cols, size, n = bufs[g].shape[1], bufs[g].shape[-2], bufs[g].shape[-1]
+        at = p * stride + first
         for k in range(cols):
-            at = p * stride + first
-            scratch[at : at + size, k * n : (k + 1) * n] = bufs[g][i, k]
+            if len(bufs[g].shape) == 4:
+                scratch[at : at + size, k * n : (k + 1) * n] = bufs[g][i, k]
+                continue
+            for part in range(3):
+                lane = (3 * k + part) * n
+                scratch[at : at + size, lane : lane + n] = bufs[g][i, k, part]
 
 
 def const_spec(shape):
@@ -1251,35 +1223,43 @@
     info = plan(sets, pad_offsets)
     row_order = my_row ^ jnp.arange(nr, dtype=jnp.int32)
 
-    vectors = [
-        norm1_gain,
-        norm1_bias,
-        norm2_gain,
-        norm2_bias,
-        proj_bias,
-        fc2_bias,
-        qv_bias[0],
-        qv_bias[1],
-        fc1_bias,
-    ]
     hidden = fc1_weight.shape[1]
     half = hidden // 2
     fc2_t = fc2_weight.T
-    size = 8 * width + hidden
-    qkv_stack = col_exchange(pack_first(qkv_weight.reshape(bw, 3 * width), vectors, cols))
+    qkv_stack = gather_cols(jnp.transpose(qkv_weight, (1, 0, 2)), cols)
     x_sent = spread(tokens_in, info, cols, per, rows)
     x_pieces = col_exchange(x_sent)
-    lines = 3 * size // (3 * width)
-    vecs = qkv_stack[:, bw : bw + lines].astype(F32)
-    vecs = jnp.sum(vecs.reshape(cols, 3, size), axis=1)
-    qkv_a = list(gather_rows(qkv_stack[:, : bw // 2], nr, False))[-1]
-    qkv_b = list(gather_rows(qkv_stack[:, bw // 2 : bw], nr, True))[-1]
+    qkv_stack = after(qkv_stack, x_sent)
+    hop_a = gather_rows(qkv_stack[:, :, : bw // 2], nr, False)
+    hop_b = gather_rows(qkv_stack[:, :, bw // 2 :], nr, True)
+    first_a, first_b = next(hop_a), next(hop_b)
+    g_sent = spread(after(out_grad, *first_a, *first_b), info, cols, per, rows)
+    for _ in outer_bits(nr)[1:]:
+        first_a, first_b = hop_a.send(None), hop_b.send(None)
+    qkv_a, qkv_b = hop_a.send((g_sent,)), hop_b.send((g_sent,))
+    small_args = (norm1_gain, proj_bias, fc2_bias, qv_bias, fc1_bias)
+    norm1_gain, proj_bias, fc2_bias, qv_bias, fc1_bias = lax.optimization_barrier(
+        (*small_args, *qkv_a, *qkv_b)
+    )[:5]
+    vec = jnp.concatenate(
+        [
+            norm1_gain,
+            norm1_bias,
+            norm2_gain,
+            norm2_bias,
+            proj_bias.astype(F32),
+            fc2_bias.astype(F32),
+            qv_bias[0].astype(F32),
+            qv_bias[1].astype(F32),
+            fc1_bias.astype(F32),
+        ]
+    )
+    vecs = [vec] + [lax.ppermute(vec, "col", [(i, i ^ k) for i in range(cols)]) for k in range(1, cols)]
+    vecs = pick_rows(jnp.stack(vecs), me ^ jnp.arange(cols, dtype=jnp.int32))
     wide0 = jnp.concatenate([fc1_weight[:, :half], proj_weight.T, fc2_t[:, :half]], axis=1)
     wide1 = jnp.concatenate([fc1_weight[:, half:], fc2_t[:, half:]], axis=1)
     stack0 = gather_cols(after(wide0, x_pieces, *qkv_a, *qkv_b), cols)
     first = half + width
-    g_sent = spread(after(out_grad, x_sent), info, cols, per, rows)
-
     features = vecs[:, : 6 * width].reshape(cols, 6, width // bw, bw)
     features = features.transpose(0, 2, 1, 3).reshape(nr, 6, bw)
     features = pick_rows(features, row_order).transpose(1, 0, 2).reshape(6, 1, D)
@@ -1296,12 +1276,9 @@
     shifts = jnp.asarray(shifts_np)
     onehot = jnp.asarray(onehot_np, BF)
     tables = table_matrix(table_height, table_width)
-    stack0 = after(stack0, n1)
-    hops0 = [gather_rows(stack0[:, :, :first], nr, False), gather_rows(stack0[:, :, first:], nr, True)]
     stack1 = gather_cols(after(wide1, stack0), cols)
-    bufs0 = [next(hop) for hop in hops0]
     held = ()
-    arrived = [stack0]
+    arrived = []
     bits = outer_bits(nr)
     for part, base in enumerate(range(0, cols, cols // SPLITS)):
         held = attend(
@@ -1319,11 +1296,18 @@
         att = held[0]
         arrived = []
         if part == 0:
+            stack0 = after(stack0, att)
+            hops0 = [
+                gather_rows(stack0[:, :, :first], nr, False),
+                gather_rows(stack0[:, :, first:], nr, True),
+            ]
+            bufs0 = [next(hop) for hop in hops0]
+        if part == 1:
             stack1 = after(stack1, att)
             g_pieces = col_exchange(after(g_sent, stack1))
             bufs0 = [hop.send((att, *bufs0[0], *bufs0[1])) for hop in hops0]
             arrived = [stack1]
-        if part == 2:
+        if part == 3:
             for _ in range(len(bits) - 2):
                 bufs0 = [hop.send(None) for hop in hops0]
             bufs0 = [hop.send((att, *bufs0[0], *bufs0[1])) for hop in hops0]
@@ -1333,10 +1317,9 @@
                 gather_rows(stack1[:, :, half:], nr, True),
             ]
             bufs1 = [next(hop) for hop in hops1]
-        if part == 3:
-            bufs1 = [hop.send((att, *bufs1[0], *bufs1[1])) for hop in hops1]
     att, exps, inv = held
     resid, n2 = proj_norm(bufs0[0], att, x_full, bias_p, gain2, bias2, cols, rows, nr)
+    bufs1 = [hop.send((n2, *bufs1[0], *bufs1[1])) for hop in hops1]
     g_full = join(g_pieces, info, cols, rows, nr)
     fc1_bufs, fc2_bufs = [bufs0[0]], [bufs0[1]]
 

time: 635 us -> 614 us (0.967)
  waiting for transfers between devices: 102 us -> 91.7 us
  local copies, waits for them, and re-layouts: 42.6 us -> 32.4 us
    all_to_all x10, waiting for transfers between devices: 56.9 us -> 34.3 us  [col_exchange(): return lax.all_to_all(values, 'col', 0, 0, tiled=True)]
    ppermute x0 -> x3, waiting for transfers between devices: none -> 9.25 us  [body(): lax.ppermute(vec, 'col', [(i, i ^ k) for i in range(cols)])]
    unnamed x117 -> x136, local copies, waits for them, and re-layouts: 21.3 us -> 17 us
  transfers between devices with their start and end apart: 61 -> 64, of which waited for: 19 -> 26; matrix products, arithmetic and copies ran while one was open for 7% -> 6% of each run, Pallas kernels for 55% -> 56%
where the time goes in v4:
time: 614 us; the launch traced here: 604 us
  Pallas kernels  364 us (59%)
  waiting for transfers between devices  91.7 us (15%)
  starting transfers between devices  90.1 us (15%)
  local copies, waits for them, and re-layouts  32.4 us (5%)
  other arithmetic  23.2 us (4%)
    pallas_call x4, Pallas kernels, attend_back(): pl.pallas_call(partial(attend_back_kernel, width, len(held)), out_shape=[...  73.7 us
    pallas_call x4, Pallas kernels, attend(): pl.pallas_call(partial(attend_kernel, width, len(held)), out_shape=[jax.S...  56.2 us
    pallas_call x2, Pallas kernels, mlp_grads(): pl.pallas_call(partial(mlp_grads_kernel, nr), out_shape=[act, act, half,...  54.4 us
    all_to_all x10, starting transfers between devices, col_exchange(): return lax.all_to_all(values, 'col', 0, 0, tiled=True)  43.5 us
    ppermute x45, waiting for transfers between devices, row_swap(): return lax.ppermute(values, 'row', [(i, i ^ bit) for i in range(nr)])  42.8 us
    all_to_all x10, waiting for transfers between devices, col_exchange(): return lax.all_to_all(values, 'col', 0, 0, tiled=True)  34.3 us
    ppermute x45, starting transfers between devices, row_swap(): return lax.ppermute(values, 'row', [(i, i ^ bit) for i in range(nr)])  33.2 us
    pallas_call x8, Pallas kernels, reduce_weight(): pl.pallas_call(partial(add_kernel, sizes), out_shape=[jax.ShapeDtypeStruc...  22 us
  transfers between devices with their start and end apart: 64, of which 26 were waited for; matrix products, arithmetic and copies ran while one was open for 6% of the time, Pallas kernels for 56%

profile of v4, /device:TPU:0, one launch (start us, length us, event | category | flops | bytes accessed | tf_op | source)
XLA Modules:
  0.0 603.9 jit_solution(4347917769803998726)
XLA Ops:
  2.5 6.3 %all-to-all-start.1 = ((bf16[4,3,128,256]{3,2,1,0:T(8,128)(2,1)}), bf16[4,3,128,256]{3,2,1,0:T(8,128)(2,1)S(1)}, u32[]{:S(2)}, u32[]{:S(2)}) async-start(bf16[4,3,128,256]{3,2,1,0:T(8,128)(2,1)} %broadcast_in_dim.162), calls=%async_computation.1 | async-start | bytes 1572864 | tf_op jit(solution)/shard_map/all_to_all | solution.py:990
  8.8 2.1 plan.1.info
  11.6 10.5 %spread.2 = bf16[4,1088,256]{2,1,0:T(8,128)(2,1)} custom-call(s32[201]{0:T(256)} %plan.1.info, bf16[4096,256]{1,0:T(8,128)(2,1)} %x_ref.1), custom_call_target="tpu_custom_call" | custom-call | flops 7699999744 | bytes 7000000 | tf_op jit(solution)/shard_map/spread/pallas_call | solution.py:175
  22.1 6.9 %all-to-all-done.1 = bf16[4,3,128,256]{3,2,1,0:T(8,128)(2,1)S(1)} async-done(((bf16[4,3,128,256]{3,2,1,0:T(8,128)(2,1)}), bf16[4,3,128,256]{3,2,1,0:T(8,128)(2,1)S(1)}, u32[]{:S(2)}, u32[]{:S(2)}) %all-to-all-start.1) | async-done | bytes 786464 | tf_op jit(solution)/shard_map/all_to_all | solution.py:990
  28.9 3.6 all-to-all-start
  40.3 3.5 collective-permute-done
  43.8 2.1 pad_maximum_fusion.4.refs_1_.refs_0_
  51.5 10.5 %spread.3 = bf16[4,1088,256]{2,1,0:T(8,128)(2,1)} custom-call(s32[201]{0:T(256)} %plan.1.info, bf16[4096,256]{1,0:T(8,128)(2,1)} %x_ref.2), custom_call_target="tpu_custom_call" | custom-call | flops 7699999744 | bytes 7000000 | tf_op jit(solution)/shard_map/spread/pallas_call | solution.py:175
  63.8 3.2 collective-permute-done.5.refs_6_.refs_5_
  67.2 2.3 collective-permute-done.7.refs_8_.refs_7_
  69.7 3.3 collective-permute-start.10
  75.4 8.7 %collective-permute-done.9 = f32[3072]{0:T(1024)S(1)} collective-permute-done((f32[3072]{0:T(1024)S(1)}, f32[3072]{0:T(1024)S(1)}, u32[]{:S(2)}, u32[]{:S(2)}) %collective-permute-start.9) | collective-permute-done | bytes 12320 | tf_op jit(solution)/shard_map/ppermute | solution.py:1257
  87.7 3.5 all-to-all-start.2
  91.3 14.9 %norm_qkv.1 = (bf16[1088,1024]{1,0:T(8,128)(2,1)}, bf16[1088,1024]{1,0:T(8,128)(2,1)}, bf16[1088,3072]{1,0:T(8,128)(2,1)}) custom-call(s32[201]{0:T(256)} %plan.1.info, bf16[4,1088,256]{2,1,0:T(8,128)(2,1)} %copy-done.9, bf16[2,4,3,64,256]{4,3,2,1,0:T(8,128)(2,1)} %pad_maximum_fusion.4.refs_1_.refs_0_, ...), custom_call_target="tpu_custom_call" | custom-call | flops 20899999744 | bytes 19000000 | tf_op jit(solution)/shard_map/norm_qkv/pallas_call | solution.py:339
  106.2 14.0 %attend.4 = (bf16[1088,1024]{1,0:T(8,128)(2,1)}, bf16[16,1400,256]{2,1,0:T(8,128)(2,1)}, f32[1400,1024]{1,0:T(8,128)}) custom-call(s32[201]{0:T(256)} %plan.1.info, bf16[1088,3072]{1,0:T(8,128)(2,1)} %get-tuple-element.211.qkv, bf16[128,128]{1,0:T(8,128)(2,1)} %pad_maximum_fusion.12.tables, s32[200,128]{1,0:T(8,128)} %constant.51.clone.shifts, ...), custom_call_target="tpu_custom_call" | custom-call | flops 15399999488 | bytes 14000000 | tf_op jit(solution)/shard_map/attend/pallas_call | solution.py:804
  127.3 3.5 all-to-all-start.3
  130.8 14.0 %attend.5 = (bf16[1088,1024]{1,0:T(8,128)(2,1)}, bf16[16,1400,256]{2,1,0:T(8,128)(2,1)}, f32[1400,1024]{1,0:T(8,128)}) custom-call(s32[201]{0:T(256)} %plan.1.info, bf16[1088,3072]{1,0:T(8,128)(2,1)} %get-tuple-element.211.qkv, bf16[128,128]{1,0:T(8,128)(2,1)} %pad_maximum_fusion.12.tables, ...), custom_call_target="tpu_custom_call", output_to_operand_aliasing={{0}: (5, {}), {1}: (6, {}), {2}: (7, {})} | custom-call | flops 15399999488 | bytes 14000000 | tf_op jit(solution)/shard_map/attend/pallas_call | solution.py:804
  146.7 2.1 pad_maximum_fusion.1.refs_4_.refs_0_
  149.3 6.1 %all-to-all-done.3 = bf16[4,128,1024]{2,1,0:T(8,128)(2,1)S(1)} async-done(((bf16[4,128,1024]{2,1,0:T(8,128)(2,1)}), bf16[4,128,1024]{2,1,0:T(8,128)(2,1)S(1)}, u32[]{:S(2)}, u32[]{:S(2)}) %all-to-all-start.3) | async-done | bytes 1048608 | tf_op jit(solution)/shard_map/all_to_all | solution.py:990
  155.4 3.8 all-to-all-start.4
  159.3 14.0 %attend.6 = (bf16[1088,1024]{1,0:T(8,128)(2,1)}, bf16[16,1400,256]{2,1,0:T(8,128)(2,1)}, f32[1400,1024]{1,0:T(8,128)}) custom-call(s32[201]{0:T(256)} %plan.1.info, bf16[1088,3072]{1,0:T(8,128)(2,1)} %get-tuple-element.211.qkv, bf16[128,128]{1,0:T(8,128)(2,1)} %pad_maximum_fusion.12.tables, ...), custom_call_target="tpu_custom_call", output_to_operand_aliasing={{0}: (5, {}), {1}: (6, {}), {2}: (7, {})} | custom-call | flops 15399999488 | bytes 14000000 | tf_op jit(solution)/shard_map/attend/pallas_call | solution.py:804
  173.3 14.0 %attend.7 = (bf16[1088,1024]{1,0:T(8,128)(2,1)}, bf16[16,1400,256]{2,1,0:T(8,128)(2,1)}, f32[1400,1024]{1,0:T(8,128)}) custom-call(s32[201]{0:T(256)} %plan.1.info, bf16[1088,3072]{1,0:T(8,128)(2,1)} %get-tuple-element.211.qkv, bf16[128,128]{1,0:T(8,128)(2,1)} %pad_maximum_fusion.12.tables, ...), custom_call_target="tpu_custom_call", output_to_operand_aliasing={{0}: (5, {}), {1}: (6, {}), {2}: (7, {})} | custom-call | flops 15399999488 | bytes 14000000 | tf_op jit(solution)/shard_map/attend/pallas_call | solution.py:804
  191.2 7.9 %proj_norm.1 = (f32[1088,1024]{1,0:T(8,128)}, bf16[1088,1024]{1,0:T(8,128)(2,1)}) custom-call(bf16[2,4,128,768]{3,2,1,0:T(8,128)(2,1)} %pad_maximum_fusion.refs_0_, bf16[2,4,128,768]{3,2,1,0:T(8,128)(2,1)} %collective-permute-done.14.refs_1_, bf16[2,4,128,768]{3,2,1,0:T(8,128)(2,1)} %collective-permute-done.18.refs_2_, ...), custom_call_target="tpu_custom_call" | custom-call | flops 12099999744 | bytes 11000000 | tf_op jit(solution)/shard_map/proj_norm/pallas_call | solution.py:412
  199.1 4.5 collective-permute-done.17
  203.5 2.3 pad_maximum_fusion.2.refs_4_
  211.1 4.8 join.1.refs_9_.refs_11_
  215.9 27.0 %mlp_grads.2 = (bf16[1088,2048]{1,0:T(8,128)(2,1)}, bf16[1088,2048]{1,0:T(8,128)(2,1)}, bf16[4,4,128,1024]{3,2,1,0:T(8,128)(2,1)}, bf16[4,4,128,1024]{3,2,1,0:T(8,128)(2,1)}, f32[4,8,512]{2,1,0:T(8,128)}) custom-call(bf16[2,4,128,768]{3,2,1,0:T(8,128)(2,1)} %pad_maximum_fusion.refs_0_, bf16[2,4,128,768]{3,2,1,0:T(8,128)(2,1)} %collective-permute-done.14.refs_1_, ...), custom_call_target="tpu_custom_call" | custom-call | flops 41799999488 | bytes 38000000 | tf_op jit(solution)/shard_map/mlp_grads/pallas_call | solution.py:469
  244.7 2.2 collective-permute-done.24.refs_7_
  246.9 2.0 collective-permute-done.26.refs_3_.refs_7_
  249.9 27.4 %mlp_grads.3 = (bf16[1088,2048]{1,0:T(8,128)(2,1)}, bf16[1088,2048]{1,0:T(8,128)(2,1)}, bf16[4,4,128,1024]{3,2,1,0:T(8,128)(2,1)}, bf16[4,4,128,1024]{3,2,1,0:T(8,128)(2,1)}, f32[4,8,512]{2,1,0:T(8,128)}) custom-call(bf16[2,4,128,512]{3,2,1,0:T(8,128)(2,1)} %copy-done.13, bf16[2,4,128,512]{3,2,1,0:T(8,128)(2,1)} %collective-permute-done.22.refs_1_.refs_5_, ...), custom_call_target="tpu_custom_call" | custom-call | flops 41799999488 | bytes 38000000 | tf_op jit(solution)/shard_map/mlp_grads/pallas_call | solution.py:469
  280.2 3.4 add_rows.8
  285.3 17.6 %block_rows.1 = bf16[4,1088,256]{2,1,0:T(8,128)(2,1)} custom-call(s32[201]{0:T(256)} %plan.1.info, bf16[2,4,128,512]{3,2,1,0:T(8,128)(2,1)} %pad_maximum_fusion.1.refs_4_.refs_0_, bf16[2,4,128,512]{3,2,1,0:T(8,128)(2,1)} %collective-permute-done.13.refs_5_.refs_1_, bf16[2,4,128,512]{3,2,1,0:T(8,128)(2,1)} %collective-permute-done.15.refs_6_.refs_2_, ...), custom_call_target="tpu_custom_call" | custom-call | flops 28600000512 | bytes 26000000 | tf_op jit(solution)/shard_map/block_rows/pallas_call | solution.py:516
  302.9 5.2 all-to-all-start.5
  311.2 3.0 add_rows.9
  316.0 3.3 add_rows.10
  321.5 19.4 %mlp_back.1 = (f32[1088,1024]{1,0:T(8,128)}, bf16[1088,1024]{1,0:T(8,128)(2,1)}, f32[4,8,1024]{2,1,0:T(8,128)}) custom-call(bf16[2,4,128,768]{3,2,1,0:T(8,128)(2,1)} %pad_maximum_fusion.refs_0_, bf16[2,4,128,768]{3,2,1,0:T(8,128)(2,1)} %collective-permute-done.14.refs_1_, bf16[2,4,128,768]{3,2,1,0:T(8,128)(2,1)} %collective-permute-done.18.refs_2_, ...), custom_call_target="tpu_custom_call" | custom-call | flops 30799998976 | bytes 28000000 | tf_op jit(solution)/shard_map/mlp_back/pallas_call | solution.py:562
  342.2 9.6 %proj_back.1 = (bf16[1088,1024]{1,0:T(8,128)(2,1)}, bf16[4,4,128,256]{3,2,1,0:T(8,128)(2,1)}, bf16[4,4,128,256]{3,2,1,0:T(8,128)(2,1)}) custom-call(bf16[2,4,128,768]{3,2,1,0:T(8,128)(2,1)} %pad_maximum_fusion.refs_0_, bf16[2,4,128,768]{3,2,1,0:T(8,128)(2,1)} %collective-permute-done.14.refs_1_, bf16[2,4,128,768]{3,2,1,0:T(8,128)(2,1)} %collective-permute-done.18.refs_2_, ...), custom_call_target="tpu_custom_call" | custom-call | flops 12099999744 | bytes 11000000 | tf_op jit(solution)/shard_map/proj_back/pallas_call | solution.py:594
  351.9 18.4 %attend_back.4 = (bf16[1088,3072]{1,0:T(8,128)(2,1)}, f32[128,256]{1,0:T(8,128)}, f32[8,768]{1,0:T(8,128)}) custom-call(s32[201]{0:T(256)} %plan.1.info, bf16[1088,3072]{1,0:T(8,128)(2,1)} %get-tuple-element.211.qkv, bf16[16,1400,256]{2,1,0:T(8,128)(2,1)} %get-tuple-element.179.exps, f32[1400,1024]{1,0:T(8,128)} %get-tuple-element.180.inv, ...), custom_call_target="tpu_custom_call" | custom-call | flops 14300000256 | bytes 13000000 | tf_op jit(solution)/shard_map/attend_back/pallas_call | solution.py:939
  372.3 3.0 add_rows.11
  378.1 2.0 add_rows.12
  381.3 3.7 add_cols.3
  385.1 5.1 all-to-all-start.6
  391.3 18.5 %attend_back.5 = (bf16[1088,3072]{1,0:T(8,128)(2,1)}, f32[128,256]{1,0:T(8,128)}, f32[8,768]{1,0:T(8,128)}) custom-call(s32[201]{0:T(256)} %plan.1.info, bf16[1088,3072]{1,0:T(8,128)(2,1)} %get-tuple-element.211.qkv, bf16[16,1400,256]{2,1,0:T(8,128)(2,1)} %get-tuple-element.179.exps, ...), custom_call_target="tpu_custom_call", output_to_operand_aliasing={{0}: (9, {})} | custom-call | flops 14300000256 | bytes 13000000 | tf_op jit(solution)/shard_map/attend_back/pallas_call | solution.py:939
  413.5 18.4 %attend_back.6 = (bf16[1088,3072]{1,0:T(8,128)(2,1)}, f32[128,256]{1,0:T(8,128)}, f32[8,768]{1,0:T(8,128)}) custom-call(s32[201]{0:T(256)} %plan.1.info, bf16[1088,3072]{1,0:T(8,128)(2,1)} %get-tuple-element.211.qkv, bf16[16,1400,256]{2,1,0:T(8,128)(2,1)} %get-tuple-element.179.exps, ...), custom_call_target="tpu_custom_call", output_to_operand_aliasing={{0}: (9, {})} | custom-call | flops 14300000256 | bytes 13000000 | tf_op jit(solution)/shard_map/attend_back/pallas_call | solution.py:939
  432.6 4.1 add_cols.4
  436.7 4.8 all-to-all-start.7
  441.6 18.4 %attend_back.7 = (bf16[1088,3072]{1,0:T(8,128)(2,1)}, f32[128,256]{1,0:T(8,128)}, f32[8,768]{1,0:T(8,128)}) custom-call(s32[201]{0:T(256)} %plan.1.info, bf16[1088,3072]{1,0:T(8,128)(2,1)} %get-tuple-element.211.qkv, bf16[16,1400,256]{2,1,0:T(8,128)(2,1)} %get-tuple-element.179.exps, ...), custom_call_target="tpu_custom_call", output_to_operand_aliasing={{0}: (9, {})} | custom-call | flops 14300000256 | bytes 13000000 | tf_op jit(solution)/shard_map/attend_back/pallas_call | solution.py:939
  460.1 12.7 %qkv_grad.1 = (bf16[4,4,128,768]{3,2,1,0:T(8,128)(2,1)}, bf16[4,4,128,768]{3,2,1,0:T(8,128)(2,1)}) custom-call(bf16[1088,1024]{1,0:T(8,128)(2,1)} %get-tuple-element.213.n1, bf16[1088,3072]{1,0:T(8,128)(2,1)} %get-tuple-element.235.dqkv.refs_8_), custom_call_target="tpu_custom_call" | custom-call | flops 15399999488 | bytes 14000000 | tf_op jit(solution)/shard_map/qkv_grad/pallas_call | solution.py:615
  474.0 2.1 collective-permute-start.40
  476.0 2.4 collective-permute-start.41
  478.5 10.0 %collect.2 = bf16[4096,256]{1,0:T(8,128)(2,1)} custom-call(s32[201]{0:T(256)} %plan.1.info, bf16[4,1088,256]{2,1,0:T(8,128)(2,1)} %all-to-all-done.5.pieces), custom_call_target="tpu_custom_call" | custom-call | flops 8800000000 | bytes 8000000 | tf_op jit(solution)/shard_map/collect/pallas_call | solution.py:225
  490.6 2.8 add_rows.14
  493.4 16.3 %input_back.1 = (bf16[4,1088,256]{2,1,0:T(8,128)(2,1)}, f32[2,8,1024]{2,1,0:T(8,128)}) custom-call(s32[201]{0:T(256)} %plan.1.info, bf16[2,4,3,64,256]{4,3,2,1,0:T(8,128)(2,1)} %pad_maximum_fusion.4.refs_1_.refs_0_, bf16[2,4,3,64,256]{4,3,2,1,0:T(8,128)(2,1)} %collective-permute-done.1.refs_2_.refs_1_, ...), custom_call_target="tpu_custom_call" | custom-call | flops 27499999232 | bytes 25000000 | tf_op jit(solution)/shard_map/input_back/pallas_call | solution.py:652
  511.8 3.3 collective-permute-start.45
  516.7 3.8 collective-permute-done.46
  520.5 3.6 all-to-all-start.8
  526.5 15.3 %collective-permute-done.47.refs_2_ = bf16[2,4,64,768]{3,2,1,0:T(8,128)(2,1)S(1)} collective-permute-done((bf16[2,4,64,768]{3,2,1,0:T(8,128)(2,1)}, bf16[2,4,64,768]{3,2,1,0:T(8,128)(2,1)S(1)}, u32[]{:S(2)}, u32[]{:S(2)}) %collective-permute-start.47) | collective-permute-done | bytes 786464 | tf_op jit(solution)/shard_map/ppermute | solution.py:994
  543.6 2.6 add_rows.15
  549.1 2.4 collective-permute-done.50
  558.8 14.7 %all-to-all-done.8.pieces = bf16[4,1088,256]{2,1,0:T(8,128)(2,1)S(1)} async-done(((bf16[4,1088,256]{2,1,0:T(8,128)(2,1)}), bf16[4,1088,256]{2,1,0:T(8,128)(2,1)S(1)}, u32[]{:S(2)}, u32[]{:S(2)}) %all-to-all-start.8) | async-done | bytes 2228256 | tf_op jit(solution)/shard_map/all_to_all | solution.py:990
  575.7 3.1 add_cols.5
  578.8 3.9 all-to-all-start.9
  587.3 10.8 %collect.3 = f32[4096,256]{1,0:T(8,128)} custom-call(s32[201]{0:T(256)} %plan.1.info, bf16[4,1088,256]{2,1,0:T(8,128)(2,1)} %copy-done.10), custom_call_target="tpu_custom_call" | custom-call | flops 8800000000 | bytes 8000000 | tf_op jit(solution)/shard_map/collect/pallas_call | solution.py:225
  598.1 4.2 all-to-all-done.9
  (339 shorter events, 98.6 us)
Async XLA Ops:
  2.5 26.4 %all-to-all-start.1 = ((bf16[4,3,128,256]{3,2,1,0:T(8,128)(2,1)}), bf16[4,3,128,256]{3,2,1,0:T(8,128)(2,1)S(1)}, u32[]{:S(2)}, u32[]{:S(2)}) async-start(bf16[4,3,128,256]{3,2,1,0:T(8,128)(2,1)} %broadcast_in_dim.162), calls=%async_computation.1 | async-start | bytes 1572864 | tf_op jit(solution)/shard_map/all_to_all | solution.py:990
  28.9 57.0 %all-to-all-start = ((bf16[4,1088,256]{2,1,0:T(8,128)(2,1)}), bf16[4,1088,256]{2,1,0:T(8,128)(2,1)S(1)}, u32[]{:S(2)}, u32[]{:S(2)}) async-start(bf16[4,1088,256]{2,1,0:T(8,128)(2,1)} %spread.2), calls=%async_computation | async-start | bytes 4456448 | tf_op jit(solution)/shard_map/all_to_all | solution.py:990
  33.4 10.4 %collective-permute-start = (bf16[1,4,3,64,256]{4,3,2,1,0:T(8,128)(2,1)}, bf16[1,4,3,64,256]{4,3,2,1,0:T(8,128)(2,1)}, u32[]{:S(2)}, u32[]{:S(2)}) collective-permute-start(bf16[1,4,3,64,256]{4,3,2,1,0:T(8,128)(2,1)} %get-tuple-element.339), channel_id=1, source_target_pairs={{0,8},{4,12},{8,0},{12,4},{16,24},{20,28},{24,16},{28,20},{1,9},{5... | collective-permute-start | bytes 1179656 | tf_op jit(solution)/shard_map/ppermute | solution.py:994
  35.9 11.6 %collective-permute-start.2 = (bf16[1,4,3,64,256]{4,3,2,1,0:T(8,128)(2,1)S(1)}, bf16[1,4,3,64,256]{4,3,2,1,0:T(8,128)(2,1)}, u32[]{:S(2)}, u32[]{:S(2)}) collective-permute-start(bf16[1,4,3,64,256]{4,3,2,1,0:T(8,128)(2,1)S(1)} %get-tuple-element.338), channel_id=1, source_target_pairs={{0,16},{4,20},{8,24},{12,28},{16,0},{20,4},{24,8},{28,12},{1,17},{... | collective-permute-start | bytes 1179656 | tf_op jit(solution)/shard_map/ppermute | solution.py:994
  45.9 17.9 %collective-permute-start.1 = (bf16[2,4,3,64,256]{4,3,2,1,0:T(8,128)(2,1)}, bf16[2,4,3,64,256]{4,3,2,1,0:T(8,128)(2,1)}, u32[]{:S(2)}, u32[]{:S(2)}) collective-permute-start(bf16[2,4,3,64,256]{4,3,2,1,0:T(8,128)(2,1)} %pad_maximum_fusion.4.refs_1_.refs_0_), channel_id=1, source_target_pairs={{0,16},{4,20},{8,24},{12,28},{16,0},{20,4},{24,8},{28,12},{1,17},{... | collective-permute-start | bytes 2359304 | tf_op jit(solution)/shard_map/ppermute | solution.py:994
  49.4 17.6 %collective-permute-start.5 = (bf16[2,4,3,64,256]{4,3,2,1,0:T(8,128)(2,1)}, bf16[2,4,3,64,256]{4,3,2,1,0:T(8,128)(2,1)}, u32[]{:S(2)}, u32[]{:S(2)}) collective-permute-start(bf16[2,4,3,64,256]{4,3,2,1,0:T(8,128)(2,1)} %pad_maximum_fusion.5.refs_5_.refs_4_), channel_id=1, source_target_pairs={{0,8},{4,12},{8,0},{12,4},{16,24},{20,28},{24,16},{28,20},{1,9},{5... | collective-permute-start | bytes 2359304 | tf_op jit(solution)/shard_map/ppermute | solution.py:994
  51.0 16.2 %collective-permute-start.3 = (bf16[2,4,3,64,256]{4,3,2,1,0:T(8,128)(2,1)}, bf16[2,4,3,64,256]{4,3,2,1,0:T(8,128)(2,1)}, u32[]{:S(2)}, u32[]{:S(2)}) collective-permute-start(bf16[2,4,3,64,256]{4,3,2,1,0:T(8,128)(2,1)} %pad_maximum_fusion.4.refs_1_.refs_0_), channel_id=1, source_target_pairs={{0,4},{4,0},{8,12},{12,8},{16,20},{20,16},{24,28},{28,24},{1,5},{5... | collective-permute-start | bytes 2359304 | tf_op jit(solution)/shard_map/ppermute | solution.py:994
  51.0 16.2 %collective-permute-start.6 = (bf16[2,4,3,64,256]{4,3,2,1,0:T(8,128)(2,1)}, bf16[2,4,3,64,256]{4,3,2,1,0:T(8,128)(2,1)}, u32[]{:S(2)}, u32[]{:S(2)}) collective-permute-start(bf16[2,4,3,64,256]{4,3,2,1,0:T(8,128)(2,1)} %pad_maximum_fusion.5.refs_5_.refs_4_), channel_id=1, source_target_pairs={{0,4},{4,0},{8,12},{12,8},{16,20},{20,16},{24,28},{28,24},{1,5},{5... | collective-permute-start | bytes 2359304 | tf_op jit(solution)/shard_map/ppermute | solution.py:994
  63.8 3.4 collective-permute-start.4
  67.0 2.5 collective-permute-start.7
  69.7 5.7 collective-permute-start.10
  73.0 11.1 %collective-permute-start.9 = (f32[3072]{0:T(1024)S(1)}, f32[3072]{0:T(1024)S(1)}, u32[]{:S(2)}, u32[]{:S(2)}) collective-permute-start(f32[3072]{0:T(1024)S(1)} %constant_dynamic-update-slice_fusion.6), channel_id=1, source_target_pairs={{0,2},{1,3},{2,0},{3,1},{4,6},{5,7},{6,4},{7,5},{8,10},{9,11},{10,... | collective-permute-start | bytes 36872 | tf_op jit(solution)/shard_map/ppermute | solution.py:1257
  73.0 11.1 %collective-permute-start.8 = (f32[3072]{0:T(1024)S(1)}, f32[3072]{0:T(1024)S(1)}, u32[]{:S(2)}, u32[]{:S(2)}) collective-permute-start(f32[3072]{0:T(1024)S(1)} %constant_dynamic-update-slice_fusion.6), channel_id=1, source_target_pairs={{0,1},{1,0},{2,3},{3,2},{4,5},{5,4},{6,7},{7,6},{8,9},{9,8},{10,11... | collective-permute-start | bytes 36872 | tf_op jit(solution)/shard_map/ppermute | solution.py:1257
  87.7 34.3 %all-to-all-start.2 = ((bf16[4,128,1280]{2,1,0:T(8,128)(2,1)}), bf16[4,128,1280]{2,1,0:T(8,128)(2,1)S(1)}, u32[]{:S(2)}, u32[]{:S(2)}) async-start(bf16[4,128,1280]{2,1,0:T(8,128)(2,1)} %broadcast_in_dim.165), calls=%async_computation.2 | async-start | bytes 2621440 | tf_op jit(solution)/shard_map/all_to_all | solution.py:990
  123.0 21.9 %collective-permute-start.11 = (bf16[1,4,128,512]{3,2,1,0:T(8,128)(2,1)}, bf16[1,4,128,512]{3,2,1,0:T(8,128)(2,1)S(1)}, u32[]{:S(2)}, u32[]{:S(2)}) collective-permute-start(bf16[1,4,128,512]{3,2,1,0:T(8,128)(2,1)} %slice_bitcast_fusion.3), channel_id=1, source_target_pairs={{0,16},{4,20},{8,24},{12,28},{16,0},{20,4},{24,8},{28,12},{1,17},{... | collective-permute-start | bytes 1572872 | tf_op jit(solution)/shard_map/ppermute | solution.py:994
  124.6 20.3 %collective-permute-start.12 = (bf16[1,4,128,768]{3,2,1,0:T(8,128)(2,1)S(1)}, bf16[1,4,128,768]{3,2,1,0:T(8,128)(2,1)S(1)}, u32[]{:S(2)}, u32[]{:S(2)}) collective-permute-start(bf16[1,4,128,768]{3,2,1,0:T(8,128)(2,1)S(1)} %slice_bitcast_fusion), channel_id=1, source_target_pairs={{0,8},{4,12},{8,0},{12,4},{16,24},{20,28},{24,16},{28,20},{1,9},{5... | collective-permute-start | bytes 2359304 | tf_op jit(solution)/shard_map/ppermute | solution.py:994
  127.3 28.1 %all-to-all-start.3 = ((bf16[4,128,1024]{2,1,0:T(8,128)(2,1)}), bf16[4,128,1024]{2,1,0:T(8,128)(2,1)S(1)}, u32[]{:S(2)}, u32[]{:S(2)}) async-start(bf16[4,128,1024]{2,1,0:T(8,128)(2,1)} %broadcast_in_dim.175), calls=%async_computation.3 | async-start | bytes 2097152 | tf_op jit(solution)/shard_map/all_to_all | solution.py:990
  146.2 41.2 %collective-permute-start.14 = (bf16[2,4,128,768]{3,2,1,0:T(8,128)(2,1)}, bf16[2,4,128,768]{3,2,1,0:T(8,128)(2,1)}, u32[]{:S(2)}, u32[]{:S(2)}) collective-permute-start(bf16[2,4,128,768]{3,2,1,0:T(8,128)(2,1)} %pad_maximum_fusion.refs_0_), channel_id=1, source_target_pairs={{0,16},{4,20},{8,24},{12,28},{16,0},{20,4},{24,8},{28,12},{1,17},{... | collective-permute-start | bytes 4718600 | tf_op jit(solution)/shard_map/ppermute | solution.py:994
  146.7 43.8 %collective-permute-start.18 = (bf16[2,4,128,768]{3,2,1,0:T(8,128)(2,1)}, bf16[2,4,128,768]{3,2,1,0:T(8,128)(2,1)}, u32[]{:S(2)}, u32[]{:S(2)}) collective-permute-start(bf16[2,4,128,768]{3,2,1,0:T(8,128)(2,1)} %pad_maximum_fusion.refs_0_), channel_id=1, source_target_pairs={{0,4},{4,0},{8,12},{12,8},{16,20},{20,16},{24,28},{28,24},{1,5},{5... | collective-permute-start | bytes 4718600 | tf_op jit(solution)/shard_map/ppermute | solution.py:994
  148.8 38.6 %collective-permute-start.13 = (bf16[2,4,128,512]{3,2,1,0:T(8,128)(2,1)}, bf16[2,4,128,512]{3,2,1,0:T(8,128)(2,1)}, u32[]{:S(2)}, u32[]{:S(2)}) collective-permute-start(bf16[2,4,128,512]{3,2,1,0:T(8,128)(2,1)} %pad_maximum_fusion.1.refs_4_.refs_0_), channel_id=1, source_target_pairs={{0,8},{4,12},{8,0},{12,4},{16,24},{20,28},{24,16},{28,20},{1,9},{5... | collective-permute-start | bytes 3145736 | tf_op jit(solution)/shard_map/ppermute | solution.py:994
  155.4 54.3 %all-to-all-start.4 = ((bf16[4,1088,256]{2,1,0:T(8,128)(2,1)}), bf16[4,1088,256]{2,1,0:T(8,128)(2,1)S(1)}, u32[]{:S(2)}, u32[]{:S(2)}) async-start(bf16[4,1088,256]{2,1,0:T(8,128)(2,1)} %spread.3), calls=%async_computation.4 | async-start | bytes 4456448 | tf_op jit(solution)/shard_map/all_to_all | solution.py:990
  187.4 3.8 collective-permute-start.19
  188.1 27.8 %collective-permute-start.15 = (bf16[2,4,128,512]{3,2,1,0:T(8,128)(2,1)}, bf16[2,4,128,512]{3,2,1,0:T(8,128)(2,1)}, u32[]{:S(2)}, u32[]{:S(2)}) collective-permute-start(bf16[2,4,128,512]{3,2,1,0:T(8,128)(2,1)} %pad_maximum_fusion.1.refs_4_.refs_0_), channel_id=1, source_target_pairs={{0,4},{4,0},{8,12},{12,8},{16,20},{20,16},{24,28},{28,24},{1,5},{5... | collective-permute-start | bytes 3145736 | tf_op jit(solution)/shard_map/ppermute | solution.py:994
  189.5 14.1 %collective-permute-start.17 = (bf16[1,4,128,512]{3,2,1,0:T(8,128)(2,1)}, bf16[1,4,128,512]{3,2,1,0:T(8,128)(2,1)S(1)}, u32[]{:S(2)}, u32[]{:S(2)}) collective-permute-start(bf16[1,4,128,512]{3,2,1,0:T(8,128)(2,1)} %get-tuple-element.337), channel_id=1, source_target_pairs={{0,16},{4,20},{8,24},{12,28},{16,0},{20,4},{24,8},{28,12},{1,17},{... | collective-permute-start | bytes 1572872 | tf_op jit(solution)/shard_map/ppermute | solution.py:994
  190.0 13.6 %collective-permute-start.20 = (bf16[1,4,128,512]{3,2,1,0:T(8,128)(2,1)S(1)}, bf16[1,4,128,512]{3,2,1,0:T(8,128)(2,1)S(1)}, u32[]{:S(2)}, u32[]{:S(2)}) collective-permute-start(bf16[1,4,128,512]{3,2,1,0:T(8,128)(2,1)S(1)} %get-tuple-element.336), channel_id=1, source_target_pairs={{0,8},{4,12},{8,0},{12,4},{16,24},{20,28},{24,16},{28,20},{1,9},{5... | collective-permute-start | bytes 1572872 | tf_op jit(solution)/shard_map/ppermute | solution.py:994
  190.5 25.4 %collective-permute-start.16 = (bf16[2,4,128,512]{3,2,1,0:T(8,128)(2,1)}, bf16[2,4,128,512]{3,2,1,0:T(8,128)(2,1)}, u32[]{:S(2)}, u32[]{:S(2)}) collective-permute-start(bf16[2,4,128,512]{3,2,1,0:T(8,128)(2,1)} %collective-permute-done.13.refs_5_.refs_1_), channel_id=1, source_target_pairs={{0,4},{4,0},{8,12},{12,8},{16,20},{20,16},{24,28},{28,24},{1,5},{5... | collective-permute-start | bytes 3145736 | tf_op jit(solution)/shard_map/ppermute | solution.py:994
  205.8 37.1 %collective-permute-start.21 = (bf16[2,4,128,512]{3,2,1,0:T(8,128)(2,1)}, bf16[2,4,128,512]{3,2,1,0:T(8,128)(2,1)}, u32[]{:S(2)}, u32[]{:S(2)}) collective-permute-start(bf16[2,4,128,512]{3,2,1,0:T(8,128)(2,1)} %pad_maximum_fusion.2.refs_4_), channel_id=1, source_target_pairs={{0,8},{4,12},{8,0},{12,4},{16,24},{20,28},{24,16},{28,20},{1,9},{5... | collective-permute-start | bytes 3145736 | tf_op jit(solution)/shard_map/ppermute | solution.py:994
  206.4 38.3 %collective-permute-start.23 = (bf16[2,4,128,512]{3,2,1,0:T(8,128)(2,1)}, bf16[2,4,128,512]{3,2,1,0:T(8,128)(2,1)}, u32[]{:S(2)}, u32[]{:S(2)}) collective-permute-start(bf16[2,4,128,512]{3,2,1,0:T(8,128)(2,1)} %pad_maximum_fusion.2.refs_4_), channel_id=1, source_target_pairs={{0,4},{4,0},{8,12},{12,8},{16,20},{20,16},{24,28},{28,24},{1,5},{5... | collective-permute-start | bytes 3145736 | tf_op jit(solution)/shard_map/ppermute | solution.py:994
  207.5 35.4 %collective-permute-start.22 = (bf16[2,4,128,512]{3,2,1,0:T(8,128)(2,1)S(1)}, bf16[2,4,128,512]{3,2,1,0:T(8,128)(2,1)}, u32[]{:S(2)}, u32[]{:S(2)}) collective-permute-start(bf16[2,4,128,512]{3,2,1,0:T(8,128)(2,1)S(1)} %pad_maximum_fusion.3.refs_0_.refs_4_), channel_id=1, source_target_pairs={{0,16},{4,20},{8,24},{12,28},{16,0},{20,4},{24,8},{28,12},{1,17},{... | collective-permute-start | bytes 3145736 | tf_op jit(solution)/shard_map/ppermute | solution.py:994
  215.9 28.7 %collective-permute-start.25 = (bf16[2,4,128,512]{3,2,1,0:T(8,128)(2,1)S(1)}, bf16[2,4,128,512]{3,2,1,0:T(8,128)(2,1)S(1)}, u32[]{:S(2)}, u32[]{:S(2)}) collective-permute-start(bf16[2,4,128,512]{3,2,1,0:T(8,128)(2,1)S(1)} %pad_maximum_fusion.3.refs_0_.refs_4_), channel_id=1, source_target_pairs={{0,4},{4,0},{8,12},{12,8},{16,20},{20,16},{24,28},{28,24},{1,5},{5... | collective-permute-start | bytes 3145736 | tf_op jit(solution)/shard_map/ppermute | solution.py:994
  243.0 3.9 collective-permute-start.24
  243.5 5.4 collective-permute-start.26
  244.2 36.0 %collective-permute-start.28 = (bf16[4,4,128,1024]{3,2,1,0:T(8,128)(2,1)}, bf16[4,4,128,1024]{3,2,1,0:T(8,128)(2,1)}, u32[]{:S(2)}, u32[]{:S(2)}) collective-permute-start(bf16[4,4,128,1024]{3,2,1,0:T(8,128)(2,1)} %get-tuple-element.185), channel_id=1, source_target_pairs={{0,4},{4,0},{8,12},{12,8},{16,20},{20,16},{24,28},{28,24},{1,5},{5... | collective-permute-start | bytes 12582920 | tf_op jit(solution)/shard_map/ppermute | solution.py:994
  277.3 8.0 %collective-permute-start.27 = (bf16[4,4,128,1024]{3,2,1,0:T(8,128)(2,1)}, bf16[4,4,128,1024]{3,2,1,0:T(8,128)(2,1)}, u32[]{:S(2)}, u32[]{:S(2)}) collective-permute-start(bf16[4,4,128,1024]{3,2,1,0:T(8,128)(2,1)} %get-tuple-element.175), channel_id=1, source_target_pairs={{0,4},{4,0},{8,12},{12,8},{16,20},{20,16},{24,28},{28,24},{1,5},{5... | collective-permute-start | bytes 12582920 | tf_op jit(solution)/shard_map/ppermute | solution.py:994
  283.6 25.7 %collective-permute-start.29 = (bf16[2,4,128,512]{3,2,1,0:T(8,128)(2,1)}, bf16[2,4,128,512]{3,2,1,0:T(8,128)(2,1)S(1)}, u32[]{:S(2)}, u32[]{:S(2)}) collective-permute-start(bf16[2,4,128,512]{3,2,1,0:T(8,128)(2,1)} %get-tuple-element.187), channel_id=1, source_target_pairs={{0,16},{4,20},{8,24},{12,28},{16,0},{20,4},{24,8},{28,12},{1,17},{... | collective-permute-start | bytes 3145736 | tf_op jit(solution)/shard_map/ppermute | solution.py:994
  284.1 25.4 %collective-permute-start.30 = (bf16[2,4,128,512]{3,2,1,0:T(8,128)(2,1)}, bf16[2,4,128,512]{3,2,1,0:T(8,128)(2,1)S(1)}, u32[]{:S(2)}, u32[]{:S(2)}) collective-permute-start(bf16[2,4,128,512]{3,2,1,0:T(8,128)(2,1)} %get-tuple-element.188), channel_id=1, source_target_pairs={{0,8},{4,12},{8,0},{12,4},{16,24},{20,28},{24,16},{28,20},{1,9},{5... | collective-permute-start | bytes 3145736 | tf_op jit(solution)/shard_map/ppermute | solution.py:994
  302.9 78.4 %all-to-all-start.5 = ((bf16[4,1088,256]{2,1,0:T(8,128)(2,1)}), bf16[4,1088,256]{2,1,0:T(8,128)(2,1)}, u32[]{:S(2)}, u32[]{:S(2)}) async-start(bf16[4,1088,256]{2,1,0:T(8,128)(2,1)} %block_rows.1), calls=%async_computation.5 | async-start | bytes 4456448 | tf_op jit(solution)/shard_map/all_to_all | solution.py:990
  314.2 28.0 %collective-permute-start.31 = (bf16[1,4,128,512]{3,2,1,0:T(8,128)(2,1)}, bf16[1,4,128,512]{3,2,1,0:T(8,128)(2,1)S(1)}, u32[]{:S(2)}, u32[]{:S(2)}) collective-permute-start(bf16[1,4,128,512]{3,2,1,0:T(8,128)(2,1)} %get-tuple-element.190), channel_id=1, source_target_pairs={{0,8},{4,12},{8,0},{12,4},{16,24},{20,28},{24,16},{28,20},{1,9},{5... | collective-permute-start | bytes 1572872 | tf_op jit(solution)/shard_map/ppermute | solution.py:994
  315.2 26.9 %collective-permute-start.32 = (bf16[1,4,128,512]{3,2,1,0:T(8,128)(2,1)}, bf16[1,4,128,512]{3,2,1,0:T(8,128)(2,1)S(1)}, u32[]{:S(2)}, u32[]{:S(2)}) collective-permute-start(bf16[1,4,128,512]{3,2,1,0:T(8,128)(2,1)} %get-tuple-element.191), channel_id=1, source_target_pairs={{0,16},{4,20},{8,24},{12,28},{16,0},{20,4},{24,8},{28,12},{1,17},{... | collective-permute-start | bytes 1572872 | tf_op jit(solution)/shard_map/ppermute | solution.py:994
  319.3 51.0 %collective-permute-start.33 = (bf16[2,4,128,512]{3,2,1,0:T(8,128)(2,1)}, bf16[2,4,128,512]{3,2,1,0:T(8,128)(2,1)S(1)}, u32[]{:S(2)}, u32[]{:S(2)}) collective-permute-start(bf16[2,4,128,512]{3,2,1,0:T(8,128)(2,1)} %get-tuple-element.198), channel_id=1, source_target_pairs={{0,16},{4,20},{8,24},{12,28},{16,0},{20,4},{24,8},{28,12},{1,17},{... | collective-permute-start | bytes 3145736 | tf_op jit(solution)/shard_map/ppermute | solution.py:994
  320.6 49.7 %collective-permute-start.34 = (bf16[2,4,128,512]{3,2,1,0:T(8,128)(2,1)}, bf16[2,4,128,512]{3,2,1,0:T(8,128)(2,1)S(1)}, u32[]{:S(2)}, u32[]{:S(2)}) collective-permute-start(bf16[2,4,128,512]{3,2,1,0:T(8,128)(2,1)} %get-tuple-element.199), channel_id=1, source_target_pairs={{0,8},{4,12},{8,0},{12,4},{16,24},{20,28},{24,16},{28,20},{1,9},{5... | collective-permute-start | bytes 3145736 | tf_op jit(solution)/shard_map/ppermute | solution.py:994
  351.8 25.3 %collective-permute-start.37 = (bf16[4,4,128,256]{3,2,1,0:T(8,128)(2,1)}, bf16[4,4,128,256]{3,2,1,0:T(8,128)(2,1)S(1)}, u32[]{:S(2)}, u32[]{:S(2)}) collective-permute-start(bf16[4,4,128,256]{3,2,1,0:T(8,128)(2,1)} %get-tuple-element.207), channel_id=1, source_target_pairs={{0,4},{4,0},{8,12},{12,8},{16,20},{20,16},{24,28},{28,24},{1,5},{5... | collective-permute-start | bytes 3145736 | tf_op jit(solution)/shard_map/ppermute | solution.py:994
  375.3 14.9 %collective-permute-start.35 = (bf16[1,4,128,512]{3,2,1,0:T(8,128)(2,1)}, bf16[1,4,128,512]{3,2,1,0:T(8,128)(2,1)S(1)}, u32[]{:S(2)}, u32[]{:S(2)}) collective-permute-start(bf16[1,4,128,512]{3,2,1,0:T(8,128)(2,1)} %get-tuple-element.201), channel_id=1, source_target_pairs={{0,8},{4,12},{8,0},{12,4},{16,24},{20,28},{24,16},{28,20},{1,9},{5... | collective-permute-start | bytes 1572872 | tf_op jit(solution)/shard_map/ppermute | solution.py:994
  376.3 15.0 %collective-permute-start.36 = (bf16[1,4,128,512]{3,2,1,0:T(8,128)(2,1)}, bf16[1,4,128,512]{3,2,1,0:T(8,128)(2,1)S(1)}, u32[]{:S(2)}, u32[]{:S(2)}) collective-permute-start(bf16[1,4,128,512]{3,2,1,0:T(8,128)(2,1)} %get-tuple-element.202), channel_id=1, source_target_pairs={{0,16},{4,20},{8,24},{12,28},{16,0},{20,4},{24,8},{28,12},{1,17},{... | collective-permute-start | bytes 1572872 | tf_op jit(solution)/shard_map/ppermute | solution.py:994
  380.1 29.7 %collective-permute-start.38 = (bf16[2,4,128,256]{3,2,1,0:T(8,128)(2,1)}, bf16[2,4,128,256]{3,2,1,0:T(8,128)(2,1)S(1)}, u32[]{:S(2)}, u32[]{:S(2)}) collective-permute-start(bf16[2,4,128,256]{3,2,1,0:T(8,128)(2,1)} %add_rows.12), channel_id=1, source_target_pairs={{0,16},{4,20},{8,24},{12,28},{16,0},{20,4},{24,8},{28,12},{1,17},{... | collective-permute-start | bytes 1572872 | tf_op jit(solution)/shard_map/ppermute | solution.py:994
  385.1 46.8 %all-to-all-start.6 = ((bf16[4,128,1024]{2,1,0:T(8,128)(2,1)}), bf16[4,128,1024]{2,1,0:T(8,128)(2,1)S(1)}, u32[]{:S(2)}, u32[]{:S(2)}) async-start(bf16[4,128,1024]{2,1,0:T(8,128)(2,1)} %add_cols.3), calls=%async_computation.6 | async-start | bytes 2097152 | tf_op jit(solution)/shard_map/all_to_all | solution.py:990
  412.5 19.4 %collective-permute-start.39 = (bf16[1,4,128,256]{3,2,1,0:T(8,128)(2,1)}, bf16[1,4,128,256]{3,2,1,0:T(8,128)(2,1)S(1)}, u32[]{:S(2)}, u32[]{:S(2)}) collective-permute-start(bf16[1,4,128,256]{3,2,1,0:T(8,128)(2,1)} %add_rows.13), channel_id=1, source_target_pairs={{0,8},{4,12},{8,0},{12,4},{16,24},{20,28},{24,16},{28,20},{1,9},{5... | collective-permute-start | bytes 786440 | tf_op jit(solution)/shard_map/ppermute | solution.py:994
  436.7 56.7 %all-to-all-start.7 = ((bf16[4,128,1280]{2,1,0:T(8,128)(2,1)}), bf16[4,128,1280]{2,1,0:T(8,128)(2,1)}, u32[]{:S(2)}, u32[]{:S(2)}) async-start(bf16[4,128,1280]{2,1,0:T(8,128)(2,1)} %add_cols.4), calls=%async_computation.7 | async-start | bytes 2621440 | tf_op jit(solution)/shard_map/all_to_all | solution.py:990
  473.3 15.6 %collective-permute-start.43 = (bf16[4,4,128,768]{3,2,1,0:T(8,128)(2,1)}, bf16[4,4,128,768]{3,2,1,0:T(8,128)(2,1)S(1)}, u32[]{:S(2)}, u32[]{:S(2)}) collective-permute-start(bf16[4,4,128,768]{3,2,1,0:T(8,128)(2,1)} %get-tuple-element.231), channel_id=1, source_target_pairs={{0,4},{4,0},{8,12},{12,8},{16,20},{20,16},{24,28},{28,24},{1,5},{5... | collective-permute-start | bytes 9437192 | tf_op jit(solution)/shard_map/ppermute | solution.py:994
  474.0 14.5 %collective-permute-start.40 = (f32[6016]{0:T(1024)S(1)}, f32[6016]{0:T(1024)S(1)}, u32[]{:S(2)}, u32[]{:S(2)}) collective-permute-start(f32[6016]{0:T(1024)S(1)} %get-tuple-element.334), channel_id=1, source_target_pairs={{0,1},{1,0},{2,3},{3,2},{4,5},{5,4},{6,7},{7,6},{8,9},{9,8},{10,11... | collective-permute-start | bytes 72200 | tf_op jit(solution)/shard_map/ppermute | solution.py:1172
  476.0 12.4 %collective-permute-start.41 = (f32[6016]{0:T(1024)S(1)}, f32[6016]{0:T(1024)S(1)}, u32[]{:S(2)}, u32[]{:S(2)}) collective-permute-start(f32[6016]{0:T(1024)S(1)} %get-tuple-element.333), channel_id=1, source_target_pairs={{0,2},{1,3},{2,0},{3,1},{4,6},{5,7},{6,4},{7,5},{8,10},{9,11},{10,... | collective-permute-start | bytes 72200 | tf_op jit(solution)/shard_map/ppermute | solution.py:1172
  478.4 10.1 %collective-permute-start.42 = (f32[6016]{0:T(1024)S(1)}, f32[6016]{0:T(1024)S(1)}, u32[]{:S(2)}, u32[]{:S(2)}) collective-permute-start(f32[6016]{0:T(1024)S(1)} %get-tuple-element.332), channel_id=1, source_target_pairs={{0,3},{1,2},{2,1},{3,0},{4,7},{5,6},{6,5},{7,4},{8,11},{9,10},{10,... | collective-permute-start | bytes 72200 | tf_op jit(solution)/shard_map/ppermute | solution.py:1172
  510.7 4.5 collective-permute-start.44
  511.8 4.8 collective-permute-start.45
  515.1 5.4 collective-permute-start.46
  520.5 53.0 %all-to-all-start.8 = ((bf16[4,1088,256]{2,1,0:T(8,128)(2,1)}), bf16[4,1088,256]{2,1,0:T(8,128)(2,1)S(1)}, u32[]{:S(2)}, u32[]{:S(2)}) async-start(bf16[4,1088,256]{2,1,0:T(8,128)(2,1)} %get-tuple-element.239), calls=%async_computation.8 | async-start | bytes 4456448 | tf_op jit(solution)/shard_map/all_to_all | solution.py:990
  524.1 17.7 %collective-permute-start.47 = (bf16[2,4,64,768]{3,2,1,0:T(8,128)(2,1)}, bf16[2,4,64,768]{3,2,1,0:T(8,128)(2,1)S(1)}, u32[]{:S(2)}, u32[]{:S(2)}) collective-permute-start(bf16[2,4,64,768]{3,2,1,0:T(8,128)(2,1)} %get-tuple-element.233), channel_id=1, source_target_pairs={{0,16},{4,20},{8,24},{12,28},{16,0},{20,4},{24,8},{28,12},{1,17},{... | collective-permute-start | bytes 2359304 | tf_op jit(solution)/shard_map/ppermute | solution.py:994
  525.2 17.3 %collective-permute-start.48 = (bf16[2,4,64,768]{3,2,1,0:T(8,128)(2,1)}, bf16[2,4,64,768]{3,2,1,0:T(8,128)(2,1)S(1)}, u32[]{:S(2)}, u32[]{:S(2)}) collective-permute-start(bf16[2,4,64,768]{3,2,1,0:T(8,128)(2,1)} %get-tuple-element.234), channel_id=1, source_target_pairs={{0,8},{4,12},{8,0},{12,4},{16,24},{20,28},{24,16},{28,20},{1,9},{5... | collective-permute-start | bytes 2359304 | tf_op jit(solution)/shard_map/ppermute | solution.py:994
  546.2 1.3 collective-permute-start.49
  547.5 3.9 collective-permute-start.50
  551.5 4.2 collective-permute-start.51
  552.4 21.1 %collective-permute-start.52 = (bf16[1,4,64,768]{3,2,1,0:T(8,128)(2,1)}, bf16[1,4,64,768]{3,2,1,0:T(8,128)(2,1)S(1)}, u32[]{:S(2)}, u32[]{:S(2)}) collective-permute-start(bf16[1,4,64,768]{3,2,1,0:T(8,128)(2,1)} %get-tuple-element.245), channel_id=1, source_target_pairs={{0,8},{4,12},{8,0},{12,4},{16,24},{20,28},{24,16},{28,20},{1,9},{5... | collective-permute-start | bytes 1179656 | tf_op jit(solution)/shard_map/ppermute | solution.py:994
  553.8 19.7 %collective-permute-start.53 = (bf16[1,4,64,768]{3,2,1,0:T(8,128)(2,1)}, bf16[1,4,64,768]{3,2,1,0:T(8,128)(2,1)S(1)}, u32[]{:S(2)}, u32[]{:S(2)}) collective-permute-start(bf16[1,4,64,768]{3,2,1,0:T(8,128)(2,1)} %get-tuple-element.246), channel_id=1, source_target_pairs={{0,16},{4,20},{8,24},{12,28},{16,0},{20,4},{24,8},{28,12},{1,17},{... | collective-permute-start | bytes 1179656 | tf_op jit(solution)/shard_map/ppermute | solution.py:994
  578.8 23.4 %all-to-all-start.9 = ((bf16[4,128,768]{2,1,0:T(8,128)(2,1)}), bf16[4,128,768]{2,1,0:T(8,128)(2,1)S(1)}, u32[]{:S(2)}, u32[]{:S(2)}) async-start(bf16[4,128,768]{2,1,0:T(8,128)(2,1)} %add_cols.5), calls=%async_computation.9 | async-start | bytes 1572864 | tf_op jit(solution)/shard_map/all_to_all | solution.py:990
  (59 other events, 712.7 us)

commit v5 on v4

--- a/solution.py
+++ b/solution.py
@@ -640,9 +640,21 @@
     grad = nt_dot(dqkv[...], weight[...])
     back, hat = norm_back(grad, x[...].astype(F32), gain[...])
     whole[...] = resid_grad[...] + back
-    take_features(whole, pieces, info, max(1, 128 * nr // D))
     sums[0] += eight(grad * hat)
     sums[1] += eight(grad)
+
+    @pl.when(pl.program_id(0) == BLOCKS - 1)
+    def _():
+        lines = []
+        for v in range(2):
+            left = jnp.sum(sums[v], axis=0, keepdims=True)
+            for _ in range(3):
+                lines.append(left.astype(BF).astype(F32))
+                left = left - lines[-1]
+        lines.append(jnp.zeros((2, D), F32))
+        whole[whole.shape[0] - TAIL : whole.shape[0] - TAIL + 8, :] = jnp.concatenate(lines, axis=0)
+
+    take_features(whole, pieces, info, max(1, 128 * nr // D))
 
 
 def input_back(bufs_a, bufs_b, dqkv, x, resid_grad, gain, info, cols, rows, nr):
@@ -651,7 +663,7 @@
     piece = jax.ShapeDtypeStruct((cols, rows, width), BF)
     return pl.pallas_call(
         partial(input_back_kernel, cols, nr),
-        out_shape=[piece, jax.ShapeDtypeStruct((2, 8, D), F32)],
+        out_shape=[piece],
         grid_spec=pltpu.PrefetchScalarGridSpec(
             num_scalar_prefetch=1,
             grid=(BLOCKS,),
@@ -659,13 +671,17 @@
             + [pl.BlockSpec((rows // BLOCKS, 3 * D), lambda i, s: (i, 0)), row_spec, row_spec]
             + [const_spec((1, D))],
             out_specs=[pl.BlockSpec((cols, rows // BLOCKS, width), lambda i, s: (0, i, 0))]
-            + [pl.BlockSpec((2, 8, D), lambda i, s: (0, 0, 0))],
-            scratch_shapes=[pltpu.VMEM((rows // BLOCKS, D), F32), pltpu.VMEM((D, 3 * D), BF)],
+,
+            scratch_shapes=[
+                pltpu.VMEM((2, 8, D), F32),
+                pltpu.VMEM((rows // BLOCKS, D), F32),
+                pltpu.VMEM((D, 3 * D), BF),
+            ],
         ),
         compiler_params=params(),
         cost_estimate=cost(25),
         name="input_back",
-    )(info, *bufs_a, *bufs_b, dqkv, x, resid_grad, gain)
+    )(info, *bufs_a, *bufs_b, dqkv, x, resid_grad, gain)[0]
 
 
 def rel_constants():
@@ -1172,8 +1188,6 @@
         arrived.append(lax.ppermute(sent, "col", [(i, i ^ k) for i in range(cols)]))
     gate = yield arrived[1:]
     arrived = list(lax.optimization_barrier((*arrived, *(gate or ())))[:cols])
-    if whole is None:
-        yield sum(arrived[1:], arrived[0])
     order = me ^ jnp.arange(cols, dtype=jnp.int32)
     total = jnp.sum(pick_rows(jnp.stack(arrived), order), axis=0)
     yield total[:size], total[size:]
@@ -1183,8 +1197,8 @@
     bit = 1
     while bit < nr:
         total = total + row_swap(total, bit, nr)
+        yield total
         bit *= 2
-    return total
 
 
 def pick_rows(values, order):
@@ -1421,17 +1435,17 @@
         [by_col(sums2), bias_cols[:, 0], bias_cols[:, 2]] + hidden_sums, axis=1
     )
     early = sum_cols(small, table_flat, me, cols)
-    next(early)
+    early_arrived = next(early)
     keep, send = qkv_grad(after(n1, dqkv), dqkv, cols, rows, nr)
     sends.append(reduce_weight(keep, send, -2, cols, nr))
     core3 = next(sends[3])
     block_out = collect(after(block_pieces, keep), sets, info, BF)
     rows3 = sends[3].send((*core3, block_out))
     small, table_flat = early.send((block_out,))
-    in_sent, in_sums = input_back(
+    in_sent = input_back(
         qkv_a,
         qkv_b,
-        after(dqkv, block_out, arrived1, small, *rows3.sent),
+        after(dqkv, block_out, arrived1, *early_arrived, *rows3.sent),
         x_full,
         resid_grad,
         gain1,
@@ -1440,20 +1454,19 @@
         rows,
         nr,
     )
-    late = sum_cols(by_col(in_sums), None, me, cols)
-    late_arrived = next(late)
-    in_pieces = col_exchange(after(in_sent, *late_arrived))
+    in_pieces = col_exchange(in_sent)
     rows3 = sends[3].send((in_sent,))
     for _ in range(len(outer_bits(nr)) - 2):
         rows3 = sends[3].send(None)
     sizes = [2 * width, small.shape[0], table_flat.shape[0]]
-    total = sum_rows(
-        jnp.concatenate([late.send(None), small, after(table_flat, *rows3.sent)]), nr
-    )
-    done3, arrived3 = finish_weights([sends[3].send(None)], in_pieces, total)
+    late = in_pieces[:, rows - TAIL : rows - TAIL + 6].astype(F32).reshape(cols, 2, 3, width)
+    done3, arrived3 = finish_weights([sends[3].send(None)], in_pieces)
+    late = jnp.sum(after(late, done3), axis=(0, 2)).reshape(-1)
+    totals = list(sum_rows(jnp.concatenate([late, small, table_flat]), nr))
+    total = totals[-1]
     late, small = total[: sizes[0]], total[sizes[0] : sizes[0] + sizes[1]]
     table_flat = total[sizes[0] + sizes[1] :].reshape(2, 27, HD)
-    input_grad = collect(after(in_pieces, done3), sets, info, F32)
+    input_grad = collect(after(in_pieces, totals[-2]), sets, info, F32)
     (qkv_w_grad,) = last_sum(arrived3, [3 * width])
     fc_grads = last_sum(arrived0, [2 * half], done3)
     fc_grad, proj_w_grad = last_sum(arrived1, [2 * half, width], done3)

time: 614 us -> 607 us (0.989)
    unnamed x136 -> x134, local copies, waits for them, and re-layouts: 17 us -> 16.9 us
  transfers between devices with their start and end apart: 64 -> 61, of which waited for: 26 -> 20; matrix products, arithmetic and copies ran while one was open for 6% -> 6% of each run, Pallas kernels for 56% -> 57%
where the time goes in v5:
time: 607 us; the launch traced here: 597 us
  Pallas kernels  364 us (60%)
  waiting for transfers between devices  89.2 us (15%)
  starting transfers between devices  86.7 us (14%)
  local copies, waits for them, and re-layouts  32.3 us (5%)
  other arithmetic  22.2 us (4%)
    pallas_call x4, Pallas kernels, attend_back(): pl.pallas_call(partial(attend_back_kernel, width, len(held)), out_shape=[...  73.6 us
    pallas_call x4, Pallas kernels, attend(): pl.pallas_call(partial(attend_kernel, width, len(held)), out_shape=[jax.S...  56.1 us
    pallas_call x2, Pallas kernels, mlp_grads(): pl.pallas_call(partial(mlp_grads_kernel, nr), out_shape=[act, act, half,...  54.4 us
    all_to_all x10, starting transfers between devices, col_exchange(): return lax.all_to_all(values, 'col', 0, 0, tiled=True)  44.9 us
    all_to_all x10, waiting for transfers between devices, col_exchange(): return lax.all_to_all(values, 'col', 0, 0, tiled=True)  40.2 us
    ppermute x45, waiting for transfers between devices, row_swap(): return lax.ppermute(values, 'row', [(i, i ^ bit) for i in range(nr)])  39.7 us
    ppermute x45, starting transfers between devices, row_swap(): return lax.ppermute(values, 'row', [(i, i ^ bit) for i in range(nr)])  32.9 us
    pallas_call x8, Pallas kernels, reduce_weight(): pl.pallas_call(partial(add_kernel, sizes), out_shape=[jax.ShapeDtypeStruc...  21.9 us
  transfers between devices with their start and end apart: 61, of which 20 were waited for; matrix products, arithmetic and copies ran while one was open for 6% of the time, Pallas kernels for 57%

profile of v5, /device:TPU:0, one launch (start us, length us, event | category | flops | bytes accessed | tf_op | source)
XLA Modules:
  0.0 596.8 jit_solution(4513182390467266746)
XLA Ops:
  0.6 1.9 broadcast_in_dim.139
  2.5 6.3 %all-to-all-start.1 = ((bf16[4,3,128,256]{3,2,1,0:T(8,128)(2,1)}), bf16[4,3,128,256]{3,2,1,0:T(8,128)(2,1)S(1)}, u32[]{:S(2)}, u32[]{:S(2)}) async-start(bf16[4,3,128,256]{3,2,1,0:T(8,128)(2,1)} %broadcast_in_dim.139), calls=%async_computation.1 | async-start | bytes 1572864 | tf_op jit(solution)/shard_map/all_to_all | solution.py:1006
  8.8 2.1 plan.1.info
  11.6 10.5 %spread.2 = bf16[4,1088,256]{2,1,0:T(8,128)(2,1)} custom-call(s32[201]{0:T(256)} %plan.1.info, bf16[4096,256]{1,0:T(8,128)(2,1)} %x_ref.1), custom_call_target="tpu_custom_call" | custom-call | flops 7699999744 | bytes 7000000 | tf_op jit(solution)/shard_map/spread/pallas_call | solution.py:175
  22.1 6.9 %all-to-all-done.1 = bf16[4,3,128,256]{3,2,1,0:T(8,128)(2,1)S(1)} async-done(((bf16[4,3,128,256]{3,2,1,0:T(8,128)(2,1)}), bf16[4,3,128,256]{3,2,1,0:T(8,128)(2,1)S(1)}, u32[]{:S(2)}, u32[]{:S(2)}) %all-to-all-start.1) | async-done | bytes 786464 | tf_op jit(solution)/shard_map/all_to_all | solution.py:1006
  28.9 3.6 all-to-all-start
  40.3 3.5 collective-permute-done
  43.8 2.1 pad_maximum_fusion.4.refs_1_.refs_0_
  47.5 1.9 pad_maximum_fusion.5.refs_5_.refs_4_
  51.6 10.5 %spread.3 = bf16[4,1088,256]{2,1,0:T(8,128)(2,1)} custom-call(s32[201]{0:T(256)} %plan.1.info, bf16[4096,256]{1,0:T(8,128)(2,1)} %x_ref.2), custom_call_target="tpu_custom_call" | custom-call | flops 7699999744 | bytes 7000000 | tf_op jit(solution)/shard_map/spread/pallas_call | solution.py:175
  63.8 3.2 collective-permute-done.5.refs_6_.refs_5_
  67.3 2.3 collective-permute-done.7.refs_8_.refs_7_
  69.7 3.3 collective-permute-start.10
  75.4 8.7 %collective-permute-done.9 = f32[3072]{0:T(1024)S(1)} collective-permute-done((f32[3072]{0:T(1024)S(1)}, f32[3072]{0:T(1024)S(1)}, u32[]{:S(2)}, u32[]{:S(2)}) %collective-permute-start.9) | collective-permute-done | bytes 12320 | tf_op jit(solution)/shard_map/ppermute | solution.py:1271
  87.7 3.5 all-to-all-start.2
  91.3 14.9 %norm_qkv.1 = (bf16[1088,1024]{1,0:T(8,128)(2,1)}, bf16[1088,1024]{1,0:T(8,128)(2,1)}, bf16[1088,3072]{1,0:T(8,128)(2,1)}) custom-call(s32[201]{0:T(256)} %plan.1.info, bf16[4,1088,256]{2,1,0:T(8,128)(2,1)} %copy-done.10, bf16[2,4,3,64,256]{4,3,2,1,0:T(8,128)(2,1)} %pad_maximum_fusion.4.refs_1_.refs_0_, ...), custom_call_target="tpu_custom_call" | custom-call | flops 20899999744 | bytes 19000000 | tf_op jit(solution)/shard_map/norm_qkv/pallas_call | solution.py:339
  106.2 14.0 %attend.4 = (bf16[1088,1024]{1,0:T(8,128)(2,1)}, bf16[16,1400,256]{2,1,0:T(8,128)(2,1)}, f32[1400,1024]{1,0:T(8,128)}) custom-call(s32[201]{0:T(256)} %plan.1.info, bf16[1088,3072]{1,0:T(8,128)(2,1)} %get-tuple-element.204.qkv, bf16[128,128]{1,0:T(8,128)(2,1)} %pad_maximum_fusion.12.tables, s32[200,128]{1,0:T(8,128)} %constant.41.clone.shifts, ...), custom_call_target="tpu_custom_call" | custom-call | flops 15399999488 | bytes 14000000 | tf_op jit(solution)/shard_map/attend/pallas_call | solution.py:820
  120.2 1.9 all-to-all-done.2
  127.3 3.5 all-to-all-start.3
  130.8 14.1 %attend.5 = (bf16[1088,1024]{1,0:T(8,128)(2,1)}, bf16[16,1400,256]{2,1,0:T(8,128)(2,1)}, f32[1400,1024]{1,0:T(8,128)}) custom-call(s32[201]{0:T(256)} %plan.1.info, bf16[1088,3072]{1,0:T(8,128)(2,1)} %get-tuple-element.204.qkv, bf16[128,128]{1,0:T(8,128)(2,1)} %pad_maximum_fusion.12.tables, ...), custom_call_target="tpu_custom_call", output_to_operand_aliasing={{0}: (5, {}), {1}: (6, {}), {2}: (7, {})} | custom-call | flops 15399999488 | bytes 14000000 | tf_op jit(solution)/shard_map/attend/pallas_call | solution.py:820
  146.7 2.1 pad_maximum_fusion.1.refs_4_.refs_0_
  149.3 6.1 %all-to-all-done.3 = bf16[4,128,1024]{2,1,0:T(8,128)(2,1)S(1)} async-done(((bf16[4,128,1024]{2,1,0:T(8,128)(2,1)}), bf16[4,128,1024]{2,1,0:T(8,128)(2,1)S(1)}, u32[]{:S(2)}, u32[]{:S(2)}) %all-to-all-start.3) | async-done | bytes 1048608 | tf_op jit(solution)/shard_map/all_to_all | solution.py:1006
  155.4 3.8 all-to-all-start.4
  159.3 14.0 %attend.6 = (bf16[1088,1024]{1,0:T(8,128)(2,1)}, bf16[16,1400,256]{2,1,0:T(8,128)(2,1)}, f32[1400,1024]{1,0:T(8,128)}) custom-call(s32[201]{0:T(256)} %plan.1.info, bf16[1088,3072]{1,0:T(8,128)(2,1)} %get-tuple-element.204.qkv, bf16[128,128]{1,0:T(8,128)(2,1)} %pad_maximum_fusion.12.tables, ...), custom_call_target="tpu_custom_call", output_to_operand_aliasing={{0}: (5, {}), {1}: (6, {}), {2}: (7, {})} | custom-call | flops 15399999488 | bytes 14000000 | tf_op jit(solution)/shard_map/attend/pallas_call | solution.py:820
  173.3 14.0 %attend.7 = (bf16[1088,1024]{1,0:T(8,128)(2,1)}, bf16[16,1400,256]{2,1,0:T(8,128)(2,1)}, f32[1400,1024]{1,0:T(8,128)}) custom-call(s32[201]{0:T(256)} %plan.1.info, bf16[1088,3072]{1,0:T(8,128)(2,1)} %get-tuple-element.204.qkv, bf16[128,128]{1,0:T(8,128)(2,1)} %pad_maximum_fusion.12.tables, ...), custom_call_target="tpu_custom_call", output_to_operand_aliasing={{0}: (5, {}), {1}: (6, {}), {2}: (7, {})} | custom-call | flops 15399999488 | bytes 14000000 | tf_op jit(solution)/shard_map/attend/pallas_call | solution.py:820
  191.2 7.9 %proj_norm.1 = (f32[1088,1024]{1,0:T(8,128)}, bf16[1088,1024]{1,0:T(8,128)(2,1)}) custom-call(bf16[2,4,128,768]{3,2,1,0:T(8,128)(2,1)} %pad_maximum_fusion.refs_0_, bf16[2,4,128,768]{3,2,1,0:T(8,128)(2,1)} %collective-permute-done.14.refs_1_, bf16[2,4,128,768]{3,2,1,0:T(8,128)(2,1)} %collective-permute-done.18.refs_2_, ...), custom_call_target="tpu_custom_call" | custom-call | flops 12099999744 | bytes 11000000 | tf_op jit(solution)/shard_map/proj_norm/pallas_call | solution.py:412
  199.0 4.5 collective-permute-done.17
  203.5 2.3 pad_maximum_fusion.2.refs_4_
  211.1 4.8 join.1.refs_9_.refs_11_
  215.9 27.0 %mlp_grads.2 = (bf16[1088,2048]{1,0:T(8,128)(2,1)}, bf16[1088,2048]{1,0:T(8,128)(2,1)}, bf16[4,4,128,1024]{3,2,1,0:T(8,128)(2,1)}, bf16[4,4,128,1024]{3,2,1,0:T(8,128)(2,1)}, f32[4,8,512]{2,1,0:T(8,128)}) custom-call(bf16[2,4,128,768]{3,2,1,0:T(8,128)(2,1)} %pad_maximum_fusion.refs_0_, bf16[2,4,128,768]{3,2,1,0:T(8,128)(2,1)} %collective-permute-done.14.refs_1_, ...), custom_call_target="tpu_custom_call" | custom-call | flops 41799999488 | bytes 38000000 | tf_op jit(solution)/shard_map/mlp_grads/pallas_call | solution.py:469
  244.6 2.2 collective-permute-done.24.refs_7_
  246.8 2.1 collective-permute-done.26.refs_3_.refs_7_
  249.8 27.4 %mlp_grads.3 = (bf16[1088,2048]{1,0:T(8,128)(2,1)}, bf16[1088,2048]{1,0:T(8,128)(2,1)}, bf16[4,4,128,1024]{3,2,1,0:T(8,128)(2,1)}, bf16[4,4,128,1024]{3,2,1,0:T(8,128)(2,1)}, f32[4,8,512]{2,1,0:T(8,128)}) custom-call(bf16[2,4,128,512]{3,2,1,0:T(8,128)(2,1)} %copy-done.13, bf16[2,4,128,512]{3,2,1,0:T(8,128)(2,1)} %collective-permute-done.22.refs_1_.refs_5_, ...), custom_call_target="tpu_custom_call" | custom-call | flops 41799999488 | bytes 38000000 | tf_op jit(solution)/shard_map/mlp_grads/pallas_call | solution.py:469
  280.1 3.3 add_rows.8
  285.2 17.6 %block_rows.1 = bf16[4,1088,256]{2,1,0:T(8,128)(2,1)} custom-call(s32[201]{0:T(256)} %plan.1.info, bf16[2,4,128,512]{3,2,1,0:T(8,128)(2,1)} %pad_maximum_fusion.1.refs_4_.refs_0_, bf16[2,4,128,512]{3,2,1,0:T(8,128)(2,1)} %collective-permute-done.13.refs_5_.refs_1_, bf16[2,4,128,512]{3,2,1,0:T(8,128)(2,1)} %collective-permute-done.15.refs_6_.refs_2_, ...), custom_call_target="tpu_custom_call" | custom-call | flops 28600000512 | bytes 26000000 | tf_op jit(solution)/shard_map/block_rows/pallas_call | solution.py:516
  302.8 5.2 all-to-all-start.5
  311.1 3.0 add_rows.9
  315.9 3.3 add_rows.10
  321.4 19.4 %mlp_back.1 = (f32[1088,1024]{1,0:T(8,128)}, bf16[1088,1024]{1,0:T(8,128)(2,1)}, f32[4,8,1024]{2,1,0:T(8,128)}) custom-call(bf16[2,4,128,768]{3,2,1,0:T(8,128)(2,1)} %pad_maximum_fusion.refs_0_, bf16[2,4,128,768]{3,2,1,0:T(8,128)(2,1)} %collective-permute-done.14.refs_1_, bf16[2,4,128,768]{3,2,1,0:T(8,128)(2,1)} %collective-permute-done.18.refs_2_, ...), custom_call_target="tpu_custom_call" | custom-call | flops 30799998976 | bytes 28000000 | tf_op jit(solution)/shard_map/mlp_back/pallas_call | solution.py:562
  342.0 9.6 %proj_back.1 = (bf16[1088,1024]{1,0:T(8,128)(2,1)}, bf16[4,4,128,256]{3,2,1,0:T(8,128)(2,1)}, bf16[4,4,128,256]{3,2,1,0:T(8,128)(2,1)}) custom-call(bf16[2,4,128,768]{3,2,1,0:T(8,128)(2,1)} %pad_maximum_fusion.refs_0_, bf16[2,4,128,768]{3,2,1,0:T(8,128)(2,1)} %collective-permute-done.14.refs_1_, bf16[2,4,128,768]{3,2,1,0:T(8,128)(2,1)} %collective-permute-done.18.refs_2_, ...), custom_call_target="tpu_custom_call" | custom-call | flops 12099999744 | bytes 11000000 | tf_op jit(solution)/shard_map/proj_back/pallas_call | solution.py:594
  351.8 18.4 %attend_back.4 = (bf16[1088,3072]{1,0:T(8,128)(2,1)}, f32[128,256]{1,0:T(8,128)}, f32[8,768]{1,0:T(8,128)}) custom-call(s32[201]{0:T(256)} %plan.1.info, bf16[1088,3072]{1,0:T(8,128)(2,1)} %get-tuple-element.204.qkv, bf16[16,1400,256]{2,1,0:T(8,128)(2,1)} %get-tuple-element.172.exps, f32[1400,1024]{1,0:T(8,128)} %get-tuple-element.173.inv, ...), custom_call_target="tpu_custom_call" | custom-call | flops 14300000256 | bytes 13000000 | tf_op jit(solution)/shard_map/attend_back/pallas_call | solution.py:955
  372.1 3.0 add_rows.11
  378.0 1.9 add_rows.12
  381.2 3.7 add_cols.3
  384.9 5.3 all-to-all-start.6
  391.1 18.5 %attend_back.5 = (bf16[1088,3072]{1,0:T(8,128)(2,1)}, f32[128,256]{1,0:T(8,128)}, f32[8,768]{1,0:T(8,128)}) custom-call(s32[201]{0:T(256)} %plan.1.info, bf16[1088,3072]{1,0:T(8,128)(2,1)} %get-tuple-element.204.qkv, bf16[16,1400,256]{2,1,0:T(8,128)(2,1)} %get-tuple-element.172.exps, ...), custom_call_target="tpu_custom_call", output_to_operand_aliasing={{0}: (9, {})} | custom-call | flops 14300000256 | bytes 13000000 | tf_op jit(solution)/shard_map/attend_back/pallas_call | solution.py:955
  410.5 1.9 add_rows.13
  413.3 18.4 %attend_back.6 = (bf16[1088,3072]{1,0:T(8,128)(2,1)}, f32[128,256]{1,0:T(8,128)}, f32[8,768]{1,0:T(8,128)}) custom-call(s32[201]{0:T(256)} %plan.1.info, bf16[1088,3072]{1,0:T(8,128)(2,1)} %get-tuple-element.204.qkv, bf16[16,1400,256]{2,1,0:T(8,128)(2,1)} %get-tuple-element.172.exps, ...), custom_call_target="tpu_custom_call", output_to_operand_aliasing={{0}: (9, {})} | custom-call | flops 14300000256 | bytes 13000000 | tf_op jit(solution)/shard_map/attend_back/pallas_call | solution.py:955
  432.4 4.1 add_cols.4
  436.6 4.6 all-to-all-start.7
  441.2 18.4 %attend_back.7 = (bf16[1088,3072]{1,0:T(8,128)(2,1)}, f32[128,256]{1,0:T(8,128)}, f32[8,768]{1,0:T(8,128)}) custom-call(s32[201]{0:T(256)} %plan.1.info, bf16[1088,3072]{1,0:T(8,128)(2,1)} %get-tuple-element.204.qkv, bf16[16,1400,256]{2,1,0:T(8,128)(2,1)} %get-tuple-element.172.exps, ...), custom_call_target="tpu_custom_call", output_to_operand_aliasing={{0}: (9, {})} | custom-call | flops 14300000256 | bytes 13000000 | tf_op jit(solution)/shard_map/attend_back/pallas_call | solution.py:955
  459.7 12.7 %qkv_grad.1 = (bf16[4,4,128,768]{3,2,1,0:T(8,128)(2,1)}, bf16[4,4,128,768]{3,2,1,0:T(8,128)(2,1)}) custom-call(bf16[1088,1024]{1,0:T(8,128)(2,1)} %get-tuple-element.206.n1, bf16[1088,3072]{1,0:T(8,128)(2,1)} %get-tuple-element.224.dqkv.refs_8_), custom_call_target="tpu_custom_call" | custom-call | flops 15399999488 | bytes 14000000 | tf_op jit(solution)/shard_map/qkv_grad/pallas_call | solution.py:615
  473.5 2.1 collective-permute-start.40
  475.6 2.4 collective-permute-start.41
  478.1 10.0 %collect.2 = bf16[4096,256]{1,0:T(8,128)(2,1)} custom-call(s32[201]{0:T(256)} %plan.1.info, bf16[4,1088,256]{2,1,0:T(8,128)(2,1)} %all-to-all-done.5.pieces), custom_call_target="tpu_custom_call" | custom-call | flops 8800000000 | bytes 8000000 | tf_op jit(solution)/shard_map/collect/pallas_call | solution.py:225
  489.8 2.8 add_rows.14
  492.6 16.3 %input_back.1 = bf16[4,1088,256]{2,1,0:T(8,128)(2,1)} custom-call(s32[201]{0:T(256)} %plan.1.info, bf16[2,4,3,64,256]{4,3,2,1,0:T(8,128)(2,1)} %pad_maximum_fusion.4.refs_1_.refs_0_, bf16[2,4,3,64,256]{4,3,2,1,0:T(8,128)(2,1)} %collective-permute-done.1.refs_2_.refs_1_, bf16[2,4,3,64,256]{4,3,2,1,0:T(8,128)(2,1)} %collective-permute-done.3.refs_3_.refs_2_, ...), custom_call_target="tpu_custom_call" | custom-call | flops 27499999232 | bytes 25000000 | tf_op jit(solution)/shard_map/input_back/pallas_call | solution.py:664
  508.9 5.0 all-to-all-start.8
  516.4 16.6 %collective-permute-done.44.refs_2_ = bf16[2,4,64,768]{3,2,1,0:T(8,128)(2,1)S(1)} collective-permute-done((bf16[2,4,64,768]{3,2,1,0:T(8,128)(2,1)}, bf16[2,4,64,768]{3,2,1,0:T(8,128)(2,1)S(1)}, u32[]{:S(2)}, u32[]{:S(2)}) %collective-permute-start.44) | collective-permute-done | bytes 786464 | tf_op jit(solution)/shard_map/ppermute | solution.py:1010
  534.8 2.6 add_rows.15
  540.1 24.7 %all-to-all-done.8.pieces = bf16[4,1088,256]{2,1,0:T(8,128)(2,1)S(1)} async-done(((bf16[4,1088,256]{2,1,0:T(8,128)(2,1)}), bf16[4,1088,256]{2,1,0:T(8,128)(2,1)S(1)}, u32[]{:S(2)}, u32[]{:S(2)}) %all-to-all-start.8) | async-done | bytes 2228256 | tf_op jit(solution)/shard_map/all_to_all | solution.py:1006
  567.0 3.1 add_cols.5
  570.1 3.9 all-to-all-start.9
  581.1 10.8 %collect.3 = f32[4096,256]{1,0:T(8,128)} custom-call(s32[201]{0:T(256)} %plan.1.info, bf16[4,1088,256]{2,1,0:T(8,128)(2,1)} %copy-done.9), custom_call_target="tpu_custom_call" | custom-call | flops 8800000000 | bytes 8000000 | tf_op jit(solution)/shard_map/collect/pallas_call | solution.py:225
  (326 shorter events, 84.9 us)
Async XLA Ops:
  2.5 26.4 %all-to-all-start.1 = ((bf16[4,3,128,256]{3,2,1,0:T(8,128)(2,1)}), bf16[4,3,128,256]{3,2,1,0:T(8,128)(2,1)S(1)}, u32[]{:S(2)}, u32[]{:S(2)}) async-start(bf16[4,3,128,256]{3,2,1,0:T(8,128)(2,1)} %broadcast_in_dim.139), calls=%async_computation.1 | async-start | bytes 1572864 | tf_op jit(solution)/shard_map/all_to_all | solution.py:1006
  28.9 57.0 %all-to-all-start = ((bf16[4,1088,256]{2,1,0:T(8,128)(2,1)}), bf16[4,1088,256]{2,1,0:T(8,128)(2,1)S(1)}, u32[]{:S(2)}, u32[]{:S(2)}) async-start(bf16[4,1088,256]{2,1,0:T(8,128)(2,1)} %spread.2), calls=%async_computation | async-start | bytes 4456448 | tf_op jit(solution)/shard_map/all_to_all | solution.py:1006
  33.4 10.4 %collective-permute-start = (bf16[1,4,3,64,256]{4,3,2,1,0:T(8,128)(2,1)}, bf16[1,4,3,64,256]{4,3,2,1,0:T(8,128)(2,1)}, u32[]{:S(2)}, u32[]{:S(2)}) collective-permute-start(bf16[1,4,3,64,256]{4,3,2,1,0:T(8,128)(2,1)} %get-tuple-element.325), channel_id=1, source_target_pairs={{0,8},{4,12},{8,0},{12,4},{16,24},{20,28},{24,16},{28,20},{1,9},{5... | collective-permute-start | bytes 1179656 | tf_op jit(solution)/shard_map/ppermute | solution.py:1010
  35.9 11.6 %collective-permute-start.2 = (bf16[1,4,3,64,256]{4,3,2,1,0:T(8,128)(2,1)S(1)}, bf16[1,4,3,64,256]{4,3,2,1,0:T(8,128)(2,1)}, u32[]{:S(2)}, u32[]{:S(2)}) collective-permute-start(bf16[1,4,3,64,256]{4,3,2,1,0:T(8,128)(2,1)S(1)} %get-tuple-element.324), channel_id=1, source_target_pairs={{0,16},{4,20},{8,24},{12,28},{16,0},{20,4},{24,8},{28,12},{1,17},{... | collective-permute-start | bytes 1179656 | tf_op jit(solution)/shard_map/ppermute | solution.py:1010
  38.7 35.5 %copy-start.25 = (bf16[64,128]{1,0:T(8,128)(2,1)}, bf16[64,128]{1,0:T(8,128)(2,1)S(1)}, u32[]{:S(2)}) copy-start(bf16[64,128]{1,0:T(8,128)(2,1)S(1)} %get-tuple-element.358) | copy-start | bytes 49156
  38.7 35.5 %copy-start.27 = (bf16[64,128]{1,0:T(8,128)(2,1)}, bf16[64,128]{1,0:T(8,128)(2,1)S(1)}, u32[]{:S(2)}) copy-start(bf16[64,128]{1,0:T(8,128)(2,1)S(1)} %get-tuple-element.359) | copy-start | bytes 49156
  45.9 17.9 %collective-permute-start.1 = (bf16[2,4,3,64,256]{4,3,2,1,0:T(8,128)(2,1)}, bf16[2,4,3,64,256]{4,3,2,1,0:T(8,128)(2,1)}, u32[]{:S(2)}, u32[]{:S(2)}) collective-permute-start(bf16[2,4,3,64,256]{4,3,2,1,0:T(8,128)(2,1)} %pad_maximum_fusion.4.refs_1_.refs_0_), channel_id=1, source_target_pairs={{0,16},{4,20},{8,24},{12,28},{16,0},{20,4},{24,8},{28,12},{1,17},{... | collective-permute-start | bytes 2359304 | tf_op jit(solution)/shard_map/ppermute | solution.py:1010
  49.4 17.6 %collective-permute-start.5 = (bf16[2,4,3,64,256]{4,3,2,1,0:T(8,128)(2,1)}, bf16[2,4,3,64,256]{4,3,2,1,0:T(8,128)(2,1)}, u32[]{:S(2)}, u32[]{:S(2)}) collective-permute-start(bf16[2,4,3,64,256]{4,3,2,1,0:T(8,128)(2,1)} %pad_maximum_fusion.5.refs_5_.refs_4_), channel_id=1, source_target_pairs={{0,8},{4,12},{8,0},{12,4},{16,24},{20,28},{24,16},{28,20},{1,9},{5... | collective-permute-start | bytes 2359304 | tf_op jit(solution)/shard_map/ppermute | solution.py:1010
  51.0 16.2 %collective-permute-start.3 = (bf16[2,4,3,64,256]{4,3,2,1,0:T(8,128)(2,1)}, bf16[2,4,3,64,256]{4,3,2,1,0:T(8,128)(2,1)}, u32[]{:S(2)}, u32[]{:S(2)}) collective-permute-start(bf16[2,4,3,64,256]{4,3,2,1,0:T(8,128)(2,1)} %pad_maximum_fusion.4.refs_1_.refs_0_), channel_id=1, source_target_pairs={{0,4},{4,0},{8,12},{12,8},{16,20},{20,16},{24,28},{28,24},{1,5},{5... | collective-permute-start | bytes 2359304 | tf_op jit(solution)/shard_map/ppermute | solution.py:1010
  51.1 16.2 %collective-permute-start.6 = (bf16[2,4,3,64,256]{4,3,2,1,0:T(8,128)(2,1)}, bf16[2,4,3,64,256]{4,3,2,1,0:T(8,128)(2,1)}, u32[]{:S(2)}, u32[]{:S(2)}) collective-permute-start(bf16[2,4,3,64,256]{4,3,2,1,0:T(8,128)(2,1)} %pad_maximum_fusion.5.refs_5_.refs_4_), channel_id=1, source_target_pairs={{0,4},{4,0},{8,12},{12,8},{16,20},{20,16},{24,28},{28,24},{1,5},{5... | collective-permute-start | bytes 2359304 | tf_op jit(solution)/shard_map/ppermute | solution.py:1010
  63.8 3.4 collective-permute-start.4
  67.0 2.5 collective-permute-start.7
  69.7 5.7 collective-permute-start.10
  73.0 11.1 %collective-permute-start.9 = (f32[3072]{0:T(1024)S(1)}, f32[3072]{0:T(1024)S(1)}, u32[]{:S(2)}, u32[]{:S(2)}) collective-permute-start(f32[3072]{0:T(1024)S(1)} %constant_dynamic-update-slice_fusion.6), channel_id=1, source_target_pairs={{0,2},{1,3},{2,0},{3,1},{4,6},{5,7},{6,4},{7,5},{8,10},{9,11},{10,... | collective-permute-start | bytes 36872 | tf_op jit(solution)/shard_map/ppermute | solution.py:1271
  73.0 11.1 %collective-permute-start.8 = (f32[3072]{0:T(1024)S(1)}, f32[3072]{0:T(1024)S(1)}, u32[]{:S(2)}, u32[]{:S(2)}) collective-permute-start(f32[3072]{0:T(1024)S(1)} %constant_dynamic-update-slice_fusion.6), channel_id=1, source_target_pairs={{0,1},{1,0},{2,3},{3,2},{4,5},{5,4},{6,7},{7,6},{8,9},{9,8},{10,11... | collective-permute-start | bytes 36872 | tf_op jit(solution)/shard_map/ppermute | solution.py:1271
  87.7 34.3 %all-to-all-start.2 = ((bf16[4,128,1280]{2,1,0:T(8,128)(2,1)}), bf16[4,128,1280]{2,1,0:T(8,128)(2,1)S(1)}, u32[]{:S(2)}, u32[]{:S(2)}) async-start(bf16[4,128,1280]{2,1,0:T(8,128)(2,1)} %broadcast_in_dim.142), calls=%async_computation.2 | async-start | bytes 2621440 | tf_op jit(solution)/shard_map/all_to_all | solution.py:1006
  123.0 21.9 %collective-permute-start.11 = (bf16[1,4,128,512]{3,2,1,0:T(8,128)(2,1)}, bf16[1,4,128,512]{3,2,1,0:T(8,128)(2,1)S(1)}, u32[]{:S(2)}, u32[]{:S(2)}) collective-permute-start(bf16[1,4,128,512]{3,2,1,0:T(8,128)(2,1)} %slice_bitcast_fusion.3), channel_id=1, source_target_pairs={{0,16},{4,20},{8,24},{12,28},{16,0},{20,4},{24,8},{28,12},{1,17},{... | collective-permute-start | bytes 1572872 | tf_op jit(solution)/shard_map/ppermute | solution.py:1010
  124.6 20.3 %collective-permute-start.12 = (bf16[1,4,128,768]{3,2,1,0:T(8,128)(2,1)S(1)}, bf16[1,4,128,768]{3,2,1,0:T(8,128)(2,1)S(1)}, u32[]{:S(2)}, u32[]{:S(2)}) collective-permute-start(bf16[1,4,128,768]{3,2,1,0:T(8,128)(2,1)S(1)} %slice_bitcast_fusion), channel_id=1, source_target_pairs={{0,8},{4,12},{8,0},{12,4},{16,24},{20,28},{24,16},{28,20},{1,9},{5... | collective-permute-start | bytes 2359304 | tf_op jit(solution)/shard_map/ppermute | solution.py:1010
  127.3 28.1 %all-to-all-start.3 = ((bf16[4,128,1024]{2,1,0:T(8,128)(2,1)}), bf16[4,128,1024]{2,1,0:T(8,128)(2,1)S(1)}, u32[]{:S(2)}, u32[]{:S(2)}) async-start(bf16[4,128,1024]{2,1,0:T(8,128)(2,1)} %broadcast_in_dim.152), calls=%async_computation.3 | async-start | bytes 2097152 | tf_op jit(solution)/shard_map/all_to_all | solution.py:1006
  146.2 41.2 %collective-permute-start.14 = (bf16[2,4,128,768]{3,2,1,0:T(8,128)(2,1)}, bf16[2,4,128,768]{3,2,1,0:T(8,128)(2,1)}, u32[]{:S(2)}, u32[]{:S(2)}) collective-permute-start(bf16[2,4,128,768]{3,2,1,0:T(8,128)(2,1)} %pad_maximum_fusion.refs_0_), channel_id=1, source_target_pairs={{0,16},{4,20},{8,24},{12,28},{16,0},{20,4},{24,8},{28,12},{1,17},{... | collective-permute-start | bytes 4718600 | tf_op jit(solution)/shard_map/ppermute | solution.py:1010
  146.7 43.8 %collective-permute-start.18 = (bf16[2,4,128,768]{3,2,1,0:T(8,128)(2,1)}, bf16[2,4,128,768]{3,2,1,0:T(8,128)(2,1)}, u32[]{:S(2)}, u32[]{:S(2)}) collective-permute-start(bf16[2,4,128,768]{3,2,1,0:T(8,128)(2,1)} %pad_maximum_fusion.refs_0_), channel_id=1, source_target_pairs={{0,4},{4,0},{8,12},{12,8},{16,20},{20,16},{24,28},{28,24},{1,5},{5... | collective-permute-start | bytes 4718600 | tf_op jit(solution)/shard_map/ppermute | solution.py:1010
  148.8 38.5 %collective-permute-start.13 = (bf16[2,4,128,512]{3,2,1,0:T(8,128)(2,1)}, bf16[2,4,128,512]{3,2,1,0:T(8,128)(2,1)}, u32[]{:S(2)}, u32[]{:S(2)}) collective-permute-start(bf16[2,4,128,512]{3,2,1,0:T(8,128)(2,1)} %pad_maximum_fusion.1.refs_4_.refs_0_), channel_id=1, source_target_pairs={{0,8},{4,12},{8,0},{12,4},{16,24},{20,28},{24,16},{28,20},{1,9},{5... | collective-permute-start | bytes 3145736 | tf_op jit(solution)/shard_map/ppermute | solution.py:1010
  155.4 54.3 %all-to-all-start.4 = ((bf16[4,1088,256]{2,1,0:T(8,128)(2,1)}), bf16[4,1088,256]{2,1,0:T(8,128)(2,1)S(1)}, u32[]{:S(2)}, u32[]{:S(2)}) async-start(bf16[4,1088,256]{2,1,0:T(8,128)(2,1)} %spread.3), calls=%async_computation.4 | async-start | bytes 4456448 | tf_op jit(solution)/shard_map/all_to_all | solution.py:1006
  187.3 3.8 collective-permute-start.19
  188.0 27.8 %collective-permute-start.15 = (bf16[2,4,128,512]{3,2,1,0:T(8,128)(2,1)}, bf16[2,4,128,512]{3,2,1,0:T(8,128)(2,1)}, u32[]{:S(2)}, u32[]{:S(2)}) collective-permute-start(bf16[2,4,128,512]{3,2,1,0:T(8,128)(2,1)} %pad_maximum_fusion.1.refs_4_.refs_0_), channel_id=1, source_target_pairs={{0,4},{4,0},{8,12},{12,8},{16,20},{20,16},{24,28},{28,24},{1,5},{5... | collective-permute-start | bytes 3145736 | tf_op jit(solution)/shard_map/ppermute | solution.py:1010
  189.4 14.1 %collective-permute-start.17 = (bf16[1,4,128,512]{3,2,1,0:T(8,128)(2,1)}, bf16[1,4,128,512]{3,2,1,0:T(8,128)(2,1)S(1)}, u32[]{:S(2)}, u32[]{:S(2)}) collective-permute-start(bf16[1,4,128,512]{3,2,1,0:T(8,128)(2,1)} %get-tuple-element.323), channel_id=1, source_target_pairs={{0,16},{4,20},{8,24},{12,28},{16,0},{20,4},{24,8},{28,12},{1,17},{... | collective-permute-start | bytes 1572872 | tf_op jit(solution)/shard_map/ppermute | solution.py:1010
  189.9 13.6 %collective-permute-start.20 = (bf16[1,4,128,512]{3,2,1,0:T(8,128)(2,1)S(1)}, bf16[1,4,128,512]{3,2,1,0:T(8,128)(2,1)S(1)}, u32[]{:S(2)}, u32[]{:S(2)}) collective-permute-start(bf16[1,4,128,512]{3,2,1,0:T(8,128)(2,1)S(1)} %get-tuple-element.322), channel_id=1, source_target_pairs={{0,8},{4,12},{8,0},{12,4},{16,24},{20,28},{24,16},{28,20},{1,9},{5... | collective-permute-start | bytes 1572872 | tf_op jit(solution)/shard_map/ppermute | solution.py:1010
  190.5 25.4 %collective-permute-start.16 = (bf16[2,4,128,512]{3,2,1,0:T(8,128)(2,1)}, bf16[2,4,128,512]{3,2,1,0:T(8,128)(2,1)}, u32[]{:S(2)}, u32[]{:S(2)}) collective-permute-start(bf16[2,4,128,512]{3,2,1,0:T(8,128)(2,1)} %collective-permute-done.13.refs_5_.refs_1_), channel_id=1, source_target_pairs={{0,4},{4,0},{8,12},{12,8},{16,20},{20,16},{24,28},{28,24},{1,5},{5... | collective-permute-start | bytes 3145736 | tf_op jit(solution)/shard_map/ppermute | solution.py:1010
  205.8 37.1 %collective-permute-start.21 = (bf16[2,4,128,512]{3,2,1,0:T(8,128)(2,1)}, bf16[2,4,128,512]{3,2,1,0:T(8,128)(2,1)}, u32[]{:S(2)}, u32[]{:S(2)}) collective-permute-start(bf16[2,4,128,512]{3,2,1,0:T(8,128)(2,1)} %pad_maximum_fusion.2.refs_4_), channel_id=1, source_target_pairs={{0,8},{4,12},{8,0},{12,4},{16,24},{20,28},{24,16},{28,20},{1,9},{5... | collective-permute-start | bytes 3145736 | tf_op jit(solution)/shard_map/ppermute | solution.py:1010
  206.4 38.2 %collective-permute-start.23 = (bf16[2,4,128,512]{3,2,1,0:T(8,128)(2,1)}, bf16[2,4,128,512]{3,2,1,0:T(8,128)(2,1)}, u32[]{:S(2)}, u32[]{:S(2)}) collective-permute-start(bf16[2,4,128,512]{3,2,1,0:T(8,128)(2,1)} %pad_maximum_fusion.2.refs_4_), channel_id=1, source_target_pairs={{0,4},{4,0},{8,12},{12,8},{16,20},{20,16},{24,28},{28,24},{1,5},{5... | collective-permute-start | bytes 3145736 | tf_op jit(solution)/shard_map/ppermute | solution.py:1010
  207.5 35.4 %collective-permute-start.22 = (bf16[2,4,128,512]{3,2,1,0:T(8,128)(2,1)S(1)}, bf16[2,4,128,512]{3,2,1,0:T(8,128)(2,1)}, u32[]{:S(2)}, u32[]{:S(2)}) collective-permute-start(bf16[2,4,128,512]{3,2,1,0:T(8,128)(2,1)S(1)} %pad_maximum_fusion.3.refs_0_.refs_4_), channel_id=1, source_target_pairs={{0,16},{4,20},{8,24},{12,28},{16,0},{20,4},{24,8},{28,12},{1,17},{... | collective-permute-start | bytes 3145736 | tf_op jit(solution)/shard_map/ppermute | solution.py:1010
  215.9 28.7 %collective-permute-start.25 = (bf16[2,4,128,512]{3,2,1,0:T(8,128)(2,1)S(1)}, bf16[2,4,128,512]{3,2,1,0:T(8,128)(2,1)S(1)}, u32[]{:S(2)}, u32[]{:S(2)}) collective-permute-start(bf16[2,4,128,512]{3,2,1,0:T(8,128)(2,1)S(1)} %pad_maximum_fusion.3.refs_0_.refs_4_), channel_id=1, source_target_pairs={{0,4},{4,0},{8,12},{12,8},{16,20},{20,16},{24,28},{28,24},{1,5},{5... | collective-permute-start | bytes 3145736 | tf_op jit(solution)/shard_map/ppermute | solution.py:1010
  242.9 3.9 collective-permute-start.24
  243.5 5.4 collective-permute-start.26
  244.2 33.9 %copy-start.34 = (f32[4,8,512]{2,1,0:T(8,128)S(1)}, f32[4,8,512]{2,1,0:T(8,128)}, u32[]{:S(2)}) copy-start(f32[4,8,512]{2,1,0:T(8,128)} %get-tuple-element.214) | copy-start | bytes 196612
  244.2 36.0 %collective-permute-start.28 = (bf16[4,4,128,1024]{3,2,1,0:T(8,128)(2,1)}, bf16[4,4,128,1024]{3,2,1,0:T(8,128)(2,1)}, u32[]{:S(2)}, u32[]{:S(2)}) collective-permute-start(bf16[4,4,128,1024]{3,2,1,0:T(8,128)(2,1)} %get-tuple-element.178), channel_id=1, source_target_pairs={{0,4},{4,0},{8,12},{12,8},{16,20},{20,16},{24,28},{28,24},{1,5},{5... | collective-permute-start | bytes 12582920 | tf_op jit(solution)/shard_map/ppermute | solution.py:1010
  277.2 8.0 %collective-permute-start.27 = (bf16[4,4,128,1024]{3,2,1,0:T(8,128)(2,1)}, bf16[4,4,128,1024]{3,2,1,0:T(8,128)(2,1)}, u32[]{:S(2)}, u32[]{:S(2)}) collective-permute-start(bf16[4,4,128,1024]{3,2,1,0:T(8,128)(2,1)} %get-tuple-element.168), channel_id=1, source_target_pairs={{0,4},{4,0},{8,12},{12,8},{16,20},{20,16},{24,28},{28,24},{1,5},{5... | collective-permute-start | bytes 12582920 | tf_op jit(solution)/shard_map/ppermute | solution.py:1010
  283.5 25.6 %collective-permute-start.29 = (bf16[2,4,128,512]{3,2,1,0:T(8,128)(2,1)}, bf16[2,4,128,512]{3,2,1,0:T(8,128)(2,1)S(1)}, u32[]{:S(2)}, u32[]{:S(2)}) collective-permute-start(bf16[2,4,128,512]{3,2,1,0:T(8,128)(2,1)} %get-tuple-element.180), channel_id=1, source_target_pairs={{0,16},{4,20},{8,24},{12,28},{16,0},{20,4},{24,8},{28,12},{1,17},{... | collective-permute-start | bytes 3145736 | tf_op jit(solution)/shard_map/ppermute | solution.py:1010
  284.0 25.3 %collective-permute-start.30 = (bf16[2,4,128,512]{3,2,1,0:T(8,128)(2,1)}, bf16[2,4,128,512]{3,2,1,0:T(8,128)(2,1)S(1)}, u32[]{:S(2)}, u32[]{:S(2)}) collective-permute-start(bf16[2,4,128,512]{3,2,1,0:T(8,128)(2,1)} %get-tuple-element.181), channel_id=1, source_target_pairs={{0,8},{4,12},{8,0},{12,4},{16,24},{20,28},{24,16},{28,20},{1,9},{5... | collective-permute-start | bytes 3145736 | tf_op jit(solution)/shard_map/ppermute | solution.py:1010
  302.8 78.4 %all-to-all-start.5 = ((bf16[4,1088,256]{2,1,0:T(8,128)(2,1)}), bf16[4,1088,256]{2,1,0:T(8,128)(2,1)}, u32[]{:S(2)}, u32[]{:S(2)}) async-start(bf16[4,1088,256]{2,1,0:T(8,128)(2,1)} %block_rows.1), calls=%async_computation.5 | async-start | bytes 4456448 | tf_op jit(solution)/shard_map/all_to_all | solution.py:1006
  314.1 27.9 %collective-permute-start.31 = (bf16[1,4,128,512]{3,2,1,0:T(8,128)(2,1)}, bf16[1,4,128,512]{3,2,1,0:T(8,128)(2,1)S(1)}, u32[]{:S(2)}, u32[]{:S(2)}) collective-permute-start(bf16[1,4,128,512]{3,2,1,0:T(8,128)(2,1)} %get-tuple-element.183), channel_id=1, source_target_pairs={{0,8},{4,12},{8,0},{12,4},{16,24},{20,28},{24,16},{28,20},{1,9},{5... | collective-permute-start | bytes 1572872 | tf_op jit(solution)/shard_map/ppermute | solution.py:1010
  315.1 26.9 %collective-permute-start.32 = (bf16[1,4,128,512]{3,2,1,0:T(8,128)(2,1)}, bf16[1,4,128,512]{3,2,1,0:T(8,128)(2,1)S(1)}, u32[]{:S(2)}, u32[]{:S(2)}) collective-permute-start(bf16[1,4,128,512]{3,2,1,0:T(8,128)(2,1)} %get-tuple-element.184), channel_id=1, source_target_pairs={{0,16},{4,20},{8,24},{12,28},{16,0},{20,4},{24,8},{28,12},{1,17},{... | collective-permute-start | bytes 1572872 | tf_op jit(solution)/shard_map/ppermute | solution.py:1010
  319.2 51.0 %collective-permute-start.33 = (bf16[2,4,128,512]{3,2,1,0:T(8,128)(2,1)}, bf16[2,4,128,512]{3,2,1,0:T(8,128)(2,1)S(1)}, u32[]{:S(2)}, u32[]{:S(2)}) collective-permute-start(bf16[2,4,128,512]{3,2,1,0:T(8,128)(2,1)} %get-tuple-element.191), channel_id=1, source_target_pairs={{0,16},{4,20},{8,24},{12,28},{16,0},{20,4},{24,8},{28,12},{1,17},{... | collective-permute-start | bytes 3145736 | tf_op jit(solution)/shard_map/ppermute | solution.py:1010
  320.4 49.7 %collective-permute-start.34 = (bf16[2,4,128,512]{3,2,1,0:T(8,128)(2,1)}, bf16[2,4,128,512]{3,2,1,0:T(8,128)(2,1)S(1)}, u32[]{:S(2)}, u32[]{:S(2)}) collective-permute-start(bf16[2,4,128,512]{3,2,1,0:T(8,128)(2,1)} %get-tuple-element.192), channel_id=1, source_target_pairs={{0,8},{4,12},{8,0},{12,4},{16,24},{20,28},{24,16},{28,20},{1,9},{5... | collective-permute-start | bytes 3145736 | tf_op jit(solution)/shard_map/ppermute | solution.py:1010
  351.7 25.3 %collective-permute-start.37 = (bf16[4,4,128,256]{3,2,1,0:T(8,128)(2,1)}, bf16[4,4,128,256]{3,2,1,0:T(8,128)(2,1)S(1)}, u32[]{:S(2)}, u32[]{:S(2)}) collective-permute-start(bf16[4,4,128,256]{3,2,1,0:T(8,128)(2,1)} %get-tuple-element.200), channel_id=1, source_target_pairs={{0,4},{4,0},{8,12},{12,8},{16,20},{20,16},{24,28},{28,24},{1,5},{5... | collective-permute-start | bytes 3145736 | tf_op jit(solution)/shard_map/ppermute | solution.py:1010
  375.1 15.1 %collective-permute-start.35 = (bf16[1,4,128,512]{3,2,1,0:T(8,128)(2,1)}, bf16[1,4,128,512]{3,2,1,0:T(8,128)(2,1)S(1)}, u32[]{:S(2)}, u32[]{:S(2)}) collective-permute-start(bf16[1,4,128,512]{3,2,1,0:T(8,128)(2,1)} %get-tuple-element.194), channel_id=1, source_target_pairs={{0,8},{4,12},{8,0},{12,4},{16,24},{20,28},{24,16},{28,20},{1,9},{5... | collective-permute-start | bytes 1572872 | tf_op jit(solution)/shard_map/ppermute | solution.py:1010
  376.2 15.0 %collective-permute-start.36 = (bf16[1,4,128,512]{3,2,1,0:T(8,128)(2,1)}, bf16[1,4,128,512]{3,2,1,0:T(8,128)(2,1)S(1)}, u32[]{:S(2)}, u32[]{:S(2)}) collective-permute-start(bf16[1,4,128,512]{3,2,1,0:T(8,128)(2,1)} %get-tuple-element.195), channel_id=1, source_target_pairs={{0,16},{4,20},{8,24},{12,28},{16,0},{20,4},{24,8},{28,12},{1,17},{... | collective-permute-start | bytes 1572872 | tf_op jit(solution)/shard_map/ppermute | solution.py:1010
  379.9 29.7 %collective-permute-start.38 = (bf16[2,4,128,256]{3,2,1,0:T(8,128)(2,1)}, bf16[2,4,128,256]{3,2,1,0:T(8,128)(2,1)S(1)}, u32[]{:S(2)}, u32[]{:S(2)}) collective-permute-start(bf16[2,4,128,256]{3,2,1,0:T(8,128)(2,1)} %add_rows.12), channel_id=1, source_target_pairs={{0,16},{4,20},{8,24},{12,28},{16,0},{20,4},{24,8},{28,12},{1,17},{... | collective-permute-start | bytes 1572872 | tf_op jit(solution)/shard_map/ppermute | solution.py:1010
  384.9 46.9 %all-to-all-start.6 = ((bf16[4,128,1024]{2,1,0:T(8,128)(2,1)}), bf16[4,128,1024]{2,1,0:T(8,128)(2,1)S(1)}, u32[]{:S(2)}, u32[]{:S(2)}) async-start(bf16[4,128,1024]{2,1,0:T(8,128)(2,1)} %add_cols.3), calls=%async_computation.6 | async-start | bytes 2097152 | tf_op jit(solution)/shard_map/all_to_all | solution.py:1006
  412.4 19.4 %collective-permute-start.39 = (bf16[1,4,128,256]{3,2,1,0:T(8,128)(2,1)}, bf16[1,4,128,256]{3,2,1,0:T(8,128)(2,1)S(1)}, u32[]{:S(2)}, u32[]{:S(2)}) collective-permute-start(bf16[1,4,128,256]{3,2,1,0:T(8,128)(2,1)} %add_rows.13), channel_id=1, source_target_pairs={{0,8},{4,12},{8,0},{12,4},{16,24},{20,28},{24,16},{28,20},{1,9},{5... | collective-permute-start | bytes 786440 | tf_op jit(solution)/shard_map/ppermute | solution.py:1010
  436.6 56.0 %all-to-all-start.7 = ((bf16[4,128,1280]{2,1,0:T(8,128)(2,1)}), bf16[4,128,1280]{2,1,0:T(8,128)(2,1)}, u32[]{:S(2)}, u32[]{:S(2)}) async-start(bf16[4,128,1280]{2,1,0:T(8,128)(2,1)} %add_cols.4), calls=%async_computation.7 | async-start | bytes 2621440 | tf_op jit(solution)/shard_map/all_to_all | solution.py:1006
  472.8 15.3 %collective-permute-start.43 = (bf16[4,4,128,768]{3,2,1,0:T(8,128)(2,1)}, bf16[4,4,128,768]{3,2,1,0:T(8,128)(2,1)S(1)}, u32[]{:S(2)}, u32[]{:S(2)}) collective-permute-start(bf16[4,4,128,768]{3,2,1,0:T(8,128)(2,1)} %get-tuple-element.220), channel_id=1, source_target_pairs={{0,4},{4,0},{8,12},{12,8},{16,20},{20,16},{24,28},{28,24},{1,5},{5... | collective-permute-start | bytes 9437192 | tf_op jit(solution)/shard_map/ppermute | solution.py:1010
  473.5 19.0 %collective-permute-start.40 = (f32[6016]{0:T(1024)S(1)}, f32[6016]{0:T(1024)S(1)}, u32[]{:S(2)}, u32[]{:S(2)}) collective-permute-start(f32[6016]{0:T(1024)S(1)} %get-tuple-element.321), channel_id=1, source_target_pairs={{0,1},{1,0},{2,3},{3,2},{4,5},{5,4},{6,7},{7,6},{8,9},{9,8},{10,11... | collective-permute-start | bytes 72200 | tf_op jit(solution)/shard_map/ppermute | solution.py:1188
  475.6 17.0 %collective-permute-start.41 = (f32[6016]{0:T(1024)S(1)}, f32[6016]{0:T(1024)S(1)}, u32[]{:S(2)}, u32[]{:S(2)}) collective-permute-start(f32[6016]{0:T(1024)S(1)} %get-tuple-element.320), channel_id=1, source_target_pairs={{0,2},{1,3},{2,0},{3,1},{4,6},{5,7},{6,4},{7,5},{8,10},{9,11},{10,... | collective-permute-start | bytes 72200 | tf_op jit(solution)/shard_map/ppermute | solution.py:1188
  478.0 14.6 %collective-permute-start.42 = (f32[6016]{0:T(1024)S(1)}, f32[6016]{0:T(1024)S(1)}, u32[]{:S(2)}, u32[]{:S(2)}) collective-permute-start(f32[6016]{0:T(1024)S(1)} %get-tuple-element.319), channel_id=1, source_target_pairs={{0,3},{1,2},{2,1},{3,0},{4,7},{5,6},{6,5},{7,4},{8,11},{9,10},{10,... | collective-permute-start | bytes 72200 | tf_op jit(solution)/shard_map/ppermute | solution.py:1188
  508.9 55.8 %all-to-all-start.8 = ((bf16[4,1088,256]{2,1,0:T(8,128)(2,1)}), bf16[4,1088,256]{2,1,0:T(8,128)(2,1)S(1)}, u32[]{:S(2)}, u32[]{:S(2)}) async-start(bf16[4,1088,256]{2,1,0:T(8,128)(2,1)} %input_back.1), calls=%async_computation.8 | async-start | bytes 4456448 | tf_op jit(solution)/shard_map/all_to_all | solution.py:1006
  514.0 19.0 %collective-permute-start.44 = (bf16[2,4,64,768]{3,2,1,0:T(8,128)(2,1)}, bf16[2,4,64,768]{3,2,1,0:T(8,128)(2,1)S(1)}, u32[]{:S(2)}, u32[]{:S(2)}) collective-permute-start(bf16[2,4,64,768]{3,2,1,0:T(8,128)(2,1)} %get-tuple-element.222), channel_id=1, source_target_pairs={{0,16},{4,20},{8,24},{12,28},{16,0},{20,4},{24,8},{28,12},{1,17},{... | collective-permute-start | bytes 2359304 | tf_op jit(solution)/shard_map/ppermute | solution.py:1010
  514.9 18.7 %collective-permute-start.45 = (bf16[2,4,64,768]{3,2,1,0:T(8,128)(2,1)}, bf16[2,4,64,768]{3,2,1,0:T(8,128)(2,1)S(1)}, u32[]{:S(2)}, u32[]{:S(2)}) collective-permute-start(bf16[2,4,64,768]{3,2,1,0:T(8,128)(2,1)} %get-tuple-element.223), channel_id=1, source_target_pairs={{0,8},{4,12},{8,0},{12,4},{16,24},{20,28},{24,16},{28,20},{1,9},{5... | collective-permute-start | bytes 2359304 | tf_op jit(solution)/shard_map/ppermute | solution.py:1010
  537.4 27.4 %collective-permute-start.46 = (bf16[1,4,64,768]{3,2,1,0:T(8,128)(2,1)}, bf16[1,4,64,768]{3,2,1,0:T(8,128)(2,1)S(1)}, u32[]{:S(2)}, u32[]{:S(2)}) collective-permute-start(bf16[1,4,64,768]{3,2,1,0:T(8,128)(2,1)} %get-tuple-element.228), channel_id=1, source_target_pairs={{0,8},{4,12},{8,0},{12,4},{16,24},{20,28},{24,16},{28,20},{1,9},{5... | collective-permute-start | bytes 1179656 | tf_op jit(solution)/shard_map/ppermute | solution.py:1010
  538.9 25.9 %collective-permute-start.47 = (bf16[1,4,64,768]{3,2,1,0:T(8,128)(2,1)}, bf16[1,4,64,768]{3,2,1,0:T(8,128)(2,1)S(1)}, u32[]{:S(2)}, u32[]{:S(2)}) collective-permute-start(bf16[1,4,64,768]{3,2,1,0:T(8,128)(2,1)} %get-tuple-element.229), channel_id=1, source_target_pairs={{0,16},{4,20},{8,24},{12,28},{16,0},{20,4},{24,8},{28,12},{1,17},{... | collective-permute-start | bytes 1179656 | tf_op jit(solution)/shard_map/ppermute | solution.py:1010
  570.1 25.0 %all-to-all-start.9 = ((bf16[4,128,768]{2,1,0:T(8,128)(2,1)}), bf16[4,128,768]{2,1,0:T(8,128)(2,1)S(1)}, u32[]{:S(2)}, u32[]{:S(2)}) async-start(bf16[4,128,768]{2,1,0:T(8,128)(2,1)} %add_cols.5), calls=%async_computation.9 | async-start | bytes 1572864 | tf_op jit(solution)/shard_map/all_to_all | solution.py:1006
  574.1 2.0 collective-permute-start.48
  576.1 4.2 collective-permute-start.49
  580.3 11.7 %collective-permute-start.50 = (f32[6528]{0:T(1024)S(1)}, f32[6528]{0:T(1024)S(1)}, u32[]{:S(2)}, u32[]{:S(2)}) collective-permute-start(f32[6528]{0:T(1024)S(1)} %add.57), channel_id=1, source_target_pairs={{0,16},{4,20},{8,24},{12,28},{16,0},{20,4},{24,8},{28,12},{1,17},{... | collective-permute-start | bytes 78344 | tf_op jit(solution)/shard_map/ppermute | solution.py:1010
  (55 other events, 602.6 us)

commit v6 on v5

--- a/solution.py
+++ b/solution.py
@@ -289,7 +289,7 @@
     return [1 << b for b in range(1, nr.bit_length() - 1)]
 
 
-def load_rows(bufs, flip, scratch, nr, first=0):
+def load_rows(bufs, flip, scratch, nr, first=0, me=0):
     stride = D // nr
     for p, (g, i) in enumerate(row_places(nr, flip)):
         cols, size, n = bufs[g].shape[1], bufs[g].shape[-2], bufs[g].shape[-1]
@@ -300,7 +300,7 @@
                 continue
             for part in range(3):
                 lane = (3 * k + part) * n
-                scratch[at : at + size, lane : lane + n] = bufs[g][i, k, part]
+                scratch[at : at + size, lane : lane + n] = bufs[g][i, me ^ k, part]
 
 
 def const_spec(shape):
@@ -317,8 +317,8 @@
 
     @pl.when(pl.program_id(0) == 0)
     def _():
-        load_rows(bufs_a, False, weight, nr)
-        load_rows(bufs_b, True, weight, nr, bw // 2)
+        load_rows(bufs_a, False, weight, nr, 0, info[0])
+        load_rows(bufs_b, True, weight, nr, bw // 2, info[0])
 
     place_features(pieces, info, parts, whole)
     values = whole[...]
@@ -633,8 +633,8 @@
 
     @pl.when(pl.program_id(0) == 0)
     def _():
-        load_rows(bufs_a, False, weight, nr)
-        load_rows(bufs_b, True, weight, nr, bw // 2)
+        load_rows(bufs_a, False, weight, nr, 0, info[0])
+        load_rows(bufs_b, True, weight, nr, bw // 2, info[0])
         sums[...] = jnp.zeros_like(sums)
 
     grad = nt_dot(dqkv[...], weight[...])
@@ -1240,7 +1240,11 @@
     hidden = fc1_weight.shape[1]
     half = hidden // 2
     fc2_t = fc2_weight.T
-    qkv_stack = gather_cols(jnp.transpose(qkv_weight, (1, 0, 2)), cols)
+    qkv_own = jnp.transpose(qkv_weight, (1, 0, 2))
+    qkv_stack = jnp.stack(
+        [qkv_own]
+        + [lax.ppermute(qkv_own, "col", [(i, i ^ k) for i in range(cols)]) for k in range(1, cols)]
+    )
     x_sent = spread(tokens_in, info, cols, per, rows)
     x_pieces = col_exchange(x_sent)
     qkv_stack = after(qkv_stack, x_sent)

time: 607 us -> 599 us (0.987)
    all_to_all x10 -> x9, waiting for transfers between devices: 40.2 us -> 33.3 us  [col_exchange(): return lax.all_to_all(values, 'col', 0, 0, tiled=True)]
    all_to_all x10 -> x9, starting transfers between devices: 44.9 us -> 40.1 us  [col_exchange(): return lax.all_to_all(values, 'col', 0, 0, tiled=True)]
    unnamed x134 -> x140, local copies, waits for them, and re-layouts: 16.9 us -> 17.7 us
  transfers between devices with their start and end apart: 61 -> 63, of which waited for: 20 -> 19; matrix products, arithmetic and copies ran while one was open for 6% -> 6% of each run, Pallas kernels for 57% -> 58%
where the time goes in v6:
time: 599 us; the launch traced here: 588 us
  Pallas kernels  364 us (61%)
  starting transfers between devices  87.7 us (15%)
  waiting for transfers between devices  83.6 us (14%)
  local copies, waits for them, and re-layouts  29.4 us (5%)
  other arithmetic  20.8 us (3%)
    pallas_call x4, Pallas kernels, attend_back(): pl.pallas_call(partial(attend_back_kernel, width, len(held)), out_shape=[...  73.9 us
    pallas_call x4, Pallas kernels, attend(): pl.pallas_call(partial(attend_kernel, width, len(held)), out_shape=[jax.S...  56.2 us
    pallas_call x2, Pallas kernels, mlp_grads(): pl.pallas_call(partial(mlp_grads_kernel, nr), out_shape=[act, act, half,...  54.3 us
    ppermute x45, waiting for transfers between devices, row_swap(): return lax.ppermute(values, 'row', [(i, i ^ bit) for i in range(nr)])  40.4 us
    all_to_all x9, starting transfers between devices, col_exchange(): return lax.all_to_all(values, 'col', 0, 0, tiled=True)  40.1 us
    all_to_all x9, waiting for transfers between devices, col_exchange(): return lax.all_to_all(values, 'col', 0, 0, tiled=True)  33.3 us
    ppermute x45, starting transfers between devices, row_swap(): return lax.ppermute(values, 'row', [(i, i ^ bit) for i in range(nr)])  32.9 us
    pallas_call x8, Pallas kernels, reduce_weight(): pl.pallas_call(partial(add_kernel, sizes), out_shape=[jax.ShapeDtypeStruc...  21.9 us
  transfers between devices with their start and end apart: 63, of which 19 were waited for; matrix products, arithmetic and copies ran while one was open for 6% of the time, Pallas kernels for 58%

profile of v6, /device:TPU:0, one launch (start us, length us, event | category | flops | bytes accessed | tf_op | source)
XLA Modules:
  0.0 588.3 jit_solution(14483345741743952050)
XLA Ops:
  0.6 5.1 collective-permute-start.2
  6.4 2.0 plan.1.info
  8.4 10.5 %spread.2 = bf16[4,1088,256]{2,1,0:T(8,128)(2,1)} custom-call(s32[201]{0:T(256)} %plan.1.info, bf16[4096,256]{1,0:T(8,128)(2,1)} %x_ref.1), custom_call_target="tpu_custom_call" | custom-call | flops 7699999744 | bytes 7000000 | tf_op jit(solution)/shard_map/spread/pallas_call | solution.py:175
  18.8 5.1 all-to-all-start
  30.2 4.6 collective-permute-done.3
  34.8 2.0 pad_maximum_fusion.5.refs_1_.refs_0_
  38.3 1.9 pad_maximum_fusion.6.refs_5_.refs_4_
  42.4 10.5 %spread.3 = bf16[4,1088,256]{2,1,0:T(8,128)(2,1)} custom-call(s32[201]{0:T(256)} %plan.1.info, bf16[4096,256]{1,0:T(8,128)(2,1)} %x_ref.2), custom_call_target="tpu_custom_call" | custom-call | flops 7699999744 | bytes 7000000 | tf_op jit(solution)/shard_map/spread/pallas_call | solution.py:175
  54.3 3.2 collective-permute-done.8.refs_6_.refs_5_
  57.7 2.3 collective-permute-done.10.refs_8_.refs_7_
  60.2 3.3 collective-permute-start.13
  65.9 9.3 %collective-permute-done.12 = f32[3072]{0:T(1024)S(1)} collective-permute-done((f32[3072]{0:T(1024)S(1)}, f32[3072]{0:T(1024)S(1)}, u32[]{:S(2)}, u32[]{:S(2)}) %collective-permute-start.12) | collective-permute-done | bytes 12320 | tf_op jit(solution)/shard_map/ppermute | solution.py:1275
  78.8 3.5 all-to-all-start.1
  82.4 14.9 %norm_qkv.1 = (bf16[1088,1024]{1,0:T(8,128)(2,1)}, bf16[1088,1024]{1,0:T(8,128)(2,1)}, bf16[1088,3072]{1,0:T(8,128)(2,1)}) custom-call(s32[201]{0:T(256)} %plan.1.info, bf16[4,1088,256]{2,1,0:T(8,128)(2,1)} %copy-done.10, bf16[2,4,3,64,256]{4,3,2,1,0:T(8,128)(2,1)} %pad_maximum_fusion.5.refs_1_.refs_0_, ...), custom_call_target="tpu_custom_call" | custom-call | flops 20899999744 | bytes 19000000 | tf_op jit(solution)/shard_map/norm_qkv/pallas_call | solution.py:339
  97.3 14.1 %attend.4 = (bf16[1088,1024]{1,0:T(8,128)(2,1)}, bf16[16,1400,256]{2,1,0:T(8,128)(2,1)}, f32[1400,1024]{1,0:T(8,128)}) custom-call(s32[201]{0:T(256)} %plan.1.info, bf16[1088,3072]{1,0:T(8,128)(2,1)} %get-tuple-element.204.qkv, bf16[128,128]{1,0:T(8,128)(2,1)} %pad_maximum_fusion.13.tables, s32[200,128]{1,0:T(8,128)} %constant.41.clone.shifts, ...), custom_call_target="tpu_custom_call" | custom-call | flops 15399999488 | bytes 14000000 | tf_op jit(solution)/shard_map/attend/pallas_call | solution.py:820
  111.4 1.8 all-to-all-done.1
  118.4 3.5 all-to-all-start.2
  121.9 14.0 %attend.5 = (bf16[1088,1024]{1,0:T(8,128)(2,1)}, bf16[16,1400,256]{2,1,0:T(8,128)(2,1)}, f32[1400,1024]{1,0:T(8,128)}) custom-call(s32[201]{0:T(256)} %plan.1.info, bf16[1088,3072]{1,0:T(8,128)(2,1)} %get-tuple-element.204.qkv, bf16[128,128]{1,0:T(8,128)(2,1)} %pad_maximum_fusion.13.tables, ...), custom_call_target="tpu_custom_call", output_to_operand_aliasing={{0}: (5, {}), {1}: (6, {}), {2}: (7, {})} | custom-call | flops 15399999488 | bytes 14000000 | tf_op jit(solution)/shard_map/attend/pallas_call | solution.py:820
  137.7 2.1 pad_maximum_fusion.1.refs_4_.refs_0_
  140.4 6.1 %all-to-all-done.2 = bf16[4,128,1024]{2,1,0:T(8,128)(2,1)S(1)} async-done(((bf16[4,128,1024]{2,1,0:T(8,128)(2,1)}), bf16[4,128,1024]{2,1,0:T(8,128)(2,1)S(1)}, u32[]{:S(2)}, u32[]{:S(2)}) %all-to-all-start.2) | async-done | bytes 1048608 | tf_op jit(solution)/shard_map/all_to_all | solution.py:1006
  146.5 3.8 all-to-all-start.3
  150.4 14.0 %attend.6 = (bf16[1088,1024]{1,0:T(8,128)(2,1)}, bf16[16,1400,256]{2,1,0:T(8,128)(2,1)}, f32[1400,1024]{1,0:T(8,128)}) custom-call(s32[201]{0:T(256)} %plan.1.info, bf16[1088,3072]{1,0:T(8,128)(2,1)} %get-tuple-element.204.qkv, bf16[128,128]{1,0:T(8,128)(2,1)} %pad_maximum_fusion.13.tables, ...), custom_call_target="tpu_custom_call", output_to_operand_aliasing={{0}: (5, {}), {1}: (6, {}), {2}: (7, {})} | custom-call | flops 15399999488 | bytes 14000000 | tf_op jit(solution)/shard_map/attend/pallas_call | solution.py:820
  164.4 14.1 %attend.7 = (bf16[1088,1024]{1,0:T(8,128)(2,1)}, bf16[16,1400,256]{2,1,0:T(8,128)(2,1)}, f32[1400,1024]{1,0:T(8,128)}) custom-call(s32[201]{0:T(256)} %plan.1.info, bf16[1088,3072]{1,0:T(8,128)(2,1)} %get-tuple-element.204.qkv, bf16[128,128]{1,0:T(8,128)(2,1)} %pad_maximum_fusion.13.tables, ...), custom_call_target="tpu_custom_call", output_to_operand_aliasing={{0}: (5, {}), {1}: (6, {}), {2}: (7, {})} | custom-call | flops 15399999488 | bytes 14000000 | tf_op jit(solution)/shard_map/attend/pallas_call | solution.py:820
  182.3 7.8 %proj_norm.1 = (f32[1088,1024]{1,0:T(8,128)}, bf16[1088,1024]{1,0:T(8,128)(2,1)}) custom-call(bf16[2,4,128,768]{3,2,1,0:T(8,128)(2,1)} %pad_maximum_fusion.refs_0_, bf16[2,4,128,768]{3,2,1,0:T(8,128)(2,1)} %collective-permute-done.17.refs_1_, bf16[2,4,128,768]{3,2,1,0:T(8,128)(2,1)} %collective-permute-done.21.refs_2_, ...), custom_call_target="tpu_custom_call" | custom-call | flops 12099999744 | bytes 11000000 | tf_op jit(solution)/shard_map/proj_norm/pallas_call | solution.py:412
  190.2 4.5 collective-permute-done.20
  194.7 2.3 pad_maximum_fusion.2.refs_4_
  202.2 4.8 join.1.refs_9_.refs_11_
  207.0 27.0 %mlp_grads.2 = (bf16[1088,2048]{1,0:T(8,128)(2,1)}, bf16[1088,2048]{1,0:T(8,128)(2,1)}, bf16[4,4,128,1024]{3,2,1,0:T(8,128)(2,1)}, bf16[4,4,128,1024]{3,2,1,0:T(8,128)(2,1)}, f32[4,8,512]{2,1,0:T(8,128)}) custom-call(bf16[2,4,128,768]{3,2,1,0:T(8,128)(2,1)} %pad_maximum_fusion.refs_0_, bf16[2,4,128,768]{3,2,1,0:T(8,128)(2,1)} %collective-permute-done.17.refs_1_, ...), custom_call_target="tpu_custom_call" | custom-call | flops 41799999488 | bytes 38000000 | tf_op jit(solution)/shard_map/mlp_grads/pallas_call | solution.py:469
  235.7 2.2 collective-permute-done.27.refs_7_
  237.9 2.1 collective-permute-done.29.refs_3_.refs_7_
  241.0 27.3 %mlp_grads.3 = (bf16[1088,2048]{1,0:T(8,128)(2,1)}, bf16[1088,2048]{1,0:T(8,128)(2,1)}, bf16[4,4,128,1024]{3,2,1,0:T(8,128)(2,1)}, bf16[4,4,128,1024]{3,2,1,0:T(8,128)(2,1)}, f32[4,8,512]{2,1,0:T(8,128)}) custom-call(bf16[2,4,128,512]{3,2,1,0:T(8,128)(2,1)} %copy-done.13, bf16[2,4,128,512]{3,2,1,0:T(8,128)(2,1)} %collective-permute-done.25.refs_1_.refs_5_, ...), custom_call_target="tpu_custom_call" | custom-call | flops 41799999488 | bytes 38000000 | tf_op jit(solution)/shard_map/mlp_grads/pallas_call | solution.py:469
  271.2 3.3 add_rows.8
  276.3 17.6 %block_rows.1 = bf16[4,1088,256]{2,1,0:T(8,128)(2,1)} custom-call(s32[201]{0:T(256)} %plan.1.info, bf16[2,4,128,512]{3,2,1,0:T(8,128)(2,1)} %pad_maximum_fusion.1.refs_4_.refs_0_, bf16[2,4,128,512]{3,2,1,0:T(8,128)(2,1)} %collective-permute-done.16.refs_5_.refs_1_, bf16[2,4,128,512]{3,2,1,0:T(8,128)(2,1)} %collective-permute-done.18.refs_6_.refs_2_, ...), custom_call_target="tpu_custom_call" | custom-call | flops 28600000512 | bytes 26000000 | tf_op jit(solution)/shard_map/block_rows/pallas_call | solution.py:516
  293.9 5.2 all-to-all-start.4
  302.2 3.0 add_rows.9
  307.0 3.3 add_rows.10
  312.5 19.4 %mlp_back.1 = (f32[1088,1024]{1,0:T(8,128)}, bf16[1088,1024]{1,0:T(8,128)(2,1)}, f32[4,8,1024]{2,1,0:T(8,128)}) custom-call(bf16[2,4,128,768]{3,2,1,0:T(8,128)(2,1)} %pad_maximum_fusion.refs_0_, bf16[2,4,128,768]{3,2,1,0:T(8,128)(2,1)} %collective-permute-done.17.refs_1_, bf16[2,4,128,768]{3,2,1,0:T(8,128)(2,1)} %collective-permute-done.21.refs_2_, ...), custom_call_target="tpu_custom_call" | custom-call | flops 30799998976 | bytes 28000000 | tf_op jit(solution)/shard_map/mlp_back/pallas_call | solution.py:562
  333.2 9.7 %proj_back.1 = (bf16[1088,1024]{1,0:T(8,128)(2,1)}, bf16[4,4,128,256]{3,2,1,0:T(8,128)(2,1)}, bf16[4,4,128,256]{3,2,1,0:T(8,128)(2,1)}) custom-call(bf16[2,4,128,768]{3,2,1,0:T(8,128)(2,1)} %pad_maximum_fusion.refs_0_, bf16[2,4,128,768]{3,2,1,0:T(8,128)(2,1)} %collective-permute-done.17.refs_1_, bf16[2,4,128,768]{3,2,1,0:T(8,128)(2,1)} %collective-permute-done.21.refs_2_, ...), custom_call_target="tpu_custom_call" | custom-call | flops 12099999744 | bytes 11000000 | tf_op jit(solution)/shard_map/proj_back/pallas_call | solution.py:594
  342.9 18.6 %attend_back.4 = (bf16[1088,3072]{1,0:T(8,128)(2,1)}, f32[128,256]{1,0:T(8,128)}, f32[8,768]{1,0:T(8,128)}) custom-call(s32[201]{0:T(256)} %plan.1.info, bf16[1088,3072]{1,0:T(8,128)(2,1)} %get-tuple-element.204.qkv, bf16[16,1400,256]{2,1,0:T(8,128)(2,1)} %get-tuple-element.172.exps, f32[1400,1024]{1,0:T(8,128)} %get-tuple-element.173.inv, ...), custom_call_target="tpu_custom_call" | custom-call | flops 14300000256 | bytes 13000000 | tf_op jit(solution)/shard_map/attend_back/pallas_call | solution.py:955
  363.5 3.0 add_rows.11
  369.4 2.0 add_rows.12
  372.7 3.7 add_cols.3
  376.4 5.3 all-to-all-start.5
  382.6 18.4 %attend_back.5 = (bf16[1088,3072]{1,0:T(8,128)(2,1)}, f32[128,256]{1,0:T(8,128)}, f32[8,768]{1,0:T(8,128)}) custom-call(s32[201]{0:T(256)} %plan.1.info, bf16[1088,3072]{1,0:T(8,128)(2,1)} %get-tuple-element.204.qkv, bf16[16,1400,256]{2,1,0:T(8,128)(2,1)} %get-tuple-element.172.exps, ...), custom_call_target="tpu_custom_call", output_to_operand_aliasing={{0}: (9, {})} | custom-call | flops 14300000256 | bytes 13000000 | tf_op jit(solution)/shard_map/attend_back/pallas_call | solution.py:955
  401.9 1.9 add_rows.13
  404.7 18.5 %attend_back.6 = (bf16[1088,3072]{1,0:T(8,128)(2,1)}, f32[128,256]{1,0:T(8,128)}, f32[8,768]{1,0:T(8,128)}) custom-call(s32[201]{0:T(256)} %plan.1.info, bf16[1088,3072]{1,0:T(8,128)(2,1)} %get-tuple-element.204.qkv, bf16[16,1400,256]{2,1,0:T(8,128)(2,1)} %get-tuple-element.172.exps, ...), custom_call_target="tpu_custom_call", output_to_operand_aliasing={{0}: (9, {})} | custom-call | flops 14300000256 | bytes 13000000 | tf_op jit(solution)/shard_map/attend_back/pallas_call | solution.py:955
  423.9 4.2 add_cols.4
  428.0 4.7 all-to-all-start.6
  432.7 18.4 %attend_back.7 = (bf16[1088,3072]{1,0:T(8,128)(2,1)}, f32[128,256]{1,0:T(8,128)}, f32[8,768]{1,0:T(8,128)}) custom-call(s32[201]{0:T(256)} %plan.1.info, bf16[1088,3072]{1,0:T(8,128)(2,1)} %get-tuple-element.204.qkv, bf16[16,1400,256]{2,1,0:T(8,128)(2,1)} %get-tuple-element.172.exps, ...), custom_call_target="tpu_custom_call", output_to_operand_aliasing={{0}: (9, {})} | custom-call | flops 14300000256 | bytes 13000000 | tf_op jit(solution)/shard_map/attend_back/pallas_call | solution.py:955
  451.2 12.7 %qkv_grad.1 = (bf16[4,4,128,768]{3,2,1,0:T(8,128)(2,1)}, bf16[4,4,128,768]{3,2,1,0:T(8,128)(2,1)}) custom-call(bf16[1088,1024]{1,0:T(8,128)(2,1)} %get-tuple-element.206.n1, bf16[1088,3072]{1,0:T(8,128)(2,1)} %get-tuple-element.224.dqkv.refs_8_), custom_call_target="tpu_custom_call" | custom-call | flops 15399999488 | bytes 14000000 | tf_op jit(solution)/shard_map/qkv_grad/pallas_call | solution.py:615
  465.1 2.1 collective-permute-start.43
  467.2 2.4 collective-permute-start.44
  469.6 10.0 %collect.2 = bf16[4096,256]{1,0:T(8,128)(2,1)} custom-call(s32[201]{0:T(256)} %plan.1.info, bf16[4,1088,256]{2,1,0:T(8,128)(2,1)} %all-to-all-done.4.pieces), custom_call_target="tpu_custom_call" | custom-call | flops 8800000000 | bytes 8000000 | tf_op jit(solution)/shard_map/collect/pallas_call | solution.py:225
  479.6 1.7 copy-done
  481.3 2.8 add_rows.14
  484.2 16.3 %input_back.1 = bf16[4,1088,256]{2,1,0:T(8,128)(2,1)} custom-call(s32[201]{0:T(256)} %plan.1.info, bf16[2,4,3,64,256]{4,3,2,1,0:T(8,128)(2,1)} %pad_maximum_fusion.5.refs_1_.refs_0_, bf16[2,4,3,64,256]{4,3,2,1,0:T(8,128)(2,1)} %collective-permute-done.4.refs_2_.refs_1_, bf16[2,4,3,64,256]{4,3,2,1,0:T(8,128)(2,1)} %collective-permute-done.6.refs_3_.refs_2_, ...), custom_call_target="tpu_custom_call" | custom-call | flops 27499999232 | bytes 25000000 | tf_op jit(solution)/shard_map/input_back/pallas_call | solution.py:664
  500.5 5.0 all-to-all-start.7
  507.9 16.6 %collective-permute-done.47.refs_2_ = bf16[2,4,64,768]{3,2,1,0:T(8,128)(2,1)S(1)} collective-permute-done((bf16[2,4,64,768]{3,2,1,0:T(8,128)(2,1)}, bf16[2,4,64,768]{3,2,1,0:T(8,128)(2,1)S(1)}, u32[]{:S(2)}, u32[]{:S(2)}) %collective-permute-start.47) | collective-permute-done | bytes 786464 | tf_op jit(solution)/shard_map/ppermute | solution.py:1010
  526.3 2.6 add_rows.15
  531.5 24.7 %all-to-all-done.7.pieces = bf16[4,1088,256]{2,1,0:T(8,128)(2,1)S(1)} async-done(((bf16[4,1088,256]{2,1,0:T(8,128)(2,1)}), bf16[4,1088,256]{2,1,0:T(8,128)(2,1)S(1)}, u32[]{:S(2)}, u32[]{:S(2)}) %all-to-all-start.7) | async-done | bytes 2228256 | tf_op jit(solution)/shard_map/all_to_all | solution.py:1006
  558.5 3.1 add_cols.5
  561.6 3.9 all-to-all-start.8
  565.6 1.6 convert_reduce_fusion
  572.6 10.8 %collect.3 = f32[4096,256]{1,0:T(8,128)} custom-call(s32[201]{0:T(256)} %plan.1.info, bf16[4,1088,256]{2,1,0:T(8,128)(2,1)} %copy-done.9), custom_call_target="tpu_custom_call" | custom-call | flops 8800000000 | bytes 8000000 | tf_op jit(solution)/shard_map/collect/pallas_call | solution.py:225
  (336 shorter events, 79.5 us)
Async XLA Ops:
  0.6 24.0 %collective-permute-start.2 = (bf16[3,128,256]{2,1,0:T(8,128)(2,1)}, bf16[3,128,256]{2,1,0:T(8,128)(2,1)S(1)}, u32[]{:S(2)}, u32[]{:S(2)}) collective-permute-start(bf16[3,128,256]{2,1,0:T(8,128)(2,1)} %bitcast.84), channel_id=1, source_target_pairs={{0,3},{1,2},{2,1},{3,0},{4,7},{5,6},{6,5},{7,4},{8,11},{9,10},{10,... | collective-permute-start | bytes 589832 | tf_op jit(solution)/shard_map/ppermute | solution.py:1246
  5.8 18.9 %collective-permute-start.1 = (bf16[3,128,256]{2,1,0:T(8,128)(2,1)}, bf16[3,128,256]{2,1,0:T(8,128)(2,1)S(1)}, u32[]{:S(2)}, u32[]{:S(2)}) collective-permute-start(bf16[3,128,256]{2,1,0:T(8,128)(2,1)} %bitcast.85), channel_id=1, source_target_pairs={{0,2},{1,3},{2,0},{3,1},{4,6},{5,7},{6,4},{7,5},{8,10},{9,11},{10,... | collective-permute-start | bytes 589832 | tf_op jit(solution)/shard_map/ppermute | solution.py:1246
  5.8 18.9 %collective-permute-start = (bf16[3,128,256]{2,1,0:T(8,128)(2,1)}, bf16[3,128,256]{2,1,0:T(8,128)(2,1)S(1)}, u32[]{:S(2)}, u32[]{:S(2)}) collective-permute-start(bf16[3,128,256]{2,1,0:T(8,128)(2,1)} %bitcast.86), channel_id=1, source_target_pairs={{0,1},{1,0},{2,3},{3,2},{4,5},{5,4},{6,7},{7,6},{8,9},{9,8},{10,11... | collective-permute-start | bytes 589832 | tf_op jit(solution)/shard_map/ppermute | solution.py:1246
  18.8 58.2 %all-to-all-start = ((bf16[4,1088,256]{2,1,0:T(8,128)(2,1)}), bf16[4,1088,256]{2,1,0:T(8,128)(2,1)S(1)}, u32[]{:S(2)}, u32[]{:S(2)}) async-start(bf16[4,1088,256]{2,1,0:T(8,128)(2,1)} %spread.2), calls=%async_computation | async-start | bytes 4456448 | tf_op jit(solution)/shard_map/all_to_all | solution.py:1006
  24.9 9.9 %collective-permute-start.3 = (bf16[1,4,3,64,256]{4,3,2,1,0:T(8,128)(2,1)S(1)}, bf16[1,4,3,64,256]{4,3,2,1,0:T(8,128)(2,1)}, u32[]{:S(2)}, u32[]{:S(2)}) collective-permute-start(bf16[1,4,3,64,256]{4,3,2,1,0:T(8,128)(2,1)S(1)} %get-tuple-element.325), channel_id=1, source_target_pairs={{0,8},{4,12},{8,0},{12,4},{16,24},{20,28},{24,16},{28,20},{1,9},{5... | collective-permute-start | bytes 1179656 | tf_op jit(solution)/shard_map/ppermute | solution.py:1010
  26.5 11.8 %collective-permute-start.5 = (bf16[1,4,3,64,256]{4,3,2,1,0:T(8,128)(2,1)S(1)}, bf16[1,4,3,64,256]{4,3,2,1,0:T(8,128)(2,1)}, u32[]{:S(2)}, u32[]{:S(2)}) collective-permute-start(bf16[1,4,3,64,256]{4,3,2,1,0:T(8,128)(2,1)S(1)} %get-tuple-element.324), channel_id=1, source_target_pairs={{0,16},{4,20},{8,24},{12,28},{16,0},{20,4},{24,8},{28,12},{1,17},{... | collective-permute-start | bytes 1179656 | tf_op jit(solution)/shard_map/ppermute | solution.py:1010
  29.2 35.5 %copy-start.28 = (bf16[64,128]{1,0:T(8,128)(2,1)}, bf16[64,128]{1,0:T(8,128)(2,1)S(1)}, u32[]{:S(2)}) copy-start(bf16[64,128]{1,0:T(8,128)(2,1)S(1)} %get-tuple-element.359) | copy-start | bytes 49156
  36.8 17.6 %collective-permute-start.4 = (bf16[2,4,3,64,256]{4,3,2,1,0:T(8,128)(2,1)}, bf16[2,4,3,64,256]{4,3,2,1,0:T(8,128)(2,1)}, u32[]{:S(2)}, u32[]{:S(2)}) collective-permute-start(bf16[2,4,3,64,256]{4,3,2,1,0:T(8,128)(2,1)} %pad_maximum_fusion.5.refs_1_.refs_0_), channel_id=1, source_target_pairs={{0,16},{4,20},{8,24},{12,28},{16,0},{20,4},{24,8},{28,12},{1,17},{... | collective-permute-start | bytes 2359304 | tf_op jit(solution)/shard_map/ppermute | solution.py:1010
  40.2 17.3 %collective-permute-start.8 = (bf16[2,4,3,64,256]{4,3,2,1,0:T(8,128)(2,1)}, bf16[2,4,3,64,256]{4,3,2,1,0:T(8,128)(2,1)}, u32[]{:S(2)}, u32[]{:S(2)}) collective-permute-start(bf16[2,4,3,64,256]{4,3,2,1,0:T(8,128)(2,1)} %pad_maximum_fusion.6.refs_5_.refs_4_), channel_id=1, source_target_pairs={{0,8},{4,12},{8,0},{12,4},{16,24},{20,28},{24,16},{28,20},{1,9},{5... | collective-permute-start | bytes 2359304 | tf_op jit(solution)/shard_map/ppermute | solution.py:1010
  41.8 15.9 %collective-permute-start.6 = (bf16[2,4,3,64,256]{4,3,2,1,0:T(8,128)(2,1)}, bf16[2,4,3,64,256]{4,3,2,1,0:T(8,128)(2,1)}, u32[]{:S(2)}, u32[]{:S(2)}) collective-permute-start(bf16[2,4,3,64,256]{4,3,2,1,0:T(8,128)(2,1)} %pad_maximum_fusion.5.refs_1_.refs_0_), channel_id=1, source_target_pairs={{0,4},{4,0},{8,12},{12,8},{16,20},{20,16},{24,28},{28,24},{1,5},{5... | collective-permute-start | bytes 2359304 | tf_op jit(solution)/shard_map/ppermute | solution.py:1010
  41.9 15.8 %collective-permute-start.9 = (bf16[2,4,3,64,256]{4,3,2,1,0:T(8,128)(2,1)}, bf16[2,4,3,64,256]{4,3,2,1,0:T(8,128)(2,1)}, u32[]{:S(2)}, u32[]{:S(2)}) collective-permute-start(bf16[2,4,3,64,256]{4,3,2,1,0:T(8,128)(2,1)} %pad_maximum_fusion.6.refs_5_.refs_4_), channel_id=1, source_target_pairs={{0,4},{4,0},{8,12},{12,8},{16,20},{20,16},{24,28},{28,24},{1,5},{5... | collective-permute-start | bytes 2359304 | tf_op jit(solution)/shard_map/ppermute | solution.py:1010
  54.3 3.4 collective-permute-start.7
  57.5 2.5 collective-permute-start.10
  60.2 5.7 collective-permute-start.13
  63.5 11.7 %collective-permute-start.12 = (f32[3072]{0:T(1024)S(1)}, f32[3072]{0:T(1024)S(1)}, u32[]{:S(2)}, u32[]{:S(2)}) collective-permute-start(f32[3072]{0:T(1024)S(1)} %constant_dynamic-update-slice_fusion.6), channel_id=1, source_target_pairs={{0,2},{1,3},{2,0},{3,1},{4,6},{5,7},{6,4},{7,5},{8,10},{9,11},{10,... | collective-permute-start | bytes 36872 | tf_op jit(solution)/shard_map/ppermute | solution.py:1275
  63.5 11.7 %collective-permute-start.11 = (f32[3072]{0:T(1024)S(1)}, f32[3072]{0:T(1024)S(1)}, u32[]{:S(2)}, u32[]{:S(2)}) collective-permute-start(f32[3072]{0:T(1024)S(1)} %constant_dynamic-update-slice_fusion.6), channel_id=1, source_target_pairs={{0,1},{1,0},{2,3},{3,2},{4,5},{5,4},{6,7},{7,6},{8,9},{9,8},{10,11... | collective-permute-start | bytes 36872 | tf_op jit(solution)/shard_map/ppermute | solution.py:1275
  78.8 34.4 %all-to-all-start.1 = ((bf16[4,128,1280]{2,1,0:T(8,128)(2,1)}), bf16[4,128,1280]{2,1,0:T(8,128)(2,1)S(1)}, u32[]{:S(2)}, u32[]{:S(2)}) async-start(bf16[4,128,1280]{2,1,0:T(8,128)(2,1)} %broadcast_in_dim.135), calls=%async_computation.1 | async-start | bytes 2621440 | tf_op jit(solution)/shard_map/all_to_all | solution.py:1006
  114.1 21.9 %collective-permute-start.14 = (bf16[1,4,128,512]{3,2,1,0:T(8,128)(2,1)}, bf16[1,4,128,512]{3,2,1,0:T(8,128)(2,1)S(1)}, u32[]{:S(2)}, u32[]{:S(2)}) collective-permute-start(bf16[1,4,128,512]{3,2,1,0:T(8,128)(2,1)} %slice_bitcast_fusion.3), channel_id=1, source_target_pairs={{0,16},{4,20},{8,24},{12,28},{16,0},{20,4},{24,8},{28,12},{1,17},{... | collective-permute-start | bytes 1572872 | tf_op jit(solution)/shard_map/ppermute | solution.py:1010
  115.7 20.3 %collective-permute-start.15 = (bf16[1,4,128,768]{3,2,1,0:T(8,128)(2,1)S(1)}, bf16[1,4,128,768]{3,2,1,0:T(8,128)(2,1)S(1)}, u32[]{:S(2)}, u32[]{:S(2)}) collective-permute-start(bf16[1,4,128,768]{3,2,1,0:T(8,128)(2,1)S(1)} %slice_bitcast_fusion), channel_id=1, source_target_pairs={{0,8},{4,12},{8,0},{12,4},{16,24},{20,28},{24,16},{28,20},{1,9},{5... | collective-permute-start | bytes 2359304 | tf_op jit(solution)/shard_map/ppermute | solution.py:1010
  118.4 28.1 %all-to-all-start.2 = ((bf16[4,128,1024]{2,1,0:T(8,128)(2,1)}), bf16[4,128,1024]{2,1,0:T(8,128)(2,1)S(1)}, u32[]{:S(2)}, u32[]{:S(2)}) async-start(bf16[4,128,1024]{2,1,0:T(8,128)(2,1)} %broadcast_in_dim.145), calls=%async_computation.2 | async-start | bytes 2097152 | tf_op jit(solution)/shard_map/all_to_all | solution.py:1006
  137.2 41.3 %collective-permute-start.17 = (bf16[2,4,128,768]{3,2,1,0:T(8,128)(2,1)}, bf16[2,4,128,768]{3,2,1,0:T(8,128)(2,1)}, u32[]{:S(2)}, u32[]{:S(2)}) collective-permute-start(bf16[2,4,128,768]{3,2,1,0:T(8,128)(2,1)} %pad_maximum_fusion.refs_0_), channel_id=1, source_target_pairs={{0,16},{4,20},{8,24},{12,28},{16,0},{20,4},{24,8},{28,12},{1,17},{... | collective-permute-start | bytes 4718600 | tf_op jit(solution)/shard_map/ppermute | solution.py:1010
  137.7 43.9 %collective-permute-start.21 = (bf16[2,4,128,768]{3,2,1,0:T(8,128)(2,1)}, bf16[2,4,128,768]{3,2,1,0:T(8,128)(2,1)}, u32[]{:S(2)}, u32[]{:S(2)}) collective-permute-start(bf16[2,4,128,768]{3,2,1,0:T(8,128)(2,1)} %pad_maximum_fusion.refs_0_), channel_id=1, source_target_pairs={{0,4},{4,0},{8,12},{12,8},{16,20},{20,16},{24,28},{28,24},{1,5},{5... | collective-permute-start | bytes 4718600 | tf_op jit(solution)/shard_map/ppermute | solution.py:1010
  139.9 38.6 %collective-permute-start.16 = (bf16[2,4,128,512]{3,2,1,0:T(8,128)(2,1)}, bf16[2,4,128,512]{3,2,1,0:T(8,128)(2,1)}, u32[]{:S(2)}, u32[]{:S(2)}) collective-permute-start(bf16[2,4,128,512]{3,2,1,0:T(8,128)(2,1)} %pad_maximum_fusion.1.refs_4_.refs_0_), channel_id=1, source_target_pairs={{0,8},{4,12},{8,0},{12,4},{16,24},{20,28},{24,16},{28,20},{1,9},{5... | collective-permute-start | bytes 3145736 | tf_op jit(solution)/shard_map/ppermute | solution.py:1010
  146.5 54.3 %all-to-all-start.3 = ((bf16[4,1088,256]{2,1,0:T(8,128)(2,1)}), bf16[4,1088,256]{2,1,0:T(8,128)(2,1)S(1)}, u32[]{:S(2)}, u32[]{:S(2)}) async-start(bf16[4,1088,256]{2,1,0:T(8,128)(2,1)} %spread.3), calls=%async_computation.3 | async-start | bytes 4456448 | tf_op jit(solution)/shard_map/all_to_all | solution.py:1006
  178.5 3.8 collective-permute-start.22
  179.2 27.8 %collective-permute-start.18 = (bf16[2,4,128,512]{3,2,1,0:T(8,128)(2,1)}, bf16[2,4,128,512]{3,2,1,0:T(8,128)(2,1)}, u32[]{:S(2)}, u32[]{:S(2)}) collective-permute-start(bf16[2,4,128,512]{3,2,1,0:T(8,128)(2,1)} %pad_maximum_fusion.1.refs_4_.refs_0_), channel_id=1, source_target_pairs={{0,4},{4,0},{8,12},{12,8},{16,20},{20,16},{24,28},{28,24},{1,5},{5... | collective-permute-start | bytes 3145736 | tf_op jit(solution)/shard_map/ppermute | solution.py:1010
  180.6 14.1 %collective-permute-start.20 = (bf16[1,4,128,512]{3,2,1,0:T(8,128)(2,1)}, bf16[1,4,128,512]{3,2,1,0:T(8,128)(2,1)S(1)}, u32[]{:S(2)}, u32[]{:S(2)}) collective-permute-start(bf16[1,4,128,512]{3,2,1,0:T(8,128)(2,1)} %get-tuple-element.323), channel_id=1, source_target_pairs={{0,16},{4,20},{8,24},{12,28},{16,0},{20,4},{24,8},{28,12},{1,17},{... | collective-permute-start | bytes 1572872 | tf_op jit(solution)/shard_map/ppermute | solution.py:1010
  181.1 13.6 %collective-permute-start.23 = (bf16[1,4,128,512]{3,2,1,0:T(8,128)(2,1)S(1)}, bf16[1,4,128,512]{3,2,1,0:T(8,128)(2,1)S(1)}, u32[]{:S(2)}, u32[]{:S(2)}) collective-permute-start(bf16[1,4,128,512]{3,2,1,0:T(8,128)(2,1)S(1)} %get-tuple-element.322), channel_id=1, source_target_pairs={{0,8},{4,12},{8,0},{12,4},{16,24},{20,28},{24,16},{28,20},{1,9},{5... | collective-permute-start | bytes 1572872 | tf_op jit(solution)/shard_map/ppermute | solution.py:1010
  181.6 25.4 %collective-permute-start.19 = (bf16[2,4,128,512]{3,2,1,0:T(8,128)(2,1)}, bf16[2,4,128,512]{3,2,1,0:T(8,128)(2,1)}, u32[]{:S(2)}, u32[]{:S(2)}) collective-permute-start(bf16[2,4,128,512]{3,2,1,0:T(8,128)(2,1)} %collective-permute-done.16.refs_5_.refs_1_), channel_id=1, source_target_pairs={{0,4},{4,0},{8,12},{12,8},{16,20},{20,16},{24,28},{28,24},{1,5},{5... | collective-permute-start | bytes 3145736 | tf_op jit(solution)/shard_map/ppermute | solution.py:1010
  197.0 37.0 %collective-permute-start.24 = (bf16[2,4,128,512]{3,2,1,0:T(8,128)(2,1)}, bf16[2,4,128,512]{3,2,1,0:T(8,128)(2,1)}, u32[]{:S(2)}, u32[]{:S(2)}) collective-permute-start(bf16[2,4,128,512]{3,2,1,0:T(8,128)(2,1)} %pad_maximum_fusion.2.refs_4_), channel_id=1, source_target_pairs={{0,8},{4,12},{8,0},{12,4},{16,24},{20,28},{24,16},{28,20},{1,9},{5... | collective-permute-start | bytes 3145736 | tf_op jit(solution)/shard_map/ppermute | solution.py:1010
  197.5 38.2 %collective-permute-start.26 = (bf16[2,4,128,512]{3,2,1,0:T(8,128)(2,1)}, bf16[2,4,128,512]{3,2,1,0:T(8,128)(2,1)}, u32[]{:S(2)}, u32[]{:S(2)}) collective-permute-start(bf16[2,4,128,512]{3,2,1,0:T(8,128)(2,1)} %pad_maximum_fusion.2.refs_4_), channel_id=1, source_target_pairs={{0,4},{4,0},{8,12},{12,8},{16,20},{20,16},{24,28},{28,24},{1,5},{5... | collective-permute-start | bytes 3145736 | tf_op jit(solution)/shard_map/ppermute | solution.py:1010
  198.7 35.4 %collective-permute-start.25 = (bf16[2,4,128,512]{3,2,1,0:T(8,128)(2,1)S(1)}, bf16[2,4,128,512]{3,2,1,0:T(8,128)(2,1)}, u32[]{:S(2)}, u32[]{:S(2)}) collective-permute-start(bf16[2,4,128,512]{3,2,1,0:T(8,128)(2,1)S(1)} %pad_maximum_fusion.3.refs_0_.refs_4_), channel_id=1, source_target_pairs={{0,16},{4,20},{8,24},{12,28},{16,0},{20,4},{24,8},{28,12},{1,17},{... | collective-permute-start | bytes 3145736 | tf_op jit(solution)/shard_map/ppermute | solution.py:1010
  207.0 28.7 %collective-permute-start.28 = (bf16[2,4,128,512]{3,2,1,0:T(8,128)(2,1)S(1)}, bf16[2,4,128,512]{3,2,1,0:T(8,128)(2,1)S(1)}, u32[]{:S(2)}, u32[]{:S(2)}) collective-permute-start(bf16[2,4,128,512]{3,2,1,0:T(8,128)(2,1)S(1)} %pad_maximum_fusion.3.refs_0_.refs_4_), channel_id=1, source_target_pairs={{0,4},{4,0},{8,12},{12,8},{16,20},{20,16},{24,28},{28,24},{1,5},{5... | collective-permute-start | bytes 3145736 | tf_op jit(solution)/shard_map/ppermute | solution.py:1010
  234.0 3.9 collective-permute-start.27
  234.6 5.4 collective-permute-start.29
  235.3 36.0 %collective-permute-start.31 = (bf16[4,4,128,1024]{3,2,1,0:T(8,128)(2,1)}, bf16[4,4,128,1024]{3,2,1,0:T(8,128)(2,1)}, u32[]{:S(2)}, u32[]{:S(2)}) collective-permute-start(bf16[4,4,128,1024]{3,2,1,0:T(8,128)(2,1)} %get-tuple-element.178), channel_id=1, source_target_pairs={{0,4},{4,0},{8,12},{12,8},{16,20},{20,16},{24,28},{28,24},{1,5},{5... | collective-permute-start | bytes 12582920 | tf_op jit(solution)/shard_map/ppermute | solution.py:1010
  268.3 8.0 %collective-permute-start.30 = (bf16[4,4,128,1024]{3,2,1,0:T(8,128)(2,1)}, bf16[4,4,128,1024]{3,2,1,0:T(8,128)(2,1)}, u32[]{:S(2)}, u32[]{:S(2)}) collective-permute-start(bf16[4,4,128,1024]{3,2,1,0:T(8,128)(2,1)} %get-tuple-element.168), channel_id=1, source_target_pairs={{0,4},{4,0},{8,12},{12,8},{16,20},{20,16},{24,28},{28,24},{1,5},{5... | collective-permute-start | bytes 12582920 | tf_op jit(solution)/shard_map/ppermute | solution.py:1010
  274.6 25.6 %collective-permute-start.32 = (bf16[2,4,128,512]{3,2,1,0:T(8,128)(2,1)}, bf16[2,4,128,512]{3,2,1,0:T(8,128)(2,1)S(1)}, u32[]{:S(2)}, u32[]{:S(2)}) collective-permute-start(bf16[2,4,128,512]{3,2,1,0:T(8,128)(2,1)} %get-tuple-element.180), channel_id=1, source_target_pairs={{0,16},{4,20},{8,24},{12,28},{16,0},{20,4},{24,8},{28,12},{1,17},{... | collective-permute-start | bytes 3145736 | tf_op jit(solution)/shard_map/ppermute | solution.py:1010
  275.1 25.4 %collective-permute-start.33 = (bf16[2,4,128,512]{3,2,1,0:T(8,128)(2,1)}, bf16[2,4,128,512]{3,2,1,0:T(8,128)(2,1)S(1)}, u32[]{:S(2)}, u32[]{:S(2)}) collective-permute-start(bf16[2,4,128,512]{3,2,1,0:T(8,128)(2,1)} %get-tuple-element.181), channel_id=1, source_target_pairs={{0,8},{4,12},{8,0},{12,4},{16,24},{20,28},{24,16},{28,20},{1,9},{5... | collective-permute-start | bytes 3145736 | tf_op jit(solution)/shard_map/ppermute | solution.py:1010
  293.9 78.7 %all-to-all-start.4 = ((bf16[4,1088,256]{2,1,0:T(8,128)(2,1)}), bf16[4,1088,256]{2,1,0:T(8,128)(2,1)}, u32[]{:S(2)}, u32[]{:S(2)}) async-start(bf16[4,1088,256]{2,1,0:T(8,128)(2,1)} %block_rows.1), calls=%async_computation.4 | async-start | bytes 4456448 | tf_op jit(solution)/shard_map/all_to_all | solution.py:1006
  305.2 28.0 %collective-permute-start.34 = (bf16[1,4,128,512]{3,2,1,0:T(8,128)(2,1)}, bf16[1,4,128,512]{3,2,1,0:T(8,128)(2,1)S(1)}, u32[]{:S(2)}, u32[]{:S(2)}) collective-permute-start(bf16[1,4,128,512]{3,2,1,0:T(8,128)(2,1)} %get-tuple-element.183), channel_id=1, source_target_pairs={{0,8},{4,12},{8,0},{12,4},{16,24},{20,28},{24,16},{28,20},{1,9},{5... | collective-permute-start | bytes 1572872 | tf_op jit(solution)/shard_map/ppermute | solution.py:1010
  306.3 26.9 %collective-permute-start.35 = (bf16[1,4,128,512]{3,2,1,0:T(8,128)(2,1)}, bf16[1,4,128,512]{3,2,1,0:T(8,128)(2,1)S(1)}, u32[]{:S(2)}, u32[]{:S(2)}) collective-permute-start(bf16[1,4,128,512]{3,2,1,0:T(8,128)(2,1)} %get-tuple-element.184), channel_id=1, source_target_pairs={{0,16},{4,20},{8,24},{12,28},{16,0},{20,4},{24,8},{28,12},{1,17},{... | collective-permute-start | bytes 1572872 | tf_op jit(solution)/shard_map/ppermute | solution.py:1010
  310.4 51.2 %collective-permute-start.36 = (bf16[2,4,128,512]{3,2,1,0:T(8,128)(2,1)}, bf16[2,4,128,512]{3,2,1,0:T(8,128)(2,1)S(1)}, u32[]{:S(2)}, u32[]{:S(2)}) collective-permute-start(bf16[2,4,128,512]{3,2,1,0:T(8,128)(2,1)} %get-tuple-element.191), channel_id=1, source_target_pairs={{0,16},{4,20},{8,24},{12,28},{16,0},{20,4},{24,8},{28,12},{1,17},{... | collective-permute-start | bytes 3145736 | tf_op jit(solution)/shard_map/ppermute | solution.py:1010
  311.6 50.0 %collective-permute-start.37 = (bf16[2,4,128,512]{3,2,1,0:T(8,128)(2,1)}, bf16[2,4,128,512]{3,2,1,0:T(8,128)(2,1)S(1)}, u32[]{:S(2)}, u32[]{:S(2)}) collective-permute-start(bf16[2,4,128,512]{3,2,1,0:T(8,128)(2,1)} %get-tuple-element.192), channel_id=1, source_target_pairs={{0,8},{4,12},{8,0},{12,4},{16,24},{20,28},{24,16},{28,20},{1,9},{5... | collective-permute-start | bytes 3145736 | tf_op jit(solution)/shard_map/ppermute | solution.py:1010
  342.9 25.6 %collective-permute-start.40 = (bf16[4,4,128,256]{3,2,1,0:T(8,128)(2,1)}, bf16[4,4,128,256]{3,2,1,0:T(8,128)(2,1)S(1)}, u32[]{:S(2)}, u32[]{:S(2)}) collective-permute-start(bf16[4,4,128,256]{3,2,1,0:T(8,128)(2,1)} %get-tuple-element.200), channel_id=1, source_target_pairs={{0,4},{4,0},{8,12},{12,8},{16,20},{20,16},{24,28},{28,24},{1,5},{5... | collective-permute-start | bytes 3145736 | tf_op jit(solution)/shard_map/ppermute | solution.py:1010
  366.5 15.1 %collective-permute-start.38 = (bf16[1,4,128,512]{3,2,1,0:T(8,128)(2,1)}, bf16[1,4,128,512]{3,2,1,0:T(8,128)(2,1)S(1)}, u32[]{:S(2)}, u32[]{:S(2)}) collective-permute-start(bf16[1,4,128,512]{3,2,1,0:T(8,128)(2,1)} %get-tuple-element.194), channel_id=1, source_target_pairs={{0,8},{4,12},{8,0},{12,4},{16,24},{20,28},{24,16},{28,20},{1,9},{5... | collective-permute-start | bytes 1572872 | tf_op jit(solution)/shard_map/ppermute | solution.py:1010
  367.6 15.0 %collective-permute-start.39 = (bf16[1,4,128,512]{3,2,1,0:T(8,128)(2,1)}, bf16[1,4,128,512]{3,2,1,0:T(8,128)(2,1)S(1)}, u32[]{:S(2)}, u32[]{:S(2)}) collective-permute-start(bf16[1,4,128,512]{3,2,1,0:T(8,128)(2,1)} %get-tuple-element.195), channel_id=1, source_target_pairs={{0,16},{4,20},{8,24},{12,28},{16,0},{20,4},{24,8},{28,12},{1,17},{... | collective-permute-start | bytes 1572872 | tf_op jit(solution)/shard_map/ppermute | solution.py:1010
  371.4 29.7 %collective-permute-start.41 = (bf16[2,4,128,256]{3,2,1,0:T(8,128)(2,1)}, bf16[2,4,128,256]{3,2,1,0:T(8,128)(2,1)S(1)}, u32[]{:S(2)}, u32[]{:S(2)}) collective-permute-start(bf16[2,4,128,256]{3,2,1,0:T(8,128)(2,1)} %add_rows.12), channel_id=1, source_target_pairs={{0,16},{4,20},{8,24},{12,28},{16,0},{20,4},{24,8},{28,12},{1,17},{... | collective-permute-start | bytes 1572872 | tf_op jit(solution)/shard_map/ppermute | solution.py:1010
  376.4 46.8 %all-to-all-start.5 = ((bf16[4,128,1024]{2,1,0:T(8,128)(2,1)}), bf16[4,128,1024]{2,1,0:T(8,128)(2,1)S(1)}, u32[]{:S(2)}, u32[]{:S(2)}) async-start(bf16[4,128,1024]{2,1,0:T(8,128)(2,1)} %add_cols.3), calls=%async_computation.5 | async-start | bytes 2097152 | tf_op jit(solution)/shard_map/all_to_all | solution.py:1006
  403.8 19.4 %collective-permute-start.42 = (bf16[1,4,128,256]{3,2,1,0:T(8,128)(2,1)}, bf16[1,4,128,256]{3,2,1,0:T(8,128)(2,1)S(1)}, u32[]{:S(2)}, u32[]{:S(2)}) collective-permute-start(bf16[1,4,128,256]{3,2,1,0:T(8,128)(2,1)} %add_rows.13), channel_id=1, source_target_pairs={{0,8},{4,12},{8,0},{12,4},{16,24},{20,28},{24,16},{28,20},{1,9},{5... | collective-permute-start | bytes 786440 | tf_op jit(solution)/shard_map/ppermute | solution.py:1010
  428.0 56.1 %all-to-all-start.6 = ((bf16[4,128,1280]{2,1,0:T(8,128)(2,1)}), bf16[4,128,1280]{2,1,0:T(8,128)(2,1)}, u32[]{:S(2)}, u32[]{:S(2)}) async-start(bf16[4,128,1280]{2,1,0:T(8,128)(2,1)} %add_cols.4), calls=%async_computation.6 | async-start | bytes 2621440 | tf_op jit(solution)/shard_map/all_to_all | solution.py:1006
  464.3 15.3 %collective-permute-start.46 = (bf16[4,4,128,768]{3,2,1,0:T(8,128)(2,1)}, bf16[4,4,128,768]{3,2,1,0:T(8,128)(2,1)S(1)}, u32[]{:S(2)}, u32[]{:S(2)}) collective-permute-start(bf16[4,4,128,768]{3,2,1,0:T(8,128)(2,1)} %get-tuple-element.220), channel_id=1, source_target_pairs={{0,4},{4,0},{8,12},{12,8},{16,20},{20,16},{24,28},{28,24},{1,5},{5... | collective-permute-start | bytes 9437192 | tf_op jit(solution)/shard_map/ppermute | solution.py:1010
  465.1 19.0 %collective-permute-start.43 = (f32[6016]{0:T(1024)S(1)}, f32[6016]{0:T(1024)S(1)}, u32[]{:S(2)}, u32[]{:S(2)}) collective-permute-start(f32[6016]{0:T(1024)S(1)} %get-tuple-element.321), channel_id=1, source_target_pairs={{0,1},{1,0},{2,3},{3,2},{4,5},{5,4},{6,7},{7,6},{8,9},{9,8},{10,11... | collective-permute-start | bytes 72200 | tf_op jit(solution)/shard_map/ppermute | solution.py:1188
  467.2 17.0 %collective-permute-start.44 = (f32[6016]{0:T(1024)S(1)}, f32[6016]{0:T(1024)S(1)}, u32[]{:S(2)}, u32[]{:S(2)}) collective-permute-start(f32[6016]{0:T(1024)S(1)} %get-tuple-element.320), channel_id=1, source_target_pairs={{0,2},{1,3},{2,0},{3,1},{4,6},{5,7},{6,4},{7,5},{8,10},{9,11},{10,... | collective-permute-start | bytes 72200 | tf_op jit(solution)/shard_map/ppermute | solution.py:1188
  469.5 14.6 %collective-permute-start.45 = (f32[6016]{0:T(1024)S(1)}, f32[6016]{0:T(1024)S(1)}, u32[]{:S(2)}, u32[]{:S(2)}) collective-permute-start(f32[6016]{0:T(1024)S(1)} %get-tuple-element.319), channel_id=1, source_target_pairs={{0,3},{1,2},{2,1},{3,0},{4,7},{5,6},{6,5},{7,4},{8,11},{9,10},{10,... | collective-permute-start | bytes 72200 | tf_op jit(solution)/shard_map/ppermute | solution.py:1188
  500.5 55.8 %all-to-all-start.7 = ((bf16[4,1088,256]{2,1,0:T(8,128)(2,1)}), bf16[4,1088,256]{2,1,0:T(8,128)(2,1)S(1)}, u32[]{:S(2)}, u32[]{:S(2)}) async-start(bf16[4,1088,256]{2,1,0:T(8,128)(2,1)} %input_back.1), calls=%async_computation.7 | async-start | bytes 4456448 | tf_op jit(solution)/shard_map/all_to_all | solution.py:1006
  505.5 19.0 %collective-permute-start.47 = (bf16[2,4,64,768]{3,2,1,0:T(8,128)(2,1)}, bf16[2,4,64,768]{3,2,1,0:T(8,128)(2,1)S(1)}, u32[]{:S(2)}, u32[]{:S(2)}) collective-permute-start(bf16[2,4,64,768]{3,2,1,0:T(8,128)(2,1)} %get-tuple-element.222), channel_id=1, source_target_pairs={{0,16},{4,20},{8,24},{12,28},{16,0},{20,4},{24,8},{28,12},{1,17},{... | collective-permute-start | bytes 2359304 | tf_op jit(solution)/shard_map/ppermute | solution.py:1010
  506.4 18.7 %collective-permute-start.48 = (bf16[2,4,64,768]{3,2,1,0:T(8,128)(2,1)}, bf16[2,4,64,768]{3,2,1,0:T(8,128)(2,1)S(1)}, u32[]{:S(2)}, u32[]{:S(2)}) collective-permute-start(bf16[2,4,64,768]{3,2,1,0:T(8,128)(2,1)} %get-tuple-element.223), channel_id=1, source_target_pairs={{0,8},{4,12},{8,0},{12,4},{16,24},{20,28},{24,16},{28,20},{1,9},{5... | collective-permute-start | bytes 2359304 | tf_op jit(solution)/shard_map/ppermute | solution.py:1010
  528.9 27.4 %collective-permute-start.49 = (bf16[1,4,64,768]{3,2,1,0:T(8,128)(2,1)}, bf16[1,4,64,768]{3,2,1,0:T(8,128)(2,1)S(1)}, u32[]{:S(2)}, u32[]{:S(2)}) collective-permute-start(bf16[1,4,64,768]{3,2,1,0:T(8,128)(2,1)} %get-tuple-element.228), channel_id=1, source_target_pairs={{0,8},{4,12},{8,0},{12,4},{16,24},{20,28},{24,16},{28,20},{1,9},{5... | collective-permute-start | bytes 1179656 | tf_op jit(solution)/shard_map/ppermute | solution.py:1010
  530.4 25.9 %collective-permute-start.50 = (bf16[1,4,64,768]{3,2,1,0:T(8,128)(2,1)}, bf16[1,4,64,768]{3,2,1,0:T(8,128)(2,1)S(1)}, u32[]{:S(2)}, u32[]{:S(2)}) collective-permute-start(bf16[1,4,64,768]{3,2,1,0:T(8,128)(2,1)} %get-tuple-element.229), channel_id=1, source_target_pairs={{0,16},{4,20},{8,24},{12,28},{16,0},{20,4},{24,8},{28,12},{1,17},{... | collective-permute-start | bytes 1179656 | tf_op jit(solution)/shard_map/ppermute | solution.py:1010
  561.6 25.0 %all-to-all-start.8 = ((bf16[4,128,768]{2,1,0:T(8,128)(2,1)}), bf16[4,128,768]{2,1,0:T(8,128)(2,1)S(1)}, u32[]{:S(2)}, u32[]{:S(2)}) async-start(bf16[4,128,768]{2,1,0:T(8,128)(2,1)} %add_cols.5), calls=%async_computation.8 | async-start | bytes 1572864 | tf_op jit(solution)/shard_map/all_to_all | solution.py:1006
  565.6 2.0 collective-permute-start.51
  567.6 4.2 collective-permute-start.52
  571.8 11.7 %collective-permute-start.53 = (f32[6528]{0:T(1024)S(1)}, f32[6528]{0:T(1024)S(1)}, u32[]{:S(2)}, u32[]{:S(2)}) collective-permute-start(f32[6528]{0:T(1024)S(1)} %add.57), channel_id=1, source_target_pairs={{0,16},{4,20},{8,24},{12,28},{16,0},{20,4},{24,8},{28,12},{1,17},{... | collective-permute-start | bytes 78344 | tf_op jit(solution)/shard_map/ppermute | solution.py:1010
  (60 other events, 684.2 us)

commit v7 on v6

--- a/solution.py
+++ b/solution.py
@@ -1149,7 +1149,7 @@
         lane += n
 
 
-def finish_weights(parts, *gate):
+def finish_weights(parts, *gate, last=()):
     cols, bw, _ = parts[0][4]
     groups = [(sizes, axis, shape[2]) for sizes, axis, _, _, shape in parts]
     wide = sum(n for _, _, n in groups)
@@ -1165,6 +1165,7 @@
         cost_estimate=cost(3),
         name="add_cols",
     )(*arrays)
+    outs = after(outs, *last)
     return outs, col_exchange(outs)
 
 
@@ -1464,13 +1465,13 @@
         rows3 = sends[3].send(None)
     sizes = [2 * width, small.shape[0], table_flat.shape[0]]
     late = in_pieces[:, rows - TAIL : rows - TAIL + 6].astype(F32).reshape(cols, 2, 3, width)
-    done3, arrived3 = finish_weights([sends[3].send(None)], in_pieces)
+    done3, arrived3 = finish_weights([sends[3].send(None)], in_sent, last=(in_pieces,))
     late = jnp.sum(after(late, done3), axis=(0, 2)).reshape(-1)
     totals = list(sum_rows(jnp.concatenate([late, small, table_flat]), nr))
     total = totals[-1]
     late, small = total[: sizes[0]], total[sizes[0] : sizes[0] + sizes[1]]
     table_flat = total[sizes[0] + sizes[1] :].reshape(2, 27, HD)
-    input_grad = collect(after(in_pieces, totals[-2]), sets, info, F32)
+    input_grad = collect(after(in_pieces, totals[0]), sets, info, F32)
     (qkv_w_grad,) = last_sum(arrived3, [3 * width])
     fc_grads = last_sum(arrived0, [2 * half], done3)
     fc_grad, proj_w_grad = last_sum(arrived1, [2 * half, width], done3)

time: 599 us -> 595 us (level)
    all_to_all x9, waiting for transfers between devices: 33.3 us -> 21.2 us  [col_exchange(): return lax.all_to_all(values, 'col', 0, 0, tiled=True)]
    ppermute x45, waiting for transfers between devices: 40.4 us -> 48.7 us  [row_swap(): return lax.ppermute(values, 'row', [(i, i ^ bit) for i in range(nr)])]
  transfers between devices with their start and end apart: 63 -> 63, of which waited for: 19 -> 21; matrix products, arithmetic and copies ran while one was open for 6% -> 6% of each run, Pallas kernels for 58% -> 59%
where the time goes in v7:
time: 595 us; the launch traced here: 584 us
  Pallas kernels  364 us (61%)
  starting transfers between devices  87.6 us (15%)
  waiting for transfers between devices  79.8 us (13%)
  local copies, waits for them, and re-layouts  29.3 us (5%)
  other arithmetic  20.8 us (3%)
    pallas_call x4, Pallas kernels, attend_back(): pl.pallas_call(partial(attend_back_kernel, width, len(held)), out_shape=[...  73.9 us
    pallas_call x4, Pallas kernels, attend(): pl.pallas_call(partial(attend_kernel, width, len(held)), out_shape=[jax.S...  56.2 us
    pallas_call x2, Pallas kernels, mlp_grads(): pl.pallas_call(partial(mlp_grads_kernel, nr), out_shape=[act, act, half,...  54.3 us
    ppermute x45, waiting for transfers between devices, row_swap(): return lax.ppermute(values, 'row', [(i, i ^ bit) for i in range(nr)])  48.7 us
    all_to_all x9, starting transfers between devices, col_exchange(): return lax.all_to_all(values, 'col', 0, 0, tiled=True)  40.1 us
    ppermute x45, starting transfers between devices, row_swap(): return lax.ppermute(values, 'row', [(i, i ^ bit) for i in range(nr)])  32.8 us
    pallas_call x8, Pallas kernels, reduce_weight(): pl.pallas_call(partial(add_kernel, sizes), out_shape=[jax.ShapeDtypeStruc...  21.9 us
    all_to_all x9, waiting for transfers between devices, col_exchange(): return lax.all_to_all(values, 'col', 0, 0, tiled=True)  21.2 us
  transfers between devices with their start and end apart: 63, of which 21 were waited for; matrix products, arithmetic and copies ran while one was open for 6% of the time, Pallas kernels for 59%

profile of v7, /device:TPU:0, one launch (start us, length us, event | category | flops | bytes accessed | tf_op | source)
XLA Modules:
  0.0 584.3 jit_solution(2643306933416406857)
XLA Ops:
  0.6 5.1 collective-permute-start.2
  6.4 2.0 plan.1.info
  8.4 10.5 %spread.2 = bf16[4,1088,256]{2,1,0:T(8,128)(2,1)} custom-call(s32[201]{0:T(256)} %plan.1.info, bf16[4096,256]{1,0:T(8,128)(2,1)} %x_ref.1), custom_call_target="tpu_custom_call" | custom-call | flops 7699999744 | bytes 7000000 | tf_op jit(solution)/shard_map/spread/pallas_call | solution.py:175
  18.8 5.1 all-to-all-start
  30.2 4.6 collective-permute-done.3
  34.8 2.0 pad_maximum_fusion.5.refs_1_.refs_0_
  38.3 1.9 pad_maximum_fusion.6.refs_5_.refs_4_
  42.4 10.5 %spread.3 = bf16[4,1088,256]{2,1,0:T(8,128)(2,1)} custom-call(s32[201]{0:T(256)} %plan.1.info, bf16[4096,256]{1,0:T(8,128)(2,1)} %x_ref.2), custom_call_target="tpu_custom_call" | custom-call | flops 7699999744 | bytes 7000000 | tf_op jit(solution)/shard_map/spread/pallas_call | solution.py:175
  54.3 3.2 collective-permute-done.8.refs_6_.refs_5_
  57.7 2.3 collective-permute-done.10.refs_8_.refs_7_
  60.2 3.3 collective-permute-start.13
  65.9 9.3 %collective-permute-done.12 = f32[3072]{0:T(1024)S(1)} collective-permute-done((f32[3072]{0:T(1024)S(1)}, f32[3072]{0:T(1024)S(1)}, u32[]{:S(2)}, u32[]{:S(2)}) %collective-permute-start.12) | collective-permute-done | bytes 12320 | tf_op jit(solution)/shard_map/ppermute | solution.py:1276
  78.8 3.5 all-to-all-start.1
  82.4 14.9 %norm_qkv.1 = (bf16[1088,1024]{1,0:T(8,128)(2,1)}, bf16[1088,1024]{1,0:T(8,128)(2,1)}, bf16[1088,3072]{1,0:T(8,128)(2,1)}) custom-call(s32[201]{0:T(256)} %plan.1.info, bf16[4,1088,256]{2,1,0:T(8,128)(2,1)} %copy-done.10, bf16[2,4,3,64,256]{4,3,2,1,0:T(8,128)(2,1)} %pad_maximum_fusion.5.refs_1_.refs_0_, ...), custom_call_target="tpu_custom_call" | custom-call | flops 20899999744 | bytes 19000000 | tf_op jit(solution)/shard_map/norm_qkv/pallas_call | solution.py:339
  97.3 14.1 %attend.4 = (bf16[1088,1024]{1,0:T(8,128)(2,1)}, bf16[16,1400,256]{2,1,0:T(8,128)(2,1)}, f32[1400,1024]{1,0:T(8,128)}) custom-call(s32[201]{0:T(256)} %plan.1.info, bf16[1088,3072]{1,0:T(8,128)(2,1)} %get-tuple-element.204.qkv, bf16[128,128]{1,0:T(8,128)(2,1)} %pad_maximum_fusion.13.tables, s32[200,128]{1,0:T(8,128)} %constant.41.clone.shifts, ...), custom_call_target="tpu_custom_call" | custom-call | flops 15399999488 | bytes 14000000 | tf_op jit(solution)/shard_map/attend/pallas_call | solution.py:820
  111.4 1.8 all-to-all-done.1
  118.4 3.5 all-to-all-start.2
  121.9 14.0 %attend.5 = (bf16[1088,1024]{1,0:T(8,128)(2,1)}, bf16[16,1400,256]{2,1,0:T(8,128)(2,1)}, f32[1400,1024]{1,0:T(8,128)}) custom-call(s32[201]{0:T(256)} %plan.1.info, bf16[1088,3072]{1,0:T(8,128)(2,1)} %get-tuple-element.204.qkv, bf16[128,128]{1,0:T(8,128)(2,1)} %pad_maximum_fusion.13.tables, ...), custom_call_target="tpu_custom_call", output_to_operand_aliasing={{0}: (5, {}), {1}: (6, {}), {2}: (7, {})} | custom-call | flops 15399999488 | bytes 14000000 | tf_op jit(solution)/shard_map/attend/pallas_call | solution.py:820
  137.8 2.1 pad_maximum_fusion.1.refs_4_.refs_0_
  140.4 6.1 %all-to-all-done.2 = bf16[4,128,1024]{2,1,0:T(8,128)(2,1)S(1)} async-done(((bf16[4,128,1024]{2,1,0:T(8,128)(2,1)}), bf16[4,128,1024]{2,1,0:T(8,128)(2,1)S(1)}, u32[]{:S(2)}, u32[]{:S(2)}) %all-to-all-start.2) | async-done | bytes 1048608 | tf_op jit(solution)/shard_map/all_to_all | solution.py:1006
  146.6 3.8 all-to-all-start.3
  150.4 14.0 %attend.6 = (bf16[1088,1024]{1,0:T(8,128)(2,1)}, bf16[16,1400,256]{2,1,0:T(8,128)(2,1)}, f32[1400,1024]{1,0:T(8,128)}) custom-call(s32[201]{0:T(256)} %plan.1.info, bf16[1088,3072]{1,0:T(8,128)(2,1)} %get-tuple-element.204.qkv, bf16[128,128]{1,0:T(8,128)(2,1)} %pad_maximum_fusion.13.tables, ...), custom_call_target="tpu_custom_call", output_to_operand_aliasing={{0}: (5, {}), {1}: (6, {}), {2}: (7, {})} | custom-call | flops 15399999488 | bytes 14000000 | tf_op jit(solution)/shard_map/attend/pallas_call | solution.py:820
  164.4 14.1 %attend.7 = (bf16[1088,1024]{1,0:T(8,128)(2,1)}, bf16[16,1400,256]{2,1,0:T(8,128)(2,1)}, f32[1400,1024]{1,0:T(8,128)}) custom-call(s32[201]{0:T(256)} %plan.1.info, bf16[1088,3072]{1,0:T(8,128)(2,1)} %get-tuple-element.204.qkv, bf16[128,128]{1,0:T(8,128)(2,1)} %pad_maximum_fusion.13.tables, ...), custom_call_target="tpu_custom_call", output_to_operand_aliasing={{0}: (5, {}), {1}: (6, {}), {2}: (7, {})} | custom-call | flops 15399999488 | bytes 14000000 | tf_op jit(solution)/shard_map/attend/pallas_call | solution.py:820
  182.3 7.8 %proj_norm.1 = (f32[1088,1024]{1,0:T(8,128)}, bf16[1088,1024]{1,0:T(8,128)(2,1)}) custom-call(bf16[2,4,128,768]{3,2,1,0:T(8,128)(2,1)} %pad_maximum_fusion.refs_0_, bf16[2,4,128,768]{3,2,1,0:T(8,128)(2,1)} %collective-permute-done.17.refs_1_, bf16[2,4,128,768]{3,2,1,0:T(8,128)(2,1)} %collective-permute-done.21.refs_2_, ...), custom_call_target="tpu_custom_call" | custom-call | flops 12099999744 | bytes 11000000 | tf_op jit(solution)/shard_map/proj_norm/pallas_call | solution.py:412
  190.2 4.5 collective-permute-done.20
  194.7 2.3 pad_maximum_fusion.2.refs_4_
  202.2 4.8 join.1.refs_9_.refs_11_
  207.0 27.0 %mlp_grads.2 = (bf16[1088,2048]{1,0:T(8,128)(2,1)}, bf16[1088,2048]{1,0:T(8,128)(2,1)}, bf16[4,4,128,1024]{3,2,1,0:T(8,128)(2,1)}, bf16[4,4,128,1024]{3,2,1,0:T(8,128)(2,1)}, f32[4,8,512]{2,1,0:T(8,128)}) custom-call(bf16[2,4,128,768]{3,2,1,0:T(8,128)(2,1)} %pad_maximum_fusion.refs_0_, bf16[2,4,128,768]{3,2,1,0:T(8,128)(2,1)} %collective-permute-done.17.refs_1_, ...), custom_call_target="tpu_custom_call" | custom-call | flops 41799999488 | bytes 38000000 | tf_op jit(solution)/shard_map/mlp_grads/pallas_call | solution.py:469
  235.7 2.2 collective-permute-done.27.refs_7_
  237.9 2.1 collective-permute-done.29.refs_3_.refs_7_
  241.0 27.3 %mlp_grads.3 = (bf16[1088,2048]{1,0:T(8,128)(2,1)}, bf16[1088,2048]{1,0:T(8,128)(2,1)}, bf16[4,4,128,1024]{3,2,1,0:T(8,128)(2,1)}, bf16[4,4,128,1024]{3,2,1,0:T(8,128)(2,1)}, f32[4,8,512]{2,1,0:T(8,128)}) custom-call(bf16[2,4,128,512]{3,2,1,0:T(8,128)(2,1)} %copy-done.13, bf16[2,4,128,512]{3,2,1,0:T(8,128)(2,1)} %collective-permute-done.25.refs_1_.refs_5_, ...), custom_call_target="tpu_custom_call" | custom-call | flops 41799999488 | bytes 38000000 | tf_op jit(solution)/shard_map/mlp_grads/pallas_call | solution.py:469
  271.2 3.3 add_rows.8
  276.4 17.6 %block_rows.1 = bf16[4,1088,256]{2,1,0:T(8,128)(2,1)} custom-call(s32[201]{0:T(256)} %plan.1.info, bf16[2,4,128,512]{3,2,1,0:T(8,128)(2,1)} %pad_maximum_fusion.1.refs_4_.refs_0_, bf16[2,4,128,512]{3,2,1,0:T(8,128)(2,1)} %collective-permute-done.16.refs_5_.refs_1_, bf16[2,4,128,512]{3,2,1,0:T(8,128)(2,1)} %collective-permute-done.18.refs_6_.refs_2_, ...), custom_call_target="tpu_custom_call" | custom-call | flops 28600000512 | bytes 26000000 | tf_op jit(solution)/shard_map/block_rows/pallas_call | solution.py:516
  294.0 5.2 all-to-all-start.4
  302.2 3.0 add_rows.9
  307.1 3.3 add_rows.10
  312.6 19.4 %mlp_back.1 = (f32[1088,1024]{1,0:T(8,128)}, bf16[1088,1024]{1,0:T(8,128)(2,1)}, f32[4,8,1024]{2,1,0:T(8,128)}) custom-call(bf16[2,4,128,768]{3,2,1,0:T(8,128)(2,1)} %pad_maximum_fusion.refs_0_, bf16[2,4,128,768]{3,2,1,0:T(8,128)(2,1)} %collective-permute-done.17.refs_1_, bf16[2,4,128,768]{3,2,1,0:T(8,128)(2,1)} %collective-permute-done.21.refs_2_, ...), custom_call_target="tpu_custom_call" | custom-call | flops 30799998976 | bytes 28000000 | tf_op jit(solution)/shard_map/mlp_back/pallas_call | solution.py:562
  333.2 9.7 %proj_back.1 = (bf16[1088,1024]{1,0:T(8,128)(2,1)}, bf16[4,4,128,256]{3,2,1,0:T(8,128)(2,1)}, bf16[4,4,128,256]{3,2,1,0:T(8,128)(2,1)}) custom-call(bf16[2,4,128,768]{3,2,1,0:T(8,128)(2,1)} %pad_maximum_fusion.refs_0_, bf16[2,4,128,768]{3,2,1,0:T(8,128)(2,1)} %collective-permute-done.17.refs_1_, bf16[2,4,128,768]{3,2,1,0:T(8,128)(2,1)} %collective-permute-done.21.refs_2_, ...), custom_call_target="tpu_custom_call" | custom-call | flops 12099999744 | bytes 11000000 | tf_op jit(solution)/shard_map/proj_back/pallas_call | solution.py:594
  343.0 18.6 %attend_back.4 = (bf16[1088,3072]{1,0:T(8,128)(2,1)}, f32[128,256]{1,0:T(8,128)}, f32[8,768]{1,0:T(8,128)}) custom-call(s32[201]{0:T(256)} %plan.1.info, bf16[1088,3072]{1,0:T(8,128)(2,1)} %get-tuple-element.204.qkv, bf16[16,1400,256]{2,1,0:T(8,128)(2,1)} %get-tuple-element.172.exps, f32[1400,1024]{1,0:T(8,128)} %get-tuple-element.173.inv, ...), custom_call_target="tpu_custom_call" | custom-call | flops 14300000256 | bytes 13000000 | tf_op jit(solution)/shard_map/attend_back/pallas_call | solution.py:955
  363.6 3.0 add_rows.11
  369.5 2.0 add_rows.12
  372.7 3.7 add_cols.3
  376.4 5.2 all-to-all-start.5
  382.6 18.4 %attend_back.5 = (bf16[1088,3072]{1,0:T(8,128)(2,1)}, f32[128,256]{1,0:T(8,128)}, f32[8,768]{1,0:T(8,128)}) custom-call(s32[201]{0:T(256)} %plan.1.info, bf16[1088,3072]{1,0:T(8,128)(2,1)} %get-tuple-element.204.qkv, bf16[16,1400,256]{2,1,0:T(8,128)(2,1)} %get-tuple-element.172.exps, ...), custom_call_target="tpu_custom_call", output_to_operand_aliasing={{0}: (9, {})} | custom-call | flops 14300000256 | bytes 13000000 | tf_op jit(solution)/shard_map/attend_back/pallas_call | solution.py:955
  401.9 1.9 add_rows.13
  404.7 18.5 %attend_back.6 = (bf16[1088,3072]{1,0:T(8,128)(2,1)}, f32[128,256]{1,0:T(8,128)}, f32[8,768]{1,0:T(8,128)}) custom-call(s32[201]{0:T(256)} %plan.1.info, bf16[1088,3072]{1,0:T(8,128)(2,1)} %get-tuple-element.204.qkv, bf16[16,1400,256]{2,1,0:T(8,128)(2,1)} %get-tuple-element.172.exps, ...), custom_call_target="tpu_custom_call", output_to_operand_aliasing={{0}: (9, {})} | custom-call | flops 14300000256 | bytes 13000000 | tf_op jit(solution)/shard_map/attend_back/pallas_call | solution.py:955
  423.9 4.2 add_cols.4
  428.0 4.7 all-to-all-start.6
  432.7 18.4 %attend_back.7 = (bf16[1088,3072]{1,0:T(8,128)(2,1)}, f32[128,256]{1,0:T(8,128)}, f32[8,768]{1,0:T(8,128)}) custom-call(s32[201]{0:T(256)} %plan.1.info, bf16[1088,3072]{1,0:T(8,128)(2,1)} %get-tuple-element.204.qkv, bf16[16,1400,256]{2,1,0:T(8,128)(2,1)} %get-tuple-element.172.exps, ...), custom_call_target="tpu_custom_call", output_to_operand_aliasing={{0}: (9, {})} | custom-call | flops 14300000256 | bytes 13000000 | tf_op jit(solution)/shard_map/attend_back/pallas_call | solution.py:955
  451.2 12.7 %qkv_grad.1 = (bf16[4,4,128,768]{3,2,1,0:T(8,128)(2,1)}, bf16[4,4,128,768]{3,2,1,0:T(8,128)(2,1)}) custom-call(bf16[1088,1024]{1,0:T(8,128)(2,1)} %get-tuple-element.206.n1, bf16[1088,3072]{1,0:T(8,128)(2,1)} %get-tuple-element.224.dqkv.refs_8_), custom_call_target="tpu_custom_call" | custom-call | flops 15399999488 | bytes 14000000 | tf_op jit(solution)/shard_map/qkv_grad/pallas_call | solution.py:615
  465.1 2.1 collective-permute-start.43
  467.2 2.4 collective-permute-start.44
  469.6 10.0 %collect.2 = bf16[4096,256]{1,0:T(8,128)(2,1)} custom-call(s32[201]{0:T(256)} %plan.1.info, bf16[4,1088,256]{2,1,0:T(8,128)(2,1)} %all-to-all-done.4.pieces), custom_call_target="tpu_custom_call" | custom-call | flops 8800000000 | bytes 8000000 | tf_op jit(solution)/shard_map/collect/pallas_call | solution.py:225
  479.6 1.7 copy-done
  481.3 2.8 add_rows.14
  484.2 16.3 %input_back.1 = bf16[4,1088,256]{2,1,0:T(8,128)(2,1)} custom-call(s32[201]{0:T(256)} %plan.1.info, bf16[2,4,3,64,256]{4,3,2,1,0:T(8,128)(2,1)} %pad_maximum_fusion.5.refs_1_.refs_0_, bf16[2,4,3,64,256]{4,3,2,1,0:T(8,128)(2,1)} %collective-permute-done.4.refs_2_.refs_1_, bf16[2,4,3,64,256]{4,3,2,1,0:T(8,128)(2,1)} %collective-permute-done.6.refs_3_.refs_2_, ...), custom_call_target="tpu_custom_call" | custom-call | flops 27499999232 | bytes 25000000 | tf_op jit(solution)/shard_map/input_back/pallas_call | solution.py:664
  500.5 5.0 all-to-all-start.7
  507.8 16.7 %collective-permute-done.47.refs_2_ = bf16[2,4,64,768]{3,2,1,0:T(8,128)(2,1)S(1)} collective-permute-done((bf16[2,4,64,768]{3,2,1,0:T(8,128)(2,1)}, bf16[2,4,64,768]{3,2,1,0:T(8,128)(2,1)S(1)}, u32[]{:S(2)}, u32[]{:S(2)}) %collective-permute-start.47) | collective-permute-done | bytes 786464 | tf_op jit(solution)/shard_map/ppermute | solution.py:1010
  526.3 2.6 add_rows.15
  531.5 7.1 %collective-permute-done.49.refs_3_ = bf16[1,4,64,768]{3,2,1,0:T(8,128)(2,1)S(1)} collective-permute-done((bf16[1,4,64,768]{3,2,1,0:T(8,128)(2,1)}, bf16[1,4,64,768]{3,2,1,0:T(8,128)(2,1)S(1)}, u32[]{:S(2)}, u32[]{:S(2)}) %collective-permute-start.49) | collective-permute-done | bytes 393248 | tf_op jit(solution)/shard_map/ppermute | solution.py:1010
  540.5 3.1 add_cols.5
  543.7 12.6 %all-to-all-done.7.pieces = bf16[4,1088,256]{2,1,0:T(8,128)(2,1)S(1)} async-done(((bf16[4,1088,256]{2,1,0:T(8,128)(2,1)}), bf16[4,1088,256]{2,1,0:T(8,128)(2,1)S(1)}, u32[]{:S(2)}, u32[]{:S(2)}) %all-to-all-start.7) | async-done | bytes 2228256 | tf_op jit(solution)/shard_map/all_to_all | solution.py:1006
  557.7 3.9 all-to-all-start.8
  568.6 10.8 %collect.3 = f32[4096,256]{1,0:T(8,128)} custom-call(s32[201]{0:T(256)} %plan.1.info, bf16[4,1088,256]{2,1,0:T(8,128)(2,1)} %copy-done.9), custom_call_target="tpu_custom_call" | custom-call | flops 8800000000 | bytes 8000000 | tf_op jit(solution)/shard_map/collect/pallas_call | solution.py:225
  (336 shorter events, 82.2 us)
Async XLA Ops:
  0.6 24.0 %collective-permute-start.2 = (bf16[3,128,256]{2,1,0:T(8,128)(2,1)}, bf16[3,128,256]{2,1,0:T(8,128)(2,1)S(1)}, u32[]{:S(2)}, u32[]{:S(2)}) collective-permute-start(bf16[3,128,256]{2,1,0:T(8,128)(2,1)} %bitcast.84), channel_id=1, source_target_pairs={{0,3},{1,2},{2,1},{3,0},{4,7},{5,6},{6,5},{7,4},{8,11},{9,10},{10,... | collective-permute-start | bytes 589832 | tf_op jit(solution)/shard_map/ppermute | solution.py:1247
  5.8 18.9 %collective-permute-start.1 = (bf16[3,128,256]{2,1,0:T(8,128)(2,1)}, bf16[3,128,256]{2,1,0:T(8,128)(2,1)S(1)}, u32[]{:S(2)}, u32[]{:S(2)}) collective-permute-start(bf16[3,128,256]{2,1,0:T(8,128)(2,1)} %bitcast.85), channel_id=1, source_target_pairs={{0,2},{1,3},{2,0},{3,1},{4,6},{5,7},{6,4},{7,5},{8,10},{9,11},{10,... | collective-permute-start | bytes 589832 | tf_op jit(solution)/shard_map/ppermute | solution.py:1247
  5.8 18.9 %collective-permute-start = (bf16[3,128,256]{2,1,0:T(8,128)(2,1)}, bf16[3,128,256]{2,1,0:T(8,128)(2,1)S(1)}, u32[]{:S(2)}, u32[]{:S(2)}) collective-permute-start(bf16[3,128,256]{2,1,0:T(8,128)(2,1)} %bitcast.86), channel_id=1, source_target_pairs={{0,1},{1,0},{2,3},{3,2},{4,5},{5,4},{6,7},{7,6},{8,9},{9,8},{10,11... | collective-permute-start | bytes 589832 | tf_op jit(solution)/shard_map/ppermute | solution.py:1247
  18.8 58.2 %all-to-all-start = ((bf16[4,1088,256]{2,1,0:T(8,128)(2,1)}), bf16[4,1088,256]{2,1,0:T(8,128)(2,1)S(1)}, u32[]{:S(2)}, u32[]{:S(2)}) async-start(bf16[4,1088,256]{2,1,0:T(8,128)(2,1)} %spread.2), calls=%async_computation | async-start | bytes 4456448 | tf_op jit(solution)/shard_map/all_to_all | solution.py:1006
  24.9 9.9 %collective-permute-start.3 = (bf16[1,4,3,64,256]{4,3,2,1,0:T(8,128)(2,1)S(1)}, bf16[1,4,3,64,256]{4,3,2,1,0:T(8,128)(2,1)}, u32[]{:S(2)}, u32[]{:S(2)}) collective-permute-start(bf16[1,4,3,64,256]{4,3,2,1,0:T(8,128)(2,1)S(1)} %get-tuple-element.325), channel_id=1, source_target_pairs={{0,8},{4,12},{8,0},{12,4},{16,24},{20,28},{24,16},{28,20},{1,9},{5... | collective-permute-start | bytes 1179656 | tf_op jit(solution)/shard_map/ppermute | solution.py:1010
  26.4 11.8 %collective-permute-start.5 = (bf16[1,4,3,64,256]{4,3,2,1,0:T(8,128)(2,1)S(1)}, bf16[1,4,3,64,256]{4,3,2,1,0:T(8,128)(2,1)}, u32[]{:S(2)}, u32[]{:S(2)}) collective-permute-start(bf16[1,4,3,64,256]{4,3,2,1,0:T(8,128)(2,1)S(1)} %get-tuple-element.324), channel_id=1, source_target_pairs={{0,16},{4,20},{8,24},{12,28},{16,0},{20,4},{24,8},{28,12},{1,17},{... | collective-permute-start | bytes 1179656 | tf_op jit(solution)/shard_map/ppermute | solution.py:1010
  29.2 35.5 %copy-start.28 = (bf16[64,128]{1,0:T(8,128)(2,1)}, bf16[64,128]{1,0:T(8,128)(2,1)S(1)}, u32[]{:S(2)}) copy-start(bf16[64,128]{1,0:T(8,128)(2,1)S(1)} %get-tuple-element.359) | copy-start | bytes 49156
  36.8 17.6 %collective-permute-start.4 = (bf16[2,4,3,64,256]{4,3,2,1,0:T(8,128)(2,1)}, bf16[2,4,3,64,256]{4,3,2,1,0:T(8,128)(2,1)}, u32[]{:S(2)}, u32[]{:S(2)}) collective-permute-start(bf16[2,4,3,64,256]{4,3,2,1,0:T(8,128)(2,1)} %pad_maximum_fusion.5.refs_1_.refs_0_), channel_id=1, source_target_pairs={{0,16},{4,20},{8,24},{12,28},{16,0},{20,4},{24,8},{28,12},{1,17},{... | collective-permute-start | bytes 2359304 | tf_op jit(solution)/shard_map/ppermute | solution.py:1010
  40.2 17.3 %collective-permute-start.8 = (bf16[2,4,3,64,256]{4,3,2,1,0:T(8,128)(2,1)}, bf16[2,4,3,64,256]{4,3,2,1,0:T(8,128)(2,1)}, u32[]{:S(2)}, u32[]{:S(2)}) collective-permute-start(bf16[2,4,3,64,256]{4,3,2,1,0:T(8,128)(2,1)} %pad_maximum_fusion.6.refs_5_.refs_4_), channel_id=1, source_target_pairs={{0,8},{4,12},{8,0},{12,4},{16,24},{20,28},{24,16},{28,20},{1,9},{5... | collective-permute-start | bytes 2359304 | tf_op jit(solution)/shard_map/ppermute | solution.py:1010
  41.9 15.9 %collective-permute-start.6 = (bf16[2,4,3,64,256]{4,3,2,1,0:T(8,128)(2,1)}, bf16[2,4,3,64,256]{4,3,2,1,0:T(8,128)(2,1)}, u32[]{:S(2)}, u32[]{:S(2)}) collective-permute-start(bf16[2,4,3,64,256]{4,3,2,1,0:T(8,128)(2,1)} %pad_maximum_fusion.5.refs_1_.refs_0_), channel_id=1, source_target_pairs={{0,4},{4,0},{8,12},{12,8},{16,20},{20,16},{24,28},{28,24},{1,5},{5... | collective-permute-start | bytes 2359304 | tf_op jit(solution)/shard_map/ppermute | solution.py:1010
  41.9 15.8 %collective-permute-start.9 = (bf16[2,4,3,64,256]{4,3,2,1,0:T(8,128)(2,1)}, bf16[2,4,3,64,256]{4,3,2,1,0:T(8,128)(2,1)}, u32[]{:S(2)}, u32[]{:S(2)}) collective-permute-start(bf16[2,4,3,64,256]{4,3,2,1,0:T(8,128)(2,1)} %pad_maximum_fusion.6.refs_5_.refs_4_), channel_id=1, source_target_pairs={{0,4},{4,0},{8,12},{12,8},{16,20},{20,16},{24,28},{28,24},{1,5},{5... | collective-permute-start | bytes 2359304 | tf_op jit(solution)/shard_map/ppermute | solution.py:1010
  54.3 3.4 collective-permute-start.7
  57.5 2.5 collective-permute-start.10
  60.2 5.7 collective-permute-start.13
  63.5 11.7 %collective-permute-start.12 = (f32[3072]{0:T(1024)S(1)}, f32[3072]{0:T(1024)S(1)}, u32[]{:S(2)}, u32[]{:S(2)}) collective-permute-start(f32[3072]{0:T(1024)S(1)} %constant_dynamic-update-slice_fusion.6), channel_id=1, source_target_pairs={{0,2},{1,3},{2,0},{3,1},{4,6},{5,7},{6,4},{7,5},{8,10},{9,11},{10,... | collective-permute-start | bytes 36872 | tf_op jit(solution)/shard_map/ppermute | solution.py:1276
  63.5 11.7 %collective-permute-start.11 = (f32[3072]{0:T(1024)S(1)}, f32[3072]{0:T(1024)S(1)}, u32[]{:S(2)}, u32[]{:S(2)}) collective-permute-start(f32[3072]{0:T(1024)S(1)} %constant_dynamic-update-slice_fusion.6), channel_id=1, source_target_pairs={{0,1},{1,0},{2,3},{3,2},{4,5},{5,4},{6,7},{7,6},{8,9},{9,8},{10,11... | collective-permute-start | bytes 36872 | tf_op jit(solution)/shard_map/ppermute | solution.py:1276
  78.8 34.4 %all-to-all-start.1 = ((bf16[4,128,1280]{2,1,0:T(8,128)(2,1)}), bf16[4,128,1280]{2,1,0:T(8,128)(2,1)S(1)}, u32[]{:S(2)}, u32[]{:S(2)}) async-start(bf16[4,128,1280]{2,1,0:T(8,128)(2,1)} %broadcast_in_dim.135), calls=%async_computation.1 | async-start | bytes 2621440 | tf_op jit(solution)/shard_map/all_to_all | solution.py:1006
  114.1 21.9 %collective-permute-start.14 = (bf16[1,4,128,512]{3,2,1,0:T(8,128)(2,1)}, bf16[1,4,128,512]{3,2,1,0:T(8,128)(2,1)S(1)}, u32[]{:S(2)}, u32[]{:S(2)}) collective-permute-start(bf16[1,4,128,512]{3,2,1,0:T(8,128)(2,1)} %slice_bitcast_fusion.3), channel_id=1, source_target_pairs={{0,16},{4,20},{8,24},{12,28},{16,0},{20,4},{24,8},{28,12},{1,17},{... | collective-permute-start | bytes 1572872 | tf_op jit(solution)/shard_map/ppermute | solution.py:1010
  115.7 20.3 %collective-permute-start.15 = (bf16[1,4,128,768]{3,2,1,0:T(8,128)(2,1)S(1)}, bf16[1,4,128,768]{3,2,1,0:T(8,128)(2,1)S(1)}, u32[]{:S(2)}, u32[]{:S(2)}) collective-permute-start(bf16[1,4,128,768]{3,2,1,0:T(8,128)(2,1)S(1)} %slice_bitcast_fusion), channel_id=1, source_target_pairs={{0,8},{4,12},{8,0},{12,4},{16,24},{20,28},{24,16},{28,20},{1,9},{5... | collective-permute-start | bytes 2359304 | tf_op jit(solution)/shard_map/ppermute | solution.py:1010
  118.4 28.1 %all-to-all-start.2 = ((bf16[4,128,1024]{2,1,0:T(8,128)(2,1)}), bf16[4,128,1024]{2,1,0:T(8,128)(2,1)S(1)}, u32[]{:S(2)}, u32[]{:S(2)}) async-start(bf16[4,128,1024]{2,1,0:T(8,128)(2,1)} %broadcast_in_dim.145), calls=%async_computation.2 | async-start | bytes 2097152 | tf_op jit(solution)/shard_map/all_to_all | solution.py:1006
  137.3 41.3 %collective-permute-start.17 = (bf16[2,4,128,768]{3,2,1,0:T(8,128)(2,1)}, bf16[2,4,128,768]{3,2,1,0:T(8,128)(2,1)}, u32[]{:S(2)}, u32[]{:S(2)}) collective-permute-start(bf16[2,4,128,768]{3,2,1,0:T(8,128)(2,1)} %pad_maximum_fusion.refs_0_), channel_id=1, source_target_pairs={{0,16},{4,20},{8,24},{12,28},{16,0},{20,4},{24,8},{28,12},{1,17},{... | collective-permute-start | bytes 4718600 | tf_op jit(solution)/shard_map/ppermute | solution.py:1010
  137.8 43.9 %collective-permute-start.21 = (bf16[2,4,128,768]{3,2,1,0:T(8,128)(2,1)}, bf16[2,4,128,768]{3,2,1,0:T(8,128)(2,1)}, u32[]{:S(2)}, u32[]{:S(2)}) collective-permute-start(bf16[2,4,128,768]{3,2,1,0:T(8,128)(2,1)} %pad_maximum_fusion.refs_0_), channel_id=1, source_target_pairs={{0,4},{4,0},{8,12},{12,8},{16,20},{20,16},{24,28},{28,24},{1,5},{5... | collective-permute-start | bytes 4718600 | tf_op jit(solution)/shard_map/ppermute | solution.py:1010
  139.9 38.6 %collective-permute-start.16 = (bf16[2,4,128,512]{3,2,1,0:T(8,128)(2,1)}, bf16[2,4,128,512]{3,2,1,0:T(8,128)(2,1)}, u32[]{:S(2)}, u32[]{:S(2)}) collective-permute-start(bf16[2,4,128,512]{3,2,1,0:T(8,128)(2,1)} %pad_maximum_fusion.1.refs_4_.refs_0_), channel_id=1, source_target_pairs={{0,8},{4,12},{8,0},{12,4},{16,24},{20,28},{24,16},{28,20},{1,9},{5... | collective-permute-start | bytes 3145736 | tf_op jit(solution)/shard_map/ppermute | solution.py:1010
  146.6 54.3 %all-to-all-start.3 = ((bf16[4,1088,256]{2,1,0:T(8,128)(2,1)}), bf16[4,1088,256]{2,1,0:T(8,128)(2,1)S(1)}, u32[]{:S(2)}, u32[]{:S(2)}) async-start(bf16[4,1088,256]{2,1,0:T(8,128)(2,1)} %spread.3), calls=%async_computation.3 | async-start | bytes 4456448 | tf_op jit(solution)/shard_map/all_to_all | solution.py:1006
  178.5 3.8 collective-permute-start.22
  179.2 27.8 %collective-permute-start.18 = (bf16[2,4,128,512]{3,2,1,0:T(8,128)(2,1)}, bf16[2,4,128,512]{3,2,1,0:T(8,128)(2,1)}, u32[]{:S(2)}, u32[]{:S(2)}) collective-permute-start(bf16[2,4,128,512]{3,2,1,0:T(8,128)(2,1)} %pad_maximum_fusion.1.refs_4_.refs_0_), channel_id=1, source_target_pairs={{0,4},{4,0},{8,12},{12,8},{16,20},{20,16},{24,28},{28,24},{1,5},{5... | collective-permute-start | bytes 3145736 | tf_op jit(solution)/shard_map/ppermute | solution.py:1010
  180.6 14.1 %collective-permute-start.20 = (bf16[1,4,128,512]{3,2,1,0:T(8,128)(2,1)}, bf16[1,4,128,512]{3,2,1,0:T(8,128)(2,1)S(1)}, u32[]{:S(2)}, u32[]{:S(2)}) collective-permute-start(bf16[1,4,128,512]{3,2,1,0:T(8,128)(2,1)} %get-tuple-element.323), channel_id=1, source_target_pairs={{0,16},{4,20},{8,24},{12,28},{16,0},{20,4},{24,8},{28,12},{1,17},{... | collective-permute-start | bytes 1572872 | tf_op jit(solution)/shard_map/ppermute | solution.py:1010
  181.1 13.6 %collective-permute-start.23 = (bf16[1,4,128,512]{3,2,1,0:T(8,128)(2,1)S(1)}, bf16[1,4,128,512]{3,2,1,0:T(8,128)(2,1)S(1)}, u32[]{:S(2)}, u32[]{:S(2)}) collective-permute-start(bf16[1,4,128,512]{3,2,1,0:T(8,128)(2,1)S(1)} %get-tuple-element.322), channel_id=1, source_target_pairs={{0,8},{4,12},{8,0},{12,4},{16,24},{20,28},{24,16},{28,20},{1,9},{5... | collective-permute-start | bytes 1572872 | tf_op jit(solution)/shard_map/ppermute | solution.py:1010
  181.6 25.4 %collective-permute-start.19 = (bf16[2,4,128,512]{3,2,1,0:T(8,128)(2,1)}, bf16[2,4,128,512]{3,2,1,0:T(8,128)(2,1)}, u32[]{:S(2)}, u32[]{:S(2)}) collective-permute-start(bf16[2,4,128,512]{3,2,1,0:T(8,128)(2,1)} %collective-permute-done.16.refs_5_.refs_1_), channel_id=1, source_target_pairs={{0,4},{4,0},{8,12},{12,8},{16,20},{20,16},{24,28},{28,24},{1,5},{5... | collective-permute-start | bytes 3145736 | tf_op jit(solution)/shard_map/ppermute | solution.py:1010
  197.0 37.0 %collective-permute-start.24 = (bf16[2,4,128,512]{3,2,1,0:T(8,128)(2,1)}, bf16[2,4,128,512]{3,2,1,0:T(8,128)(2,1)}, u32[]{:S(2)}, u32[]{:S(2)}) collective-permute-start(bf16[2,4,128,512]{3,2,1,0:T(8,128)(2,1)} %pad_maximum_fusion.2.refs_4_), channel_id=1, source_target_pairs={{0,8},{4,12},{8,0},{12,4},{16,24},{20,28},{24,16},{28,20},{1,9},{5... | collective-permute-start | bytes 3145736 | tf_op jit(solution)/shard_map/ppermute | solution.py:1010
  197.5 38.2 %collective-permute-start.26 = (bf16[2,4,128,512]{3,2,1,0:T(8,128)(2,1)}, bf16[2,4,128,512]{3,2,1,0:T(8,128)(2,1)}, u32[]{:S(2)}, u32[]{:S(2)}) collective-permute-start(bf16[2,4,128,512]{3,2,1,0:T(8,128)(2,1)} %pad_maximum_fusion.2.refs_4_), channel_id=1, source_target_pairs={{0,4},{4,0},{8,12},{12,8},{16,20},{20,16},{24,28},{28,24},{1,5},{5... | collective-permute-start | bytes 3145736 | tf_op jit(solution)/shard_map/ppermute | solution.py:1010
  198.7 35.4 %collective-permute-start.25 = (bf16[2,4,128,512]{3,2,1,0:T(8,128)(2,1)S(1)}, bf16[2,4,128,512]{3,2,1,0:T(8,128)(2,1)}, u32[]{:S(2)}, u32[]{:S(2)}) collective-permute-start(bf16[2,4,128,512]{3,2,1,0:T(8,128)(2,1)S(1)} %pad_maximum_fusion.3.refs_0_.refs_4_), channel_id=1, source_target_pairs={{0,16},{4,20},{8,24},{12,28},{16,0},{20,4},{24,8},{28,12},{1,17},{... | collective-permute-start | bytes 3145736 | tf_op jit(solution)/shard_map/ppermute | solution.py:1010
  207.0 28.7 %collective-permute-start.28 = (bf16[2,4,128,512]{3,2,1,0:T(8,128)(2,1)S(1)}, bf16[2,4,128,512]{3,2,1,0:T(8,128)(2,1)S(1)}, u32[]{:S(2)}, u32[]{:S(2)}) collective-permute-start(bf16[2,4,128,512]{3,2,1,0:T(8,128)(2,1)S(1)} %pad_maximum_fusion.3.refs_0_.refs_4_), channel_id=1, source_target_pairs={{0,4},{4,0},{8,12},{12,8},{16,20},{20,16},{24,28},{28,24},{1,5},{5... | collective-permute-start | bytes 3145736 | tf_op jit(solution)/shard_map/ppermute | solution.py:1010
  234.0 3.9 collective-permute-start.27
  234.6 5.4 collective-permute-start.29
  235.3 36.0 %collective-permute-start.31 = (bf16[4,4,128,1024]{3,2,1,0:T(8,128)(2,1)}, bf16[4,4,128,1024]{3,2,1,0:T(8,128)(2,1)}, u32[]{:S(2)}, u32[]{:S(2)}) collective-permute-start(bf16[4,4,128,1024]{3,2,1,0:T(8,128)(2,1)} %get-tuple-element.178), channel_id=1, source_target_pairs={{0,4},{4,0},{8,12},{12,8},{16,20},{20,16},{24,28},{28,24},{1,5},{5... | collective-permute-start | bytes 12582920 | tf_op jit(solution)/shard_map/ppermute | solution.py:1010
  268.3 8.0 %collective-permute-start.30 = (bf16[4,4,128,1024]{3,2,1,0:T(8,128)(2,1)}, bf16[4,4,128,1024]{3,2,1,0:T(8,128)(2,1)}, u32[]{:S(2)}, u32[]{:S(2)}) collective-permute-start(bf16[4,4,128,1024]{3,2,1,0:T(8,128)(2,1)} %get-tuple-element.168), channel_id=1, source_target_pairs={{0,4},{4,0},{8,12},{12,8},{16,20},{20,16},{24,28},{28,24},{1,5},{5... | collective-permute-start | bytes 12582920 | tf_op jit(solution)/shard_map/ppermute | solution.py:1010
  274.6 25.6 %collective-permute-start.32 = (bf16[2,4,128,512]{3,2,1,0:T(8,128)(2,1)}, bf16[2,4,128,512]{3,2,1,0:T(8,128)(2,1)S(1)}, u32[]{:S(2)}, u32[]{:S(2)}) collective-permute-start(bf16[2,4,128,512]{3,2,1,0:T(8,128)(2,1)} %get-tuple-element.180), channel_id=1, source_target_pairs={{0,16},{4,20},{8,24},{12,28},{16,0},{20,4},{24,8},{28,12},{1,17},{... | collective-permute-start | bytes 3145736 | tf_op jit(solution)/shard_map/ppermute | solution.py:1010
  275.1 25.4 %collective-permute-start.33 = (bf16[2,4,128,512]{3,2,1,0:T(8,128)(2,1)}, bf16[2,4,128,512]{3,2,1,0:T(8,128)(2,1)S(1)}, u32[]{:S(2)}, u32[]{:S(2)}) collective-permute-start(bf16[2,4,128,512]{3,2,1,0:T(8,128)(2,1)} %get-tuple-element.181), channel_id=1, source_target_pairs={{0,8},{4,12},{8,0},{12,4},{16,24},{20,28},{24,16},{28,20},{1,9},{5... | collective-permute-start | bytes 3145736 | tf_op jit(solution)/shard_map/ppermute | solution.py:1010
  294.0 78.7 %all-to-all-start.4 = ((bf16[4,1088,256]{2,1,0:T(8,128)(2,1)}), bf16[4,1088,256]{2,1,0:T(8,128)(2,1)}, u32[]{:S(2)}, u32[]{:S(2)}) async-start(bf16[4,1088,256]{2,1,0:T(8,128)(2,1)} %block_rows.1), calls=%async_computation.4 | async-start | bytes 4456448 | tf_op jit(solution)/shard_map/all_to_all | solution.py:1006
  305.2 28.0 %collective-permute-start.34 = (bf16[1,4,128,512]{3,2,1,0:T(8,128)(2,1)}, bf16[1,4,128,512]{3,2,1,0:T(8,128)(2,1)S(1)}, u32[]{:S(2)}, u32[]{:S(2)}) collective-permute-start(bf16[1,4,128,512]{3,2,1,0:T(8,128)(2,1)} %get-tuple-element.183), channel_id=1, source_target_pairs={{0,8},{4,12},{8,0},{12,4},{16,24},{20,28},{24,16},{28,20},{1,9},{5... | collective-permute-start | bytes 1572872 | tf_op jit(solution)/shard_map/ppermute | solution.py:1010
  306.3 26.9 %collective-permute-start.35 = (bf16[1,4,128,512]{3,2,1,0:T(8,128)(2,1)}, bf16[1,4,128,512]{3,2,1,0:T(8,128)(2,1)S(1)}, u32[]{:S(2)}, u32[]{:S(2)}) collective-permute-start(bf16[1,4,128,512]{3,2,1,0:T(8,128)(2,1)} %get-tuple-element.184), channel_id=1, source_target_pairs={{0,16},{4,20},{8,24},{12,28},{16,0},{20,4},{24,8},{28,12},{1,17},{... | collective-permute-start | bytes 1572872 | tf_op jit(solution)/shard_map/ppermute | solution.py:1010
  310.4 51.2 %collective-permute-start.36 = (bf16[2,4,128,512]{3,2,1,0:T(8,128)(2,1)}, bf16[2,4,128,512]{3,2,1,0:T(8,128)(2,1)S(1)}, u32[]{:S(2)}, u32[]{:S(2)}) collective-permute-start(bf16[2,4,128,512]{3,2,1,0:T(8,128)(2,1)} %get-tuple-element.191), channel_id=1, source_target_pairs={{0,16},{4,20},{8,24},{12,28},{16,0},{20,4},{24,8},{28,12},{1,17},{... | collective-permute-start | bytes 3145736 | tf_op jit(solution)/shard_map/ppermute | solution.py:1010
  311.6 50.0 %collective-permute-start.37 = (bf16[2,4,128,512]{3,2,1,0:T(8,128)(2,1)}, bf16[2,4,128,512]{3,2,1,0:T(8,128)(2,1)S(1)}, u32[]{:S(2)}, u32[]{:S(2)}) collective-permute-start(bf16[2,4,128,512]{3,2,1,0:T(8,128)(2,1)} %get-tuple-element.192), channel_id=1, source_target_pairs={{0,8},{4,12},{8,0},{12,4},{16,24},{20,28},{24,16},{28,20},{1,9},{5... | collective-permute-start | bytes 3145736 | tf_op jit(solution)/shard_map/ppermute | solution.py:1010
  342.9 25.6 %collective-permute-start.40 = (bf16[4,4,128,256]{3,2,1,0:T(8,128)(2,1)}, bf16[4,4,128,256]{3,2,1,0:T(8,128)(2,1)S(1)}, u32[]{:S(2)}, u32[]{:S(2)}) collective-permute-start(bf16[4,4,128,256]{3,2,1,0:T(8,128)(2,1)} %get-tuple-element.200), channel_id=1, source_target_pairs={{0,4},{4,0},{8,12},{12,8},{16,20},{20,16},{24,28},{28,24},{1,5},{5... | collective-permute-start | bytes 3145736 | tf_op jit(solution)/shard_map/ppermute | solution.py:1010
  366.6 15.1 %collective-permute-start.38 = (bf16[1,4,128,512]{3,2,1,0:T(8,128)(2,1)}, bf16[1,4,128,512]{3,2,1,0:T(8,128)(2,1)S(1)}, u32[]{:S(2)}, u32[]{:S(2)}) collective-permute-start(bf16[1,4,128,512]{3,2,1,0:T(8,128)(2,1)} %get-tuple-element.194), channel_id=1, source_target_pairs={{0,8},{4,12},{8,0},{12,4},{16,24},{20,28},{24,16},{28,20},{1,9},{5... | collective-permute-start | bytes 1572872 | tf_op jit(solution)/shard_map/ppermute | solution.py:1010
  367.7 15.0 %collective-permute-start.39 = (bf16[1,4,128,512]{3,2,1,0:T(8,128)(2,1)}, bf16[1,4,128,512]{3,2,1,0:T(8,128)(2,1)S(1)}, u32[]{:S(2)}, u32[]{:S(2)}) collective-permute-start(bf16[1,4,128,512]{3,2,1,0:T(8,128)(2,1)} %get-tuple-element.195), channel_id=1, source_target_pairs={{0,16},{4,20},{8,24},{12,28},{16,0},{20,4},{24,8},{28,12},{1,17},{... | collective-permute-start | bytes 1572872 | tf_op jit(solution)/shard_map/ppermute | solution.py:1010
  371.4 29.7 %collective-permute-start.41 = (bf16[2,4,128,256]{3,2,1,0:T(8,128)(2,1)}, bf16[2,4,128,256]{3,2,1,0:T(8,128)(2,1)S(1)}, u32[]{:S(2)}, u32[]{:S(2)}) collective-permute-start(bf16[2,4,128,256]{3,2,1,0:T(8,128)(2,1)} %add_rows.12), channel_id=1, source_target_pairs={{0,16},{4,20},{8,24},{12,28},{16,0},{20,4},{24,8},{28,12},{1,17},{... | collective-permute-start | bytes 1572872 | tf_op jit(solution)/shard_map/ppermute | solution.py:1010
  376.4 46.8 %all-to-all-start.5 = ((bf16[4,128,1024]{2,1,0:T(8,128)(2,1)}), bf16[4,128,1024]{2,1,0:T(8,128)(2,1)S(1)}, u32[]{:S(2)}, u32[]{:S(2)}) async-start(bf16[4,128,1024]{2,1,0:T(8,128)(2,1)} %add_cols.3), calls=%async_computation.5 | async-start | bytes 2097152 | tf_op jit(solution)/shard_map/all_to_all | solution.py:1006
  403.8 19.4 %collective-permute-start.42 = (bf16[1,4,128,256]{3,2,1,0:T(8,128)(2,1)}, bf16[1,4,128,256]{3,2,1,0:T(8,128)(2,1)S(1)}, u32[]{:S(2)}, u32[]{:S(2)}) collective-permute-start(bf16[1,4,128,256]{3,2,1,0:T(8,128)(2,1)} %add_rows.13), channel_id=1, source_target_pairs={{0,8},{4,12},{8,0},{12,4},{16,24},{20,28},{24,16},{28,20},{1,9},{5... | collective-permute-start | bytes 786440 | tf_op jit(solution)/shard_map/ppermute | solution.py:1010
  428.0 56.1 %all-to-all-start.6 = ((bf16[4,128,1280]{2,1,0:T(8,128)(2,1)}), bf16[4,128,1280]{2,1,0:T(8,128)(2,1)}, u32[]{:S(2)}, u32[]{:S(2)}) async-start(bf16[4,128,1280]{2,1,0:T(8,128)(2,1)} %add_cols.4), calls=%async_computation.6 | async-start | bytes 2621440 | tf_op jit(solution)/shard_map/all_to_all | solution.py:1006
  464.3 15.3 %collective-permute-start.46 = (bf16[4,4,128,768]{3,2,1,0:T(8,128)(2,1)}, bf16[4,4,128,768]{3,2,1,0:T(8,128)(2,1)S(1)}, u32[]{:S(2)}, u32[]{:S(2)}) collective-permute-start(bf16[4,4,128,768]{3,2,1,0:T(8,128)(2,1)} %get-tuple-element.220), channel_id=1, source_target_pairs={{0,4},{4,0},{8,12},{12,8},{16,20},{20,16},{24,28},{28,24},{1,5},{5... | collective-permute-start | bytes 9437192 | tf_op jit(solution)/shard_map/ppermute | solution.py:1010
  465.1 19.0 %collective-permute-start.43 = (f32[6016]{0:T(1024)S(1)}, f32[6016]{0:T(1024)S(1)}, u32[]{:S(2)}, u32[]{:S(2)}) collective-permute-start(f32[6016]{0:T(1024)S(1)} %get-tuple-element.321), channel_id=1, source_target_pairs={{0,1},{1,0},{2,3},{3,2},{4,5},{5,4},{6,7},{7,6},{8,9},{9,8},{10,11... | collective-permute-start | bytes 72200 | tf_op jit(solution)/shard_map/ppermute | solution.py:1189
  467.2 17.0 %collective-permute-start.44 = (f32[6016]{0:T(1024)S(1)}, f32[6016]{0:T(1024)S(1)}, u32[]{:S(2)}, u32[]{:S(2)}) collective-permute-start(f32[6016]{0:T(1024)S(1)} %get-tuple-element.320), channel_id=1, source_target_pairs={{0,2},{1,3},{2,0},{3,1},{4,6},{5,7},{6,4},{7,5},{8,10},{9,11},{10,... | collective-permute-start | bytes 72200 | tf_op jit(solution)/shard_map/ppermute | solution.py:1189
  469.5 14.6 %collective-permute-start.45 = (f32[6016]{0:T(1024)S(1)}, f32[6016]{0:T(1024)S(1)}, u32[]{:S(2)}, u32[]{:S(2)}) collective-permute-start(f32[6016]{0:T(1024)S(1)} %get-tuple-element.319), channel_id=1, source_target_pairs={{0,3},{1,2},{2,1},{3,0},{4,7},{5,6},{6,5},{7,4},{8,11},{9,10},{10,... | collective-permute-start | bytes 72200 | tf_op jit(solution)/shard_map/ppermute | solution.py:1189
  500.5 55.8 %all-to-all-start.7 = ((bf16[4,1088,256]{2,1,0:T(8,128)(2,1)}), bf16[4,1088,256]{2,1,0:T(8,128)(2,1)S(1)}, u32[]{:S(2)}, u32[]{:S(2)}) async-start(bf16[4,1088,256]{2,1,0:T(8,128)(2,1)} %input_back.1), calls=%async_computation.7 | async-start | bytes 4456448 | tf_op jit(solution)/shard_map/all_to_all | solution.py:1006
  505.5 19.0 %collective-permute-start.47 = (bf16[2,4,64,768]{3,2,1,0:T(8,128)(2,1)}, bf16[2,4,64,768]{3,2,1,0:T(8,128)(2,1)S(1)}, u32[]{:S(2)}, u32[]{:S(2)}) collective-permute-start(bf16[2,4,64,768]{3,2,1,0:T(8,128)(2,1)} %get-tuple-element.222), channel_id=1, source_target_pairs={{0,16},{4,20},{8,24},{12,28},{16,0},{20,4},{24,8},{28,12},{1,17},{... | collective-permute-start | bytes 2359304 | tf_op jit(solution)/shard_map/ppermute | solution.py:1010
  506.4 18.7 %collective-permute-start.48 = (bf16[2,4,64,768]{3,2,1,0:T(8,128)(2,1)}, bf16[2,4,64,768]{3,2,1,0:T(8,128)(2,1)S(1)}, u32[]{:S(2)}, u32[]{:S(2)}) collective-permute-start(bf16[2,4,64,768]{3,2,1,0:T(8,128)(2,1)} %get-tuple-element.223), channel_id=1, source_target_pairs={{0,8},{4,12},{8,0},{12,4},{16,24},{20,28},{24,16},{28,20},{1,9},{5... | collective-permute-start | bytes 2359304 | tf_op jit(solution)/shard_map/ppermute | solution.py:1010
  528.9 9.7 %collective-permute-start.49 = (bf16[1,4,64,768]{3,2,1,0:T(8,128)(2,1)}, bf16[1,4,64,768]{3,2,1,0:T(8,128)(2,1)S(1)}, u32[]{:S(2)}, u32[]{:S(2)}) collective-permute-start(bf16[1,4,64,768]{3,2,1,0:T(8,128)(2,1)} %get-tuple-element.227), channel_id=1, source_target_pairs={{0,8},{4,12},{8,0},{12,4},{16,24},{20,28},{24,16},{28,20},{1,9},{5... | collective-permute-start | bytes 1179656 | tf_op jit(solution)/shard_map/ppermute | solution.py:1010
  530.4 9.4 %collective-permute-start.50 = (bf16[1,4,64,768]{3,2,1,0:T(8,128)(2,1)}, bf16[1,4,64,768]{3,2,1,0:T(8,128)(2,1)S(1)}, u32[]{:S(2)}, u32[]{:S(2)}) collective-permute-start(bf16[1,4,64,768]{3,2,1,0:T(8,128)(2,1)} %get-tuple-element.228), channel_id=1, source_target_pairs={{0,16},{4,20},{8,24},{12,28},{16,0},{20,4},{24,8},{28,12},{1,17},{... | collective-permute-start | bytes 1179656 | tf_op jit(solution)/shard_map/ppermute | solution.py:1010
  557.7 25.0 %all-to-all-start.8 = ((bf16[4,128,768]{2,1,0:T(8,128)(2,1)}), bf16[4,128,768]{2,1,0:T(8,128)(2,1)S(1)}, u32[]{:S(2)}, u32[]{:S(2)}) async-start(bf16[4,128,768]{2,1,0:T(8,128)(2,1)} %add_cols.5), calls=%async_computation.8 | async-start | bytes 1572864 | tf_op jit(solution)/shard_map/all_to_all | solution.py:1006
  561.6 2.0 collective-permute-start.51
  563.6 4.2 collective-permute-start.52
  567.8 11.7 %collective-permute-start.53 = (f32[6528]{0:T(1024)S(1)}, f32[6528]{0:T(1024)S(1)}, u32[]{:S(2)}, u32[]{:S(2)}) collective-permute-start(f32[6528]{0:T(1024)S(1)} %add.57), channel_id=1, source_target_pairs={{0,16},{4,20},{8,24},{12,28},{16,0},{20,4},{24,8},{28,12},{1,17},{... | collective-permute-start | bytes 78344 | tf_op jit(solution)/shard_map/ppermute | solution.py:1010
  (60 other events, 683.9 us)
